TPU v7x, 32 devices: a whole 2x2x4 slice. The times are simulated.
32 devices in a mesh: dir: 2 (over x), slab: 8 (over z, y), tile: 2 (over core).
Axes of the slice: x: 2, y: 2, z: 4, core: 2. Of those that a mesh axis runs over, the one named last changes fastest.
Arguments:
- voxels: float32 [4, 64, 64, 512], P(None, 'slab', 'tile'), may hold values from -2.5 to 2.5
- offsets: int32 [2, 64, 512], P('dir', 'tile'), may hold values from 0 to 511
- heading: int32 [2, 64, 512], P('dir', 'tile'), may hold values from 0 to 1
- cotangent: float32 [2, 3, 64, 512], P('dir', None, 'tile'), may hold values from -6 to 6
Outputs:
- image: float32 [2, 3, 64, 512], P('dir', None, 'tile', 'slab')
- voxel_grad: float32 [4, 64, 64, 512], P(None, 'slab', 'tile', 'dir')
Inputs may be any that keep to these rules, and one draw needn't show every extreme that they name: `offsets`: A code packs three sub-cell positions as p + 8 * m + 8 * 8 * n (p along depth, m along rows, n along columns).
All inputs are finite; a program needn't handle non-finite values.
Results may differ from a plain program's by a relative error of at most 0.0003.
Values sent between devices are 32-bit elements; how exact they have to be, the bound alone decides.
No kernel may reach another device: no remote copies, remote signals or barrier semaphores. Data moves between devices by JAX's collectives and lax.ppermute only.
A program may use at most 64 MiB of HBM per device.

v0:
```python
import jax
import jax.numpy as jnp
from jax import lax
from jax.sharding import PartitionSpec as P

LEVELS = 8


def padded(block, sides, width):
    for axis, dim in sides:
        count = lax.axis_size(axis)
        forward = [(i, i + 1) for i in range(count - 1)]
        backward = [(target, source) for source, target in forward]
        low = lax.ppermute(
            lax.slice_in_dim(block, block.shape[dim] - width, None, axis=dim), axis, forward
        )
        high = lax.ppermute(lax.slice_in_dim(block, 0, width, axis=dim), axis, backward)
        block = jnp.concatenate([low, block, high], axis=dim)
    return block


def entering(array, axis, combine, identity, reverse):
    devices, position = (lax.axis_size(axis), lax.axis_index(axis))
    everything = lax.all_gather(array, axis)
    start = jnp.broadcast_to(jnp.asarray(identity, array.dtype), array.shape)

    def turn(k, before):
        at = devices - 1 - k if reverse else k
        reached = at > position if reverse else at < position
        new = combine(before, everything[at])
        return jnp.where(reached, new, before)

    return lax.fori_loop(0, devices, turn, start)


def tap_weights(codes):
    level = LEVELS
    fz = (codes % level).astype(jnp.float32)
    fy = (codes // level % level).astype(jnp.float32)
    fx = (codes // (level * level)).astype(jnp.float32)

    def three(raw):
        f = (raw + 0.5) / level - 0.5
        return (jnp.maximum(-f, 0.0), 1.0 - jnp.abs(f), jnp.maximum(f, 0.0))

    return (three(fz), three(fy), three(fx))


def combine_sum(earlier, later):
    return earlier + later


def per_device(voxels, offsets, heading, cotangent):
    planes, rows, total_cols = (voxels.shape[1], voxels.shape[2], voxels.shape[3])
    depth = planes * lax.axis_size("slab")
    scale = 2.0 / depth
    padded_grid = padded(voxels, (("slab", 1), ("tile", 2)), 1)
    padded_grid = jnp.pad(padded_grid, ((0, 0), (0, 0), (0, 0), (2, 2)))
    grid = padded_grid[:, :, :, 1 : total_cols + 3]
    forward = heading == 0
    wz, wy, wx = tap_weights(offsets)
    plane = None
    for b in range(3):
        for e in range(3):
            term = (wy[b] * wx[e])[:, None, None] * grid[
                None, :, :, b : b + rows, e : e + total_cols
            ]
            plane = term if plane is None else plane + term
    values = None
    for a in range(3):
        term = wz[a][:, None, None] * plane[:, :, a : a + planes]
        values = term if values is None else values + term
    sigma = jax.nn.softplus(values[:, 0]) * scale
    colour = jax.nn.sigmoid(values[:, 1:])
    alpha = 1.0 - jnp.exp(-sigma)
    ahead = jnp.cumsum(sigma, axis=1) - sigma
    depth_sum = jnp.sum(sigma, axis=1)
    local_front = jnp.where(forward[:, None], ahead, depth_sum[:, None] - ahead - sigma)
    glow = jnp.exp(-local_front) * alpha
    local_image = jnp.sum(glow[:, None] * colour, axis=2)
    zeros = jnp.zeros_like(depth_sum)
    lower = entering(depth_sum, "slab", combine_sum, zeros, False)
    higher = entering(depth_sum, "slab", combine_sum, zeros, True)
    before = jnp.where(forward, lower, higher)
    reach = jnp.exp(-before)
    parts = reach[:, None] * local_image
    image = lax.psum_scatter(parts, "slab", scatter_dimension=3, tiled=True)
    pull = cotangent * depth
    shade = jnp.sum(pull[:, :, None] * colour, axis=1)
    local_pull = jnp.sum(glow * shade, axis=1)
    weighted = reach * local_pull
    lead_low = entering(weighted, "slab", combine_sum, zeros, False)
    lead_high = entering(weighted, "slab", combine_sum, zeros, True)
    lead = jnp.where(forward, lead_low, lead_high)
    whole = lead_low + weighted + lead_high
    through = reach[:, None] * glow
    share = through * shade
    before_share = jnp.cumsum(share, axis=1) - share
    share_sum = jnp.sum(share, axis=1)
    ahead_share = lead[:, None] + jnp.where(
        forward[:, None], before_share, share_sum[:, None] - before_share - share
    )
    behind = whole[:, None] - ahead_share - share
    d_sigma = jnp.exp(-(before[:, None] + local_front + sigma)) * shade - behind
    grad_density = d_sigma * jax.nn.sigmoid(values[:, 0]) * scale
    grad_colour = pull[:, :, None] * through[:, None] * colour * (1.0 - colour)
    sample_grad = jnp.concatenate([grad_density[:, None], grad_colour], axis=1)
    spread = padded(sample_grad, (("slab", 2), ("tile", 3)), 1)
    spread = jnp.pad(spread, ((0, 0), (0, 0), (0, 0), (0, 0), (1, 1)))
    codes_wide = padded(offsets, (("tile", 1),), 1)
    codes_wide = jnp.pad(codes_wide, ((0, 0), (0, 0), (1, 1)))
    vz, vy, vx = tap_weights(codes_wide)
    column = None
    for a in range(3):
        term = vz[a][:, None, None] * spread[:, :, 2 - a : 2 - a + planes]
        column = term if column is None else column + term
    grad = None
    for b in range(3):
        for e in range(3):
            first = 2 - e
            factor = (vy[b] * vx[e])[:, 2 - b : 2 - b + rows, first : first + total_cols]
            term = (
                factor[:, None, None]
                * column[:, :, :, 2 - b : 2 - b + rows, first : first + total_cols]
            )
            grad = term if grad is None else grad + term
    grad = jnp.sum(grad, axis=0)
    voxel_grad = lax.psum_scatter(grad, "dir", scatter_dimension=3, tiled=True)
    return (image, voxel_grad)


def solution(mesh):
    return jax.shard_map(
        per_device,
        mesh=mesh,
        in_specs=(
            P(None, "slab", "tile", None),
            P("dir", "tile", None),
            P("dir", "tile", None),
            P("dir", None, "tile", None),
        ),
        out_specs=(P("dir", None, "tile", "slab"), P(None, "slab", "tile", "dir")),
        check_vma=False,
    )
```

profile of v0, /device:TPU:16, one launch (start us, length us, event | category | flops | bytes accessed | tf_op | source)
XLA Modules:
  0.0 237.2 jit_solution(1113083677197636403)
XLA Ops:
  7.2 2.0 fusion.97
  9.2 3.4 %collective-permute-start = (f32[4,1,32,512]{3,2,1,0:T(8,128)}, f32[4,1,32,512]{3,2,1,0:T(8,128)}, u32[]{:S(2)}, u32[]{:S(2)}) collective-permute-start(f32[4,1,32,512]{3,2,1,0:T(8,128)} %get-tuple-element.513), channel_id=1, source_target_pairs={{0,2},{2,4},{4,6},{6,8},{8,10},{10,12},{12,14},{1,3},{3,5},{5,7},{... | collective-permute-start | bytes 786440 | tf_op jit(solution)/shard_map/ppermute | solution.py:14
  12.6 3.3 %collective-permute-start.1 = (f32[4,1,32,512]{3,2,1,0:T(8,128)}, f32[4,1,32,512]{3,2,1,0:T(8,128)}, u32[]{:S(2)}, u32[]{:S(2)}) collective-permute-start(f32[4,1,32,512]{3,2,1,0:T(8,128)} %get-tuple-element.512), channel_id=1, source_target_pairs={{2,0},{4,2},{6,4},{8,6},{10,8},{12,10},{14,12},{3,1},{5,3},{7,5},{... | collective-permute-start | bytes 786440 | tf_op jit(solution)/shard_map/ppermute | solution.py:17
  16.7 1.3 collective-permute-start.4
  18.0 1.3 collective-permute-start.5
  19.3 1.0 maximum_bitcast_fusion.3
  21.2 1.6 multiply_bitcast_fusion.1
  24.1 1.0 constant_dynamic-update-slice_fusion.2
  26.0 1.0 constant_dynamic-update-slice_fusion
  27.1 2.0 collective-permute-start.2
  29.1 1.3 collective-permute-start.3
  30.4 1.2 negate_maximum_fusion
  32.2 1.9 select_maximum_fusion.5
  34.1 4.4 %fusion.5 = f32[1,4,10,32,512]{4,3,2,1,0:T(8,128)S(1)} fusion(f32[4,10,34,516]{3,2,1,0:T(8,128)S(1)} %select_maximum_fusion.5, f32[4,10,1,512]{3,2,1,0:T(1,128)S(1)} %collective-permute-done.3, f32[4,10,32,512]{3,2,1,0:T(8,128)S(1)} %constant_dynamic-update-slice_fusion, f32[4,10,1,512]{3,2,1,0:T(1,128)S(1)} %collective-permute-done.2, ...), kind=kLoop, calls=%fused_computation.24 | loop fusion | flops 12451840 | bytes 21725184 | tf_op jit(solution)/shard_map/add | solution.py:68
  39.6 27.1 %all-gather = f32[256,512]{1,0:T(8,128)S(1)} all-gather(f32[32,512]{1,0:T(8,128)S(1)} %fusion.47), channel_id=2, replica_groups=mesh['dir'=2,'slab'=8,'tile'=2] {'slab'}, dimensions={0}, use_global_device_ids=true | all-gather | bytes 589824 | tf_op jit(solution)/shard_map/all_gather | solution.py:24
  68.9 2.9 %multiply_reduce_fusion = (f32[8,32,512]{2,1,0:T(8,128)S(1)}, f32[3,32,512]{2,1,0:T(8,128)}, f32[1,3,8,32,512]{4,3,2,1,0:T(8,128)S(1)}) fusion(f32[3,32,512]{2,1,0:T(8,128)S(1)} %copy-done.10, f32[1,4,8,32,512]{4,3,2,1,0:T(8,128)} %copy-done, f32[8,32,512]{2,1,0:T(8,128)S(1)} %get-tuple-element.504, f32[8,32,512]{2,1,0:T(8,128)S(1)} %get-tuple-element.503), kind=kLoop, calls=%fused_computation.69 | loop fusion | flops 4145152 | bytes 5111808 | tf_op jit(solution)/shard_map/reduce_sum | solution.py:89
  71.8 2.2 multiply_reduce_fusion.3
  74.1 33.7 %all-gather.1 = f32[8,32,512]{2,1,0:T(8,128)S(1)} all-gather(f32[1,32,512]{2,1,0:T(8,128)S(1)} %bitcast_multiply_fusion.4), channel_id=3, replica_groups=mesh['dir'=2,'slab'=8,'tile'=2] {'slab'}, dimensions={0}, use_global_device_ids=true | all-gather | bytes 589824 | tf_op jit(solution)/shard_map/all_gather | solution.py:24
  108.7 2.7 %fusion.38 = f32[1,1,8,32,512]{4,3,2,1,0:T(8,128)S(1)} fusion(f32[8,32,512]{2,1,0:T(8,128)S(1)} %get-tuple-element.462, f32[1,8,32,512]{3,2,1,0:T(8,128)S(1)} %fusion.45, f32[1,4,8,32,512]{4,3,2,1,0:T(8,128)} %copy-done, f32[32,512]{1,0:T(8,128)} %get-tuple-element.461, f32[32,512]{1,0:T(8,128)S(1)} %get-tuple-element.498, ...), kind=kOutput, calls=%fused_computation.89 | output fusion | flops 7602176 | bytes 4227072 | tf_op jit(solution)/shard_map/jit(cumsum)/reduce_window_sum | solution.py:98
  111.4 4.2 %collective-permute-start.6 = (f32[1,4,1,32,512]{4,3,2,1,0:T(8,128)S(1)}, f32[1,4,1,32,512]{4,3,2,1,0:T(8,128)S(1)}, u32[]{:S(2)}, u32[]{:S(2)}) collective-permute-start(f32[1,4,1,32,512]{4,3,2,1,0:T(8,128)S(1)} %get-tuple-element.510), channel_id=1, source_target_pairs={{0,2},{2,4},{4,6},{6,8},{8,10},{10,12},{12,14},{1,3},{3,5},{5,7},{... | collective-permute-start | bytes 786440 | tf_op jit(solution)/shard_map/ppermute | solution.py:14
  115.6 3.9 %collective-permute-start.7 = (f32[1,4,1,32,512]{4,3,2,1,0:T(8,128)S(1)}, f32[1,4,1,32,512]{4,3,2,1,0:T(8,128)S(1)}, u32[]{:S(2)}, u32[]{:S(2)}) collective-permute-start(f32[1,4,1,32,512]{4,3,2,1,0:T(8,128)S(1)} %get-tuple-element.511), channel_id=1, source_target_pairs={{2,0},{4,2},{6,4},{8,6},{10,8},{12,10},{14,12},{3,1},{5,3},{7,5},{... | collective-permute-start | bytes 786440 | tf_op jit(solution)/shard_map/ppermute | solution.py:17
  119.6 1.0 fusion.86
  120.6 1.4 collective-permute-done.6
  122.0 2.7 %collective-permute-done.7 = f32[1,4,1,32,512]{4,3,2,1,0:T(8,128)S(1)} collective-permute-done((f32[1,4,1,32,512]{4,3,2,1,0:T(8,128)S(1)}, f32[1,4,1,32,512]{4,3,2,1,0:T(8,128)S(1)}, u32[]{:S(2)}, u32[]{:S(2)}) %collective-permute-start.7) | collective-permute-done | bytes 262176 | tf_op jit(solution)/shard_map/ppermute | solution.py:17
  125.5 1.9 collective-permute-start.8
  127.4 1.5 collective-permute-start.9
  129.6 1.4 copy.10
  131.0 1.1 reshape.314
  132.2 4.3 %select_maximum_fusion = f32[1,4,10,34,514]{4,3,2,1,0:T(8,128)S(1)} fusion(f32[1,4,10,1,512]{4,3,2,1,0:T(1,128)} %collective-permute-done.9, f32[1,4,10,1,512]{4,3,2,1,0:T(1,128)} %collective-permute-done.8, f32[1,4,1,32,512]{4,3,2,1,0:T(8,128)} %copy-done.4, f32[1,4,1,32,512]{4,3,2,1,0:T(8,128)S(1)} %copy-done.3, ...), kind=kLoop, calls=%fused_computation.8 | loop fusion | flops 9786560 | bytes 5581440 | tf_op jit(solution)/shard_map/concatenate | solution.py:18
  137.6 4.4 %fusion.16 = f32[4,8,32,512]{3,2,1,0:T(8,128)} fusion(f32[1,4,8,34,514]{4,3,2,1,0:T(8,128)S(1)} %fusion.2, f32[32,512]{1,0:T(8,128)S(1)} %copy-done.17, f32[32,512]{1,0:T(8,128)S(1)} %copy-done.19, f32[32,512]{1,0:T(8,128)S(1)} %copy-done.18, f32[32,512]{1,0:T(8,128)S(1)} %copy-done.22, f32[32,512]{1,0:T(8,128)S(1)} %copy-done.21, ...), kind=kLoop, calls=%fused_computation.43 | loop fusion | flops 8912896 | bytes 21561344 | tf_op jit(solution)/shard_map/reduce_sum | solution.py:127
  142.0 53.6 %reduce-scatter.7.cloned.1.call-done = f32[64,96]{1,0:T(8,128)} async-done(((f32[512,96]{1,0:T(8,128)}), f32[64,96]{1,0:T(8,128)}) %reduce-scatter.7.cloned.1.call-update) | async-done | bytes 24592
  197.2 33.2 %reduce-scatter.5.cloned.1.call-done = f32[4,8,32,256]{3,2,1,0:T(8,128)} async-done(((f32[4,8,32,512]{3,2,1,0:T(8,128)}), f32[4,8,32,256]{3,2,1,0:T(8,128)}) %reduce-scatter.5.cloned.1.call-update) | async-done | bytes 1048592 | tf_op jit(solution)/shard_map/reduce_scatter | solution.py:128
  (119 shorter events, 13.3 us)
Async XLA Ops:
  7.2 17.9 %copy-start.1 = (f32[4,8,32,512]{3,2,1,0:T(8,128)S(1)}, f32[4,8,32,512]{3,2,1,0:T(8,128)}, u32[]{:S(2)}) copy-start(f32[4,8,32,512]{3,2,1,0:T(8,128)} %param.12) | copy-start | bytes 6291460
  7.2 188.4 %reduce-scatter.7.cloned.1.call-start = ((), (), s32[]{:S(2)}) async-start(), calls=%async_computation.3 | async-start | bytes 294912
  9.2 14.9 %collective-permute-start = (f32[4,1,32,512]{3,2,1,0:T(8,128)}, f32[4,1,32,512]{3,2,1,0:T(8,128)}, u32[]{:S(2)}, u32[]{:S(2)}) collective-permute-start(f32[4,1,32,512]{3,2,1,0:T(8,128)} %get-tuple-element.513), channel_id=1, source_target_pairs={{0,2},{2,4},{4,6},{6,8},{8,10},{10,12},{12,14},{1,3},{3,5},{5,7},{... | collective-permute-start | bytes 786440 | tf_op jit(solution)/shard_map/ppermute | solution.py:14
  12.6 13.3 %collective-permute-start.1 = (f32[4,1,32,512]{3,2,1,0:T(8,128)}, f32[4,1,32,512]{3,2,1,0:T(8,128)}, u32[]{:S(2)}, u32[]{:S(2)}) collective-permute-start(f32[4,1,32,512]{3,2,1,0:T(8,128)} %get-tuple-element.512), channel_id=1, source_target_pairs={{2,0},{4,2},{6,4},{8,6},{10,8},{12,10},{14,12},{3,1},{5,3},{7,5},{... | collective-permute-start | bytes 786440 | tf_op jit(solution)/shard_map/ppermute | solution.py:17
  16.7 6.2 %collective-permute-start.4 = (s32[1,1,512]{2,1,0:T(1,128)S(1)}, s32[1,1,512]{2,1,0:T(1,128)S(1)}, u32[]{:S(2)}, u32[]{:S(2)}) collective-permute-start(s32[1,1,512]{2,1,0:T(1,128)S(1)} %get-tuple-element.543), channel_id=1, source_target_pairs={{0,1},{2,3},{4,5},{6,7},{8,9},{10,11},{12,13},{14,15},{16,17},{18,... | collective-permute-start | bytes 6152 | tf_op jit(solution)/shard_map/ppermute | solution.py:14
  18.0 4.9 %collective-permute-start.5 = (s32[1,1,512]{2,1,0:T(1,128)S(1)}, s32[1,1,512]{2,1,0:T(1,128)S(1)}, u32[]{:S(2)}, u32[]{:S(2)}) collective-permute-start(s32[1,1,512]{2,1,0:T(1,128)S(1)} %get-tuple-element.544), channel_id=1, source_target_pairs={{1,0},{3,2},{5,4},{7,6},{9,8},{11,10},{13,12},{15,14},{17,16},{19,... | collective-permute-start | bytes 6152 | tf_op jit(solution)/shard_map/ppermute | solution.py:17
  27.1 4.5 %collective-permute-start.2 = (f32[4,10,1,512]{3,2,1,0:T(1,128)S(1)}, f32[4,10,1,512]{3,2,1,0:T(1,128)S(1)}, u32[]{:S(2)}, u32[]{:S(2)}) collective-permute-start(f32[4,10,1,512]{3,2,1,0:T(1,128)S(1)} %get-tuple-element.507), channel_id=1, source_target_pairs={{0,1},{2,3},{4,5},{6,7},{8,9},{10,11},{12,13},{14,15},{16,17},{18,... | collective-permute-start | bytes 245768 | tf_op jit(solution)/shard_map/ppermute | solution.py:14
  29.1 3.2 %collective-permute-start.3 = (f32[4,10,1,512]{3,2,1,0:T(1,128)S(1)}, f32[4,10,1,512]{3,2,1,0:T(1,128)S(1)}, u32[]{:S(2)}, u32[]{:S(2)}) collective-permute-start(f32[4,10,1,512]{3,2,1,0:T(1,128)S(1)} %get-tuple-element.508), channel_id=1, source_target_pairs={{1,0},{3,2},{5,4},{7,6},{9,8},{11,10},{13,12},{15,14},{17,16},{19,... | collective-permute-start | bytes 245768 | tf_op jit(solution)/shard_map/ppermute | solution.py:17
  38.9 30.0 %copy-start = (f32[1,4,8,32,512]{4,3,2,1,0:T(8,128)}, f32[1,4,8,32,512]{4,3,2,1,0:T(8,128)S(1)}, u32[]{:S(2)}) copy-start(f32[1,4,8,32,512]{4,3,2,1,0:T(8,128)S(1)} %fusion.24) | copy-start | bytes 6291460
  67.5 1.5 copy-start.10
  68.4 5.7 %copy-start.11 = (f32[1,32,512]{2,1,0:T(8,128)}, f32[1,32,512]{2,1,0:T(8,128)S(1)}, u32[]{:S(2)}) copy-start(f32[1,32,512]{2,1,0:T(8,128)S(1)} %get-tuple-element.499) | copy-start | bytes 196612
  74.1 34.5 %copy-start.12 = (f32[1,32,512]{2,1,0:T(8,128)S(1)}, f32[1,32,512]{2,1,0:T(8,128)}, u32[]{:S(2)}) copy-start(f32[1,32,512]{2,1,0:T(8,128)} %copy-done.11) | copy-start | bytes 196612
  108.6 10.9 %copy-start.13 = (f32[1,34,514]{2,1,0:T(8,128)S(1)}, f32[1,34,514]{2,1,0:T(8,128)}, u32[]{:S(2)}) copy-start(f32[1,34,514]{2,1,0:T(8,128)} %get-tuple-element.541) | copy-start | bytes 209716
  108.6 10.9 %copy-start.5 = (f32[1,34,514]{2,1,0:T(8,128)S(1)}, f32[1,34,514]{2,1,0:T(8,128)}, u32[]{:S(2)}) copy-start(f32[1,34,514]{2,1,0:T(8,128)} %get-tuple-element.535) | copy-start | bytes 209716
  108.6 10.9 %copy-start.6 = (f32[1,34,514]{2,1,0:T(8,128)S(1)}, f32[1,34,514]{2,1,0:T(8,128)}, u32[]{:S(2)}) copy-start(f32[1,34,514]{2,1,0:T(8,128)} %get-tuple-element.538) | copy-start | bytes 209716
  108.6 10.9 %copy-start.7 = (f32[1,34,514]{2,1,0:T(8,128)S(1)}, f32[1,34,514]{2,1,0:T(8,128)}, u32[]{:S(2)}) copy-start(f32[1,34,514]{2,1,0:T(8,128)} %get-tuple-element.539) | copy-start | bytes 209716
  108.6 10.9 %copy-start.8 = (f32[1,34,514]{2,1,0:T(8,128)S(1)}, f32[1,34,514]{2,1,0:T(8,128)}, u32[]{:S(2)}) copy-start(f32[1,34,514]{2,1,0:T(8,128)} %get-tuple-element.540) | copy-start | bytes 209716
  111.4 17.6 %copy-start.9 = (f32[3,32,512]{2,1,0:T(8,128)S(1)}, f32[3,32,512]{2,1,0:T(8,128)}, u32[]{:S(2)}) copy-start(f32[3,32,512]{2,1,0:T(8,128)} %get-tuple-element.463) | copy-start | bytes 589828
  111.4 10.6 %collective-permute-start.6 = (f32[1,4,1,32,512]{4,3,2,1,0:T(8,128)S(1)}, f32[1,4,1,32,512]{4,3,2,1,0:T(8,128)S(1)}, u32[]{:S(2)}, u32[]{:S(2)}) collective-permute-start(f32[1,4,1,32,512]{4,3,2,1,0:T(8,128)S(1)} %get-tuple-element.510), channel_id=1, source_target_pairs={{0,2},{2,4},{4,6},{6,8},{8,10},{10,12},{12,14},{1,3},{3,5},{5,7},{... | collective-permute-start | bytes 786440 | tf_op jit(solution)/shard_map/ppermute | solution.py:14
  115.6 9.1 %collective-permute-start.7 = (f32[1,4,1,32,512]{4,3,2,1,0:T(8,128)S(1)}, f32[1,4,1,32,512]{4,3,2,1,0:T(8,128)S(1)}, u32[]{:S(2)}, u32[]{:S(2)}) collective-permute-start(f32[1,4,1,32,512]{4,3,2,1,0:T(8,128)S(1)} %get-tuple-element.511), channel_id=1, source_target_pairs={{2,0},{4,2},{6,4},{8,6},{10,8},{12,10},{14,12},{3,1},{5,3},{7,5},{... | collective-permute-start | bytes 786440 | tf_op jit(solution)/shard_map/ppermute | solution.py:17
  122.0 6.9 %copy-start.2 = (f32[1,4,1,32,512]{4,3,2,1,0:T(8,128)}, f32[1,4,1,32,512]{4,3,2,1,0:T(8,128)S(1)}, u32[]{:S(2)}) copy-start(f32[1,4,1,32,512]{4,3,2,1,0:T(8,128)S(1)} %collective-permute-done.6) | copy-start | bytes 786436
  124.7 4.2 %copy-start.4 = (f32[1,4,1,32,512]{4,3,2,1,0:T(8,128)}, f32[1,4,1,32,512]{4,3,2,1,0:T(8,128)S(1)}, u32[]{:S(2)}) copy-start(f32[1,4,1,32,512]{4,3,2,1,0:T(8,128)S(1)} %collective-permute-done.7) | copy-start | bytes 786436
  125.5 6.7 %collective-permute-start.8 = (f32[1,4,10,1,512]{4,3,2,1,0:T(1,128)}, f32[1,4,10,1,512]{4,3,2,1,0:T(1,128)}, u32[]{:S(2)}, u32[]{:S(2)}) collective-permute-start(f32[1,4,10,1,512]{4,3,2,1,0:T(1,128)} %get-tuple-element.505), channel_id=1, source_target_pairs={{0,1},{2,3},{4,5},{6,7},{8,9},{10,11},{12,13},{14,15},{16,17},{18,... | collective-permute-start | bytes 245768 | tf_op jit(solution)/shard_map/ppermute | solution.py:14
  127.4 4.8 %collective-permute-start.9 = (f32[1,4,10,1,512]{4,3,2,1,0:T(1,128)}, f32[1,4,10,1,512]{4,3,2,1,0:T(1,128)}, u32[]{:S(2)}, u32[]{:S(2)}) collective-permute-start(f32[1,4,10,1,512]{4,3,2,1,0:T(1,128)} %get-tuple-element.506), channel_id=1, source_target_pairs={{1,0},{3,2},{5,4},{7,6},{9,8},{11,10},{13,12},{15,14},{17,16},{19,... | collective-permute-start | bytes 245768 | tf_op jit(solution)/shard_map/ppermute | solution.py:17
  129.6 2.6 %copy-start.3 = (f32[1,4,1,32,512]{4,3,2,1,0:T(8,128)S(1)}, f32[1,4,1,32,512]{4,3,2,1,0:T(8,128)}, u32[]{:S(2)}) copy-start(f32[1,4,1,32,512]{4,3,2,1,0:T(8,128)} %copy-done.2) | copy-start | bytes 786436
  132.1 4.4 %copy-start.14 = (f32[34,514]{1,0:T(8,128)S(1)}, f32[34,514]{1,0:T(8,128)}, u32[]{:S(2)}) copy-start(f32[34,514]{1,0:T(8,128)} %get-tuple-element.536) | copy-start | bytes 209716
  132.1 4.4 %copy-start.15 = (f32[34,514]{1,0:T(8,128)S(1)}, f32[34,514]{1,0:T(8,128)}, u32[]{:S(2)}) copy-start(f32[34,514]{1,0:T(8,128)} %get-tuple-element.537) | copy-start | bytes 209716
  132.1 4.4 %copy-start.16 = (f32[34,514]{1,0:T(8,128)S(1)}, f32[34,514]{1,0:T(8,128)}, u32[]{:S(2)}) copy-start(f32[34,514]{1,0:T(8,128)} %get-tuple-element.542) | copy-start | bytes 209716
  132.2 98.2 %reduce-scatter.5.cloned.1.call-start = ((), (), s32[]{:S(2)}) async-start(), calls=%async_computation.2 | async-start | bytes 3145728 | tf_op jit(solution)/shard_map/reduce_scatter | solution.py:128
  136.6 0.9 copy-start.21
  136.6 1.0 copy-start.22
  136.6 1.0 copy-start.23
  (4 other events, 3.5 us)
Sparse Core Ops, SparseCore 0:
  132.2 63.2 reduce-scatter.6
  198.4 31.9 reduce-scatter.4
where the time goes:
time: 240 us; the launch traced here: 237 us
  waiting for transfers between devices  92.7 us (39%)
  blocking collectives  60.9 us (25%)
  other arithmetic  34.4 us (14%)
  starting transfers between devices  24.1 us (10%)
  between operations  14.6 us (6%)
  local copies, waits for them, and re-layouts  9.54 us (4%)
    all_gather x2, blocking collectives, entering(): everything = lax.all_gather(array, axis)  60.9 us
    unnamed x3, waiting for transfers between devices  53.6 us
    reduce_scatter x1, waiting for transfers between devices, per_device(): voxel_grad = lax.psum_scatter(grad, 'dir', scatter_dimension=3, tiled=True)  33.2 us
    ppermute x5, starting transfers between devices, padded(): lax.ppermute(lax.slice_in_dim(block, block.shape[dim] - width, None, axis...  12.8 us
    ppermute x5, starting transfers between devices, padded(): lax.ppermute(lax.slice_in_dim(block, 0, width, axis=dim), axis, backward)  11.3 us
    concatenate x3, other arithmetic, padded(): block = jnp.concatenate([low, block, high], axis=dim)  7 us
    unnamed x54, local copies, waits for them, and re-layouts  5.7 us
  transfers between devices with their start and end apart: 12, of which 7 were waited for; matrix products, arithmetic and copies ran while one was open for 9% of the time, Pallas kernels for 0%

commit v1 on v0

v1 whole, which is shorter than its diff:
```python
import functools

import jax
import jax.numpy as jnp
from jax import lax
from jax.experimental import pallas as pl
from jax.experimental.pallas import tpu as pltpu
from jax.sharding import PartitionSpec as P

LEVELS = 8
BITS = LEVELS.bit_length() - 1
LANES = 128
SUB = 8
F32 = jnp.float32
VMEM = pl.BlockSpec(memory_space=pltpu.VMEM)
SMEM = pl.BlockSpec(memory_space=pltpu.SMEM)


def call(body, outs, scratch=(), aliases=None, flops=10**7, inputs=(), name=None):
    return pl.pallas_call(
        body,
        out_shape=outs,
        in_specs=list(inputs),
        out_specs=jax.tree.map(lambda _: VMEM, outs),
        scratch_shapes=list(scratch),
        input_output_aliases=aliases or {},
        cost_estimate=pl.CostEstimate(
            flops=flops, bytes_accessed=4 * 10**6, transcendentals=0
        ),
        compiler_params=pltpu.CompilerParams(vmem_limit_bytes=56 * 2**20),
        name=name,
    )


def shape(*dims):
    return jax.ShapeDtypeStruct(dims, F32)


def iota(dims, axis):
    return lax.broadcasted_iota(jnp.int32, dims, axis)


def three(raw):
    f = (raw.astype(F32) + 0.5) / LEVELS - 0.5
    return (jnp.maximum(-f, 0.0), 1.0 - jnp.abs(f), jnp.maximum(f, 0.0))


def taps_z(code):
    return three(code.astype(jnp.int32) & (LEVELS - 1))


def taps_yx(code):
    q = code.astype(jnp.int32)
    return (three((q >> BITS) & (LEVELS - 1)), three(q >> (2 * BITS)))


def message_rows(channels, rows, width):
    tiles = channels * (width // LANES)
    extra = -(-tiles // SUB) * SUB
    return tiles * rows, tiles * rows + extra, tiles * rows + extra + rows


def edge_column(tile, h):
    return jnp.where(h == 0, tile[:, :1], tile[:, LANES - 1 :])


def pack_body(info, first, last, second, penult, beside, a1, b1, a2, b2, *, width):
    h, _, s = (info[0], info[1], info[2])
    even = s % 2 == 0
    channels, _, rows, _ = first.shape
    tiles = width // LANES
    at_row, at_edge, _ = message_rows(channels, rows, width)
    planes = beside.shape[1]
    lane = iota((rows, LANES), 1)
    base = pl.multiple_of(h * width, LANES)
    side = pl.multiple_of(width - LANES * h, LANES)
    jobs = (
        (a1, last, planes - 1, first, 0),
        (b1, first, 0, last, planes - 1),
        (a2, penult, planes - 2, second, 1),
        (b2, second, 1, penult, planes - 2),
    )
    for out, when_even, k_even, when_odd, k_odd in jobs:

        def fill(block, k, out=out):
            edge = jnp.zeros((rows, LANES), F32)
            for c in range(channels):
                for j in range(tiles):
                    at = c * tiles + j
                    cols = pl.ds(base + j * LANES, LANES)
                    out[at * rows : (at + 1) * rows, :] = block[c, 0, :, cols]
                    out[at_row + at : at_row + at + 1, :] = beside[c, k : k + 1, cols]
                column = edge_column(block[c, 0, :, pl.ds(side, LANES)], h)
                corner = edge_column(beside[c, k : k + 1, pl.ds(side, LANES)], h)
                edge = jnp.where(lane == c, column, edge)
                edge = jnp.where(lane == channels + c, corner, edge)
            out[at_edge : at_edge + rows, :] = edge

        @pl.when(even)
        def _():
            fill(when_even, k_even)

        @pl.when(jnp.logical_not(even))
        def _():
            fill(when_odd, k_odd)


def shifts(window, column, h):
    dims = window.shape
    width = dims[1]
    lane = iota(dims, 1)
    left = jnp.where(h == 1, column, 0.0)
    right = jnp.where(h == 0, column, 0.0)
    minus = jnp.where(lane == 0, left, pltpu.roll(window, 1, 1))
    plus = jnp.where(lane == width - 1, right, pltpu.roll(window, width - 1, 1))
    return (minus, window, plus)


def spread_message(msg, grid, plane, h, channels, rows, width):
    tiles = width // LANES
    at_row, at_edge, _ = message_rows(channels, rows, width)
    edge = msg[at_edge : at_edge + rows, :]
    for c in range(channels):
        first = c * tiles
        window = jnp.concatenate(
            [msg[(first + j) * rows : (first + j + 1) * rows, :] for j in range(tiles)],
            axis=1,
        )
        beyond = jnp.concatenate(
            [msg[at_row + first + j : at_row + first + j + 1, :] for j in range(tiles)],
            axis=1,
        )
        beyond = jnp.broadcast_to(beyond, (SUB, width))
        corner = edge[:SUB, channels + c : channels + c + 1]
        for e, x in enumerate(shifts(window, edge[:, c : c + 1], h)):
            grid[e, c, plane, SUB : SUB + rows, :] = x
        for e, x in enumerate(shifts(beyond, corner, h)):
            grid[e, c, plane, 0:SUB, :] = x
            grid[e, c, plane, SUB + rows : 2 * SUB + rows, :] = x


def bilinear_weights(code, row0, t, rows):
    dims = code.shape
    wy, wx = taps_yx(code)
    row = iota(dims, 0) + row0
    low = jnp.where((row == 0) & (t == 0), 0.0, wy[0])
    high = jnp.where((row == rows - 1) & (t == 1), 0.0, wy[2])
    return [[y * x for x in wx] for y in (low, wy[1], high)]


def bilinear(weights, grid, c, plane, row0, cols):
    total = [None for _ in weights]
    for b in range(3):
        for e in range(3):
            v = grid[e, c, plane, row0 + b + SUB - 1 : row0 + b + 2 * SUB - 1, cols]
            for q, w in enumerate(weights):
                term = w[b][e] * v
                total[q] = term if total[q] is None else total[q] + term
    return total


def logistic(v):
    return 0.5 * jnp.tanh(0.5 * v) + 0.5


def forward_body(info, vox, beside, zlo, zhi, own, other, pay, vals, ends, grid, *, width, scale):
    h, t, s = (info[0], info[1], info[2])
    channels, planes, rows, _ = vox.shape
    base = pl.multiple_of(h * width, LANES)
    side = pl.multiple_of(width - LANES * h, LANES)
    even = s % 2 == 0
    rays = (own, other)

    def place(at, carry):
        c = at // planes
        k = at % planes
        window = vox[c, k, :, pl.ds(base, width)]
        column = edge_column(vox[c, k, :, pl.ds(side, LANES)], h)
        for e, x in enumerate(shifts(window, column, h)):
            grid[e, c, k + 1, SUB : SUB + rows, :] = x
        return carry

    lax.fori_loop(0, channels * planes, place, 0)
    for c in range(channels):
        window = beside[c, :, pl.ds(base, width)]
        column = edge_column(beside[c, :, pl.ds(side, LANES)], h)
        for e, x in enumerate(shifts(window, column, h)):
            for k in range(planes):
                grid[e, c, k + 1, SUB - 1 : SUB, :] = x[k : k + 1]
                grid[e, c, k + 1, SUB + rows : SUB + rows + 1, :] = x[k : k + 1]
    spread_message(zlo, grid, jnp.where(even, planes + 1, 0), h, channels, rows, width)
    spread_message(zhi, grid, jnp.where(even, 0, planes + 1), h, channels, rows, width)

    for i in range(rows // SUB):
        for j in range(width // LANES):
            row0 = i * SUB
            cols = slice(j * LANES, (j + 1) * LANES)
            codes = [r[0, row0 : row0 + SUB, cols] for r in rays]
            weights = [bilinear_weights(q, row0, t, rows) for q in codes]
            wz = [taps_z(q) for q in codes]

            def channel(c, carry, row0=row0, cols=cols, weights=weights, wz=wz):
                old = [None, None]
                for p in range(planes + 2):
                    new = bilinear(weights, grid, c, p, row0, cols)
                    for q in range(2):
                        if p == 1:
                            ends[q, c, 0, row0 : row0 + SUB, cols] = (
                                wz[q][1] * old[1][q] + wz[q][2] * new[q]
                            )
                        if p == planes + 1:
                            ends[q, c, 1, row0 : row0 + SUB, cols] = (
                                wz[q][0] * old[1][q] + wz[q][1] * new[q]
                            )
                        if p >= 2:
                            vals[q, c, p - 2, row0 : row0 + SUB, cols] = (
                                wz[q][0] * old[0][q]
                                + wz[q][1] * old[1][q]
                                + wz[q][2] * new[q]
                            )
                    old = [old[1], new]
                return carry

            lax.fori_loop(0, channels, channel, 0)

    tiles = width // LANES
    for q in range(2):

        def shade(at, carry, q=q):
            row = pl.ds(pl.multiple_of((at // tiles) * SUB, SUB), SUB)
            col = pl.ds(pl.multiple_of((at % tiles) * LANES, LANES), LANES)
            ahead = rays[q][1, row, col] == 0.0
            sigma = []
            for k in range(planes):
                v = vals[q, 0, k, row, col]
                sigma.append((jnp.maximum(v, 0.0) + jnp.log(1.0 + jnp.exp(-jnp.abs(v)))) * scale)
            total = functools.reduce(lambda a, b: a + b, sigma)
            run = jnp.zeros_like(total)
            light = [jnp.zeros_like(total) for _ in range(channels - 1)]
            for k in range(planes):
                front = jnp.where(ahead, run, total - run - sigma[k])
                glow = jnp.exp(-front) * (1.0 - jnp.exp(-sigma[k]))
                for c in range(channels - 1):
                    light[c] = light[c] + glow * logistic(vals[q, c + 1, k, row, col])
                run = run + sigma[k]
            pay[0, q, row, col] = total
            for c in range(channels - 1):
                pay[c + 1, q, row, col] = light[c]
            return carry

        lax.fori_loop(0, (rows // SUB) * tiles, shade, 0)


def column_body(info, zlo, zhi, own, other, vals, ends, out, grid, edge, *, width, scale, slabs):
    h, t, s = (info[0], info[1], info[2])
    _, channels, planes, rows, _ = vals.shape
    even = s % 2 == 0
    rays = (own, other)
    tiles = width // LANES
    spread_message(zlo, grid, jnp.where(even, 1, 0), h, channels, rows, width)
    spread_message(zhi, grid, jnp.where(even, 0, 1), h, channels, rows, width)
    for i in range(rows // SUB):
        for j in range(tiles):
            row0 = i * SUB
            cols = slice(j * LANES, (j + 1) * LANES)
            codes = [r[0, row0 : row0 + SUB, cols] for r in rays]
            weights = [bilinear_weights(q, row0, t, rows) for q in codes]
            wz = [taps_z(q) for q in codes]

            def channel(c, carry, row0=row0, cols=cols, weights=weights, wz=wz):
                at = slice(row0, row0 + SUB)
                for p in range(2):
                    new = bilinear(weights, grid, c, p, row0, cols)
                    for q in range(2):
                        edge[q, c, p, at, cols] = ends[q, c, p, at, cols] + wz[q][2 * p] * new[q]
                return carry

            lax.fori_loop(0, channels, channel, 0)

    for q in range(2):

        def shade(at, carry, q=q):
            row = pl.ds(pl.multiple_of((at // tiles) * SUB, SUB), SUB)
            col = pl.ds(pl.multiple_of((at % tiles) * LANES, LANES), LANES)
            ahead = rays[q][1, row, col] == 0.0
            wz = taps_z(rays[q][0, row, col])
            pull = [rays[q][2 + c, row, col] for c in range(channels - 1)]
            live = {-1: jnp.where(s > 0, 1.0, 0.0), planes: jnp.where(s < slabs - 1, 1.0, 0.0)}

            def value(c, k):
                if k < 0:
                    return edge[q, c, 0, row, col]
                if k == planes:
                    return edge[q, c, 1, row, col]
                return vals[q, c, k, row, col]

            ks = range(-1, planes + 1)
            sigma, slope = ({}, {})
            for k in ks:
                v = value(0, k)
                u = jnp.exp(-jnp.abs(v))
                sigma[k] = (jnp.maximum(v, 0.0) + jnp.log(1.0 + u)) * scale
                slope[k] = logistic(v) * scale
                if k in live:
                    slope[k] = slope[k] * live[k]
            total = functools.reduce(lambda a, b: a + b, [sigma[k] for k in range(planes)])
            run = -sigma[-1]
            share, after = ({}, {})
            tint = [{} for _ in range(channels - 1)]
            for k in ks:
                front = jnp.where(ahead, run, total - run - sigma[k])
                reach = jnp.exp(-front)
                left = jnp.exp(-sigma[k])
                glow = reach * (1.0 - left)
                if k in live:
                    glow = glow * live[k]
                hue = None
                for c in range(channels - 1):
                    colour = logistic(value(c + 1, k))
                    term = pull[c] * colour
                    hue = term if hue is None else hue + term
                    tint[c][k] = glow * term * (1.0 - colour)
                share[k] = glow * hue
                after[k] = reach * left * hue
                run = run + sigma[k]
            whole = functools.reduce(lambda a, b: a + b, [share[k] for k in range(planes)])
            run = -share[-1]
            pushed = {}
            for k in ks:
                before = jnp.where(ahead, run, whole - run - share[k])
                pushed[k] = (after[k] + before + share[k]) * slope[k]
                run = run + share[k]
            for at, field in enumerate([pushed, slope] + tint):
                for p in range(planes):
                    out[at, q, p, row, col] = (
                        wz[2] * field[p - 1] + wz[1] * field[p] + wz[0] * field[p + 1]
                    )
            return carry

        lax.fori_loop(0, (rows // SUB) * tiles, shade, 0)


def scatter_body(info, cols5, own, other, reach, rest, grad, ymsg, xmsg, weights, *, channels):
    h, t = (info[0], info[1])
    _, _, planes, rows, width = cols5.shape
    lane = iota((rows, width), 1)
    row = iota((rows, width), 0)
    tall = rows + SUB
    lane_tall = iota((tall, width), 1)
    lane_pack = iota((tall, LANES), 1)
    for q, r in enumerate((own, other)):
        wy, wx = taps_yx(r[0])
        for b in range(3):
            for e in range(3):
                weights[q, b * 3 + e] = wy[b] * wx[e]
    xmsg[...] = jnp.zeros(xmsg.shape, F32)

    def plane(p, carry):
        for c in range(channels):
            col = []
            for q in range(2):
                if c == 0:
                    col.append(reach[q] * cols5[0, q, p] - rest[q] * cols5[1, q, p])
                else:
                    col.append(reach[q] * cols5[c + 1, q, p])
            summed = []
            for e in range(3):
                part = [
                    weights[0, b * 3 + e] * col[0] + weights[1, b * 3 + e] * col[1]
                    for b in range(3)
                ]
                down = pltpu.roll(part[2], 1, 0)
                up = pltpu.roll(part[0], rows - 1, 0)
                main = part[1] + jnp.where(row == 0, 0.0, down) + jnp.where(row == rows - 1, 0.0, up)
                tail = jnp.where(t == 0, down[:SUB], pltpu.roll(up[rows - SUB :], 1, 0))
                summed.append(jnp.concatenate([main, tail], axis=0))
            right = pltpu.roll(summed[2], 1, 1)
            left = pltpu.roll(summed[0], width - 1, 1)
            both = (
                summed[1]
                + jnp.where(lane_tall == 0, 0.0, right)
                + jnp.where(lane_tall == width - 1, 0.0, left)
            )
            grad[c, p] = both[:rows]
            at = c * planes + p
            ymsg[pl.ds(at, 1), :] = both[rows : rows + 1]
            out = jnp.where(h == 0, right[:, :1], left[:, width - 1 :])
            xmsg[...] = jnp.where(lane_pack == at, out, xmsg[...])
        return carry

    lax.fori_loop(0, planes, plane, 0)
    ymsg[channels * planes : channels * planes + 1, :LANES] = xmsg[rows : rows + 1, :]


def finish_body(info, grad_in, yrow, xcol, grad):
    h, t = (info[0], info[1])
    channels, planes, rows, width = grad.shape
    row = iota((rows, width), 0)
    lane = iota((rows, width), 1)
    lane_pack = iota((rows, LANES), 1)
    at_row = row == jnp.where(t == 0, rows - 1, 0)
    at_lane = lane == jnp.where(h == 0, width - 1, 0)
    packed = xcol[...]
    for c in range(channels):
        for p in range(planes):
            at = c * planes + p
            both = jnp.where(at_row, yrow[at : at + 1, :], 0.0)
            both = both + jnp.where(at_lane, packed[:, at : at + 1], 0.0)
            grad[c, p] = grad_in[c, p] + both


def per_device(voxels, offsets, heading, cotangent):
    channels, planes, rows, total = voxels.shape
    colours = channels - 1
    dirs, slabs, cores = (lax.axis_size(a) for a in ("dir", "slab", "tile"))
    if dirs != 2 or cores != 2 or slabs & (slabs - 1):
        raise ValueError("mesh")
    width = total // dirs
    depth = planes * slabs
    scale = 2.0 / depth
    h, s, t = (lax.axis_index(a) for a in ("dir", "slab", "tile"))
    info = jnp.stack([h, t, s]).astype(jnp.int32)
    swap = [(0, 1), (1, 0)]
    tiles = width // LANES

    line = lax.dynamic_slice_in_dim(voxels, jnp.where(t == 0, rows - 1, 0), 1, axis=2)
    beside = lax.ppermute(line[:, :, 0], "tile", swap)

    _, _, height = message_rows(channels, rows, width)
    ks = (0, planes - 1, 1, planes - 2)

    def block(k):
        return pl.BlockSpec((channels, 1, rows, total), lambda i: (0, k, 0, 0))

    packed = pl.pallas_call(
        functools.partial(pack_body, width=width),
        grid=(1,),
        in_specs=[SMEM] + [block(k) for k in ks] + [VMEM],
        out_specs=[VMEM] * 4,
        out_shape=[shape(height, LANES)] * 4,
        name="pack",
    )(info, voxels, voxels, voxels, voxels, beside)
    pairs_a = [(i, i ^ 1) for i in range(slabs)]
    pairs_b = [(i, i + 1) for i in range(1, slabs - 1, 2)]
    pairs_b = pairs_b + [(b, a) for a, b in pairs_b]
    near_a = lax.ppermute(packed[0], "slab", pairs_a)
    near_b = lax.ppermute(packed[1], "slab", pairs_b)

    codes = jnp.concatenate(
        [offsets.astype(F32), heading.astype(F32), cotangent[0] * depth], axis=0
    )
    own = lax.dynamic_slice_in_dim(codes, h * width, width, axis=2)
    sent = lax.dynamic_slice_in_dim(codes, (1 - h) * width, width, axis=2)
    other = lax.ppermute(sent, "dir", swap)

    far_a = lax.ppermute(packed[2], "slab", pairs_a)
    far_b = lax.ppermute(packed[3], "slab", pairs_b)

    pay, vals, ends = call(
        functools.partial(forward_body, width=width, scale=scale),
        [
            shape(channels, 2, rows, width),
            shape(2, channels, planes, rows, width),
            shape(2, channels, 2, rows, width),
        ],
        scratch=[pltpu.VMEM((3, channels, planes + 2, rows + 2 * SUB, width), F32)],
        inputs=[SMEM] + [VMEM] * 6,
        name="forward",
    )(info, voxels, beside, near_a, near_b, own, other)

    cols5 = call(
        functools.partial(column_body, width=width, scale=scale, slabs=slabs),
        shape(channels + 1, 2, planes, rows, width),
        scratch=[
            pltpu.VMEM((3, channels, 2, rows + 2 * SUB, width), F32),
            pltpu.VMEM((2, channels, 2, rows, width), F32),
        ],
        inputs=[SMEM] + [VMEM] * 6,
        name="column",
    )(info, far_a, far_b, own, other, vals, ends)

    rays = jnp.stack([own, other], axis=1)
    forward = rays[1] == 0.0
    pull = rays[2:]
    before = jnp.zeros_like(pay[0])
    lead = jnp.zeros_like(pay[0])
    block_all = pay
    for bit in range(slabs.bit_length() - 1):
        theirs = lax.ppermute(block_all, "slab", [(i, i ^ (1 << bit)) for i in range(slabs)])
        lower = ((s >> bit) & 1) == 1
        earlier = lower == forward
        fade_theirs = jnp.exp(-theirs[0])
        fade_mine = jnp.exp(-block_all[0])
        light = jnp.where(
            earlier,
            theirs[1:] + fade_theirs * block_all[1:],
            block_all[1:] + fade_mine * theirs[1:],
        )
        weighted = jnp.sum(pull * theirs[1:], axis=0)
        lead = jnp.where(earlier, weighted + fade_theirs * lead, lead)
        before = jnp.where(earlier, before + theirs[0], before)
        block_all = jnp.concatenate([(block_all[0] + theirs[0])[None], light], axis=0)
    reach = jnp.exp(-before)
    rest = jnp.sum(pull * block_all[1:], axis=0) - lead

    grad, ymsg, xmsg = call(
        functools.partial(scatter_body, channels=channels),
        [
            shape(channels, planes, rows, width),
            shape(channels * planes + SUB, width),
            shape(rows + SUB, LANES),
        ],
        scratch=[pltpu.VMEM((2, 9, rows, width), F32)],
        inputs=[SMEM] + [VMEM] * 5,
        name="scatter",
    )(info, cols5, own, other, reach, rest)
    yrow = lax.ppermute(ymsg, "tile", swap)
    corner = yrow[channels * planes : channels * planes + 1, :LANES]
    at = jnp.arange(rows)[:, None] == jnp.where(t == 0, rows - 1, 0)
    xcol = lax.ppermute(xmsg[:rows] + jnp.where(at, corner, 0.0), "dir", swap)
    voxel_grad = call(
        finish_body,
        shape(channels, planes, rows, width),
        inputs=[SMEM] + [VMEM] * 3,
        aliases={1: 0},
        name="finish",
    )(info, grad, yrow, xcol)

    share = total // slabs
    half = slabs // dirs
    start = (s % half) * share
    mine = lax.dynamic_slice_in_dim(block_all[1:, 0], start, share, axis=2)
    sent = lax.dynamic_slice_in_dim(block_all[1:, 1], start, share, axis=2)
    got = lax.ppermute(sent, "dir", swap)
    image = jnp.where(s // half == h, mine, got)
    return (image[None], voxel_grad)


def solution(mesh):
    return jax.shard_map(
        per_device,
        mesh=mesh,
        in_specs=(
            P(None, "slab", "tile", None),
            P("dir", "tile", None),
            P("dir", "tile", None),
            P("dir", None, "tile", None),
        ),
        out_specs=(P("dir", None, "tile", "slab"), P(None, "slab", "tile", "dir")),
        check_vma=False,
    )
```

time: 240 us -> 89.3 us (0.37)
  waiting for transfers between devices: 92.7 us -> 28.5 us
  blocking collectives: 60.9 us -> 0 us
  Pallas kernels: 0 us -> 30.1 us
  other arithmetic: 34.4 us -> 9.08 us
  between operations: 14.6 us -> 0.85 us
  starting transfers between devices: 24.1 us -> 15.7 us
  local copies, waits for them, and re-layouts: 9.54 us -> 4.45 us
    all_gather x2 -> x0, blocking collectives: 60.9 us -> none  [entering(): everything = lax.all_gather(array, axis)]
    unnamed x3 -> x0, waiting for transfers between devices: 53.6 us -> none
    reduce_scatter x1 -> x0, waiting for transfers between devices: 33.2 us -> none  [per_device(): voxel_grad = lax.psum_scatter(grad, 'dir', scatter_dimension=3, tiled=True)]
    pallas_call x0 -> x5, Pallas kernels: none -> 30.1 us  [the longest x1 12.4 us: per_device(): call(functools.partial(forward_body, width=width, scale=scale), [shape(ch...]
    ppermute x10 -> x12, waiting for transfers between devices: 5.88 us -> 28.5 us  [the longest x3 10.7 us: per_device(): lax.ppermute(block_all, 'slab', [(i, i ^ 1 << bit) for i in range(slabs)])]
    reduce_sum x4 -> x1, other arithmetic: 9.85 us -> 0.12 us  [per_device(): weighted = jnp.sum(pull * theirs[1:], axis=0)]
    ppermute x10 -> x12, starting transfers between devices: 24 us -> 15.7 us  [the longest x1 5.51 us: per_device(): far_b = lax.ppermute(packed[3], 'slab', pairs_b)]
    concatenate x3, other arithmetic: 7 us -> 0.06 us  [the longest x2 0.04 us: per_device(): jnp.concatenate([(block_all[0] + theirs[0])[None], light], axis=0)]
  transfers between devices with their start and end apart: 12 -> 12, of which waited for: 7 -> 8; matrix products, arithmetic and copies ran while one was open for 9% -> 7% of each run, Pallas kernels for 0% -> 11%
where the time goes in v1:
time: 89.3 us; the launch traced here: 88.7 us
  Pallas kernels  30.1 us (34%)
  waiting for transfers between devices  28.5 us (32%)
  starting transfers between devices  15.7 us (18%)
  other arithmetic  9.08 us (10%)
  local copies, waits for them, and re-layouts  4.45 us (5%)
    pallas_call x1, Pallas kernels, per_device(): call(functools.partial(forward_body, width=width, scale=scale), [shape(ch...  12.4 us
    ppermute x3, waiting for transfers between devices, per_device(): lax.ppermute(block_all, 'slab', [(i, i ^ 1 << bit) for i in range(slabs)])  10.7 us
    ppermute x1, waiting for transfers between devices, per_device(): far_b = lax.ppermute(packed[3], 'slab', pairs_b)  8.35 us
    pallas_call x1, Pallas kernels, per_device(): call(functools.partial(column_body, width=width, scale=scale, slabs=slabs...  6.89 us
    pallas_call x1, Pallas kernels, per_device(): call(functools.partial(scatter_body, channels=channels), [shape(channels,...  5.67 us
    ppermute x1, starting transfers between devices, per_device(): far_b = lax.ppermute(packed[3], 'slab', pairs_b)  5.51 us
    ppermute x1, waiting for transfers between devices, per_device(): near_b = lax.ppermute(packed[1], 'slab', pairs_b)  4.02 us
    ppermute x3, starting transfers between devices, per_device(): lax.ppermute(block_all, 'slab', [(i, i ^ 1 << bit) for i in range(slabs)])  2.77 us
  transfers between devices with their start and end apart: 12, of which 8 were waited for; matrix products, arithmetic and copies ran while one was open for 7% of the time, Pallas kernels for 11%

profile of v1, /device:TPU:16, one launch (start us, length us, event | category | flops | bytes accessed | tf_op | source)
XLA Modules:
  0.0 88.7 jit_solution(17318563490408631899)
XLA Ops:
  0.6 1.1 %constant_dynamic-slice_fusion = f32[4,8,1,512]{3,2,1,0:T(1,128)S(1)} fusion(f32[4,8,32,512]{3,2,1,0:T(8,128)} %vox.1, s32[]{:T(128)S(6)} %select_n.72), kind=kLoop, calls=%fused_computation.50 | loop fusion | bytes 131076 | tf_op jit(solution)/shard_map/dynamic_slice | solution.py:426
  1.8 0.8 convert_element_type.6
  2.7 0.8 convert_element_type.7
  3.5 0.9 %multiply_bitcast_fusion = f32[3,32,512]{2,1,0:T(8,128)S(1)} fusion(f32[1,3,32,512]{3,2,1,0:T(8,128)} %param.7), kind=kLoop, calls=%fused_computation.11 | loop fusion | flops 49152 | bytes 393216 | tf_op jit(solution)/shard_map/mul | solution.py:450
  4.5 0.7 constant_dynamic-slice_fusion.1
  5.2 1.5 %collective-permute-start = (f32[5,32,256]{2,1,0:T(8,128)S(1)}, f32[5,32,256]{2,1,0:T(8,128)S(1)}, u32[]{:S(2)}, u32[]{:S(2)}) collective-permute-start(f32[5,32,256]{2,1,0:T(8,128)S(1)} %get-tuple-element.35), channel_id=1, source_target_pairs={{0,16},{16,0},{1,17},{17,1},{2,18},{18,2},{3,19},{19,3},{4,20},{20... | collective-permute-start | bytes 491528 | tf_op jit(solution)/shard_map/ppermute | solution.py:454
  8.0 2.6 %pack.1 = (f32[296,128]{1,0:T(8,128)}, f32[296,128]{1,0:T(8,128)}, f32[296,128]{1,0:T(8,128)}, f32[296,128]{1,0:T(8,128)}) custom-call(s32[3]{0:T(128)} %pad_add_fusion.info, f32[4,8,32,512]{3,2,1,0:T(8,128)} %vox.1, f32[4,8,32,512]{3,2,1,0:T(8,128)} %vox.1, f32[4,8,32,512]{3,2,1,0:T(8,128)} %vox.1, f32[4,8,32,512]{3,2,1,0:T(8,128)} %vox.1, ...), custom_call_target="tpu_custom_call" | custom-call | tf_op jit(solution)/shard_map/pack/pallas_call | solution.py:435
  10.6 1.5 %collective-permute-start.2 = (f32[296,128]{1,0:T(8,128)}, f32[296,128]{1,0:T(8,128)S(1)}, u32[]{:S(2)}, u32[]{:S(2)}) collective-permute-start(f32[296,128]{1,0:T(8,128)} %get-tuple-element.12), channel_id=1, source_target_pairs={{0,2},{2,0},{4,6},{6,4},{8,10},{10,8},{12,14},{14,12},{1,3},{3,1},... | collective-permute-start | bytes 454664 | tf_op jit(solution)/shard_map/ppermute | solution.py:446
  12.1 2.3 %collective-permute-start.3 = (f32[296,128]{1,0:T(8,128)}, f32[296,128]{1,0:T(8,128)S(1)}, u32[]{:S(2)}, u32[]{:S(2)}) collective-permute-start(f32[296,128]{1,0:T(8,128)} %get-tuple-element.13), channel_id=1, source_target_pairs={{2,4},{6,8},{10,12},{4,2},{8,6},{12,10},{3,5},{7,9},{11,13},{5,3},... | collective-permute-start | bytes 454664 | tf_op jit(solution)/shard_map/ppermute | solution.py:447
  14.5 2.4 %collective-permute-done.2.zlo = f32[296,128]{1,0:T(8,128)S(1)} collective-permute-done((f32[296,128]{1,0:T(8,128)}, f32[296,128]{1,0:T(8,128)S(1)}, u32[]{:S(2)}, u32[]{:S(2)}) %collective-permute-start.2) | collective-permute-done | bytes 151584 | tf_op jit(solution)/shard_map/ppermute | solution.py:446
  16.9 4.0 %collective-permute-done.3.zhi = f32[296,128]{1,0:T(8,128)S(1)} collective-permute-done((f32[296,128]{1,0:T(8,128)}, f32[296,128]{1,0:T(8,128)S(1)}, u32[]{:S(2)}, u32[]{:S(2)}) %collective-permute-start.3) | collective-permute-done | bytes 151584 | tf_op jit(solution)/shard_map/ppermute | solution.py:447
  21.6 12.4 %forward.1 = (f32[4,2,32,256]{3,2,1,0:T(8,128)}, f32[2,4,8,32,256]{4,3,2,1,0:T(8,128)}, f32[2,4,2,32,256]{4,3,2,1,0:T(8,128)}) custom-call(s32[3]{0:T(128)} %pad_add_fusion.info, f32[4,8,32,512]{3,2,1,0:T(8,128)} %vox.1, f32[4,8,512]{2,1,0:T(8,128)} %copy-done.4, f32[296,128]{1,0:T(8,128)} %copy-done.5, f32[296,128]{1,0:T(8,128)} %copy-done.6, ...), custom_call_target="tpu_custom_call" | custom-call | flops 10000000 | bytes 4000000 | tf_op jit(solution)/shard_map/forward/pallas_call | solution.py:459
  34.0 0.9 %collective-permute-start.4 = (f32[4,2,32,256]{3,2,1,0:T(8,128)}, f32[4,2,32,256]{3,2,1,0:T(8,128)S(1)}, u32[]{:S(2)}, u32[]{:S(2)}) collective-permute-start(f32[4,2,32,256]{3,2,1,0:T(8,128)} %get-tuple-element.14), channel_id=1, source_target_pairs={{0,2},{2,0},{4,6},{6,4},{8,10},{10,8},{12,14},{14,12},{1,3},{3,1},... | collective-permute-start | bytes 786440 | tf_op jit(solution)/shard_map/ppermute | solution.py:489
  34.9 0.8 compare_bitcast_fusion
  35.7 5.9 %collective-permute-done.4 = f32[4,2,32,256]{3,2,1,0:T(8,128)S(1)} collective-permute-done((f32[4,2,32,256]{3,2,1,0:T(8,128)}, f32[4,2,32,256]{3,2,1,0:T(8,128)S(1)}, u32[]{:S(2)}, u32[]{:S(2)}) %collective-permute-start.4) | collective-permute-done | bytes 262176 | tf_op jit(solution)/shard_map/ppermute | solution.py:489
  41.5 0.9 exponential_bitcast_fusion.2
  42.4 1.0 %add_select_fusion.2 = f32[3,2,32,256]{3,2,1,0:T(8,128)S(1)} fusion(f32[4,2,32,256]{3,2,1,0:T(8,128)} %get-tuple-element.14, f32[4,2,32,256]{3,2,1,0:T(8,128)S(1)} %collective-permute-done.4, f32[2,32,256]{2,1,0:T(8,128)S(1)} %get-tuple-element.38, f32[2,32,256]{2,1,0:T(8,128)S(1)} %get-tuple-element.39, pred[2,32,256]{2,1,0:T(8,128)(4,1)S(1)} %compare_bitcast_fusion.1), kind=kLoop, calls=%fused_computation.10 | loop fusion | flops 245760 | bytes 737280 | tf_op jit(solution)/shard_map/jit(_where)/select_n | solution.py:494
  43.4 1.6 %collective-permute-start.5 = (f32[4,2,32,256]{3,2,1,0:T(8,128)S(1)}, f32[4,2,32,256]{3,2,1,0:T(8,128)S(1)}, u32[]{:S(2)}, u32[]{:S(2)}) collective-permute-start(f32[4,2,32,256]{3,2,1,0:T(8,128)S(1)} %pad_maximum_fusion.1), channel_id=1, source_target_pairs={{0,4},{2,6},{4,0},{6,2},{8,12},{10,14},{12,8},{14,10},{1,5},{3,7},... | collective-permute-start | bytes 786440 | tf_op jit(solution)/shard_map/ppermute | solution.py:489
  45.1 4.8 %collective-permute-done.5 = f32[4,2,32,256]{3,2,1,0:T(8,128)S(1)} collective-permute-done((f32[4,2,32,256]{3,2,1,0:T(8,128)S(1)}, f32[4,2,32,256]{3,2,1,0:T(8,128)S(1)}, u32[]{:S(2)}, u32[]{:S(2)}) %collective-permute-start.5) | collective-permute-done | bytes 262176 | tf_op jit(solution)/shard_map/ppermute | solution.py:489
  50.2 0.7 collective-permute-start.8
  51.0 5.5 %collective-permute-start.9 = (f32[296,128]{1,0:T(8,128)S(1)}, f32[296,128]{1,0:T(8,128)S(1)}, u32[]{:S(2)}, u32[]{:S(2)}) collective-permute-start(f32[296,128]{1,0:T(8,128)S(1)} %copy-done.11), channel_id=1, source_target_pairs={{2,4},{6,8},{10,12},{4,2},{8,6},{12,10},{3,5},{7,9},{11,13},{5,3},... | collective-permute-start | bytes 454664 | tf_op jit(solution)/shard_map/ppermute | solution.py:457
  56.5 8.3 %collective-permute-done.9.zhi = f32[296,128]{1,0:T(8,128)S(1)} collective-permute-done((f32[296,128]{1,0:T(8,128)S(1)}, f32[296,128]{1,0:T(8,128)S(1)}, u32[]{:S(2)}, u32[]{:S(2)}) %collective-permute-start.9) | collective-permute-done | bytes 151584 | tf_op jit(solution)/shard_map/ppermute | solution.py:457
  65.6 6.9 %column.1.cols5 = f32[5,2,8,32,256]{4,3,2,1,0:T(8,128)} custom-call(s32[3]{0:T(128)} %pad_add_fusion.info, f32[296,128]{1,0:T(8,128)} %copy-done.7, f32[296,128]{1,0:T(8,128)} %copy-done.8, f32[5,32,256]{2,1,0:T(8,128)} %get-tuple-element.36.own, f32[5,32,256]{2,1,0:T(8,128)} %copy-done.2, f32[2,4,8,32,256]{4,3,2,1,0:T(8,128)} %get-tuple-element.17.vals, ...), custom_call_target="tpu_custom_call" | custom-call | flops 10000000 | bytes 4000000 | tf_op jit(solution)/shard_map/column/pallas_call | solution.py:471
  73.3 0.7 fusion.6.rest
  74.0 5.7 %scatter.1 = (f32[4,8,32,256]{3,2,1,0:T(8,128)}, f32[40,256]{1,0:T(8,128)}, f32[40,128]{1,0:T(8,128)}) custom-call(s32[3]{0:T(128)} %pad_add_fusion.info, f32[5,2,8,32,256]{4,3,2,1,0:T(8,128)} %column.1.cols5, f32[5,32,256]{2,1,0:T(8,128)} %get-tuple-element.36.own, f32[5,32,256]{2,1,0:T(8,128)} %copy-done.2, f32[2,32,256]{2,1,0:T(8,128)} %get-tuple-element.27.reach, ...), custom_call_target="tpu_custom_call" | custom-call | flops 10000000 | bytes 4000000 | tf_op jit(solution)/shard_map/scatter/pallas_call | solution.py:506
  80.3 0.7 collective-permute-done.10.yrow
  81.1 0.8 select_add_fusion
  81.9 0.8 collective-permute-start.11
  82.6 1.3 %collective-permute-done.7 = f32[3,32,64]{2,1,0:T(8,128)S(1)} collective-permute-done((f32[3,32,64]{2,1,0:T(8,128)S(1)}, f32[3,32,64]{2,1,0:T(8,128)S(1)}, u32[]{:S(2)}, u32[]{:S(2)}) %collective-permute-start.7) | collective-permute-done | bytes 24608 | tf_op jit(solution)/shard_map/ppermute | solution.py:534
  84.0 0.7 fusion.15
  84.7 1.0 %collective-permute-done.11.xcol = f32[32,128]{1,0:T(8,128)S(1)} collective-permute-done((f32[32,128]{1,0:T(8,128)S(1)}, f32[32,128]{1,0:T(8,128)S(1)}, u32[]{:S(2)}, u32[]{:S(2)}) %collective-permute-start.11) | collective-permute-done | bytes 16416 | tf_op jit(solution)/shard_map/ppermute | solution.py:520
  86.2 2.5 %finish.1 = f32[4,8,32,256]{3,2,1,0:T(8,128)} custom-call(s32[3]{0:T(128)} %pad_add_fusion.info, f32[4,8,32,256]{3,2,1,0:T(8,128)} %get-tuple-element.19.grad_in, f32[40,256]{1,0:T(8,128)} %copy-done.9, f32[32,128]{1,0:T(8,128)} %copy-done.10), custom_call_target="tpu_custom_call", output_to_operand_aliasing={{}: (1, {})} | custom-call | flops 10000000 | bytes 4000000 | tf_op jit(solution)/shard_map/finish/pallas_call | solution.py:521
  (49 shorter events, 5.2 us)
Async XLA Ops:
  1.8 5.6 %collective-permute-start.1 = (f32[4,8,512]{2,1,0:T(8,128)S(1)}, f32[4,8,512]{2,1,0:T(8,128)S(1)}, u32[]{:S(2)}, u32[]{:S(2)}) collective-permute-start(f32[4,8,512]{2,1,0:T(8,128)S(1)} %bitcast.88), channel_id=1, source_target_pairs={{0,1},{1,0},{2,3},{3,2},{4,5},{5,4},{6,7},{7,6},{8,9},{9,8},{10,11... | collective-permute-start | bytes 196616 | tf_op jit(solution)/shard_map/ppermute | solution.py:427
  5.2 9.2 %collective-permute-start = (f32[5,32,256]{2,1,0:T(8,128)S(1)}, f32[5,32,256]{2,1,0:T(8,128)S(1)}, u32[]{:S(2)}, u32[]{:S(2)}) collective-permute-start(f32[5,32,256]{2,1,0:T(8,128)S(1)} %get-tuple-element.35), channel_id=1, source_target_pairs={{0,16},{16,0},{1,17},{17,1},{2,18},{18,2},{3,19},{19,3},{4,20},{20... | collective-permute-start | bytes 491528 | tf_op jit(solution)/shard_map/ppermute | solution.py:454
  7.4 0.6 copy-start.4
  10.6 24.3 %copy-start = (f32[5,32,256]{2,1,0:T(8,128)S(1)}, f32[5,32,256]{2,1,0:T(8,128)}, u32[]{:S(2)}) copy-start(f32[5,32,256]{2,1,0:T(8,128)} %get-tuple-element.36.own) | copy-start | bytes 491524
  10.6 6.3 %collective-permute-start.2 = (f32[296,128]{1,0:T(8,128)}, f32[296,128]{1,0:T(8,128)S(1)}, u32[]{:S(2)}, u32[]{:S(2)}) collective-permute-start(f32[296,128]{1,0:T(8,128)} %get-tuple-element.12), channel_id=1, source_target_pairs={{0,2},{2,0},{4,6},{6,4},{8,10},{10,8},{12,14},{14,12},{1,3},{3,1},... | collective-permute-start | bytes 454664 | tf_op jit(solution)/shard_map/ppermute | solution.py:446
  12.1 8.8 %collective-permute-start.3 = (f32[296,128]{1,0:T(8,128)}, f32[296,128]{1,0:T(8,128)S(1)}, u32[]{:S(2)}, u32[]{:S(2)}) collective-permute-start(f32[296,128]{1,0:T(8,128)} %get-tuple-element.13), channel_id=1, source_target_pairs={{2,4},{6,8},{10,12},{4,2},{8,6},{12,10},{3,5},{7,9},{11,13},{5,3},... | collective-permute-start | bytes 454664 | tf_op jit(solution)/shard_map/ppermute | solution.py:447
  14.4 6.5 %copy-start.2 = (f32[5,32,256]{2,1,0:T(8,128)}, f32[5,32,256]{2,1,0:T(8,128)S(1)}, u32[]{:S(2)}) copy-start(f32[5,32,256]{2,1,0:T(8,128)S(1)} %collective-permute-done.other) | copy-start | bytes 491524
  16.9 4.0 %copy-start.5 = (f32[296,128]{1,0:T(8,128)}, f32[296,128]{1,0:T(8,128)S(1)}, u32[]{:S(2)}) copy-start(f32[296,128]{1,0:T(8,128)S(1)} %collective-permute-done.2.zlo) | copy-start | bytes 454660
  20.9 0.7 copy-start.6
  34.0 16.3 %copy-start.12 = (f32[296,128]{1,0:T(8,128)S(1)}, f32[296,128]{1,0:T(8,128)}, u32[]{:S(2)}) copy-start(f32[296,128]{1,0:T(8,128)} %get-tuple-element.15) | copy-start | bytes 454660
  34.0 17.0 %copy-start.11 = (f32[296,128]{1,0:T(8,128)S(1)}, f32[296,128]{1,0:T(8,128)}, u32[]{:S(2)}) copy-start(f32[296,128]{1,0:T(8,128)} %get-tuple-element.16) | copy-start | bytes 454660
  34.0 7.6 %collective-permute-start.4 = (f32[4,2,32,256]{3,2,1,0:T(8,128)}, f32[4,2,32,256]{3,2,1,0:T(8,128)S(1)}, u32[]{:S(2)}, u32[]{:S(2)}) collective-permute-start(f32[4,2,32,256]{3,2,1,0:T(8,128)} %get-tuple-element.14), channel_id=1, source_target_pairs={{0,2},{2,0},{4,6},{6,4},{8,10},{10,8},{12,14},{14,12},{1,3},{3,1},... | collective-permute-start | bytes 786440 | tf_op jit(solution)/shard_map/ppermute | solution.py:489
  43.4 6.5 %collective-permute-start.5 = (f32[4,2,32,256]{3,2,1,0:T(8,128)S(1)}, f32[4,2,32,256]{3,2,1,0:T(8,128)S(1)}, u32[]{:S(2)}, u32[]{:S(2)}) collective-permute-start(f32[4,2,32,256]{3,2,1,0:T(8,128)S(1)} %pad_maximum_fusion.1), channel_id=1, source_target_pairs={{0,4},{2,6},{4,0},{6,2},{8,12},{10,14},{12,8},{14,10},{1,5},{3,7},... | collective-permute-start | bytes 786440 | tf_op jit(solution)/shard_map/ppermute | solution.py:489
  50.0 22.5 %collective-permute-start.6 = (f32[4,2,32,256]{3,2,1,0:T(8,128)S(1)}, f32[4,2,32,256]{3,2,1,0:T(8,128)S(1)}, u32[]{:S(2)}, u32[]{:S(2)}) collective-permute-start(f32[4,2,32,256]{3,2,1,0:T(8,128)S(1)} %pad_maximum_fusion.2), channel_id=1, source_target_pairs={{0,8},{2,10},{4,12},{6,14},{8,0},{10,2},{12,4},{14,6},{1,9},{3,11}... | collective-permute-start | bytes 786440 | tf_op jit(solution)/shard_map/ppermute | solution.py:489
  50.2 6.3 %collective-permute-start.8 = (f32[296,128]{1,0:T(8,128)S(1)}, f32[296,128]{1,0:T(8,128)S(1)}, u32[]{:S(2)}, u32[]{:S(2)}) collective-permute-start(f32[296,128]{1,0:T(8,128)S(1)} %copy-done.12), channel_id=1, source_target_pairs={{0,2},{2,0},{4,6},{6,4},{8,10},{10,8},{12,14},{14,12},{1,3},{3,1},... | collective-permute-start | bytes 454664 | tf_op jit(solution)/shard_map/ppermute | solution.py:456
  51.0 13.9 %collective-permute-start.9 = (f32[296,128]{1,0:T(8,128)S(1)}, f32[296,128]{1,0:T(8,128)S(1)}, u32[]{:S(2)}, u32[]{:S(2)}) collective-permute-start(f32[296,128]{1,0:T(8,128)S(1)} %copy-done.11), channel_id=1, source_target_pairs={{2,4},{6,8},{10,12},{4,2},{8,6},{12,10},{3,5},{7,9},{11,13},{5,3},... | collective-permute-start | bytes 454664 | tf_op jit(solution)/shard_map/ppermute | solution.py:457
  56.5 8.4 %copy-start.7 = (f32[296,128]{1,0:T(8,128)}, f32[296,128]{1,0:T(8,128)S(1)}, u32[]{:S(2)}) copy-start(f32[296,128]{1,0:T(8,128)S(1)} %collective-permute-done.8.zlo) | copy-start | bytes 454660
  64.9 0.7 copy-start.8
  65.6 7.6 %copy-start.1 = (f32[5,32,256]{2,1,0:T(8,128)S(1)}, f32[5,32,256]{2,1,0:T(8,128)}, u32[]{:S(2)}) copy-start(f32[5,32,256]{2,1,0:T(8,128)} %get-tuple-element.36.own) | copy-start | bytes 491524
  65.6 7.6 %copy-start.3 = (f32[5,32,256]{2,1,0:T(8,128)S(1)}, f32[5,32,256]{2,1,0:T(8,128)}, u32[]{:S(2)}) copy-start(f32[5,32,256]{2,1,0:T(8,128)} %copy-done.2) | copy-start | bytes 491524
  79.6 1.4 %collective-permute-start.10 = (f32[40,256]{1,0:T(8,128)}, f32[40,256]{1,0:T(8,128)S(1)}, u32[]{:S(2)}, u32[]{:S(2)}) collective-permute-start(f32[40,256]{1,0:T(8,128)} %get-tuple-element.20), channel_id=1, source_target_pairs={{0,1},{1,0},{2,3},{3,2},{4,5},{5,4},{6,7},{7,6},{8,9},{9,8},{10,11... | collective-permute-start | bytes 122888 | tf_op jit(solution)/shard_map/ppermute | solution.py:517
  79.7 4.2 %collective-permute-start.7 = (f32[3,32,64]{2,1,0:T(8,128)S(1)}, f32[3,32,64]{2,1,0:T(8,128)S(1)}, u32[]{:S(2)}, u32[]{:S(2)}) collective-permute-start(f32[3,32,64]{2,1,0:T(8,128)S(1)} %dynamic-slice_bitcast_fusion), channel_id=1, source_target_pairs={{0,16},{16,0},{1,17},{17,1},{2,18},{18,2},{3,19},{19,3},{4,20},{20... | collective-permute-start | bytes 73736 | tf_op jit(solution)/shard_map/ppermute | solution.py:534
  81.1 4.6 %copy-start.9 = (f32[40,256]{1,0:T(8,128)}, f32[40,256]{1,0:T(8,128)S(1)}, u32[]{:S(2)}) copy-start(f32[40,256]{1,0:T(8,128)S(1)} %collective-permute-done.10.yrow) | copy-start | bytes 122884
  81.9 3.7 %collective-permute-start.11 = (f32[32,128]{1,0:T(8,128)S(1)}, f32[32,128]{1,0:T(8,128)S(1)}, u32[]{:S(2)}, u32[]{:S(2)}) collective-permute-start(f32[32,128]{1,0:T(8,128)S(1)} %select_add_fusion), channel_id=1, source_target_pairs={{0,16},{16,0},{1,17},{17,1},{2,18},{18,2},{3,19},{19,3},{4,20},{20... | collective-permute-start | bytes 49160 | tf_op jit(solution)/shard_map/ppermute | solution.py:520
  85.6 0.6 copy-start.10

commit v2 on v0

v2 whole, which is shorter than its diff:
```python
import functools

import jax
import jax.numpy as jnp
from jax import lax
from jax.experimental import pallas as pl
from jax.experimental.pallas import tpu as pltpu
from jax.sharding import PartitionSpec as P

LEVELS = 8
BITS = LEVELS.bit_length() - 1
LANES = 128
SUB = 8
F32 = jnp.float32
VMEM = pl.BlockSpec(memory_space=pltpu.VMEM)
SMEM = pl.BlockSpec(memory_space=pltpu.SMEM)
MIB = 2**20


def call(body, name, outs, args, scratch=(), limit=16, flops=10**7, specs=None, **statics):
    inputs = [SMEM] + [VMEM] * (len(args) - 1)
    return pl.pallas_call(
        functools.partial(body, **statics),
        out_shape=outs,
        grid=() if specs is None else (1,),
        in_specs=specs or inputs,
        out_specs=jax.tree.map(lambda _: VMEM, outs),
        scratch_shapes=list(scratch),
        cost_estimate=pl.CostEstimate(
            flops=flops, bytes_accessed=2 * 10**6, transcendentals=0
        ),
        compiler_params=pltpu.CompilerParams(vmem_limit_bytes=limit * MIB),
        name=name,
    )(*args)


def shape(*dims):
    return jax.ShapeDtypeStruct(dims, F32)


def iota(dims, axis):
    return lax.broadcasted_iota(jnp.int32, dims, axis)


def fraction(raw):
    return (raw.astype(F32) + 0.5) / LEVELS - 0.5


def three(raw):
    f = fraction(raw)
    return (jnp.maximum(-f, 0.0), 1.0 - jnp.abs(f), jnp.maximum(f, 0.0))


def split_code(code):
    q = code.astype(jnp.int32)
    return (q & (LEVELS - 1), (q >> BITS) & (LEVELS - 1), q >> (2 * BITS))


def logistic(v):
    return 0.5 * jnp.tanh(0.5 * v) + 0.5


def total_of(terms):
    return functools.reduce(lambda a, b: a + b, terms)


def log_soft(v):
    return jnp.maximum(v, 0.0) + jnp.log(1.0 + jnp.exp(-jnp.abs(v)))


def shifts(tiles, beside, h):
    lane = iota(tiles[0].shape, 1)
    last = LANES - 1
    zero = jnp.zeros_like(beside)
    right = [pltpu.roll(x, 1, 1) for x in tiles]
    left = [pltpu.roll(x, last, 1) for x in tiles]
    below = [jnp.where(h == 1, beside, zero)] + right[:-1]
    above = left[1:] + [jnp.where(h == 0, beside, zero)]
    minus = [jnp.where(lane == 0, b, r) for b, r in zip(below, right)]
    plus = [jnp.where(lane == last, a, x) for a, x in zip(above, left)]
    return (minus, tiles, plus)


def beside_shift(source, h):
    target = jnp.where(h == 1, 0, LANES - 1)
    return lax.rem(target - source + LANES, LANES)


def window_parts(h, width):
    base = pl.multiple_of(h * width, LANES)
    side = pl.multiple_of(width - LANES * h, LANES)
    source = jnp.where(h == 0, 0, LANES - 1)
    return base, side, source


def pack_body(info, first, last, out_a, out_b, diag_a, diag_b, *, width):
    h, t, s = (info[0], info[1], info[2])
    even = s % 2 == 0
    channels, _, rows, _ = first.shape
    count = width // LANES
    base, side, source = window_parts(h, width)
    lane = iota((rows, LANES), 1)
    row = pl.multiple_of(jnp.where(t == 0, rows - SUB, 0), SUB)
    pick = iota((SUB, LANES), 0) == jnp.where(t == 0, SUB - 1, 0)
    lane8 = iota((SUB, LANES), 1)

    def fill(block, out, diag):
        edge = jnp.zeros((rows, LANES), F32)
        corner = jnp.zeros((SUB, LANES), F32)
        for c in range(channels):
            for j in range(count):
                at = c * count + j
                cols = pl.ds(base + j * LANES, LANES)
                out[at * rows : (at + 1) * rows, :] = block[c, 0, :, cols]
                line = jnp.where(pick, block[c, 0, pl.ds(row, SUB), cols], 0.0)
                diag[at : at + 1, :] = jnp.sum(line, axis=0, keepdims=True)
            turn = lax.rem(c - source + LANES, LANES)
            cols = pl.ds(side, LANES)
            edge = jnp.where(lane == c, pltpu.roll(block[c, 0, :, cols], turn, 1), edge)
            line = jnp.where(pick, block[c, 0, pl.ds(row, SUB), cols], 0.0)
            line = jnp.sum(line, axis=0, keepdims=True)
            line = pltpu.roll(jnp.broadcast_to(line, (SUB, LANES)), turn, 1)
            corner = jnp.where(lane8 == c, line, corner)
        out[channels * count * rows :, :] = edge
        diag[channels * count :, :] = corner

    @pl.when(even)
    def _():
        fill(last, out_a, diag_a)
        fill(first, out_b, diag_b)

    @pl.when(jnp.logical_not(even))
    def _():
        fill(first, out_a, diag_a)
        fill(last, out_b, diag_b)


def code_body(info, offsets, heading, cotangent, own, sent, *, width, depth):
    h = info[0]
    for out, at in ((own, h), (sent, 1 - h)):
        cols = pl.ds(pl.multiple_of(at * width, LANES), width)
        out[0] = offsets[0, :, cols].astype(F32)
        out[1] = heading[0, :, cols].astype(F32)
        for c in range(cotangent.shape[1]):
            out[2 + c] = cotangent[0, c, :, cols] * depth


def spread_message(msg, diag, grid, plane, info, channels, rows, count):
    h, t = (info[0], info[1])
    body = channels * count
    edge = msg[body * rows :, :]
    corner = diag[body:, :]
    beyond = pl.ds(pl.multiple_of(jnp.where(t == 0, SUB + rows, 0), SUB), SUB)
    for c in range(channels):
        turn = beside_shift(c, h)
        first = c * count
        tiles = [msg[(first + j) * rows : (first + j + 1) * rows, :] for j in range(count)]
        lines = [
            jnp.broadcast_to(diag[first + j : first + j + 1, :], (SUB, LANES))
            for j in range(count)
        ]
        for e, xs in enumerate(shifts(tiles, pltpu.roll(edge, turn, 1), h)):
            for j, x in enumerate(xs):
                grid[e, c, plane, SUB : SUB + rows, j * LANES : (j + 1) * LANES] = x
        for e, xs in enumerate(shifts(lines, pltpu.roll(corner, turn, 1), h)):
            for j, x in enumerate(xs):
                grid[e, c, plane, beyond, j * LANES : (j + 1) * LANES] = x


def taps(code, row0, t, rows):
    _, m, n = split_code(code)
    fy, fx = (fraction(m), fraction(n))
    row = iota(code.shape, 0) + row0
    low = (row == 0) & (t == 0)
    high = (row == rows - 1) & (t == 1)
    up = ((fy > 0.0) & jnp.logical_not(high)) | low
    ay, ax = (jnp.abs(fy), jnp.abs(fx))
    gone = (low & (fy < 0.0)) | (high & (fy > 0.0))
    by = jnp.where(gone, 0.0, ay)
    return (up, fx > 0.0, (1.0 - ay) * (1.0 - ax), (1.0 - ay) * ax, by * (1.0 - ax), by * ax)


def bilinear(rays, grid, c, plane, row0, cols):
    v = [
        [grid[e, c, plane, row0 + b + SUB - 1 : row0 + b + 2 * SUB - 1, cols] for e in range(3)]
        for b in range(3)
    ]
    out = []
    for up, right, centre, across, along, diagonal in rays:
        row = [jnp.where(up, v[2][e], v[0][e]) for e in range(3)]
        out.append(
            centre * v[1][1]
            + across * jnp.where(right, v[1][2], v[1][0])
            + along * row[1]
            + diagonal * jnp.where(right, row[2], row[0])
        )
    return out


def ray_tiles(rays, rows, width, t):
    for i in range(rows // SUB):
        for j in range(width // LANES):
            at = slice(i * SUB, (i + 1) * SUB)
            cols = slice(j * LANES, (j + 1) * LANES)
            codes = [r[0, at, cols] for r in rays]
            yield (
                i * SUB,
                at,
                cols,
                [taps(q, i * SUB, t, rows) for q in codes],
                [three(split_code(q)[0]) for q in codes],
            )


def each_tile(rows, width, body):
    count = width // LANES

    def step(n, carry):
        row = pl.ds(pl.multiple_of((n // count) * SUB, SUB), SUB)
        col = pl.ds(pl.multiple_of((n % count) * LANES, LANES), LANES)
        body(row, col)
        return carry

    lax.fori_loop(0, (rows // SUB) * count, step, 0)


def products(left):
    ones = jnp.ones_like(left[0])
    rising, falling = ([ones], [ones])
    for x in left[:-1]:
        rising.append(rising[-1] * x)
    for x in left[:0:-1]:
        falling.append(falling[-1] * x)
    return rising, falling[::-1]


def inner_body(info, vox, line, own, other, vals, part, ends, inner, grid, *, width, scale):
    h, t = (info[0], info[1])
    channels, planes, rows, _ = vox.shape
    count = width // LANES
    base, side, source = window_parts(h, width)
    turn = beside_shift(source, h)
    rays = (own, other)

    def place(k, carry):
        for c in range(channels):
            tiles = [vox[c, k, :, pl.ds(base + j * LANES, LANES)] for j in range(count)]
            beside = pltpu.roll(vox[c, k, :, pl.ds(side, LANES)], turn, 1)
            for e, xs in enumerate(shifts(tiles, beside, h)):
                for j, x in enumerate(xs):
                    grid[e, c, k, SUB : SUB + rows, j * LANES : (j + 1) * LANES] = x
        return carry

    lax.fori_loop(0, planes, place, 0)
    beyond = pl.ds(pl.multiple_of(jnp.where(t == 0, SUB + rows, 0), SUB), SUB)
    for c in range(channels):
        tiles = [line[c, :, pl.ds(base + j * LANES, LANES)] for j in range(count)]
        beside = pltpu.roll(line[c, :, pl.ds(side, LANES)], turn, 1)
        for e, xs in enumerate(shifts(tiles, beside, h)):
            for j, x in enumerate(xs):
                for k in range(planes):
                    grid[e, c, k, beyond, j * LANES : (j + 1) * LANES] = jnp.broadcast_to(
                        x[k : k + 1], (SUB, LANES)
                    )

    for row0, at, cols, yx, wz in ray_tiles(rays, rows, width, t):

        def channel(c, carry, row0=row0, at=at, cols=cols, yx=yx, wz=wz):
            old = [None, None]
            for p in range(planes):
                new = bilinear(yx, grid, c, p, row0, cols)
                for q in range(2):
                    w = wz[q]
                    if p == 0:
                        ends[q, c, 0, at, cols] = w[2] * new[q]
                    elif p == 1:
                        part[q, c, 0, at, cols] = w[1] * old[1][q] + w[2] * new[q]
                    else:
                        vals[q, c, p - 2, at, cols] = (
                            w[0] * old[0][q] + w[1] * old[1][q] + w[2] * new[q]
                        )
                    if p == planes - 1:
                        part[q, c, 1, at, cols] = w[0] * old[1][q] + w[1] * new[q]
                        ends[q, c, 1, at, cols] = w[0] * new[q]
                old = [old[1], new]
            return carry

        lax.fori_loop(0, channels, channel, 0)

    for q in range(2):

        def shade(row, col, q=q):
            ahead = rays[q][1, row, col] == 0.0
            sigma = [log_soft(vals[q, 0, k, row, col]) * scale for k in range(planes - 2)]
            left = [jnp.exp(-x) for x in sigma]
            rising, falling = products(left)
            light = [None] * (channels - 1)
            for k in range(planes - 2):
                glow = jnp.where(ahead, rising[k], falling[k]) * (1.0 - left[k])
                for c in range(channels - 1):
                    term = glow * logistic(vals[q, c + 1, k, row, col])
                    light[c] = term if k == 0 else light[c] + term
            inner[0, q, row, col] = total_of(sigma)
            for c in range(channels - 1):
                inner[c + 1, q, row, col] = light[c]

        each_tile(rows, width, shade)


def rim_body(info, near_a, near_b, diag_a, diag_b, own, other, part, ends, inner, pay, rim, ends_out, grid, *, scale):
    t, s = (info[1], info[2])
    _, channels, _, rows, width = part.shape
    count = width // LANES
    even = s % 2 == 0
    rays = (own, other)
    spread_message(near_a, diag_a, grid, jnp.where(even, 1, 0), info, channels, rows, count)
    spread_message(near_b, diag_b, grid, jnp.where(even, 0, 1), info, channels, rows, count)
    for row0, at, cols, yx, wz in ray_tiles(rays, rows, width, t):

        def channel(c, carry, row0=row0, at=at, cols=cols, yx=yx, wz=wz):
            for p in range(2):
                new = bilinear(yx, grid, c, p, row0, cols)
                for q in range(2):
                    rim[q, c, p, at, cols] = part[q, c, p, at, cols] + wz[q][2 * p] * new[q]
                    ends_out[q, c, p, at, cols] = ends[q, c, p, at, cols] + wz[q][1] * new[q]
            return carry

        lax.fori_loop(0, channels, channel, 0)
    for q in range(2):

        def shade(row, col, q=q):
            ahead = rays[q][1, row, col] == 0.0
            sigma = [log_soft(rim[q, 0, p, row, col]) * scale for p in range(2)]
            left = [jnp.exp(-x) for x in sigma]
            middle = inner[0, q, row, col]
            through = jnp.exp(-middle)
            first = jnp.where(ahead, left[0], left[1])
            last = first * through
            pay[0, q, row, col] = sigma[0] + middle + sigma[1]
            low = jnp.where(ahead, 1.0, last) * (1.0 - left[0])
            high = jnp.where(ahead, last, 1.0) * (1.0 - left[1])
            for c in range(channels - 1):
                pay[c + 1, q, row, col] = (
                    low * logistic(rim[q, c + 1, 0, row, col])
                    + first * inner[c + 1, q, row, col]
                    + high * logistic(rim[q, c + 1, 1, row, col])
                )

        each_tile(rows, width, shade)


def column_body(own, other, vals, rim, cols5, tail, *, scale):
    _, channels, inside, rows, width = vals.shape
    planes = inside + 2
    rays = (own, other)
    for q in range(2):

        def shade(row, col, q=q):
            ahead = rays[q][1, row, col] == 0.0
            wz = three(split_code(rays[q][0, row, col])[0])
            pull = [rays[q][2 + c, row, col] for c in range(channels - 1)]

            def value(c, k):
                if k == 0 or k == planes - 1:
                    return rim[q, c, 1 if k else 0, row, col]
                return vals[q, c, k - 1, row, col]

            ks = range(planes)
            sigma = [log_soft(value(0, k)) * scale for k in ks]
            slope = [logistic(value(0, k)) * scale for k in ks]
            left = [jnp.exp(-x) for x in sigma]
            rising, falling = products(left)
            share, after = ([], [])
            tint = [[] for _ in range(channels - 1)]
            for k in ks:
                reach = jnp.where(ahead, rising[k], falling[k])
                glow = reach * (1.0 - left[k])
                hue = []
                for c in range(channels - 1):
                    colour = logistic(value(c + 1, k))
                    hue.append(pull[c] * colour)
                    tint[c].append(glow * hue[-1] * (1.0 - colour))
                hue = total_of(hue)
                share.append(glow * hue)
                after.append(reach * left[k] * hue)
            whole = total_of(share)
            run = jnp.zeros_like(whole)
            pushed = []
            for k in ks:
                upto = run + share[k]
                pushed.append((after[k] + jnp.where(ahead, upto, whole - run)) * slope[k])
                run = upto
            tail[0, q, row, col] = rising[-1] * left[-1]
            tail[1, q, row, col] = whole
            for n, field in enumerate([pushed, slope] + tint):
                for p in range(planes):
                    x = wz[1] * field[p]
                    if p > 0:
                        x = x + wz[2] * field[p - 1]
                    if p < planes - 1:
                        x = x + wz[0] * field[p + 1]
                    cols5[n, q, p, row, col] = x

        each_tile(rows, width, shade)


def outer_body(info, far_a, far_b, diag_a, diag_b, own, other, ends, tail, outer, grid, value, *, scale, slabs):
    t, s = (info[1], info[2])
    _, channels, _, rows, width = ends.shape
    count = width // LANES
    even = s % 2 == 0
    rays = (own, other)
    spread_message(far_a, diag_a, grid, jnp.where(even, 1, 0), info, channels, rows, count)
    spread_message(far_b, diag_b, grid, jnp.where(even, 0, 1), info, channels, rows, count)
    for row0, at, cols, yx, wz in ray_tiles(rays, rows, width, t):

        def channel(c, carry, row0=row0, at=at, cols=cols, yx=yx, wz=wz):
            for p in range(2):
                new = bilinear(yx, grid, c, p, row0, cols)
                for q in range(2):
                    value[q, c, p, at, cols] = ends[q, c, p, at, cols] + wz[q][2 * p] * new[q]
            return carry

        lax.fori_loop(0, channels, channel, 0)
    live = (jnp.where(s > 0, 1.0, 0.0), jnp.where(s < slabs - 1, 1.0, 0.0))
    for q in range(2):

        def shade(row, col, q=q):
            ahead = rays[q][1, row, col] == 0.0
            wz = three(split_code(rays[q][0, row, col])[0])
            pull = [rays[q][2 + c, row, col] for c in range(channels - 1)]
            through = tail[0, q, row, col]
            whole = tail[1, q, row, col]
            for p in range(2):
                v = value[q, 0, p, row, col]
                sigma = log_soft(v) * scale
                slope = logistic(v) * (scale * live[p])
                enters = ahead if p == 0 else jnp.logical_not(ahead)
                left = jnp.exp(-sigma)
                reach = jnp.where(enters, jnp.exp(sigma), through)
                glow = reach * (1.0 - left) * live[p]
                hue = []
                fields = []
                for c in range(channels - 1):
                    colour = logistic(value[q, c + 1, p, row, col])
                    hue.append(pull[c] * colour)
                    fields.append(glow * hue[-1] * (1.0 - colour))
                hue = total_of(hue)
                share = glow * hue
                upto = jnp.where(enters, 0.0, whole + share)
                pushed = (reach * left * hue + upto) * slope
                for n, field in enumerate([pushed, slope] + fields):
                    outer[n, q, p, row, col] = wz[2 - 2 * p] * field

        each_tile(rows, width, shade)


def merge_body(cols5, outer, reach, rest, columns, *, channels):
    _, _, planes, rows, width = cols5.shape

    def ray(row, col):
        for q in range(2):
            near, far = (reach[q, row, col], rest[q, row, col])
            for p in range(planes):
                side = None if 0 < p < planes - 1 else (0 if p == 0 else 1)

                def field(n):
                    x = cols5[n, q, p, row, col]
                    return x if side is None else x + outer[n, q, side, row, col]

                columns[0, q, p, row, col] = near * field(0) - far * field(1)
                for c in range(1, channels):
                    columns[c, q, p, row, col] = near * field(c + 1)

    each_tile(rows, width, ray)


def border_body(info, columns, own, other, line, edge):
    h, t = (info[0], info[1])
    channels, _, planes, rows, width = columns.shape
    count = width // LANES
    last = LANES - 1
    rays = (own, other)
    row0 = pl.multiple_of(jnp.where(t == 0, rows - SUB, 0), SUB)
    near = pl.ds(row0, SUB)
    take = jnp.where(t == 0, SUB - 1, 0)
    lane8 = iota((SUB, LANES), 1)
    pick = iota((SUB, LANES), 0) == take
    side = pl.ds(pl.multiple_of(jnp.where(h == 0, width - LANES, 0), LANES), LANES)
    down, across = ([], [])
    for r in rays:
        _, wy, wx = [three(x) for x in split_code(r[0, near, :])]
        y = jnp.where(t == 0, wy[2], wy[0])
        down.append([y * x for x in wx])
        _, wy, wx = [three(x) for x in split_code(r[0, :, side])]
        x = jnp.where(h == 0, wx[2], wx[0])
        across.append([y * x for y in wy])
    row = iota((rows, LANES), 0)
    lane = iota((rows, LANES), 1)
    source = jnp.where(h == 0, last, 0)
    edge[...] = jnp.zeros(edge.shape, F32)

    def channel(c, carry):
        for p in range(planes):
            at = c * planes + p
            strip = [columns[c, q, p, near, :] for q in range(2)]
            sums = []
            for e in range(3):
                x = total_of([down[q][e] * strip[q] for q in range(2)])
                x = jnp.sum(jnp.where(jnp.concatenate([pick] * count, axis=1), x, 0.0), axis=0, keepdims=True)
                sums.append(jnp.broadcast_to(x, (SUB, width)))
            plus = [sums[2][:, j * LANES : (j + 1) * LANES] for j in range(count)]
            minus = [sums[0][:, j * LANES : (j + 1) * LANES] for j in range(count)]
            plus = [pltpu.roll(x, 1, 1) for x in plus]
            minus = [pltpu.roll(x, last, 1) for x in minus]
            zero = jnp.zeros_like(plus[0])
            for j in range(count):
                x = sums[1][:, j * LANES : (j + 1) * LANES]
                x = x + jnp.where(lane8 == 0, plus[j - 1] if j else zero, plus[j])
                x = x + jnp.where(lane8 == last, minus[j + 1] if j < count - 1 else zero, minus[j])
                line[c, p : p + 1, j * LANES : (j + 1) * LANES] = x[:1]
            strip = [columns[c, q, p, :, side] for q in range(2)]
            part = [total_of([across[q][b] * strip[q] for q in range(2)]) for b in range(3)]
            lower = pltpu.roll(part[2], 1, 0)
            upper = pltpu.roll(part[0], rows - 1, 0)
            main = part[1] + jnp.where(row == 0, 0.0, lower) + jnp.where(row == rows - 1, 0.0, upper)
            over = jnp.where(t == 0, lower[:SUB], pltpu.roll(upper[rows - SUB :], 1, 0))
            turn = lax.rem(at - source + LANES, LANES)
            edge[:rows, :] = jnp.where(lane == at, pltpu.roll(main, turn, 1), edge[:rows, :])
            edge[rows:, :] = jnp.where(lane8 == at, pltpu.roll(over, turn, 1), edge[rows:, :])
        return carry

    lax.fori_loop(0, channels, channel, 0)


def scatter_body(columns, own, other, grad, weights):
    channels, _, planes, rows, width = columns.shape
    lane = iota((rows, width), 1)
    row = iota((rows, width), 0)
    for q, r in enumerate((own, other)):
        _, wy, wx = [three(x) for x in split_code(r[0])]
        for b in range(3):
            for e in range(3):
                weights[q, b * 3 + e] = wy[b] * wx[e]

    def plane(p, carry):
        for c in range(channels):
            col = [columns[c, q, p] for q in range(2)]
            summed = []
            for e in range(3):
                part = [
                    weights[0, b * 3 + e] * col[0] + weights[1, b * 3 + e] * col[1]
                    for b in range(3)
                ]
                down = pltpu.roll(part[2], 1, 0)
                up = pltpu.roll(part[0], rows - 1, 0)
                summed.append(
                    part[1] + jnp.where(row == 0, 0.0, down) + jnp.where(row == rows - 1, 0.0, up)
                )
            right = pltpu.roll(summed[2], 1, 1)
            left = pltpu.roll(summed[0], width - 1, 1)
            grad[c, p] = (
                summed[1]
                + jnp.where(lane == 0, 0.0, right)
                + jnp.where(lane == width - 1, 0.0, left)
            )
        return carry

    lax.fori_loop(0, planes, plane, 0)


def finish_body(info, grad_in, line, edge, corner, grad):
    h, t = (info[0], info[1])
    channels, planes, rows, width = grad.shape
    row = iota((rows, width), 0)
    lane = iota((rows, width), 1)
    last = jnp.where(t == 0, rows - 1, 0)
    at_row = row == last
    at_lane = lane == jnp.where(h == 0, width - 1, 0)
    packed = edge[...] + jnp.where(iota((rows, LANES), 0) == last, corner[:1], 0.0)

    for c in range(channels):
        for p in range(planes):
            at = c * planes + p
            both = jnp.where(at_row, line[c, p : p + 1, :], 0.0)
            both = both + jnp.where(at_lane, packed[:, at : at + 1], 0.0)
            grad[c, p] = grad_in[c, p] + both


def per_device(voxels, offsets, heading, cotangent):
    channels, planes, rows, total = voxels.shape
    dirs, slabs, cores = (lax.axis_size(a) for a in ("dir", "slab", "tile"))
    if dirs != 2 or cores != 2 or slabs & (slabs - 1):
        raise ValueError("mesh")
    width = total // dirs
    depth = planes * slabs
    scale = 2.0 / depth
    h, s, t = (lax.axis_index(a) for a in ("dir", "slab", "tile"))
    info = jnp.stack([h, t, s]).astype(jnp.int32)
    swap = [(0, 1), (1, 0)]
    count = width // LANES
    grid = lambda n: pltpu.VMEM((3, channels, n, rows + 2 * SUB, width), F32)

    pairs_a = [(i, i ^ 1) for i in range(slabs)]
    pairs_b = [(i, i + 1) for i in range(1, slabs - 1, 2)]
    pairs_b = pairs_b + [(b, a) for a, b in pairs_b]
    cross = lambda pairs: [
        (a * cores + i, b * cores + 1 - i) for a, b in pairs for i in range(cores)
    ]

    def halo(level):
        def block(k):
            return pl.BlockSpec((channels, 1, rows, total), lambda i: (0, k, 0, 0))

        big = shape(channels * count * rows + rows, LANES)
        small = shape(channels * count + SUB, LANES)
        packed = call(
            pack_body,
            f"pack{level}",
            [big, big, small, small],
            (info, voxels, voxels),
            specs=[SMEM, block(level), block(planes - 1 - level)],
            width=width,
        )
        with jax.named_scope(f"halo{level}"):
            return (
                lax.ppermute(packed[0], "slab", pairs_a),
                lax.ppermute(packed[1], "slab", pairs_b),
                lax.ppermute(packed[2], ("slab", "tile"), cross(pairs_a)),
                lax.ppermute(packed[3], ("slab", "tile"), cross(pairs_b)),
            )

    near = halo(0)
    own, sent = call(
        code_body,
        "codes",
        [shape(channels + 1, rows, width)] * 2,
        (info, offsets, heading, cotangent),
        width=width,
        depth=depth,
    )
    other = lax.ppermute(sent, "dir", swap)
    line = lax.dynamic_slice_in_dim(voxels, jnp.where(t == 0, rows - 1, 0), 1, axis=2)
    line = lax.ppermute(line[:, :, 0], "tile", swap)

    two = shape(2, channels, 2, rows, width)
    four = shape(channels, 2, rows, width)
    vals, part, ends, inner = call(
        inner_body,
        "inner",
        [shape(2, channels, planes - 2, rows, width), two, two, four],
        (info, voxels, line, own, other),
        scratch=[grid(planes)],
        limit=20,
        width=width,
        scale=scale,
    )
    pay, rim, ends = call(
        rim_body,
        "rim",
        [four, two, two],
        (info, *near, own, other, part, ends, inner),
        scratch=[grid(2)],
        scale=scale,
    )
    far = halo(1)

    cols5, tail = pl.pallas_call(
        functools.partial(column_body, scale=scale),
        out_shape=[shape(channels + 1, 2, planes, rows, width), shape(2, 2, rows, width)],
        in_specs=[VMEM] * 4,
        out_specs=[VMEM] * 2,
        cost_estimate=pl.CostEstimate(flops=10**7, bytes_accessed=2 * 10**6, transcendentals=0),
        compiler_params=pltpu.CompilerParams(vmem_limit_bytes=16 * MIB),
        name="column",
    )(own, other, vals, rim)
    outer = call(
        outer_body,
        "outer",
        shape(channels + 1, 2, 2, rows, width),
        (info, *far, own, other, ends, tail),
        scratch=[grid(2), pltpu.VMEM((2, channels, 2, rows, width), F32)],
        scale=scale,
        slabs=slabs,
    )

    rays = jnp.stack([own, other], axis=1)
    forward = rays[1] == 0.0
    pull = rays[2:]
    before = jnp.zeros_like(pay[0])
    lead = jnp.zeros_like(pay[0])
    block_all = pay
    for bit in range(slabs.bit_length() - 1):
        with jax.named_scope(f"scan{bit}"):
            theirs = lax.ppermute(block_all, "slab", [(i, i ^ (1 << bit)) for i in range(slabs)])
        lower = ((s >> bit) & 1) == 1
        earlier = lower == forward
        fade_theirs = jnp.exp(-theirs[0])
        fade_mine = jnp.exp(-block_all[0])
        light = jnp.where(
            earlier,
            theirs[1:] + fade_theirs * block_all[1:],
            block_all[1:] + fade_mine * theirs[1:],
        )
        weighted = jnp.sum(pull * theirs[1:], axis=0)
        lead = jnp.where(earlier, weighted + fade_theirs * lead, lead)
        before = jnp.where(earlier, before + theirs[0], before)
        block_all = jnp.concatenate([(block_all[0] + theirs[0])[None], light], axis=0)
    reach = jnp.exp(-before)
    rest = jnp.sum(pull * block_all[1:], axis=0) - lead

    plain = dict(
        compiler_params=pltpu.CompilerParams(vmem_limit_bytes=16 * MIB),
        cost_estimate=pl.CostEstimate(flops=10**7, bytes_accessed=2 * 10**6, transcendentals=0),
    )
    columns = pl.pallas_call(
        functools.partial(merge_body, channels=channels),
        out_shape=shape(channels, 2, planes, rows, width),
        in_specs=[VMEM] * 4,
        out_specs=VMEM,
        name="merge",
        **plain,
    )(cols5, outer, reach, rest)
    line, edge = call(
        border_body,
        "border",
        [shape(channels, planes, width), shape(rows + SUB, LANES)],
        (info, columns, own, other),
    )
    line = lax.ppermute(line, "tile", swap)
    corner = lax.ppermute(edge[rows:], ("dir", "tile"), [(i, 3 - i) for i in range(4)])
    edge = lax.ppermute(edge[:rows], "dir", swap)
    grad = pl.pallas_call(
        scatter_body,
        out_shape=shape(channels, planes, rows, width),
        in_specs=[VMEM] * 3,
        out_specs=VMEM,
        scratch_shapes=[pltpu.VMEM((2, 9, rows, width), F32)],
        name="scatter",
        **plain,
    )(columns, own, other)
    voxel_grad = call(
        finish_body,
        "finish",
        shape(channels, planes, rows, width),
        (info, grad, line, edge, corner),
    )

    share = total // slabs
    half = slabs // dirs
    start = (s % half) * share
    mine = lax.dynamic_slice_in_dim(block_all[1:, 0], start, share, axis=2)
    sent = lax.dynamic_slice_in_dim(block_all[1:, 1], start, share, axis=2)
    got = lax.ppermute(sent, "dir", swap)
    image = jnp.where(s // half == h, mine, got)
    return (image[None], voxel_grad)


def solution(mesh):
    return jax.shard_map(
        per_device,
        mesh=mesh,
        in_specs=(
            P(None, "slab", "tile", None),
            P("dir", "tile", None),
            P("dir", "tile", None),
            P("dir", None, "tile", None),
        ),
        out_specs=(P("dir", None, "tile", "slab"), P(None, "slab", "tile", "dir")),
        check_vma=False,
    )
```

time: 240 us -> 79.2 us (0.33)
  waiting for transfers between devices: 92.7 us -> 16.5 us
  blocking collectives: 60.9 us -> 0 us
  other arithmetic: 34.4 us -> 6.21 us
  Pallas kernels: 0 us -> 19.2 us
  between operations: 14.6 us -> 1.05 us
    all_gather x2 -> x0, blocking collectives: 60.9 us -> none  [entering(): everything = lax.all_gather(array, axis)]
    unnamed x3 -> x0, waiting for transfers between devices: 53.6 us -> none
    reduce_scatter x1 -> x0, waiting for transfers between devices: 33.2 us -> none  [per_device(): voxel_grad = lax.psum_scatter(grad, 'dir', scatter_dimension=3, tiled=True)]
    pallas_call x0 -> x11, Pallas kernels: none -> 19.2 us  [the longest x8 15 us: call(): pl.pallas_call(functools.partial(body, **statics), out_shape=outs, grid=(...]
    ppermute x10 -> x17, waiting for transfers between devices: 5.88 us -> 16.5 us  [the longest x3 14.1 us: per_device(): lax.ppermute(block_all, 'slab', [(i, i ^ 1 << bit) for i in range(slabs)])]
    reduce_sum x4 -> x2, other arithmetic: 9.85 us -> 1.08 us  [per_device(): weighted = jnp.sum(pull * theirs[1:], axis=0)]
    concatenate x3 -> x2, other arithmetic: 7 us -> 0.78 us  [per_device(): jnp.concatenate([(block_all[0] + theirs[0])[None], light], axis=0)]
    add x3 -> x0, other arithmetic: 5.26 us -> none  [the longest x1 4.37 us: per_device(): plane = term if plane is None else plane + term]
  transfers between devices with their start and end apart: 12 -> 17, of which waited for: 7 -> 4; matrix products, arithmetic and copies ran while one was open for 9% -> 2% of each run, Pallas kernels for 0% -> 19%
where the time goes in v2:
time: 79.2 us; the launch traced here: 78.2 us
  starting transfers between devices  25.6 us (32%)
  Pallas kernels  19.2 us (24%)
  waiting for transfers between devices  16.5 us (21%)
  local copies, waits for them, and re-layouts  9.62 us (12%)
  other arithmetic  6.21 us (8%)
  between operations  1.05 us (1%)
    pallas_call x8, Pallas kernels, call(): pl.pallas_call(functools.partial(body, **statics), out_shape=outs, grid=(...  15 us
    ppermute x3, waiting for transfers between devices, per_device(): lax.ppermute(block_all, 'slab', [(i, i ^ 1 << bit) for i in range(slabs)])  14.1 us
    unnamed x37, local copies, waits for them, and re-layouts  9.46 us
    ppermute x2, starting transfers between devices, halo(): lax.ppermute(packed[1], 'slab', pairs_b)  6.25 us
    ppermute x2, starting transfers between devices, halo(): lax.ppermute(packed[3], ('slab', 'tile'), cross(pairs_b))  6.2 us
    ppermute x3, starting transfers between devices, per_device(): lax.ppermute(block_all, 'slab', [(i, i ^ 1 << bit) for i in range(slabs)])  3.18 us
    ppermute x2, starting transfers between devices, halo(): lax.ppermute(packed[0], 'slab', pairs_a)  3.05 us
    ppermute x2, starting transfers between devices, halo(): lax.ppermute(packed[2], ('slab', 'tile'), cross(pairs_a))  2.82 us
  transfers between devices with their start and end apart: 17, of which 4 were waited for; matrix products, arithmetic and copies ran while one was open for 2% of the time, Pallas kernels for 19%

profile of v2, /device:TPU:16, one launch (start us, length us, event | category | flops | bytes accessed | tf_op | source)
XLA Modules:
  0.0 78.2 jit_solution(5251586016837935404)
XLA Ops:
  0.7 0.9 %copy-done.4 = f32[1,3,32,512]{3,2,1,0:T(8,128)S(1)} copy-done((f32[1,3,32,512]{3,2,1,0:T(8,128)S(1)}, f32[1,3,32,512]{3,2,1,0:T(8,128)}, u32[]{:S(2)}) %copy-start.4) | copy-done | bytes 196632
  1.6 0.8 %copy-done.9 = s32[1,32,512]{2,1,0:T(8,128)S(1)} copy-done((s32[1,32,512]{2,1,0:T(8,128)S(1)}, s32[1,32,512]{2,1,0:T(8,128)}, u32[]{:S(2)}) %copy-start.9) | copy-done | bytes 65560
  3.9 1.6 %collective-permute-start = (f32[5,32,256]{2,1,0:T(8,128)S(1)}, f32[5,32,256]{2,1,0:T(8,128)S(1)}, u32[]{:S(2)}, u32[]{:S(2)}) collective-permute-start(f32[5,32,256]{2,1,0:T(8,128)S(1)} %get-tuple-element.24), channel_id=1, source_target_pairs={{0,16},{16,0},{1,17},{17,1},{2,18},{18,2},{3,19},{19,3},{4,20},{20... | collective-permute-start | bytes 491528 | tf_op jit(solution)/shard_map/ppermute | solution.py:642
  5.5 1.6 %copy-done = f32[4,8,32,512]{3,2,1,0:T(8,128)S(1)} copy-done((f32[4,8,32,512]{3,2,1,0:T(8,128)S(1)}, f32[4,8,32,512]{3,2,1,0:T(8,128)}, u32[]{:S(2)}) %copy-start) | copy-done | bytes 2097176
  7.8 1.6 %collective-permute-start.1 = (f32[288,128]{1,0:T(8,128)S(1)}, f32[288,128]{1,0:T(8,128)S(1)}, u32[]{:S(2)}, u32[]{:S(2)}) collective-permute-start(f32[288,128]{1,0:T(8,128)S(1)} %get-tuple-element.25), channel_id=1, source_target_pairs={{0,2},{2,0},{4,6},{6,4},{8,10},{10,8},{12,14},{14,12},{1,3},{3,1},... | collective-permute-start | bytes 442376 | tf_op jit(solution)/shard_map/halo0/ppermute | solution.py:627
  9.3 2.3 %collective-permute-start.2 = (f32[288,128]{1,0:T(8,128)S(1)}, f32[288,128]{1,0:T(8,128)S(1)}, u32[]{:S(2)}, u32[]{:S(2)}) collective-permute-start(f32[288,128]{1,0:T(8,128)S(1)} %get-tuple-element.26), channel_id=1, source_target_pairs={{2,4},{6,8},{10,12},{4,2},{8,6},{12,10},{3,5},{7,9},{11,13},{5,3},... | collective-permute-start | bytes 442376 | tf_op jit(solution)/shard_map/halo0/ppermute | solution.py:628
  11.8 2.7 %collective-permute-start.3 = (f32[16,128]{1,0:T(8,128)S(1)}, f32[16,128]{1,0:T(8,128)S(1)}, u32[]{:S(2)}, u32[]{:S(2)}) collective-permute-start(f32[16,128]{1,0:T(8,128)S(1)} %get-tuple-element.27), channel_id=1, source_target_pairs={{0,3},{1,2},{2,1},{3,0},{4,7},{5,6},{6,5},{7,4},{8,11},{9,10},{10,... | collective-permute-start | bytes 24584 | tf_op jit(solution)/shard_map/halo0/ppermute | solution.py:629
  14.6 2.7 %collective-permute-start.4 = (f32[16,128]{1,0:T(8,128)S(1)}, f32[16,128]{1,0:T(8,128)S(1)}, u32[]{:S(2)}, u32[]{:S(2)}) collective-permute-start(f32[16,128]{1,0:T(8,128)S(1)} %get-tuple-element.28), channel_id=1, source_target_pairs={{2,5},{3,4},{6,9},{7,8},{10,13},{11,12},{4,3},{5,2},{8,7},{9,6},{1... | collective-permute-start | bytes 24584 | tf_op jit(solution)/shard_map/halo0/ppermute | solution.py:630
  17.3 4.8 %inner.1 = (f32[2,4,6,32,256]{4,3,2,1,0:T(8,128)S(1)}, f32[2,4,2,32,256]{4,3,2,1,0:T(8,128)S(1)}, f32[2,4,2,32,256]{4,3,2,1,0:T(8,128)S(1)}, f32[4,2,32,256]{3,2,1,0:T(8,128)S(1)}) custom-call(s32[3]{0:T(128)S(1)} %pad_add_fusion.info, f32[4,8,32,512]{3,2,1,0:T(8,128)S(1)} %copy-done.1, f32[4,8,512]{2,1,0:T(8,128)S(1)} %collective-permute-done.5.line, ...), custom_call_target="tpu_custom_call" | custom-call | flops 10000000 | bytes 2000000 | tf_op jit(solution)/shard_map/inner/pallas_call | solution.py:22
  23.5 0.9 %copy-done.6 = f32[288,128]{1,0:T(8,128)S(1)} copy-done((f32[288,128]{1,0:T(8,128)S(1)}, f32[288,128]{1,0:T(8,128)}, u32[]{:S(2)}) %copy-start.6) | copy-done | bytes 147480
  24.4 0.9 %copy-done.8 = f32[288,128]{1,0:T(8,128)S(1)} copy-done((f32[288,128]{1,0:T(8,128)S(1)}, f32[288,128]{1,0:T(8,128)}, u32[]{:S(2)}) %copy-start.8) | copy-done | bytes 147480
  25.3 2.1 %rim.1 = (f32[4,2,32,256]{3,2,1,0:T(8,128)S(1)}, f32[2,4,2,32,256]{4,3,2,1,0:T(8,128)S(1)}, f32[2,4,2,32,256]{4,3,2,1,0:T(8,128)S(1)}) custom-call(s32[3]{0:T(128)S(1)} %pad_add_fusion.info, f32[288,128]{1,0:T(8,128)S(1)} %copy-done.6, f32[288,128]{1,0:T(8,128)S(1)} %copy-done.8, f32[16,128]{1,0:T(8,128)S(1)} %collective-permute-done.3.diag_a, ...), custom_call_target="tpu_custom_call" | custom-call | flops 10000000 | bytes 2000000 | tf_op jit(solution)/shard_map/rim/pallas_call | solution.py:22
  28.1 8.0 %collective-permute-done.6 = f32[4,2,32,256]{3,2,1,0:T(8,128)S(1)} collective-permute-done((f32[4,2,32,256]{3,2,1,0:T(8,128)S(1)}, f32[4,2,32,256]{3,2,1,0:T(8,128)S(1)}, u32[]{:S(2)}, u32[]{:S(2)}) %collective-permute-start.6) | collective-permute-done | bytes 262176 | tf_op jit(solution)/shard_map/scan0/ppermute | solution.py:695
  36.8 1.6 %collective-permute-start.7 = (f32[4,2,32,256]{3,2,1,0:T(8,128)S(1)}, f32[4,2,32,256]{3,2,1,0:T(8,128)S(1)}, u32[]{:S(2)}, u32[]{:S(2)}) collective-permute-start(f32[4,2,32,256]{3,2,1,0:T(8,128)S(1)} %pad_maximum_fusion), channel_id=1, source_target_pairs={{0,4},{2,6},{4,0},{6,2},{8,12},{10,14},{12,8},{14,10},{1,5},{3,7},... | collective-permute-start | bytes 786440 | tf_op jit(solution)/shard_map/scan1/ppermute | solution.py:695
  38.5 6.1 %collective-permute-done.7 = f32[4,2,32,256]{3,2,1,0:T(8,128)S(1)} collective-permute-done((f32[4,2,32,256]{3,2,1,0:T(8,128)S(1)}, f32[4,2,32,256]{3,2,1,0:T(8,128)S(1)}, u32[]{:S(2)}, u32[]{:S(2)}) %collective-permute-start.7) | collective-permute-done | bytes 262176 | tf_op jit(solution)/shard_map/scan1/ppermute | solution.py:695
  46.2 1.0 %collective-permute-start.8 = (f32[4,2,32,256]{3,2,0,1:T(8,128)}, f32[4,2,32,256]{3,2,0,1:T(8,128)}, u32[]{:S(2)}, u32[]{:S(2)}) collective-permute-start(f32[4,2,32,256]{3,2,0,1:T(8,128)} %pad_maximum_fusion.1), channel_id=1, source_target_pairs={{0,8},{2,10},{4,12},{6,14},{8,0},{10,2},{12,4},{14,6},{1,9},{3,11}... | collective-permute-start | bytes 786440 | tf_op jit(solution)/shard_map/scan2/ppermute | solution.py:695
  47.2 1.4 %pack1.1 = (f32[288,128]{1,0:T(8,128)}, f32[288,128]{1,0:T(8,128)}, f32[16,128]{1,0:T(8,128)S(1)}, f32[16,128]{1,0:T(8,128)S(1)}) custom-call(s32[3]{0:T(128)S(1)} %pad_add_fusion.info, f32[4,8,32,512]{3,2,1,0:T(8,128)S(1)} %copy-done.1, f32[4,8,32,512]{3,2,1,0:T(8,128)S(1)} %copy-done.1), custom_call_target="tpu_custom_call" | custom-call | flops 10000000 | bytes 2000000 | tf_op jit(solution)/shard_map/pack1/pallas_call | solution.py:22
  48.6 1.5 %collective-permute-start.10 = (f32[288,128]{1,0:T(8,128)}, f32[288,128]{1,0:T(8,128)S(1)}, u32[]{:S(2)}, u32[]{:S(2)}) collective-permute-start(f32[288,128]{1,0:T(8,128)} %get-tuple-element.36), channel_id=1, source_target_pairs={{0,2},{2,0},{4,6},{6,4},{8,10},{10,8},{12,14},{14,12},{1,3},{3,1},... | collective-permute-start | bytes 442376 | tf_op jit(solution)/shard_map/halo1/ppermute | solution.py:627
  50.0 4.0 %collective-permute-start.11 = (f32[288,128]{1,0:T(8,128)}, f32[288,128]{1,0:T(8,128)S(1)}, u32[]{:S(2)}, u32[]{:S(2)}) collective-permute-start(f32[288,128]{1,0:T(8,128)} %get-tuple-element.37), channel_id=1, source_target_pairs={{2,4},{6,8},{10,12},{4,2},{8,6},{12,10},{3,5},{7,9},{11,13},{5,3},... | collective-permute-start | bytes 442376 | tf_op jit(solution)/shard_map/halo1/ppermute | solution.py:628
  54.1 3.5 %collective-permute-start.13 = (f32[16,128]{1,0:T(8,128)S(1)}, f32[16,128]{1,0:T(8,128)S(1)}, u32[]{:S(2)}, u32[]{:S(2)}) collective-permute-start(f32[16,128]{1,0:T(8,128)S(1)} %get-tuple-element.39), channel_id=1, source_target_pairs={{2,5},{3,4},{6,9},{7,8},{10,13},{11,12},{4,3},{5,2},{8,7},{9,6},{1... | collective-permute-start | bytes 24584 | tf_op jit(solution)/shard_map/halo1/ppermute | solution.py:630
  57.7 1.4 %copy-done.3 = f32[2,4,6,32,256]{4,3,2,1,0:T(8,128)S(1)} copy-done((f32[2,4,6,32,256]{4,3,2,1,0:T(8,128)S(1)}, f32[2,4,6,32,256]{4,3,2,1,0:T(8,128)}, u32[]{:S(2)}) %copy-start.3) | copy-done | bytes 1572888
  59.1 1.7 %column.1 = (f32[5,2,8,32,256]{4,3,2,1,0:T(8,128)S(1)}, f32[2,2,32,256]{3,2,1,0:T(8,128)S(1)}) custom-call(f32[5,32,256]{2,1,0:T(8,128)S(1)} %get-tuple-element.23.own, f32[5,32,256]{2,1,0:T(8,128)S(1)} %collective-permute-done.other, f32[2,4,6,32,256]{4,3,2,1,0:T(8,128)S(1)} %copy-done.3, f32[2,4,2,32,256]{4,3,2,1,0:T(8,128)S(1)} %get-tuple-element.34.rim), custom_call_target="tpu_custom_call" | custom-call | flops 10000000 | bytes 2000000 | tf_op jit(solution)/shard_map/column/pallas_call | solution.py:668
  60.8 2.2 %collective-permute-done.13.diag_b = f32[16,128]{1,0:T(8,128)S(1)} collective-permute-done((f32[16,128]{1,0:T(8,128)S(1)}, f32[16,128]{1,0:T(8,128)S(1)}, u32[]{:S(2)}, u32[]{:S(2)}) %collective-permute-start.13) | collective-permute-done | bytes 8224 | tf_op jit(solution)/shard_map/halo1/ppermute | solution.py:630
  63.0 2.2 %outer.1 = f32[5,2,2,32,256]{4,3,2,1,0:T(8,128)S(1)} custom-call(s32[3]{0:T(128)S(1)} %pad_add_fusion.info, f32[288,128]{1,0:T(8,128)S(1)} %collective-permute-done.10.far_a, f32[288,128]{1,0:T(8,128)S(1)} %collective-permute-done.11.far_b, f32[16,128]{1,0:T(8,128)S(1)} %collective-permute-done.12.diag_a, f32[16,128]{1,0:T(8,128)S(1)} %collective-permute-done.13.diag_b, ...), custom_call_target="tpu_custom_call" | custom-call | flops 10000000 | bytes 2000000 | tf_op jit(solution)/shard_map/outer/pallas_call | solution.py:22
  65.3 0.9 %exponential_bitcast_fusion.1 = f32[2,32,256]{2,1,0:T(8,128)S(1)} fusion(f32[4,2,32,256]{3,2,0,1:T(8,128)} %collective-permute-done.8), kind=kLoop, calls=%fused_computation.39 | loop fusion | flops 16384 | bytes 131072 | tf_op jit(solution)/shard_map/mul | solution.py:702
  66.1 0.9 %fusion.2 = (f32[2,32,256]{2,1,0:T(8,128)S(1)}, pred[2,32,256]{2,1,0:T(8,128)(4,1)S(1)}) fusion(pred[2,32,256]{2,1,0:T(8,128)(4,1)S(1)} %get-tuple-element.51, f32[4,2,32,256]{3,2,0,1:T(8,128)} %collective-permute-done.8, f32[4,2,32,256]{3,2,1,0:T(8,128)S(1)} %copy-done.14, f32[4,2,32,256]{3,2,1,0:T(8,128)S(1)} %copy-done.16, ...), kind=kLoop, calls=%fused_computation.17 | loop fusion | flops 131072 | bytes 311298 | tf_op jit(solution)/shard_map/exp | solution.py:709
  67.0 1.1 %multiply_reduce_fusion = (f32[2,32,256]{2,1,0:T(8,128)S(1)}, f32[2,32,256]{2,1,0:T(8,128)S(1)}, f32[2,32,256]{2,1,0:T(8,128)S(1)}, f32[3,2,32,256]{3,2,0,1:T(8,128)S(1)}, f32[3,2,32,256]{3,2,0,1:T(8,128)S(1)}) fusion(f32[4,2,32,256]{3,2,0,1:T(8,128)} %collective-permute-done.8, f32[5,1,32,256]{3,2,0,1:T(8,128)S(1)} %bitcast.90, ...), kind=kLoop, calls=%fused_computation.7 | loop fusion | flops 540672 | bytes 1654784 | tf_op jit(solution)/shard_map/reduce_sum | solution.py:705
  68.8 0.9 %fusion.8.rest = f32[2,32,256]{2,1,0:T(8,128)S(1)} fusion(f32[2,32,256]{2,1,0:T(8,128)S(1)} %get-tuple-element.46, pred[2,32,256]{2,1,0:T(8,128)(4,1)S(1)} %get-tuple-element.50, f32[2,32,256]{2,1,0:T(8,128)S(1)} %get-tuple-element.45, pred[2,32,256]{2,1,0:T(8,128)(4,1)S(1)} %get-tuple-element.51, f32[2,32,256]{2,1,0:T(8,128)S(1)} %fusion, ...), kind=kLoop, calls=%fused_computation.26 | loop fusion | flops 229376 | bytes 573441 | tf_op jit(solution)/shard_map/sub | solution.py:710
  70.4 1.4 %border.1 = (f32[4,8,256]{2,1,0:T(8,128)S(1)}, f32[40,128]{1,0:T(8,128)S(1)}) custom-call(s32[3]{0:T(128)S(1)} %pad_add_fusion.info, f32[4,2,8,32,256]{4,3,2,1,0:T(8,128)S(1)} %merge.1.columns, f32[5,32,256]{2,1,0:T(8,128)S(1)} %get-tuple-element.23.own, f32[5,32,256]{2,1,0:T(8,128)S(1)} %collective-permute-done.other), custom_call_target="tpu_custom_call" | custom-call | flops 10000000 | bytes 2000000 | tf_op jit(solution)/shard_map/border/pallas_call | solution.py:22
  71.9 1.5 %collective-permute-start.15 = (f32[32,128]{1,0:T(8,128)S(1)}, f32[32,128]{1,0:T(8,128)S(1)}, u32[]{:S(2)}, u32[]{:S(2)}) collective-permute-start(f32[32,128]{1,0:T(8,128)S(1)} %slice.67), channel_id=1, source_target_pairs={{0,16},{16,0},{1,17},{17,1},{2,18},{18,2},{3,19},{19,3},{4,20},{20... | collective-permute-start | bytes 49160 | tf_op jit(solution)/shard_map/ppermute | solution.py:732
  73.7 1.9 %scatter.1.grad_in = f32[4,8,32,256]{3,2,1,0:T(8,128)S(1)} custom-call(f32[4,2,8,32,256]{4,3,2,1,0:T(8,128)S(1)} %merge.1.columns, f32[5,32,256]{2,1,0:T(8,128)S(1)} %get-tuple-element.23.own, f32[5,32,256]{2,1,0:T(8,128)S(1)} %collective-permute-done.other), custom_call_target="tpu_custom_call" | custom-call | flops 10000000 | bytes 2000000 | tf_op jit(solution)/shard_map/scatter/pallas_call | solution.py:733
  76.5 1.8 %finish.1 = f32[4,8,32,256]{3,2,1,0:T(8,128)} custom-call(s32[3]{0:T(128)S(1)} %pad_add_fusion.info, f32[4,8,32,256]{3,2,1,0:T(8,128)S(1)} %scatter.1.grad_in, f32[4,8,256]{2,1,0:T(8,128)S(1)} %collective-permute-done.14.line, f32[32,128]{1,0:T(8,128)S(1)} %collective-permute-done.15.edge, f32[8,128]{1,0:T(8,128)S(1)} %collective-permute-done.16.corner), custom_call_target="tpu_custom_call" | custom-call | flops 10000000 | bytes 2000000 | tf_op jit(solution)/shard_map/finish/pallas_call | solution.py:22
  (71 shorter events, 9.3 us)
Async XLA Ops:
  0.7 0.9 %copy-start.4 = (f32[1,3,32,512]{3,2,1,0:T(8,128)S(1)}, f32[1,3,32,512]{3,2,1,0:T(8,128)}, u32[]{:S(2)}) copy-start(f32[1,3,32,512]{3,2,1,0:T(8,128)} %cotangent.1) | copy-start | bytes 589828
  1.6 0.8 %copy-start.9 = (s32[1,32,512]{2,1,0:T(8,128)S(1)}, s32[1,32,512]{2,1,0:T(8,128)}, u32[]{:S(2)}) copy-start(s32[1,32,512]{2,1,0:T(8,128)} %offsets.1) | copy-start | bytes 196612
  2.5 0.8 %copy-start.10 = (s32[1,32,512]{2,1,0:T(8,128)S(1)}, s32[1,32,512]{2,1,0:T(8,128)}, u32[]{:S(2)}) copy-start(s32[1,32,512]{2,1,0:T(8,128)} %heading.1) | copy-start | bytes 196612
  3.9 13.4 %collective-permute-start = (f32[5,32,256]{2,1,0:T(8,128)S(1)}, f32[5,32,256]{2,1,0:T(8,128)S(1)}, u32[]{:S(2)}, u32[]{:S(2)}) collective-permute-start(f32[5,32,256]{2,1,0:T(8,128)S(1)} %get-tuple-element.24), channel_id=1, source_target_pairs={{0,16},{16,0},{1,17},{17,1},{2,18},{18,2},{3,19},{19,3},{4,20},{20... | collective-permute-start | bytes 491528 | tf_op jit(solution)/shard_map/ppermute | solution.py:642
  5.5 1.6 %copy-start = (f32[4,8,32,512]{3,2,1,0:T(8,128)S(1)}, f32[4,8,32,512]{3,2,1,0:T(8,128)}, u32[]{:S(2)}) copy-start(f32[4,8,32,512]{3,2,1,0:T(8,128)} %last.3) | copy-start | bytes 6291460
  7.0 4.6 %copy-start.1 = (f32[4,8,32,512]{3,2,1,0:T(8,128)S(1)}, f32[4,8,32,512]{3,2,1,0:T(8,128)}, u32[]{:S(2)}) copy-start(f32[4,8,32,512]{3,2,1,0:T(8,128)} %last.3) | copy-start | bytes 6291460
  7.8 14.3 %collective-permute-start.1 = (f32[288,128]{1,0:T(8,128)S(1)}, f32[288,128]{1,0:T(8,128)S(1)}, u32[]{:S(2)}, u32[]{:S(2)}) collective-permute-start(f32[288,128]{1,0:T(8,128)S(1)} %get-tuple-element.25), channel_id=1, source_target_pairs={{0,2},{2,0},{4,6},{6,4},{8,10},{10,8},{12,14},{14,12},{1,3},{3,1},... | collective-permute-start | bytes 442376 | tf_op jit(solution)/shard_map/halo0/ppermute | solution.py:627
  9.3 13.5 %collective-permute-start.2 = (f32[288,128]{1,0:T(8,128)S(1)}, f32[288,128]{1,0:T(8,128)S(1)}, u32[]{:S(2)}, u32[]{:S(2)}) collective-permute-start(f32[288,128]{1,0:T(8,128)S(1)} %get-tuple-element.26), channel_id=1, source_target_pairs={{2,4},{6,8},{10,12},{4,2},{8,6},{12,10},{3,5},{7,9},{11,13},{5,3},... | collective-permute-start | bytes 442376 | tf_op jit(solution)/shard_map/halo0/ppermute | solution.py:628
  11.7 2.8 %collective-permute-start.5 = (f32[4,8,512]{2,1,0:T(8,128)S(1)}, f32[4,8,512]{2,1,0:T(8,128)S(1)}, u32[]{:S(2)}, u32[]{:S(2)}) collective-permute-start(f32[4,8,512]{2,1,0:T(8,128)S(1)} %bitcast.91), channel_id=1, source_target_pairs={{0,1},{1,0},{2,3},{3,2},{4,5},{5,4},{6,7},{7,6},{8,9},{9,8},{10,11... | collective-permute-start | bytes 196616 | tf_op jit(solution)/shard_map/ppermute | solution.py:644
  11.8 10.2 %collective-permute-start.3 = (f32[16,128]{1,0:T(8,128)S(1)}, f32[16,128]{1,0:T(8,128)S(1)}, u32[]{:S(2)}, u32[]{:S(2)}) collective-permute-start(f32[16,128]{1,0:T(8,128)S(1)} %get-tuple-element.27), channel_id=1, source_target_pairs={{0,3},{1,2},{2,1},{3,0},{4,7},{5,6},{6,5},{7,4},{8,11},{9,10},{10,... | collective-permute-start | bytes 24584 | tf_op jit(solution)/shard_map/halo0/ppermute | solution.py:629
  14.6 7.5 %collective-permute-start.4 = (f32[16,128]{1,0:T(8,128)S(1)}, f32[16,128]{1,0:T(8,128)S(1)}, u32[]{:S(2)}, u32[]{:S(2)}) collective-permute-start(f32[16,128]{1,0:T(8,128)S(1)} %get-tuple-element.28), channel_id=1, source_target_pairs={{2,5},{3,4},{6,9},{7,8},{10,13},{11,12},{4,3},{5,2},{8,7},{9,6},{1... | collective-permute-start | bytes 24584 | tf_op jit(solution)/shard_map/halo0/ppermute | solution.py:630
  22.1 23.3 %copy-start.2 = (f32[2,4,6,32,256]{4,3,2,1,0:T(8,128)}, f32[2,4,6,32,256]{4,3,2,1,0:T(8,128)S(1)}, u32[]{:S(2)}) copy-start(f32[2,4,6,32,256]{4,3,2,1,0:T(8,128)S(1)} %get-tuple-element.33.vals) | copy-start | bytes 4718596
  23.5 0.9 %copy-start.6 = (f32[288,128]{1,0:T(8,128)S(1)}, f32[288,128]{1,0:T(8,128)}, u32[]{:S(2)}) copy-start(f32[288,128]{1,0:T(8,128)} %copy-done.5) | copy-start | bytes 442372
  24.4 0.9 %copy-start.8 = (f32[288,128]{1,0:T(8,128)S(1)}, f32[288,128]{1,0:T(8,128)}, u32[]{:S(2)}) copy-start(f32[288,128]{1,0:T(8,128)} %copy-done.7) | copy-start | bytes 442372
  27.5 8.6 %collective-permute-start.6 = (f32[4,2,32,256]{3,2,1,0:T(8,128)S(1)}, f32[4,2,32,256]{3,2,1,0:T(8,128)S(1)}, u32[]{:S(2)}, u32[]{:S(2)}) collective-permute-start(f32[4,2,32,256]{3,2,1,0:T(8,128)S(1)} %get-tuple-element.32), channel_id=1, source_target_pairs={{0,2},{2,0},{4,6},{6,4},{8,10},{10,8},{12,14},{14,12},{1,3},{3,1},... | collective-permute-start | bytes 786440 | tf_op jit(solution)/shard_map/scan0/ppermute | solution.py:695
  36.8 7.8 %collective-permute-start.7 = (f32[4,2,32,256]{3,2,1,0:T(8,128)S(1)}, f32[4,2,32,256]{3,2,1,0:T(8,128)S(1)}, u32[]{:S(2)}, u32[]{:S(2)}) collective-permute-start(f32[4,2,32,256]{3,2,1,0:T(8,128)S(1)} %pad_maximum_fusion), channel_id=1, source_target_pairs={{0,4},{2,6},{4,0},{6,2},{8,12},{10,14},{12,8},{14,10},{1,5},{3,7},... | collective-permute-start | bytes 786440 | tf_op jit(solution)/shard_map/scan1/ppermute | solution.py:695
  44.6 0.8 copy-start.13
  45.4 0.8 copy-start.11
  46.2 19.1 %collective-permute-start.8 = (f32[4,2,32,256]{3,2,0,1:T(8,128)}, f32[4,2,32,256]{3,2,0,1:T(8,128)}, u32[]{:S(2)}, u32[]{:S(2)}) collective-permute-start(f32[4,2,32,256]{3,2,0,1:T(8,128)} %pad_maximum_fusion.1), channel_id=1, source_target_pairs={{0,8},{2,10},{4,12},{6,14},{8,0},{10,2},{12,4},{14,6},{1,9},{3,11}... | collective-permute-start | bytes 786440 | tf_op jit(solution)/shard_map/scan2/ppermute | solution.py:695
  48.6 14.4 %collective-permute-start.10 = (f32[288,128]{1,0:T(8,128)}, f32[288,128]{1,0:T(8,128)S(1)}, u32[]{:S(2)}, u32[]{:S(2)}) collective-permute-start(f32[288,128]{1,0:T(8,128)} %get-tuple-element.36), channel_id=1, source_target_pairs={{0,2},{2,0},{4,6},{6,4},{8,10},{10,8},{12,14},{14,12},{1,3},{3,1},... | collective-permute-start | bytes 442376 | tf_op jit(solution)/shard_map/halo1/ppermute | solution.py:627
  50.0 13.0 %collective-permute-start.11 = (f32[288,128]{1,0:T(8,128)}, f32[288,128]{1,0:T(8,128)S(1)}, u32[]{:S(2)}, u32[]{:S(2)}) collective-permute-start(f32[288,128]{1,0:T(8,128)} %get-tuple-element.37), channel_id=1, source_target_pairs={{2,4},{6,8},{10,12},{4,2},{8,6},{12,10},{3,5},{7,9},{11,13},{5,3},... | collective-permute-start | bytes 442376 | tf_op jit(solution)/shard_map/halo1/ppermute | solution.py:628
  54.0 6.7 %collective-permute-start.12 = (f32[16,128]{1,0:T(8,128)S(1)}, f32[16,128]{1,0:T(8,128)S(1)}, u32[]{:S(2)}, u32[]{:S(2)}) collective-permute-start(f32[16,128]{1,0:T(8,128)S(1)} %get-tuple-element.38), channel_id=1, source_target_pairs={{0,3},{1,2},{2,1},{3,0},{4,7},{5,6},{6,5},{7,4},{8,11},{9,10},{10,... | collective-permute-start | bytes 24584 | tf_op jit(solution)/shard_map/halo1/ppermute | solution.py:629
  54.1 8.9 %collective-permute-start.13 = (f32[16,128]{1,0:T(8,128)S(1)}, f32[16,128]{1,0:T(8,128)S(1)}, u32[]{:S(2)}, u32[]{:S(2)}) collective-permute-start(f32[16,128]{1,0:T(8,128)S(1)} %get-tuple-element.39), channel_id=1, source_target_pairs={{2,5},{3,4},{6,9},{7,8},{10,13},{11,12},{4,3},{5,2},{8,7},{9,6},{1... | collective-permute-start | bytes 24584 | tf_op jit(solution)/shard_map/halo1/ppermute | solution.py:630
  57.6 1.4 %copy-start.3 = (f32[2,4,6,32,256]{4,3,2,1,0:T(8,128)S(1)}, f32[2,4,6,32,256]{4,3,2,1,0:T(8,128)}, u32[]{:S(2)}) copy-start(f32[2,4,6,32,256]{4,3,2,1,0:T(8,128)} %copy-done.2) | copy-start | bytes 4718596
  59.1 7.1 %copy-start.14 = (f32[4,2,32,256]{3,2,1,0:T(8,128)S(1)}, f32[4,2,32,256]{3,2,1,0:T(8,128)}, u32[]{:S(2)}) copy-start(f32[4,2,32,256]{3,2,1,0:T(8,128)} %copy-done.13) | copy-start | bytes 786436
  59.1 7.1 %copy-start.16 = (f32[4,2,32,256]{3,2,1,0:T(8,128)S(1)}, f32[4,2,32,256]{3,2,1,0:T(8,128)}, u32[]{:S(2)}) copy-start(f32[4,2,32,256]{3,2,1,0:T(8,128)} %copy-done.15) | copy-start | bytes 786436
  59.1 8.0 %copy-start.12 = (f32[3,2,32,256]{3,2,0,1:T(8,128)S(1)}, f32[3,2,32,256]{3,2,0,1:T(8,128)}, u32[]{:S(2)}) copy-start(f32[3,2,32,256]{3,2,0,1:T(8,128)} %copy-done.11) | copy-start | bytes 589828
  59.1 8.0 %copy-start.17 = (f32[2,32,256]{2,1,0:T(8,128)S(1)}, f32[2,32,256]{2,1,0:T(8,128)}, u32[]{:S(2)}) copy-start(f32[2,32,256]{2,1,0:T(8,128)} %get-tuple-element.55) | copy-start | bytes 196612
  68.2 7.4 %collective-permute-start.9 = (f32[3,32,64]{2,1,0:T(8,128)S(1)}, f32[3,32,64]{2,1,0:T(8,128)S(1)}, u32[]{:S(2)}, u32[]{:S(2)}) collective-permute-start(f32[3,32,64]{2,1,0:T(8,128)S(1)} %dynamic-slice_bitcast_fusion), channel_id=1, source_target_pairs={{0,16},{16,0},{1,17},{17,1},{2,18},{18,2},{3,19},{19,3},{4,20},{20... | collective-permute-start | bytes 73736 | tf_op jit(solution)/shard_map/ppermute | solution.py:754
  71.8 4.7 %collective-permute-start.14 = (f32[4,8,256]{2,1,0:T(8,128)S(1)}, f32[4,8,256]{2,1,0:T(8,128)S(1)}, u32[]{:S(2)}, u32[]{:S(2)}) collective-permute-start(f32[4,8,256]{2,1,0:T(8,128)S(1)} %get-tuple-element.42), channel_id=1, source_target_pairs={{0,1},{1,0},{2,3},{3,2},{4,5},{5,4},{6,7},{7,6},{8,9},{9,8},{10,11... | collective-permute-start | bytes 98312 | tf_op jit(solution)/shard_map/ppermute | solution.py:730
  71.9 4.6 %collective-permute-start.15 = (f32[32,128]{1,0:T(8,128)S(1)}, f32[32,128]{1,0:T(8,128)S(1)}, u32[]{:S(2)}, u32[]{:S(2)}) collective-permute-start(f32[32,128]{1,0:T(8,128)S(1)} %slice.67), channel_id=1, source_target_pairs={{0,16},{16,0},{1,17},{17,1},{2,18},{18,2},{3,19},{19,3},{4,20},{20... | collective-permute-start | bytes 49160 | tf_op jit(solution)/shard_map/ppermute | solution.py:732
  73.4 3.0 %collective-permute-start.16 = (f32[8,128]{1,0:T(8,128)S(1)}, f32[8,128]{1,0:T(8,128)S(1)}, u32[]{:S(2)}, u32[]{:S(2)}) collective-permute-start(f32[8,128]{1,0:T(8,128)S(1)} %slice.68), channel_id=1, source_target_pairs={{0,17},{1,16},{16,1},{17,0},{2,19},{3,18},{18,3},{19,2},{4,21},{5,... | collective-permute-start | bytes 12296 | tf_op jit(solution)/shard_map/ppermute | solution.py:731
  (3 other events, 2.1 us)

commit v3 on v2

--- a/solution.py
+++ b/solution.py
@@ -6,6 +6,7 @@
 from jax.experimental import pallas as pl
 from jax.experimental.pallas import tpu as pltpu
 from jax.sharding import PartitionSpec as P
+
 
 LEVELS = 8
 BITS = LEVELS.bit_length() - 1
@@ -17,7 +18,7 @@
 MIB = 2**20
 
 
-def call(body, name, outs, args, scratch=(), limit=16, flops=10**7, specs=None, **statics):
+def call(body, outs, args, scratch=(), limit=16, flops=10**7, specs=None, **statics):
     inputs = [SMEM] + [VMEM] * (len(args) - 1)
     return pl.pallas_call(
         functools.partial(body, **statics),
@@ -30,7 +31,6 @@
             flops=flops, bytes_accessed=2 * 10**6, transcendentals=0
         ),
         compiler_params=pltpu.CompilerParams(vmem_limit_bytes=limit * MIB),
-        name=name,
     )(*args)
 
 
@@ -93,76 +93,95 @@
     return base, side, source
 
 
-def pack_body(info, first, last, out_a, out_b, diag_a, diag_b, *, width):
-    h, t, s = (info[0], info[1], info[2])
-    even = s % 2 == 0
+def first_body(info, offsets, heading, cotangent, voxels, own, sent, line, code, head, cot, strip, sems, *, width, depth):
+    h, t = (info[0], info[1])
+    channels, planes, rows, _ = voxels.shape
+    row = pl.multiple_of(jnp.where(t == 0, rows - SUB, 0), SUB)
+    copies = [
+        pltpu.make_async_copy(voxels.at[:, :, pl.ds(row, SUB), :], strip, sems.at[0]),
+        pltpu.make_async_copy(offsets, code, sems.at[1]),
+        pltpu.make_async_copy(heading, head, sems.at[2]),
+        pltpu.make_async_copy(cotangent, cot, sems.at[3]),
+    ]
+    for copy in copies:
+        copy.start()
+    copies[0].wait()
+    for c in range(channels):
+        for k in range(planes):
+            line[c, k : k + 1, :] = jnp.where(
+                t == 0, strip[c, k, SUB - 1 : SUB, :], strip[c, k, :1, :]
+            )
+    for copy in copies[1:]:
+        copy.wait()
+    for out, at in ((own, h), (sent, 1 - h)):
+        cols = pl.ds(pl.multiple_of(at * width, LANES), width)
+        out[0] = code[0, :, cols].astype(F32)
+        out[1] = head[0, :, cols].astype(F32)
+        for c in range(channels - 1):
+            out[2 + c] = cot[0, c, :, cols] * depth
+
+
+def message_rows(channels, rows, count):
+    body = channels * count * rows
+    lines = -(-channels * count // SUB) * SUB
+    return body, body + lines, body + lines + rows
+
+
+def pack_body(info, first, last, line, out_a, out_b, *, width):
+    h, s = (info[0], info[2])
     channels, _, rows, _ = first.shape
+    planes = line.shape[1]
     count = width // LANES
     base, side, source = window_parts(h, width)
+    at_line, at_edge, _ = message_rows(channels, rows, count)
     lane = iota((rows, LANES), 1)
-    row = pl.multiple_of(jnp.where(t == 0, rows - SUB, 0), SUB)
-    pick = iota((SUB, LANES), 0) == jnp.where(t == 0, SUB - 1, 0)
-    lane8 = iota((SUB, LANES), 1)
-
-    def fill(block, out, diag):
+
+    def fill(block, k, out):
         edge = jnp.zeros((rows, LANES), F32)
-        corner = jnp.zeros((SUB, LANES), F32)
         for c in range(channels):
             for j in range(count):
                 at = c * count + j
                 cols = pl.ds(base + j * LANES, LANES)
                 out[at * rows : (at + 1) * rows, :] = block[c, 0, :, cols]
-                line = jnp.where(pick, block[c, 0, pl.ds(row, SUB), cols], 0.0)
-                diag[at : at + 1, :] = jnp.sum(line, axis=0, keepdims=True)
+                out[at_line + at : at_line + at + 1, :] = line[c, k : k + 1, cols]
+            cols = pl.ds(side, LANES)
             turn = lax.rem(c - source + LANES, LANES)
-            cols = pl.ds(side, LANES)
             edge = jnp.where(lane == c, pltpu.roll(block[c, 0, :, cols], turn, 1), edge)
-            line = jnp.where(pick, block[c, 0, pl.ds(row, SUB), cols], 0.0)
-            line = jnp.sum(line, axis=0, keepdims=True)
-            line = pltpu.roll(jnp.broadcast_to(line, (SUB, LANES)), turn, 1)
-            corner = jnp.where(lane8 == c, line, corner)
-        out[channels * count * rows :, :] = edge
-        diag[channels * count :, :] = corner
-
-    @pl.when(even)
+            turn = lax.rem(channels + c - source + LANES, LANES)
+            corner = jnp.broadcast_to(line[c, k : k + 1, cols], (SUB, LANES))
+            corner = pltpu.roll(corner, turn, 1)[:1]
+            edge = jnp.where(lane == channels + c, corner, edge)
+        out[at_edge:, :] = edge
+
+    @pl.when(s % 2 == 0)
     def _():
-        fill(last, out_a, diag_a)
-        fill(first, out_b, diag_b)
-
-    @pl.when(jnp.logical_not(even))
+        fill(last, planes - 1, out_a)
+        fill(first, 0, out_b)
+
+    @pl.when(s % 2 == 1)
     def _():
-        fill(first, out_a, diag_a)
-        fill(last, out_b, diag_b)
-
-
-def code_body(info, offsets, heading, cotangent, own, sent, *, width, depth):
-    h = info[0]
-    for out, at in ((own, h), (sent, 1 - h)):
-        cols = pl.ds(pl.multiple_of(at * width, LANES), width)
-        out[0] = offsets[0, :, cols].astype(F32)
-        out[1] = heading[0, :, cols].astype(F32)
-        for c in range(cotangent.shape[1]):
-            out[2 + c] = cotangent[0, c, :, cols] * depth
-
-
-def spread_message(msg, diag, grid, plane, info, channels, rows, count):
+        fill(first, 0, out_a)
+        fill(last, planes - 1, out_b)
+
+
+def spread_message(msg, grid, plane, info, channels, rows, count):
     h, t = (info[0], info[1])
-    body = channels * count
-    edge = msg[body * rows :, :]
-    corner = diag[body:, :]
+    at_line, at_edge, _ = message_rows(channels, rows, count)
+    edge = msg[at_edge:, :]
     beyond = pl.ds(pl.multiple_of(jnp.where(t == 0, SUB + rows, 0), SUB), SUB)
     for c in range(channels):
-        turn = beside_shift(c, h)
         first = c * count
         tiles = [msg[(first + j) * rows : (first + j + 1) * rows, :] for j in range(count)]
         lines = [
-            jnp.broadcast_to(diag[first + j : first + j + 1, :], (SUB, LANES))
+            jnp.broadcast_to(msg[at_line + first + j : at_line + first + j + 1, :], (SUB, LANES))
             for j in range(count)
         ]
-        for e, xs in enumerate(shifts(tiles, pltpu.roll(edge, turn, 1), h)):
+        side = pltpu.roll(edge, beside_shift(c, h), 1)
+        corner = pltpu.roll(edge[:SUB], beside_shift(channels + c, h), 1)
+        for e, xs in enumerate(shifts(tiles, side, h)):
             for j, x in enumerate(xs):
                 grid[e, c, plane, SUB : SUB + rows, j * LANES : (j + 1) * LANES] = x
-        for e, xs in enumerate(shifts(lines, pltpu.roll(corner, turn, 1), h)):
+        for e, xs in enumerate(shifts(lines, corner, h)):
             for j, x in enumerate(xs):
                 grid[e, c, plane, beyond, j * LANES : (j + 1) * LANES] = x
 
@@ -307,14 +326,20 @@
         each_tile(rows, width, shade)
 
 
-def rim_body(info, near_a, near_b, diag_a, diag_b, own, other, part, ends, inner, pay, rim, ends_out, grid, *, scale):
+def chunk_mask(s, chunk):
+    bit = (iota((SUB, LANES), 1) >> (chunk.bit_length() - 1)) & 1
+    mine = s & 1
+    return bit == mine, jnp.where(mine == 1, LANES - chunk, chunk)
+
+
+def rim_body(info, near_a, near_b, own, other, part, ends, inner, pay, rim, ends_out, keep, send, grid, *, scale, chunk):
     t, s = (info[1], info[2])
     _, channels, _, rows, width = part.shape
     count = width // LANES
     even = s % 2 == 0
     rays = (own, other)
-    spread_message(near_a, diag_a, grid, jnp.where(even, 1, 0), info, channels, rows, count)
-    spread_message(near_b, diag_b, grid, jnp.where(even, 0, 1), info, channels, rows, count)
+    spread_message(near_a, grid, jnp.where(even, 1, 0), info, channels, rows, count)
+    spread_message(near_b, grid, jnp.where(even, 0, 1), info, channels, rows, count)
     for row0, at, cols, yx, wz in ray_tiles(rays, rows, width, t):
 
         def channel(c, carry, row0=row0, at=at, cols=cols, yx=yx, wz=wz):
@@ -326,9 +351,11 @@
             return carry
 
         lax.fori_loop(0, channels, channel, 0)
-    for q in range(2):
-
-        def shade(row, col, q=q):
+    kept, turn = chunk_mask(s, chunk)
+
+    def shade(row, col):
+        lights = []
+        for q in range(2):
             ahead = rays[q][1, row, col] == 0.0
             sigma = [log_soft(rim[q, 0, p, row, col]) * scale for p in range(2)]
             left = [jnp.exp(-x) for x in sigma]
@@ -339,20 +366,27 @@
             pay[0, q, row, col] = sigma[0] + middle + sigma[1]
             low = jnp.where(ahead, 1.0, last) * (1.0 - left[0])
             high = jnp.where(ahead, last, 1.0) * (1.0 - left[1])
-            for c in range(channels - 1):
-                pay[c + 1, q, row, col] = (
-                    low * logistic(rim[q, c + 1, 0, row, col])
-                    + first * inner[c + 1, q, row, col]
-                    + high * logistic(rim[q, c + 1, 1, row, col])
-                )
-
-        each_tile(rows, width, shade)
-
-
-def column_body(own, other, vals, rim, cols5, tail, *, scale):
+            light = [
+                low * logistic(rim[q, c + 1, 0, row, col])
+                + first * inner[c + 1, q, row, col]
+                + high * logistic(rim[q, c + 1, 1, row, col])
+                for c in range(channels - 1)
+            ]
+            pay[1, q, row, col] = total_of([rays[q][2 + c, row, col] * x for c, x in enumerate(light)])
+            lights.append(light)
+        for c, (a, b) in enumerate(zip(*lights)):
+            keep[c, row, col] = jnp.where(kept, a, pltpu.roll(b, turn, 1))
+            send[c, row, col] = jnp.where(kept, pltpu.roll(b, LANES - turn, 1), a)
+
+    each_tile(rows, width, shade)
+
+
+def column_body(info, own, other, vals, rim, ends, cols5, *, scale, slabs):
+    s = info[2]
     _, channels, inside, rows, width = vals.shape
     planes = inside + 2
     rays = (own, other)
+    live = {-1: jnp.where(s > 0, 1.0, 0.0), planes: jnp.where(s < slabs - 1, 1.0, 0.0)}
     for q in range(2):
 
         def shade(row, col, q=q):
@@ -361,116 +395,151 @@
             pull = [rays[q][2 + c, row, col] for c in range(channels - 1)]
 
             def value(c, k):
+                if k in live:
+                    return ends[q, c, 1 if k > 0 else 0, row, col]
                 if k == 0 or k == planes - 1:
                     return rim[q, c, 1 if k else 0, row, col]
                 return vals[q, c, k - 1, row, col]
 
             ks = range(planes)
-            sigma = [log_soft(value(0, k)) * scale for k in ks]
-            slope = [logistic(value(0, k)) * scale for k in ks]
-            left = [jnp.exp(-x) for x in sigma]
-            rising, falling = products(left)
-            share, after = ([], [])
-            tint = [[] for _ in range(channels - 1)]
-            for k in ks:
-                reach = jnp.where(ahead, rising[k], falling[k])
+            every = range(-1, planes + 1)
+            sigma = {k: log_soft(value(0, k)) * scale for k in every}
+            slope = {k: logistic(value(0, k)) * scale for k in every}
+            left = {k: jnp.exp(-sigma[k]) for k in every}
+            rising, falling = products([left[k] for k in ks])
+            through = rising[-1] * left[planes - 1]
+            share, after = ({}, {})
+            tint = [{} for _ in range(channels - 1)]
+            for k in every:
+                if k == -1:
+                    reach = jnp.where(ahead, jnp.exp(sigma[k]), through)
+                elif k == planes:
+                    reach = jnp.where(ahead, through, jnp.exp(sigma[k]))
+                else:
+                    reach = jnp.where(ahead, rising[k], falling[k])
                 glow = reach * (1.0 - left[k])
+                if k in live:
+                    glow = glow * live[k]
+                    slope[k] = slope[k] * live[k]
                 hue = []
                 for c in range(channels - 1):
                     colour = logistic(value(c + 1, k))
                     hue.append(pull[c] * colour)
-                    tint[c].append(glow * hue[-1] * (1.0 - colour))
+                    tint[c][k] = glow * hue[-1] * (1.0 - colour)
                 hue = total_of(hue)
-                share.append(glow * hue)
-                after.append(reach * left[k] * hue)
-            whole = total_of(share)
-            run = jnp.zeros_like(whole)
-            pushed = []
-            for k in ks:
+                share[k] = glow * hue
+                after[k] = reach * left[k] * hue
+            whole = total_of([share[k] for k in ks])
+            run = -share[-1]
+            pushed = {}
+            for k in every:
                 upto = run + share[k]
-                pushed.append((after[k] + jnp.where(ahead, upto, whole - run)) * slope[k])
+                pushed[k] = (after[k] + jnp.where(ahead, upto, whole - run)) * slope[k]
                 run = upto
-            tail[0, q, row, col] = rising[-1] * left[-1]
-            tail[1, q, row, col] = whole
             for n, field in enumerate([pushed, slope] + tint):
-                for p in range(planes):
-                    x = wz[1] * field[p]
-                    if p > 0:
-                        x = x + wz[2] * field[p - 1]
-                    if p < planes - 1:
-                        x = x + wz[0] * field[p + 1]
-                    cols5[n, q, p, row, col] = x
+                for p in ks:
+                    cols5[n, q, p, row, col] = (
+                        wz[1] * field[p] + wz[2] * field[p - 1] + wz[0] * field[p + 1]
+                    )
 
         each_tile(rows, width, shade)
 
 
-def outer_body(info, far_a, far_b, diag_a, diag_b, own, other, ends, tail, outer, grid, value, *, scale, slabs):
-    t, s = (info[1], info[2])
-    _, channels, _, rows, width = ends.shape
-    count = width // LANES
-    even = s % 2 == 0
+def ray_order(info, bit, heading):
+    lower = ((info[2] >> bit) & 1) == 1
+    return heading == jnp.where(lower, 0.0, 1.0)
+
+
+def scan_body(info, own, other, block, theirs, *refs, bit, rounds, chunk, tile_bit):
+    first = bit == 0
+    last = bit == rounds - 1
+    refs = list(refs)
+    state = None if first else refs.pop(0)
+    out_state = refs.pop(0)
+    out_block = None if last else refs.pop(0)
+    out_final = refs.pop(0) if bit == rounds - 2 else None
+    mine_scale, their_scale = refs
     rays = (own, other)
-    spread_message(far_a, diag_a, grid, jnp.where(even, 1, 0), info, channels, rows, count)
-    spread_message(far_b, diag_b, grid, jnp.where(even, 0, 1), info, channels, rows, count)
-    for row0, at, cols, yx, wz in ray_tiles(rays, rows, width, t):
-
-        def channel(c, carry, row0=row0, at=at, cols=cols, yx=yx, wz=wz):
-            for p in range(2):
-                new = bilinear(yx, grid, c, p, row0, cols)
-                for q in range(2):
-                    value[q, c, p, at, cols] = ends[q, c, p, at, cols] + wz[q][2 * p] * new[q]
-            return carry
-
-        lax.fori_loop(0, channels, channel, 0)
-    live = (jnp.where(s > 0, 1.0, 0.0), jnp.where(s < slabs - 1, 1.0, 0.0))
-    for q in range(2):
-
-        def shade(row, col, q=q):
-            ahead = rays[q][1, row, col] == 0.0
-            wz = three(split_code(rays[q][0, row, col])[0])
-            pull = [rays[q][2 + c, row, col] for c in range(channels - 1)]
-            through = tail[0, q, row, col]
-            whole = tail[1, q, row, col]
-            for p in range(2):
-                v = value[q, 0, p, row, col]
-                sigma = log_soft(v) * scale
-                slope = logistic(v) * (scale * live[p])
-                enters = ahead if p == 0 else jnp.logical_not(ahead)
-                left = jnp.exp(-sigma)
-                reach = jnp.where(enters, jnp.exp(sigma), through)
-                glow = reach * (1.0 - left) * live[p]
-                hue = []
-                fields = []
-                for c in range(channels - 1):
-                    colour = logistic(value[q, c + 1, p, row, col])
-                    hue.append(pull[c] * colour)
-                    fields.append(glow * hue[-1] * (1.0 - colour))
-                hue = total_of(hue)
-                share = glow * hue
-                upto = jnp.where(enters, 0.0, whole + share)
-                pushed = (reach * left * hue + upto) * slope
-                for n, field in enumerate([pushed, slope] + fields):
-                    outer[n, q, p, row, col] = wz[2 - 2 * p] * field
-
-        each_tile(rows, width, shade)
-
-
-def merge_body(cols5, outer, reach, rest, columns, *, channels):
+    _, rows, width = own.shape
+    kept, turn = chunk_mask(info[2], chunk)
+    halved = tile_bit is not None and bit >= tile_bit
+    my_tile = (info[2] >> (tile_bit or 0)) & 1
+
+    def ray(row, col):
+        scales = []
+        for q in range(2):
+            heading = rays[q][1, row, col]
+            earlier = ray_order(info, bit, heading)
+            depth = block[0, q, row, col]
+            before = jnp.zeros_like(depth) if first else state[0, q, row, col]
+            rest = block[1, q, row, col] if first else state[1, q, row, col]
+            if last:
+                their_depth = their_light = theirs[q, row, col]
+            else:
+                their_depth, their_light = (theirs[n, q, row, col] for n in range(2))
+            fade = jnp.exp(-depth)
+            their_fade = jnp.exp(-their_depth)
+            later = fade if first else jnp.exp(before - depth)
+            out_rest = rest + jnp.where(earlier, 0.0, later * their_light)
+            out_before = before + jnp.where(earlier, their_depth, 0.0)
+            if last:
+                reach = jnp.exp(-out_before)
+                out_state[0, q, row, col] = reach
+                out_state[1, q, row, col] = reach * out_rest
+            else:
+                out_state[0, q, row, col] = out_before
+                out_state[1, q, row, col] = out_rest
+                light = block[1, q, row, col]
+                out_depth = depth + their_depth
+                out_light = jnp.where(
+                    earlier, their_light + their_fade * light, light + fade * their_light
+                )
+                out_block[0, q, row, col] = out_depth
+                out_block[1, q, row, col] = out_light
+                if out_final is not None:
+                    out_final[q, row, col] = jnp.where(
+                        ray_order(info, bit + 1, heading), out_light, out_depth
+                    )
+            scales.append((jnp.where(earlier, their_fade, 1.0), jnp.where(earlier, 1.0, fade)))
+        packed = [jnp.where(kept, a, pltpu.roll(b, turn, 1)) for a, b in zip(*scales)]
+        for out, x in zip((mine_scale, their_scale), packed):
+            if not halved:
+                out[row, col] = x
+            else:
+
+                @pl.when(col.start == my_tile * LANES)
+                def _(out=out, x=x):
+                    out[row, :] = x
+
+    each_tile(rows, width, ray)
+
+
+def light_body(info, keep, got, mine_scale, their_scale, *outs, tile_bit):
+    mine, theirs = (mine_scale[...], their_scale[...])
+    if tile_bit is None:
+        for c in range(keep.shape[0]):
+            outs[0][c] = mine * keep[c] + theirs * got[c]
+        return
+    tile = (info[2] >> tile_bit) & 1
+    for c in range(keep.shape[0]):
+        both = mine * keep[c] + theirs * got[c]
+        low, high = (both[:, :LANES], both[:, LANES:])
+        outs[0][c] = jnp.where(tile == 0, low, high)
+        outs[1][c] = jnp.where(tile == 0, high, low)
+
+
+def merge_body(reach_rest, cols5, columns, *, channels):
     _, _, planes, rows, width = cols5.shape
 
     def ray(row, col):
         for q in range(2):
-            near, far = (reach[q, row, col], rest[q, row, col])
+            near, far = (reach_rest[0, q, row, col], reach_rest[1, q, row, col])
             for p in range(planes):
-                side = None if 0 < p < planes - 1 else (0 if p == 0 else 1)
-
-                def field(n):
-                    x = cols5[n, q, p, row, col]
-                    return x if side is None else x + outer[n, q, side, row, col]
-
-                columns[0, q, p, row, col] = near * field(0) - far * field(1)
+                columns[0, q, p, row, col] = (
+                    near * cols5[0, q, p, row, col] - far * cols5[1, q, p, row, col]
+                )
                 for c in range(1, channels):
-                    columns[c, q, p, row, col] = near * field(c + 1)
+                    columns[c, q, p, row, col] = near * cols5[c + 1, q, p, row, col]
 
     each_tile(rows, width, ray)
 
@@ -571,20 +640,18 @@
 
 def finish_body(info, grad_in, line, edge, corner, grad):
     h, t = (info[0], info[1])
-    channels, planes, rows, width = grad.shape
-    row = iota((rows, width), 0)
-    lane = iota((rows, width), 1)
+    _, planes, rows, width = grad.shape
+    c = pl.program_id(0)
+    source = jnp.where(h == 0, LANES - 1, 0)
+    side = pl.ds(pl.multiple_of(jnp.where(h == 0, width - LANES, 0), LANES), LANES)
     last = jnp.where(t == 0, rows - 1, 0)
-    at_row = row == last
-    at_lane = lane == jnp.where(h == 0, width - 1, 0)
+    at_row = iota((rows, width), 0) == last
+    at_lane = iota((rows, LANES), 1) == source
     packed = edge[...] + jnp.where(iota((rows, LANES), 0) == last, corner[:1], 0.0)
-
-    for c in range(channels):
-        for p in range(planes):
-            at = c * planes + p
-            both = jnp.where(at_row, line[c, p : p + 1, :], 0.0)
-            both = both + jnp.where(at_lane, packed[:, at : at + 1], 0.0)
-            grad[c, p] = grad_in[c, p] + both
+    for p in range(planes):
+        grad[0, p] = grad_in[0, p] + jnp.where(at_row, line[0, p : p + 1, :], 0.0)
+        turn = lax.rem(source - (c * planes + p) + LANES, LANES)
+        grad[0, p, :, side] += jnp.where(at_lane, pltpu.roll(packed, turn, 1), 0.0)
 
 
 def per_device(voxels, offsets, heading, cotangent):
@@ -600,114 +667,112 @@
     swap = [(0, 1), (1, 0)]
     count = width // LANES
     grid = lambda n: pltpu.VMEM((3, channels, n, rows + 2 * SUB, width), F32)
+    colours = channels - 1
+    half = slabs // dirs
+    chunk = total // slabs
+    rounds = slabs.bit_length() - 1
+    tile_bit = (LANES // chunk).bit_length() - 1
+    tile_bit = tile_bit if 0 < tile_bit < rounds - 1 else None
 
     pairs_a = [(i, i ^ 1) for i in range(slabs)]
     pairs_b = [(i, i + 1) for i in range(1, slabs - 1, 2)]
     pairs_b = pairs_b + [(b, a) for a, b in pairs_b]
-    cross = lambda pairs: [
-        (a * cores + i, b * cores + 1 - i) for a, b in pairs for i in range(cores)
-    ]
-
-    def halo(level):
-        def block(k):
-            return pl.BlockSpec((channels, 1, rows, total), lambda i: (0, k, 0, 0))
-
-        big = shape(channels * count * rows + rows, LANES)
-        small = shape(channels * count + SUB, LANES)
-        packed = call(
-            pack_body,
-            f"pack{level}",
-            [big, big, small, small],
-            (info, voxels, voxels),
-            specs=[SMEM, block(level), block(planes - 1 - level)],
-            width=width,
-        )
-        with jax.named_scope(f"halo{level}"):
-            return (
-                lax.ppermute(packed[0], "slab", pairs_a),
-                lax.ppermute(packed[1], "slab", pairs_b),
-                lax.ppermute(packed[2], ("slab", "tile"), cross(pairs_a)),
-                lax.ppermute(packed[3], ("slab", "tile"), cross(pairs_b)),
-            )
-
-    near = halo(0)
-    own, sent = call(
-        code_body,
-        "codes",
-        [shape(channels + 1, rows, width)] * 2,
-        (info, offsets, heading, cotangent),
+
+    hbm = pl.BlockSpec(memory_space=pltpu.HBM)
+    ray = shape(channels + 1, rows, width)
+    own, sent, line = pl.pallas_call(
+        functools.partial(first_body, width=width, depth=depth),
+        out_shape=[ray, ray, shape(channels, planes, total)],
+        in_specs=[SMEM] + [hbm] * 4,
+        out_specs=[VMEM] * 3,
+        scratch_shapes=[
+            pltpu.VMEM(offsets.shape, jnp.int32),
+            pltpu.VMEM(heading.shape, jnp.int32),
+            pltpu.VMEM(cotangent.shape, F32),
+            pltpu.VMEM((channels, planes, SUB, total), F32),
+            pltpu.SemaphoreType.DMA((4,)),
+        ],
+        compiler_params=pltpu.CompilerParams(vmem_limit_bytes=8 * MIB),
+        name="first",
+    )(info, offsets, heading, cotangent, voxels)
+    line = lax.ppermute(line, "tile", swap)
+    other = lax.ppermute(sent, "dir", swap)
+
+    def block(k):
+        return pl.BlockSpec((channels, 1, rows, total), lambda i: (0, k, 0, 0))
+
+    near = call(
+        pack_body,
+        [shape(message_rows(channels, rows, count)[2], LANES)] * 2,
+        (info, voxels, voxels, line),
+        specs=[SMEM, block(0), block(planes - 1), VMEM],
         width=width,
-        depth=depth,
     )
-    other = lax.ppermute(sent, "dir", swap)
-    line = lax.dynamic_slice_in_dim(voxels, jnp.where(t == 0, rows - 1, 0), 1, axis=2)
-    line = lax.ppermute(line[:, :, 0], "tile", swap)
+    near = [lax.ppermute(x, "slab", p) for x, p in zip(near, (pairs_a, pairs_b))]
 
     two = shape(2, channels, 2, rows, width)
-    four = shape(channels, 2, rows, width)
+    pair = shape(2, 2, rows, width)
     vals, part, ends, inner = call(
         inner_body,
-        "inner",
-        [shape(2, channels, planes - 2, rows, width), two, two, four],
+        [shape(2, channels, planes - 2, rows, width), two, two, shape(channels, 2, rows, width)],
         (info, voxels, line, own, other),
         scratch=[grid(planes)],
         limit=20,
         width=width,
         scale=scale,
     )
-    pay, rim, ends = call(
+    light = shape(colours, rows, width)
+    pay, rim, ends, keep, send = call(
         rim_body,
-        "rim",
-        [four, two, two],
+        [pair, two, two, light, light],
         (info, *near, own, other, part, ends, inner),
         scratch=[grid(2)],
         scale=scale,
+        chunk=chunk,
     )
-    far = halo(1)
-
-    cols5, tail = pl.pallas_call(
-        functools.partial(column_body, scale=scale),
-        out_shape=[shape(channels + 1, 2, planes, rows, width), shape(2, 2, rows, width)],
-        in_specs=[VMEM] * 4,
-        out_specs=[VMEM] * 2,
-        cost_estimate=pl.CostEstimate(flops=10**7, bytes_accessed=2 * 10**6, transcendentals=0),
-        compiler_params=pltpu.CompilerParams(vmem_limit_bytes=16 * MIB),
-        name="column",
-    )(own, other, vals, rim)
-    outer = call(
-        outer_body,
-        "outer",
-        shape(channels + 1, 2, 2, rows, width),
-        (info, *far, own, other, ends, tail),
-        scratch=[grid(2), pltpu.VMEM((2, channels, 2, rows, width), F32)],
+    cols5 = call(
+        column_body,
+        shape(channels + 1, 2, planes, rows, width),
+        (info, own, other, vals, rim, ends),
         scale=scale,
         slabs=slabs,
     )
 
-    rays = jnp.stack([own, other], axis=1)
-    forward = rays[1] == 0.0
-    pull = rays[2:]
-    before = jnp.zeros_like(pay[0])
-    lead = jnp.zeros_like(pay[0])
-    block_all = pay
-    for bit in range(slabs.bit_length() - 1):
-        with jax.named_scope(f"scan{bit}"):
-            theirs = lax.ppermute(block_all, "slab", [(i, i ^ (1 << bit)) for i in range(slabs)])
-        lower = ((s >> bit) & 1) == 1
-        earlier = lower == forward
-        fade_theirs = jnp.exp(-theirs[0])
-        fade_mine = jnp.exp(-block_all[0])
-        light = jnp.where(
-            earlier,
-            theirs[1:] + fade_theirs * block_all[1:],
-            block_all[1:] + fade_mine * theirs[1:],
+    message, state = (pay, ())
+    for bit in range(rounds):
+        pairs = [(i, i ^ (1 << bit)) for i in range(slabs)]
+        if bit == 1:
+            message, cols5 = lax.optimization_barrier((message, cols5))
+        last = bit == rounds - 1
+        theirs = lax.ppermute(message, "slab", pairs)
+        got = lax.ppermute(send, "slab", pairs)
+        halved = tile_bit is not None and bit >= tile_bit
+        factor = shape(rows, LANES if halved else width)
+        outs = [pair] + ([] if last else [pair])
+        outs = outs + ([shape(2, rows, width)] if bit == rounds - 2 else []) + [factor] * 2
+        state, *others, mine_scale, their_scale = call(
+            scan_body,
+            outs,
+            (info, own, other, pay, theirs) + tuple(state),
+            bit=bit,
+            rounds=rounds,
+            chunk=chunk,
+            tile_bit=tile_bit,
         )
-        weighted = jnp.sum(pull * theirs[1:], axis=0)
-        lead = jnp.where(earlier, weighted + fade_theirs * lead, lead)
-        before = jnp.where(earlier, before + theirs[0], before)
-        block_all = jnp.concatenate([(block_all[0] + theirs[0])[None], light], axis=0)
-    reach = jnp.exp(-before)
-    rest = jnp.sum(pull * block_all[1:], axis=0) - lead
+        if not last:
+            pay, message = (others[0], others[-1])
+            state = (state,)
+        if last:
+            break
+        split = tile_bit if bit + 1 == tile_bit else None
+        kept = shape(colours, rows, LANES) if split is not None else shape(*keep.shape)
+        pieces = call(
+            light_body,
+            [kept] * (1 if split is None else 2),
+            (info, keep, got, mine_scale, their_scale),
+            tile_bit=split,
+        )
+        keep, send = (pieces[0], pieces[-1])
 
     plain = dict(
         compiler_params=pltpu.CompilerParams(vmem_limit_bytes=16 * MIB),
@@ -716,20 +781,21 @@
     columns = pl.pallas_call(
         functools.partial(merge_body, channels=channels),
         out_shape=shape(channels, 2, planes, rows, width),
-        in_specs=[VMEM] * 4,
+        in_specs=[VMEM] * 2,
         out_specs=VMEM,
         name="merge",
         **plain,
-    )(cols5, outer, reach, rest)
+    )(state, cols5)
     line, edge = call(
         border_body,
-        "border",
         [shape(channels, planes, width), shape(rows + SUB, LANES)],
         (info, columns, own, other),
     )
+    line, got = lax.optimization_barrier((line, got))
+    edge, corner = (edge[:rows], edge[rows:])
+    edge = lax.ppermute(edge, "dir", swap)
+    corner = lax.ppermute(corner, ("dir", "tile"), [(i, 3 - i) for i in range(4)])
     line = lax.ppermute(line, "tile", swap)
-    corner = lax.ppermute(edge[rows:], ("dir", "tile"), [(i, 3 - i) for i in range(4)])
-    edge = lax.ppermute(edge[:rows], "dir", swap)
     grad = pl.pallas_call(
         scatter_body,
         out_shape=shape(channels, planes, rows, width),
@@ -739,18 +805,25 @@
         name="scatter",
         **plain,
     )(columns, own, other)
-    voxel_grad = call(
+    quarter = pl.BlockSpec((1, planes, rows, width), lambda c: (c, 0, 0, 0))
+    voxel_grad = pl.pallas_call(
         finish_body,
-        "finish",
-        shape(channels, planes, rows, width),
-        (info, grad, line, edge, corner),
+        out_shape=shape(channels, planes, rows, width),
+        grid=(channels,),
+        in_specs=[SMEM, quarter, pl.BlockSpec((1, planes, width), lambda c: (c, 0, 0)), VMEM, VMEM],
+        out_specs=quarter,
+        name="finish",
+        **plain,
+    )(info, grad, line, edge, corner)
+
+    keep = call(
+        light_body, shape(*keep.shape), (info, keep, got, mine_scale, their_scale), tile_bit=None
     )
-
-    share = total // slabs
-    half = slabs // dirs
-    start = (s % half) * share
-    mine = lax.dynamic_slice_in_dim(block_all[1:, 0], start, share, axis=2)
-    sent = lax.dynamic_slice_in_dim(block_all[1:, 1], start, share, axis=2)
+    start = (s % half) * chunk
+    start = lax.rem(start, LANES) if tile_bit is not None else start
+    there = jnp.where(s % 2 == 1, start - chunk, start + chunk)
+    mine = lax.dynamic_slice_in_dim(keep, start, chunk, axis=2)
+    sent = lax.dynamic_slice_in_dim(keep, there, chunk, axis=2)
     got = lax.ppermute(sent, "dir", swap)
     image = jnp.where(s // half == h, mine, got)
     return (image[None], voxel_grad)

time: 79.2 us -> 57.5 us (0.73)
  the two profiles are of different devices: /device:TPU:16 before, /device:TPU:0 now
where the time goes in v3:
time: 57.5 us; the launch traced here: 57.2 us
  Pallas kernels  22.7 us (39%)
  starting transfers between devices  18.6 us (32%)
  local copies, waits for them, and re-layouts  7.54 us (13%)
  waiting for transfers between devices  6.8 us (12%)
  other arithmetic  0.79 us (1%)
  between operations  0.78 us (1%)
    pallas_call x11, Pallas kernels, call(): pl.pallas_call(functools.partial(body, **statics), out_shape=outs, grid=(...  17 us
    unnamed x14, local copies, waits for them, and re-layouts  7.45 us
    ppermute x3, starting transfers between devices, per_device(): theirs = lax.ppermute(message, 'slab', pairs)  6.63 us
    ppermute x3, waiting for transfers between devices, per_device(): got = lax.ppermute(send, 'slab', pairs)  3.7 us
    ppermute x3, starting transfers between devices, per_device(): got = lax.ppermute(send, 'slab', pairs)  3.56 us
    ppermute x1, starting transfers between devices, per_device(): other = lax.ppermute(sent, 'dir', swap)  2.55 us
    pallas_call x1, Pallas kernels, per_device(): pl.pallas_call(finish_body, out_shape=shape(channels, planes, rows, width...  2.33 us
    ppermute x2, starting transfers between devices, per_device(): lax.ppermute(x, 'slab', p)  2.24 us
  transfers between devices with their start and end apart: 14, of which 3 were waited for; matrix products, arithmetic and copies ran while one was open for 1% of the time, Pallas kernels for 27%

profile of v3, /device:TPU:0, one launch (start us, length us, event | category | flops | bytes accessed | tf_op | source)
XLA Modules:
  0.0 57.2 jit_solution(5693720859791807008)
XLA Ops:
  0.7 1.6 %copy-done = f32[4,8,32,512]{3,2,1,0:T(8,128)S(1)} copy-done((f32[4,8,32,512]{3,2,1,0:T(8,128)S(1)}, f32[4,8,32,512]{3,2,1,0:T(8,128)}, u32[]{:S(2)}) %copy-start) | copy-done | bytes 2097176
  2.3 0.9 %copy-done.4 = f32[1,3,32,512]{3,2,1,0:T(8,128)S(1)} copy-done((f32[1,3,32,512]{3,2,1,0:T(8,128)S(1)}, f32[1,3,32,512]{3,2,1,0:T(8,128)}, u32[]{:S(2)}) %copy-start.4) | copy-done | bytes 196632
  3.2 0.8 %copy-done.5 = s32[1,32,512]{2,1,0:T(8,128)S(1)} copy-done((s32[1,32,512]{2,1,0:T(8,128)S(1)}, s32[1,32,512]{2,1,0:T(8,128)}, u32[]{:S(2)}) %copy-start.5) | copy-done | bytes 65560
  4.1 0.8 %copy-done.6 = s32[1,32,512]{2,1,0:T(8,128)S(1)} copy-done((s32[1,32,512]{2,1,0:T(8,128)S(1)}, s32[1,32,512]{2,1,0:T(8,128)}, u32[]{:S(2)}) %copy-start.6) | copy-done | bytes 65560
  4.9 1.1 %first.2 = (f32[5,32,256]{2,1,0:T(8,128)S(1)}, f32[5,32,256]{2,1,0:T(8,128)S(1)}, f32[4,8,512]{2,1,0:T(8,128)S(1)}) custom-call(s32[3]{0:T(128)S(1)} %pad_add_fusion.info, s32[1,32,512]{2,1,0:T(8,128)S(1)} %copy-done.5, s32[1,32,512]{2,1,0:T(8,128)S(1)} %copy-done.6, f32[1,3,32,512]{3,2,1,0:T(8,128)S(1)} %copy-done.4, f32[4,8,32,512]{3,2,1,0:T(8,128)S(1)} %copy-done), custom_call_target="tpu_custom_call" | custom-call | tf_op jit(solution)/shard_map/first/pallas_call | solution.py:683
  6.6 2.6 %collective-permute-start.3 = (f32[5,32,256]{2,1,0:T(8,128)S(1)}, f32[5,32,256]{2,1,0:T(8,128)S(1)}, u32[]{:S(2)}, u32[]{:S(2)}) collective-permute-start(f32[5,32,256]{2,1,0:T(8,128)S(1)} %get-tuple-element.40), channel_id=1, source_target_pairs={{0,16},{16,0},{1,17},{17,1},{2,18},{18,2},{3,19},{19,3},{4,20},{20... | collective-permute-start | bytes 491528 | tf_op jit(solution)/shard_map/ppermute | solution.py:699
  9.1 0.7 %shard_map.59 = (f32[296,128]{1,0:T(8,128)S(1)}, f32[296,128]{1,0:T(8,128)S(1)}) custom-call(s32[3]{0:T(128)S(1)} %pad_add_fusion.info, f32[4,8,32,512]{3,2,1,0:T(8,128)S(1)} %copy-done.1, f32[4,8,32,512]{3,2,1,0:T(8,128)S(1)} %copy-done.1, f32[4,8,512]{2,1,0:T(8,128)S(1)} %collective-permute-done.line), custom_call_target="tpu_custom_call" | custom-call | flops 10000000 | bytes 2000000 | tf_op jit(solution)/shard_map/pallas_call | solution.py:23
  9.8 1.6 %collective-permute-start.1 = (f32[296,128]{1,0:T(8,128)S(1)}, f32[296,128]{1,0:T(8,128)S(1)}, u32[]{:S(2)}, u32[]{:S(2)}) collective-permute-start(f32[296,128]{1,0:T(8,128)S(1)} %get-tuple-element.37), channel_id=1, source_target_pairs={{0,2},{2,0},{4,6},{6,4},{8,10},{10,8},{12,14},{14,12},{1,3},{3,1},... | collective-permute-start | bytes 454664 | tf_op jit(solution)/shard_map/ppermute | solution.py:711
  11.4 0.7 %collective-permute-start.2 = (f32[296,128]{1,0:T(8,128)S(1)}, f32[296,128]{1,0:T(8,128)S(1)}, u32[]{:S(2)}, u32[]{:S(2)}) collective-permute-start(f32[296,128]{1,0:T(8,128)S(1)} %get-tuple-element.38), channel_id=1, source_target_pairs={{2,4},{6,8},{10,12},{4,2},{8,6},{12,10},{3,5},{7,9},{11,13},{5,3},... | collective-permute-start | bytes 454664 | tf_op jit(solution)/shard_map/ppermute | solution.py:711
  12.1 1.9 %collective-permute-done.3.other = f32[5,32,256]{2,1,0:T(8,128)S(1)} collective-permute-done((f32[5,32,256]{2,1,0:T(8,128)S(1)}, f32[5,32,256]{2,1,0:T(8,128)S(1)}, u32[]{:S(2)}, u32[]{:S(2)}) %collective-permute-start.3) | collective-permute-done | bytes 163872 | tf_op jit(solution)/shard_map/ppermute | solution.py:699
  13.9 4.8 %shard_map.60 = (f32[2,4,6,32,256]{4,3,2,1,0:T(8,128)S(1)}, f32[2,4,2,32,256]{4,3,2,1,0:T(8,128)S(1)}, f32[2,4,2,32,256]{4,3,2,1,0:T(8,128)S(1)}, f32[4,2,32,256]{3,2,1,0:T(8,128)S(1)}) custom-call(s32[3]{0:T(128)S(1)} %pad_add_fusion.info, f32[4,8,32,512]{3,2,1,0:T(8,128)S(1)} %copy-done.1, f32[4,8,512]{2,1,0:T(8,128)S(1)} %collective-permute-done.line, ...), custom_call_target="tpu_custom_call" | custom-call | flops 10000000 | bytes 2000000 | tf_op jit(solution)/shard_map/pallas_call | solution.py:23
  18.7 2.4 %shard_map.61 = (f32[2,2,32,256]{3,2,1,0:T(8,128)S(1)}, f32[2,4,2,32,256]{4,3,2,1,0:T(8,128)S(1)}, f32[2,4,2,32,256]{4,3,2,1,0:T(8,128)S(1)}, f32[3,32,256]{2,1,0:T(8,128)S(1)}, f32[3,32,256]{2,1,0:T(8,128)S(1)}) custom-call(s32[3]{0:T(128)S(1)} %pad_add_fusion.info, f32[296,128]{1,0:T(8,128)S(1)} %collective-permute-done.1.near_a, ...), custom_call_target="tpu_custom_call" | custom-call | flops 10000000 | bytes 2000000 | tf_op jit(solution)/shard_map/pallas_call | solution.py:23
  21.1 2.4 %collective-permute-start.5 = (f32[2,2,32,256]{3,2,1,0:T(8,128)S(1)}, f32[2,2,32,256]{3,2,1,0:T(8,128)S(1)}, u32[]{:S(2)}, u32[]{:S(2)}) collective-permute-start(f32[2,2,32,256]{3,2,1,0:T(8,128)S(1)} %get-tuple-element.46.block), channel_id=1, source_target_pairs={{0,2},{2,0},{4,6},{6,4},{8,10},{10,8},{12,14},{14,12},{1,3},{3,1},... | collective-permute-start | bytes 393224 | tf_op jit(solution)/shard_map/ppermute | solution.py:747
  23.6 2.5 %shard_map.64.cols5 = f32[5,2,8,32,256]{4,3,2,1,0:T(8,128)S(1)} custom-call(s32[3]{0:T(128)S(1)} %pad_add_fusion.info, f32[5,32,256]{2,1,0:T(8,128)S(1)} %get-tuple-element.39.own, f32[5,32,256]{2,1,0:T(8,128)S(1)} %collective-permute-done.3.other, f32[2,4,6,32,256]{4,3,2,1,0:T(8,128)S(1)} %get-tuple-element.52.vals, ...), custom_call_target="tpu_custom_call" | custom-call | flops 10000000 | bytes 2000000 | tf_op jit(solution)/shard_map/pallas_call | solution.py:23
  26.1 1.5 %copy-done.2 = f32[5,2,8,32,256]{4,3,2,1,0:T(8,128)} copy-done((f32[5,2,8,32,256]{4,3,2,1,0:T(8,128)}, f32[5,2,8,32,256]{4,3,2,1,0:T(8,128)S(1)}, u32[]{:S(2)}) %copy-start.2) | copy-done | bytes 2621464
  27.6 1.2 %shard_map.62 = (f32[2,2,32,256]{3,2,1,0:T(8,128)S(1)}, f32[2,2,32,256]{3,2,1,0:T(8,128)S(1)}, f32[32,256]{1,0:T(8,128)S(1)}, f32[32,256]{1,0:T(8,128)S(1)}) custom-call(s32[3]{0:T(128)S(1)} %pad_add_fusion.info, f32[5,32,256]{2,1,0:T(8,128)S(1)} %get-tuple-element.39.own, f32[5,32,256]{2,1,0:T(8,128)S(1)} %collective-permute-done.3.other, ...), custom_call_target="tpu_custom_call" | custom-call | flops 10000000 | bytes 2000000 | tf_op jit(solution)/shard_map/pallas_call | solution.py:23
  28.8 1.6 %collective-permute-start.7 = (f32[2,2,32,256]{3,2,1,0:T(8,128)S(1)}, f32[2,2,32,256]{3,2,1,0:T(8,128)S(1)}, u32[]{:S(2)}, u32[]{:S(2)}) collective-permute-start(f32[2,2,32,256]{3,2,1,0:T(8,128)S(1)} %get-tuple-element.55.block), channel_id=1, source_target_pairs={{0,4},{2,6},{4,0},{6,2},{8,12},{10,14},{12,8},{14,10},{1,5},{3,7},... | collective-permute-start | bytes 393224 | tf_op jit(solution)/shard_map/ppermute | solution.py:747
  30.4 0.9 %collective-permute-start.4 = (f32[3,32,256]{2,1,0:T(8,128)S(1)}, f32[3,32,256]{2,1,0:T(8,128)S(1)}, u32[]{:S(2)}, u32[]{:S(2)}) collective-permute-start(f32[3,32,256]{2,1,0:T(8,128)S(1)} %get-tuple-element.45), channel_id=1, source_target_pairs={{0,2},{2,0},{4,6},{6,4},{8,10},{10,8},{12,14},{14,12},{1,3},{3,1},... | collective-permute-start | bytes 294920 | tf_op jit(solution)/shard_map/ppermute | solution.py:748
  31.3 3.7 %collective-permute-done.4.got = f32[3,32,256]{2,1,0:T(8,128)S(1)} collective-permute-done((f32[3,32,256]{2,1,0:T(8,128)S(1)}, f32[3,32,256]{2,1,0:T(8,128)S(1)}, u32[]{:S(2)}, u32[]{:S(2)}) %collective-permute-start.4) | collective-permute-done | bytes 98336 | tf_op jit(solution)/shard_map/ppermute | solution.py:748
  36.1 1.2 %shard_map.65 = (f32[2,2,32,256]{3,2,1,0:T(8,128)S(1)}, f32[2,2,32,256]{3,2,1,0:T(8,128)S(1)}, f32[2,32,256]{2,1,0:T(8,128)S(1)}, f32[32,128]{1,0:T(8,128)S(1)}, f32[32,128]{1,0:T(8,128)S(1)}) custom-call(s32[3]{0:T(128)S(1)} %pad_add_fusion.info, f32[5,32,256]{2,1,0:T(8,128)S(1)} %get-tuple-element.39.own, f32[5,32,256]{2,1,0:T(8,128)S(1)} %collective-permute-done.3.other, ...), custom_call_target="tpu_custom_call" | custom-call | flops 10000000 | bytes 2000000 | tf_op jit(solution)/shard_map/pallas_call | solution.py:23
  37.3 2.6 %collective-permute-start.8 = (f32[2,32,256]{2,1,0:T(8,128)S(1)}, f32[2,32,256]{2,1,0:T(8,128)S(1)}, u32[]{:S(2)}, u32[]{:S(2)}) collective-permute-start(f32[2,32,256]{2,1,0:T(8,128)S(1)} %get-tuple-element.60), channel_id=1, source_target_pairs={{0,8},{2,10},{4,12},{6,14},{8,0},{10,2},{12,4},{14,6},{1,9},{3,11}... | collective-permute-start | bytes 196616 | tf_op jit(solution)/shard_map/ppermute | solution.py:747
  40.5 2.1 %collective-permute-start.9 = (f32[3,32,128]{2,1,0:T(8,128)S(1)}, f32[3,32,128]{2,1,0:T(8,128)S(1)}, u32[]{:S(2)}, u32[]{:S(2)}) collective-permute-start(f32[3,32,128]{2,1,0:T(8,128)S(1)} %shard_map.66.keep), channel_id=1, source_target_pairs={{0,8},{2,10},{4,12},{6,14},{8,0},{10,2},{12,4},{14,6},{1,9},{3,11}... | collective-permute-start | bytes 147464 | tf_op jit(solution)/shard_map/ppermute | solution.py:748
  42.6 1.2 %collective-permute-done.8.theirs = f32[2,32,256]{2,1,0:T(8,128)S(1)} collective-permute-done((f32[2,32,256]{2,1,0:T(8,128)S(1)}, f32[2,32,256]{2,1,0:T(8,128)S(1)}, u32[]{:S(2)}, u32[]{:S(2)}) %collective-permute-start.8) | collective-permute-done | bytes 65568 | tf_op jit(solution)/shard_map/ppermute | solution.py:747
  43.8 1.2 %shard_map.67 = (f32[2,2,32,256]{3,2,1,0:T(8,128)S(1)}, f32[32,128]{1,0:T(8,128)S(1)}, f32[32,128]{1,0:T(8,128)S(1)}) custom-call(s32[3]{0:T(128)S(1)} %pad_add_fusion.info, f32[5,32,256]{2,1,0:T(8,128)S(1)} %get-tuple-element.39.own, f32[5,32,256]{2,1,0:T(8,128)S(1)} %collective-permute-done.3.other, f32[2,2,32,256]{3,2,1,0:T(8,128)S(1)} %get-tuple-element.59.block, ...), custom_call_target="tpu_custom_call" | custom-call | flops 10000000 | bytes 2000000 | tf_op jit(solution)/shard_map/pallas_call | solution.py:23
  45.0 1.7 %copy-done.3 = f32[5,2,8,32,256]{4,3,2,1,0:T(8,128)S(1)} copy-done((f32[5,2,8,32,256]{4,3,2,1,0:T(8,128)S(1)}, f32[5,2,8,32,256]{4,3,2,1,0:T(8,128)}, u32[]{:S(2)}) %copy-start.3) | copy-done | bytes 2621464
  47.2 1.4 %shard_map.68 = (f32[4,8,256]{2,1,0:T(8,128)S(1)}, f32[40,128]{1,0:T(8,128)S(1)}) custom-call(s32[3]{0:T(128)S(1)} %pad_add_fusion.info, f32[4,2,8,32,256]{4,3,2,1,0:T(8,128)S(1)} %merge.1.columns, f32[5,32,256]{2,1,0:T(8,128)S(1)} %get-tuple-element.39.own, f32[5,32,256]{2,1,0:T(8,128)S(1)} %collective-permute-done.3.other), custom_call_target="tpu_custom_call" | custom-call | flops 10000000 | bytes 2000000 | tf_op jit(solution)/shard_map/pallas_call | solution.py:23
  49.2 1.2 %collective-permute-start.10 = (f32[3,32,64]{2,1,0:T(8,128)S(1)}, f32[3,32,64]{2,1,0:T(8,128)S(1)}, u32[]{:S(2)}, u32[]{:S(2)}) collective-permute-start(f32[3,32,64]{2,1,0:T(8,128)S(1)} %constant_dynamic-slice_fusion), channel_id=1, source_target_pairs={{0,16},{16,0},{1,17},{17,1},{2,18},{18,2},{3,19},{19,3},{4,20},{20... | collective-permute-start | bytes 73736 | tf_op jit(solution)/shard_map/ppermute | solution.py:827
  50.4 0.9 %collective-permute-start.12 = (f32[32,128]{1,0:T(8,128)S(1)}, f32[32,128]{1,0:T(8,128)S(1)}, u32[]{:S(2)}, u32[]{:S(2)}) collective-permute-start(f32[32,128]{1,0:T(8,128)S(1)} %slice.6), channel_id=1, source_target_pairs={{0,16},{16,0},{1,17},{17,1},{2,18},{18,2},{3,19},{19,3},{4,20},{20... | collective-permute-start | bytes 49160 | tf_op jit(solution)/shard_map/ppermute | solution.py:796
  51.3 0.9 %collective-permute-start.13 = (f32[8,128]{1,0:T(8,128)S(1)}, f32[8,128]{1,0:T(8,128)S(1)}, u32[]{:S(2)}, u32[]{:S(2)}) collective-permute-start(f32[8,128]{1,0:T(8,128)S(1)} %slice.7), channel_id=1, source_target_pairs={{0,17},{1,16},{16,1},{17,0},{2,19},{3,18},{18,3},{19,2},{4,21},{5,... | collective-permute-start | bytes 12296 | tf_op jit(solution)/shard_map/ppermute | solution.py:797
  52.2 1.9 %scatter.1.grad_in = f32[4,8,32,256]{3,2,1,0:T(8,128)S(1)} custom-call(f32[4,2,8,32,256]{4,3,2,1,0:T(8,128)S(1)} %merge.1.columns, f32[5,32,256]{2,1,0:T(8,128)S(1)} %get-tuple-element.39.own, f32[5,32,256]{2,1,0:T(8,128)S(1)} %collective-permute-done.3.other), custom_call_target="tpu_custom_call" | custom-call | flops 10000000 | bytes 2000000 | tf_op jit(solution)/shard_map/scatter/pallas_call | solution.py:799
  54.2 0.7 %select_bitcast_fusion = f32[1,3,32,64]{3,2,1,0:T(8,128)} fusion(f32[3,32,64]{2,1,0:T(8,128)S(1)} %collective-permute-done.10, f32[3,32,128]{2,1,0:T(8,128)S(1)} %shard_map.69, s32[]{:T(128)S(6)} %select_n.35, pred[]{:T(512)S(6)} %eq.9), kind=kLoop, calls=%fused_computation | loop fusion | flops 6144 | bytes 73733 | tf_op jit(solution)/shard_map/broadcast_in_dim | solution.py:829
  54.9 2.3 %finish.1 = f32[4,8,32,256]{3,2,1,0:T(8,128)} custom-call(s32[3]{0:T(128)S(1)} %pad_add_fusion.info, f32[4,8,32,256]{3,2,1,0:T(8,128)S(1)} %scatter.1.grad_in, f32[4,8,256]{2,1,0:T(8,128)S(1)} %collective-permute-done.11.line, f32[32,128]{1,0:T(8,128)S(1)} %collective-permute-done.12.edge, f32[8,128]{1,0:T(8,128)S(1)} %collective-permute-done.13.corner), custom_call_target="tpu_custom_call" | custom-call | flops 10000000 | bytes 2000000 | tf_op jit(solution)/shard_map/finish/pallas_call | solution.py:809
  (30 shorter events, 3.4 us)
Async XLA Ops:
  0.7 1.6 %copy-start = (f32[4,8,32,512]{3,2,1,0:T(8,128)S(1)}, f32[4,8,32,512]{3,2,1,0:T(8,128)}, u32[]{:S(2)}) copy-start(f32[4,8,32,512]{3,2,1,0:T(8,128)} %vox.1) | copy-start | bytes 6291460
  2.3 0.9 %copy-start.4 = (f32[1,3,32,512]{3,2,1,0:T(8,128)S(1)}, f32[1,3,32,512]{3,2,1,0:T(8,128)}, u32[]{:S(2)}) copy-start(f32[1,3,32,512]{3,2,1,0:T(8,128)} %cotangent.1) | copy-start | bytes 589828
  3.2 0.8 %copy-start.5 = (s32[1,32,512]{2,1,0:T(8,128)S(1)}, s32[1,32,512]{2,1,0:T(8,128)}, u32[]{:S(2)}) copy-start(s32[1,32,512]{2,1,0:T(8,128)} %offsets.1) | copy-start | bytes 196612
  4.1 0.8 %copy-start.6 = (s32[1,32,512]{2,1,0:T(8,128)S(1)}, s32[1,32,512]{2,1,0:T(8,128)}, u32[]{:S(2)}) copy-start(s32[1,32,512]{2,1,0:T(8,128)} %heading.1) | copy-start | bytes 196612
  4.9 4.2 %copy-start.1 = (f32[4,8,32,512]{3,2,1,0:T(8,128)S(1)}, f32[4,8,32,512]{3,2,1,0:T(8,128)}, u32[]{:S(2)}) copy-start(f32[4,8,32,512]{3,2,1,0:T(8,128)} %vox.1) | copy-start | bytes 6291460
  6.0 3.1 %collective-permute-start = (f32[4,8,512]{2,1,0:T(8,128)S(1)}, f32[4,8,512]{2,1,0:T(8,128)S(1)}, u32[]{:S(2)}, u32[]{:S(2)}) collective-permute-start(f32[4,8,512]{2,1,0:T(8,128)S(1)} %get-tuple-element.36), channel_id=1, source_target_pairs={{0,1},{1,0},{2,3},{3,2},{4,5},{5,4},{6,7},{7,6},{8,9},{9,8},{10,11... | collective-permute-start | bytes 196616 | tf_op jit(solution)/shard_map/ppermute | solution.py:698
  6.6 7.3 %collective-permute-start.3 = (f32[5,32,256]{2,1,0:T(8,128)S(1)}, f32[5,32,256]{2,1,0:T(8,128)S(1)}, u32[]{:S(2)}, u32[]{:S(2)}) collective-permute-start(f32[5,32,256]{2,1,0:T(8,128)S(1)} %get-tuple-element.40), channel_id=1, source_target_pairs={{0,16},{16,0},{1,17},{17,1},{2,18},{18,2},{3,19},{19,3},{4,20},{20... | collective-permute-start | bytes 491528 | tf_op jit(solution)/shard_map/ppermute | solution.py:699
  9.8 8.9 %collective-permute-start.1 = (f32[296,128]{1,0:T(8,128)S(1)}, f32[296,128]{1,0:T(8,128)S(1)}, u32[]{:S(2)}, u32[]{:S(2)}) collective-permute-start(f32[296,128]{1,0:T(8,128)S(1)} %get-tuple-element.37), channel_id=1, source_target_pairs={{0,2},{2,0},{4,6},{6,4},{8,10},{10,8},{12,14},{14,12},{1,3},{3,1},... | collective-permute-start | bytes 454664 | tf_op jit(solution)/shard_map/ppermute | solution.py:711
  11.4 7.3 %collective-permute-start.2 = (f32[296,128]{1,0:T(8,128)S(1)}, f32[296,128]{1,0:T(8,128)S(1)}, u32[]{:S(2)}, u32[]{:S(2)}) collective-permute-start(f32[296,128]{1,0:T(8,128)S(1)} %get-tuple-element.38), channel_id=1, source_target_pairs={{2,4},{6,8},{10,12},{4,2},{8,6},{12,10},{3,5},{7,9},{11,13},{5,3},... | collective-permute-start | bytes 454664 | tf_op jit(solution)/shard_map/ppermute | solution.py:711
  21.1 6.5 %collective-permute-start.5 = (f32[2,2,32,256]{3,2,1,0:T(8,128)S(1)}, f32[2,2,32,256]{3,2,1,0:T(8,128)S(1)}, u32[]{:S(2)}, u32[]{:S(2)}) collective-permute-start(f32[2,2,32,256]{3,2,1,0:T(8,128)S(1)} %get-tuple-element.46.block), channel_id=1, source_target_pairs={{0,2},{2,0},{4,6},{6,4},{8,10},{10,8},{12,14},{14,12},{1,3},{3,1},... | collective-permute-start | bytes 393224 | tf_op jit(solution)/shard_map/ppermute | solution.py:747
  26.1 1.5 %copy-start.2 = (f32[5,2,8,32,256]{4,3,2,1,0:T(8,128)}, f32[5,2,8,32,256]{4,3,2,1,0:T(8,128)S(1)}, u32[]{:S(2)}) copy-start(f32[5,2,8,32,256]{4,3,2,1,0:T(8,128)S(1)} %shard_map.64.cols5) | copy-start | bytes 7864324
  28.8 7.3 %collective-permute-start.7 = (f32[2,2,32,256]{3,2,1,0:T(8,128)S(1)}, f32[2,2,32,256]{3,2,1,0:T(8,128)S(1)}, u32[]{:S(2)}, u32[]{:S(2)}) collective-permute-start(f32[2,2,32,256]{3,2,1,0:T(8,128)S(1)} %get-tuple-element.55.block), channel_id=1, source_target_pairs={{0,4},{2,6},{4,0},{6,2},{8,12},{10,14},{12,8},{14,10},{1,5},{3,7},... | collective-permute-start | bytes 393224 | tf_op jit(solution)/shard_map/ppermute | solution.py:747
  30.4 4.6 %collective-permute-start.4 = (f32[3,32,256]{2,1,0:T(8,128)S(1)}, f32[3,32,256]{2,1,0:T(8,128)S(1)}, u32[]{:S(2)}, u32[]{:S(2)}) collective-permute-start(f32[3,32,256]{2,1,0:T(8,128)S(1)} %get-tuple-element.45), channel_id=1, source_target_pairs={{0,2},{2,0},{4,6},{6,4},{8,10},{10,8},{12,14},{14,12},{1,3},{3,1},... | collective-permute-start | bytes 294920 | tf_op jit(solution)/shard_map/ppermute | solution.py:748
  35.6 4.3 %collective-permute-start.6 = (f32[3,32,128]{2,1,0:T(8,128)S(1)}, f32[3,32,128]{2,1,0:T(8,128)S(1)}, u32[]{:S(2)}, u32[]{:S(2)}) collective-permute-start(f32[3,32,128]{2,1,0:T(8,128)S(1)} %get-tuple-element.50), channel_id=1, source_target_pairs={{0,4},{2,6},{4,0},{6,2},{8,12},{10,14},{12,8},{14,10},{1,5},{3,7},... | collective-permute-start | bytes 147464 | tf_op jit(solution)/shard_map/ppermute | solution.py:748
  37.3 6.5 %collective-permute-start.8 = (f32[2,32,256]{2,1,0:T(8,128)S(1)}, f32[2,32,256]{2,1,0:T(8,128)S(1)}, u32[]{:S(2)}, u32[]{:S(2)}) collective-permute-start(f32[2,32,256]{2,1,0:T(8,128)S(1)} %get-tuple-element.60), channel_id=1, source_target_pairs={{0,8},{2,10},{4,12},{6,14},{8,0},{10,2},{12,4},{14,6},{1,9},{3,11}... | collective-permute-start | bytes 196616 | tf_op jit(solution)/shard_map/ppermute | solution.py:747
  40.5 8.1 %collective-permute-start.9 = (f32[3,32,128]{2,1,0:T(8,128)S(1)}, f32[3,32,128]{2,1,0:T(8,128)S(1)}, u32[]{:S(2)}, u32[]{:S(2)}) collective-permute-start(f32[3,32,128]{2,1,0:T(8,128)S(1)} %shard_map.66.keep), channel_id=1, source_target_pairs={{0,8},{2,10},{4,12},{6,14},{8,0},{10,2},{12,4},{14,6},{1,9},{3,11}... | collective-permute-start | bytes 147464 | tf_op jit(solution)/shard_map/ppermute | solution.py:748
  45.0 1.7 %copy-start.3 = (f32[5,2,8,32,256]{4,3,2,1,0:T(8,128)S(1)}, f32[5,2,8,32,256]{4,3,2,1,0:T(8,128)}, u32[]{:S(2)}) copy-start(f32[5,2,8,32,256]{4,3,2,1,0:T(8,128)} %copy-done.2) | copy-start | bytes 7864324
  49.2 5.0 %collective-permute-start.10 = (f32[3,32,64]{2,1,0:T(8,128)S(1)}, f32[3,32,64]{2,1,0:T(8,128)S(1)}, u32[]{:S(2)}, u32[]{:S(2)}) collective-permute-start(f32[3,32,64]{2,1,0:T(8,128)S(1)} %constant_dynamic-slice_fusion), channel_id=1, source_target_pairs={{0,16},{16,0},{1,17},{17,1},{2,18},{18,2},{3,19},{19,3},{4,20},{20... | collective-permute-start | bytes 73736 | tf_op jit(solution)/shard_map/ppermute | solution.py:827
  50.4 4.5 %collective-permute-start.11 = (f32[4,8,256]{2,1,0:T(8,128)S(1)}, f32[4,8,256]{2,1,0:T(8,128)S(1)}, u32[]{:S(2)}, u32[]{:S(2)}) collective-permute-start(f32[4,8,256]{2,1,0:T(8,128)S(1)} %get-tuple-element.68), channel_id=1, source_target_pairs={{0,1},{1,0},{2,3},{3,2},{4,5},{5,4},{6,7},{7,6},{8,9},{9,8},{10,11... | collective-permute-start | bytes 98312 | tf_op jit(solution)/shard_map/ppermute | solution.py:798
  50.4 4.5 %collective-permute-start.12 = (f32[32,128]{1,0:T(8,128)S(1)}, f32[32,128]{1,0:T(8,128)S(1)}, u32[]{:S(2)}, u32[]{:S(2)}) collective-permute-start(f32[32,128]{1,0:T(8,128)S(1)} %slice.6), channel_id=1, source_target_pairs={{0,16},{16,0},{1,17},{17,1},{2,18},{18,2},{3,19},{19,3},{4,20},{20... | collective-permute-start | bytes 49160 | tf_op jit(solution)/shard_map/ppermute | solution.py:796
  51.3 3.6 %collective-permute-start.13 = (f32[8,128]{1,0:T(8,128)S(1)}, f32[8,128]{1,0:T(8,128)S(1)}, u32[]{:S(2)}, u32[]{:S(2)}) collective-permute-start(f32[8,128]{1,0:T(8,128)S(1)} %slice.7), channel_id=1, source_target_pairs={{0,17},{1,16},{16,1},{17,0},{2,19},{3,18},{18,3},{19,2},{4,21},{5,... | collective-permute-start | bytes 12296 | tf_op jit(solution)/shard_map/ppermute | solution.py:797

commit v4 on v3

--- a/solution.py
+++ b/solution.py
@@ -231,8 +231,13 @@
             )
 
 
-def each_tile(rows, width, body):
+def each_tile(rows, width, body, unroll=False):
     count = width // LANES
+    if unroll:
+        for i in range(rows // SUB):
+            for j in range(count):
+                body(pl.ds(i * SUB, SUB), pl.ds(j * LANES, LANES))
+        return
 
     def step(n, carry):
         row = pl.ds(pl.multiple_of((n // count) * SUB, SUB), SUB)
@@ -511,7 +516,7 @@
                 def _(out=out, x=x):
                     out[row, :] = x
 
-    each_tile(rows, width, ray)
+    each_tile(rows, width, ray, unroll=True)
 
 
 def light_body(info, keep, got, mine_scale, their_scale, *outs, tile_bit):
@@ -528,8 +533,28 @@
         outs[1][c] = jnp.where(tile == 0, high, low)
 
 
-def merge_body(reach_rest, cols5, columns, *, channels):
-    _, _, planes, rows, width = cols5.shape
+def image_body(info, keep, got, mine_scale, their_scale, mine, sent, *, chunk, half, halved):
+    s = info[2]
+    start = lax.rem(s, half) * chunk
+    base = 0 if halved else (start // LANES) * LANES
+    cols = pl.ds(pl.multiple_of(base, LANES), LANES)
+    start = lax.rem(start, LANES)
+    there = jnp.where(lax.rem(s, 2) == 1, start - chunk, start + chunk)
+    for c in range(keep.shape[0]):
+        both = mine_scale[:, cols] * keep[c, :, cols] + their_scale[:, cols] * got[c, :, cols]
+        mine[c] = pltpu.roll(both, lax.rem(LANES - start, LANES), 1)[:, :chunk]
+        sent[c] = pltpu.roll(both, lax.rem(LANES - there, LANES), 1)[:, :chunk]
+
+
+def choose_body(info, mine, got, image, *, half):
+    image[0] = jnp.where(info[2] // half == info[0], mine[...], got[...])
+
+
+def merge_body(info, reach_rest, cols5, own, other, columns, line, edge, corner, strips):
+    h, t = (info[0], info[1])
+    channels, _, planes, rows, width = columns.shape
+    last = LANES - 1
+    rays = (own, other)
 
     def ray(row, col):
         for q in range(2):
@@ -543,63 +568,51 @@
 
     each_tile(rows, width, ray)
 
-
-def border_body(info, columns, own, other, line, edge):
-    h, t = (info[0], info[1])
-    channels, _, planes, rows, width = columns.shape
-    count = width // LANES
-    last = LANES - 1
-    rays = (own, other)
-    row0 = pl.multiple_of(jnp.where(t == 0, rows - SUB, 0), SUB)
-    near = pl.ds(row0, SUB)
-    take = jnp.where(t == 0, SUB - 1, 0)
-    lane8 = iota((SUB, LANES), 1)
-    pick = iota((SUB, LANES), 0) == take
-    side = pl.ds(pl.multiple_of(jnp.where(h == 0, width - LANES, 0), LANES), LANES)
-    down, across = ([], [])
+    down = []
     for r in rays:
-        _, wy, wx = [three(x) for x in split_code(r[0, near, :])]
+        code = jnp.where(t == 0, r[0, rows - 1 : rows, :], r[0, :1, :])
+        _, wy, wx = [three(x) for x in split_code(jnp.broadcast_to(code, (planes, width)))]
         y = jnp.where(t == 0, wy[2], wy[0])
         down.append([y * x for x in wx])
-        _, wy, wx = [three(x) for x in split_code(r[0, :, side])]
+    lane = iota((planes, width), 1)
+    for c in range(channels):
+        for q in range(2):
+            for p in range(planes):
+                strips[q, p : p + 1, :] = jnp.where(
+                    t == 0, columns[c, q, p, rows - 1 : rows, :], columns[c, q, p, :1, :]
+                )
+        minus, same, plus = [
+            down[0][e] * strips[0] + down[1][e] * strips[1] for e in range(3)
+        ]
+        plus = jnp.where(lane == 0, 0.0, pltpu.roll(plus, 1, 1))
+        minus = jnp.where(lane == width - 1, 0.0, pltpu.roll(minus, width - 1, 1))
+        line[c] = same + plus + minus
+
+    side = pl.ds(pl.multiple_of(jnp.where(h == 0, width - LANES, 0), LANES), LANES)
+    source = jnp.where(h == 0, last, 0)
+    lane = iota((rows, LANES), 1)
+    row = iota((rows, LANES), 0)
+    packed, across = ([], [])
+    for q, r in enumerate(rays):
+        code = pltpu.roll(r[0, :, side], lax.rem(LANES - source, LANES), 1)
+        code = jnp.broadcast_to(code[:, :1], (rows, LANES))
+        _, wy, wx = [three(x) for x in split_code(code)]
         x = jnp.where(h == 0, wx[2], wx[0])
         across.append([y * x for y in wy])
-    row = iota((rows, LANES), 0)
-    lane = iota((rows, LANES), 1)
-    source = jnp.where(h == 0, last, 0)
-    edge[...] = jnp.zeros(edge.shape, F32)
-
-    def channel(c, carry):
-        for p in range(planes):
-            at = c * planes + p
-            strip = [columns[c, q, p, near, :] for q in range(2)]
-            sums = []
-            for e in range(3):
-                x = total_of([down[q][e] * strip[q] for q in range(2)])
-                x = jnp.sum(jnp.where(jnp.concatenate([pick] * count, axis=1), x, 0.0), axis=0, keepdims=True)
-                sums.append(jnp.broadcast_to(x, (SUB, width)))
-            plus = [sums[2][:, j * LANES : (j + 1) * LANES] for j in range(count)]
-            minus = [sums[0][:, j * LANES : (j + 1) * LANES] for j in range(count)]
-            plus = [pltpu.roll(x, 1, 1) for x in plus]
-            minus = [pltpu.roll(x, last, 1) for x in minus]
-            zero = jnp.zeros_like(plus[0])
-            for j in range(count):
-                x = sums[1][:, j * LANES : (j + 1) * LANES]
-                x = x + jnp.where(lane8 == 0, plus[j - 1] if j else zero, plus[j])
-                x = x + jnp.where(lane8 == last, minus[j + 1] if j < count - 1 else zero, minus[j])
-                line[c, p : p + 1, j * LANES : (j + 1) * LANES] = x[:1]
-            strip = [columns[c, q, p, :, side] for q in range(2)]
-            part = [total_of([across[q][b] * strip[q] for q in range(2)]) for b in range(3)]
-            lower = pltpu.roll(part[2], 1, 0)
-            upper = pltpu.roll(part[0], rows - 1, 0)
-            main = part[1] + jnp.where(row == 0, 0.0, lower) + jnp.where(row == rows - 1, 0.0, upper)
-            over = jnp.where(t == 0, lower[:SUB], pltpu.roll(upper[rows - SUB :], 1, 0))
-            turn = lax.rem(at - source + LANES, LANES)
-            edge[:rows, :] = jnp.where(lane == at, pltpu.roll(main, turn, 1), edge[:rows, :])
-            edge[rows:, :] = jnp.where(lane8 == at, pltpu.roll(over, turn, 1), edge[rows:, :])
-        return carry
-
-    lax.fori_loop(0, channels, channel, 0)
+        both = jnp.zeros((rows, LANES), F32)
+        for c in range(channels):
+            for p in range(planes):
+                at = c * planes + p
+                turn = lax.rem(at - source + LANES, LANES)
+                both = jnp.where(lane == at, pltpu.roll(columns[c, q, p, :, side], turn, 1), both)
+        packed.append(both)
+    part = [across[0][b] * packed[0] + across[1][b] * packed[1] for b in range(3)]
+    lower = pltpu.roll(part[2], 1, 0)
+    upper = pltpu.roll(part[0], rows - 1, 0)
+    edge[...] = (
+        part[1] + jnp.where(row == 0, 0.0, lower) + jnp.where(row == rows - 1, 0.0, upper)
+    )
+    corner[...] = jnp.where(t == 0, lower[:SUB], pltpu.roll(upper[rows - SUB :], 1, 0))
 
 
 def scatter_body(columns, own, other, grad, weights):
@@ -638,26 +651,31 @@
     lax.fori_loop(0, planes, plane, 0)
 
 
-def finish_body(info, grad_in, line, edge, corner, grad):
+def finish_body(info, grad_in, line, edge, corner, grad, buffer, sems):
     h, t = (info[0], info[1])
-    _, planes, rows, width = grad.shape
-    c = pl.program_id(0)
+    channels, planes, rows, width = buffer.shape
     source = jnp.where(h == 0, LANES - 1, 0)
     side = pl.ds(pl.multiple_of(jnp.where(h == 0, width - LANES, 0), LANES), LANES)
     last = jnp.where(t == 0, rows - 1, 0)
     at_row = iota((rows, width), 0) == last
     at_lane = iota((rows, LANES), 1) == source
     packed = edge[...] + jnp.where(iota((rows, LANES), 0) == last, corner[:1], 0.0)
-    for p in range(planes):
-        grad[0, p] = grad_in[0, p] + jnp.where(at_row, line[0, p : p + 1, :], 0.0)
-        turn = lax.rem(source - (c * planes + p) + LANES, LANES)
-        grad[0, p, :, side] += jnp.where(at_lane, pltpu.roll(packed, turn, 1), 0.0)
+    copies = []
+    for c in range(channels):
+        for p in range(planes):
+            buffer[c, p] = grad_in[c, p] + jnp.where(at_row, line[c, p : p + 1, :], 0.0)
+            turn = lax.rem(source - (c * planes + p) + LANES, LANES)
+            buffer[c, p, :, side] += jnp.where(at_lane, pltpu.roll(packed, turn, 1), 0.0)
+        copies.append(pltpu.make_async_copy(buffer.at[c], grad.at[c], sems.at[c]))
+        copies[-1].start()
+    for copy in copies:
+        copy.wait()
 
 
 def per_device(voxels, offsets, heading, cotangent):
     channels, planes, rows, total = voxels.shape
     dirs, slabs, cores = (lax.axis_size(a) for a in ("dir", "slab", "tile"))
-    if dirs != 2 or cores != 2 or slabs & (slabs - 1):
+    if dirs != 2 or cores != 2 or slabs & (slabs - 1) or 2 * total > slabs * LANES:
         raise ValueError("mesh")
     width = total // dirs
     depth = planes * slabs
@@ -692,7 +710,7 @@
             pltpu.VMEM((channels, planes, SUB, total), F32),
             pltpu.SemaphoreType.DMA((4,)),
         ],
-        compiler_params=pltpu.CompilerParams(vmem_limit_bytes=8 * MIB),
+        compiler_params=pltpu.CompilerParams(vmem_limit_bytes=62 * MIB),
         name="first",
     )(info, offsets, heading, cotangent, voxels)
     line = lax.ppermute(line, "tile", swap)
@@ -741,8 +759,6 @@
     message, state = (pay, ())
     for bit in range(rounds):
         pairs = [(i, i ^ (1 << bit)) for i in range(slabs)]
-        if bit == 1:
-            message, cols5 = lax.optimization_barrier((message, cols5))
         last = bit == rounds - 1
         theirs = lax.ppermute(message, "slab", pairs)
         got = lax.ppermute(send, "slab", pairs)
@@ -778,21 +794,17 @@
         compiler_params=pltpu.CompilerParams(vmem_limit_bytes=16 * MIB),
         cost_estimate=pl.CostEstimate(flops=10**7, bytes_accessed=2 * 10**6, transcendentals=0),
     )
-    columns = pl.pallas_call(
-        functools.partial(merge_body, channels=channels),
-        out_shape=shape(channels, 2, planes, rows, width),
-        in_specs=[VMEM] * 2,
-        out_specs=VMEM,
-        name="merge",
-        **plain,
-    )(state, cols5)
-    line, edge = call(
-        border_body,
-        [shape(channels, planes, width), shape(rows + SUB, LANES)],
-        (info, columns, own, other),
+    columns, line, edge, corner = call(
+        merge_body,
+        [
+            shape(channels, 2, planes, rows, width),
+            shape(channels, planes, width),
+            shape(rows, LANES),
+            shape(SUB, LANES),
+        ],
+        (info, state, cols5, own, other),
+        scratch=[pltpu.VMEM((2, planes, width), F32)],
     )
-    line, got = lax.optimization_barrier((line, got))
-    edge, corner = (edge[:rows], edge[rows:])
     edge = lax.ppermute(edge, "dir", swap)
     corner = lax.ppermute(corner, ("dir", "tile"), [(i, 3 - i) for i in range(4)])
     line = lax.ppermute(line, "tile", swap)
@@ -805,28 +817,29 @@
         name="scatter",
         **plain,
     )(columns, own, other)
-    quarter = pl.BlockSpec((1, planes, rows, width), lambda c: (c, 0, 0, 0))
+    grad_shape = (channels, planes, rows, width)
     voxel_grad = pl.pallas_call(
         finish_body,
-        out_shape=shape(channels, planes, rows, width),
-        grid=(channels,),
-        in_specs=[SMEM, quarter, pl.BlockSpec((1, planes, width), lambda c: (c, 0, 0)), VMEM, VMEM],
-        out_specs=quarter,
+        out_shape=shape(*grad_shape),
+        in_specs=[SMEM] + [VMEM] * 4,
+        out_specs=hbm,
+        scratch_shapes=[pltpu.VMEM(grad_shape, F32), pltpu.SemaphoreType.DMA((channels,))],
         name="finish",
         **plain,
     )(info, grad, line, edge, corner)
 
-    keep = call(
-        light_body, shape(*keep.shape), (info, keep, got, mine_scale, their_scale), tile_bit=None
+    piece = shape(colours, rows, chunk)
+    mine, sent = call(
+        image_body,
+        [piece, piece],
+        (info, keep, got, mine_scale, their_scale),
+        chunk=chunk,
+        half=half,
+        halved=tile_bit is not None,
     )
-    start = (s % half) * chunk
-    start = lax.rem(start, LANES) if tile_bit is not None else start
-    there = jnp.where(s % 2 == 1, start - chunk, start + chunk)
-    mine = lax.dynamic_slice_in_dim(keep, start, chunk, axis=2)
-    sent = lax.dynamic_slice_in_dim(keep, there, chunk, axis=2)
     got = lax.ppermute(sent, "dir", swap)
-    image = jnp.where(s // half == h, mine, got)
-    return (image[None], voxel_grad)
+    image = call(choose_body, shape(1, colours, rows, chunk), (info, mine, got), half=half)
+    return (image, voxel_grad)
 
 
 def solution(mesh):

time: 57.5 us -> 56.1 us (0.976)
  the two profiles are of different devices: /device:TPU:0 before, /device:TPU:1 now
where the time goes in v4:
time: 56.1 us; the launch traced here: 56 us
  Pallas kernels  24.3 us (43%)
  starting transfers between devices  22.9 us (41%)
  waiting for transfers between devices  5.74 us (10%)
  local copies, waits for them, and re-layouts  1.6 us (3%)
  between operations  0.76 us (1%)
  other arithmetic  0.62 us (1%)
    pallas_call x12, Pallas kernels, call(): pl.pallas_call(functools.partial(body, **statics), out_shape=outs, grid=(...  17.9 us
    ppermute x3, starting transfers between devices, per_device(): theirs = lax.ppermute(message, 'slab', pairs)  6.09 us
    ppermute x2, starting transfers between devices, per_device(): line = lax.ppermute(line, 'tile', swap)  5.72 us
    ppermute x3, starting transfers between devices, per_device(): got = lax.ppermute(send, 'slab', pairs)  3.31 us
    ppermute x3, waiting for transfers between devices, per_device(): theirs = lax.ppermute(message, 'slab', pairs)  2.96 us
    pallas_call x1, Pallas kernels, per_device(): pl.pallas_call(functools.partial(first_body, width=width, depth=depth), o...  2.72 us
    ppermute x1, starting transfers between devices, per_device(): other = lax.ppermute(sent, 'dir', swap)  2.69 us
    ppermute x3, waiting for transfers between devices, per_device(): got = lax.ppermute(send, 'slab', pairs)  2.3 us
  transfers between devices with their start and end apart: 14, of which 3 were waited for; matrix products, arithmetic and copies ran while one was open for 0% of the time, Pallas kernels for 30%

profile of v4, /device:TPU:1, one launch (start us, length us, event | category | flops | bytes accessed | tf_op | source)
XLA Modules:
  0.0 56.0 jit_solution(2554192020012884167)
XLA Ops:
  0.6 0.6 %pad_add_fusion.info = s32[3]{0:T(128)} fusion(s32[1]{0:T(128)} %bitcast.2, s32[1]{0:T(128)} %bitcast.1, s32[1]{0:T(128)} %bitcast), kind=kLoop, calls=%fused_computation | loop fusion | flops 6 | bytes 24 | tf_op jit(solution)/shard_map/stack | solution.py:684
  1.3 2.7 %first.2 = (f32[5,32,256]{2,1,0:T(8,128)}, f32[5,32,256]{2,1,0:T(8,128)}, f32[4,8,512]{2,1,0:T(8,128)}) custom-call(s32[3]{0:T(128)} %pad_add_fusion.info, s32[1,32,512]{2,1,0:T(8,128)} %offsets.1, s32[1,32,512]{2,1,0:T(8,128)} %heading.1, f32[1,3,32,512]{3,2,1,0:T(8,128)} %cotangent.1, f32[4,8,32,512]{3,2,1,0:T(8,128)} %vox.1), custom_call_target="tpu_custom_call" | custom-call | tf_op jit(solution)/shard_map/first/pallas_call | solution.py:701
  4.1 2.7 %collective-permute-start.3 = (f32[5,32,256]{2,1,0:T(8,128)}, f32[5,32,256]{2,1,0:T(8,128)S(1)}, u32[]{:S(2)}, u32[]{:S(2)}) collective-permute-start(f32[5,32,256]{2,1,0:T(8,128)} %get-tuple-element.40), channel_id=1, source_target_pairs={{0,16},{16,0},{1,17},{17,1},{2,18},{18,2},{3,19},{19,3},{4,20},{20... | collective-permute-start | bytes 491528 | tf_op jit(solution)/shard_map/ppermute | solution.py:717
  6.8 1.6 %copy-done = f32[4,8,32,512]{3,2,1,0:T(8,128)S(1)} copy-done((f32[4,8,32,512]{3,2,1,0:T(8,128)S(1)}, f32[4,8,32,512]{3,2,1,0:T(8,128)}, u32[]{:S(2)}) %copy-start) | copy-done | bytes 2097176
  8.4 0.7 %shard_map.59 = (f32[296,128]{1,0:T(8,128)S(1)}, f32[296,128]{1,0:T(8,128)S(1)}) custom-call(s32[3]{0:T(128)S(1)} %copy-done.3, f32[4,8,32,512]{3,2,1,0:T(8,128)S(1)} %copy-done, f32[4,8,32,512]{3,2,1,0:T(8,128)S(1)} %copy-done, f32[4,8,512]{2,1,0:T(8,128)S(1)} %collective-permute-done.line), custom_call_target="tpu_custom_call" | custom-call | flops 10000000 | bytes 2000000 | tf_op jit(solution)/shard_map/pallas_call | solution.py:23
  9.0 1.3 %collective-permute-start.1 = (f32[296,128]{1,0:T(8,128)S(1)}, f32[296,128]{1,0:T(8,128)S(1)}, u32[]{:S(2)}, u32[]{:S(2)}) collective-permute-start(f32[296,128]{1,0:T(8,128)S(1)} %get-tuple-element.37), channel_id=1, source_target_pairs={{0,2},{2,0},{4,6},{6,4},{8,10},{10,8},{12,14},{14,12},{1,3},{3,1},... | collective-permute-start | bytes 454664 | tf_op jit(solution)/shard_map/ppermute | solution.py:729
  10.3 0.7 %collective-permute-start.2 = (f32[296,128]{1,0:T(8,128)S(1)}, f32[296,128]{1,0:T(8,128)S(1)}, u32[]{:S(2)}, u32[]{:S(2)}) collective-permute-start(f32[296,128]{1,0:T(8,128)S(1)} %get-tuple-element.38), channel_id=1, source_target_pairs={{2,4},{6,8},{10,12},{4,2},{8,6},{12,10},{3,5},{7,9},{11,13},{5,3},... | collective-permute-start | bytes 454664 | tf_op jit(solution)/shard_map/ppermute | solution.py:729
  11.0 0.5 collective-permute-done.3.other
  11.5 4.8 %shard_map.60 = (f32[2,4,6,32,256]{4,3,2,1,0:T(8,128)S(1)}, f32[2,4,2,32,256]{4,3,2,1,0:T(8,128)S(1)}, f32[2,4,2,32,256]{4,3,2,1,0:T(8,128)S(1)}, f32[4,2,32,256]{3,2,1,0:T(8,128)S(1)}) custom-call(s32[3]{0:T(128)S(1)} %copy-done.3, f32[4,8,32,512]{3,2,1,0:T(8,128)S(1)} %copy-done.1, f32[4,8,512]{2,1,0:T(8,128)S(1)} %collective-permute-done.line, ...), custom_call_target="tpu_custom_call" | custom-call | flops 10000000 | bytes 2000000 | tf_op jit(solution)/shard_map/pallas_call | solution.py:23
  16.3 2.4 %shard_map.61 = (f32[2,2,32,256]{3,2,1,0:T(8,128)S(1)}, f32[2,4,2,32,256]{4,3,2,1,0:T(8,128)S(1)}, f32[2,4,2,32,256]{4,3,2,1,0:T(8,128)S(1)}, f32[3,32,256]{2,1,0:T(8,128)S(1)}, f32[3,32,256]{2,1,0:T(8,128)S(1)}) custom-call(s32[3]{0:T(128)S(1)} %copy-done.3, f32[296,128]{1,0:T(8,128)S(1)} %collective-permute-done.1.near_a, ...), custom_call_target="tpu_custom_call" | custom-call | flops 10000000 | bytes 2000000 | tf_op jit(solution)/shard_map/pallas_call | solution.py:23
  18.7 3.3 %collective-permute-start.5 = (f32[2,2,32,256]{3,2,1,0:T(8,128)S(1)}, f32[2,2,32,256]{3,2,1,0:T(8,128)S(1)}, u32[]{:S(2)}, u32[]{:S(2)}) collective-permute-start(f32[2,2,32,256]{3,2,1,0:T(8,128)S(1)} %get-tuple-element.46.block), channel_id=1, source_target_pairs={{0,2},{2,0},{4,6},{6,4},{8,10},{10,8},{12,14},{14,12},{1,3},{3,1},... | collective-permute-start | bytes 393224 | tf_op jit(solution)/shard_map/ppermute | solution.py:763
  22.0 3.0 %collective-permute-done.5.theirs = f32[2,2,32,256]{3,2,1,0:T(8,128)S(1)} collective-permute-done((f32[2,2,32,256]{3,2,1,0:T(8,128)S(1)}, f32[2,2,32,256]{3,2,1,0:T(8,128)S(1)}, u32[]{:S(2)}, u32[]{:S(2)}) %collective-permute-start.5) | collective-permute-done | bytes 131104 | tf_op jit(solution)/shard_map/ppermute | solution.py:763
  24.9 0.6 %shard_map.62 = (f32[2,2,32,256]{3,2,1,0:T(8,128)S(1)}, f32[2,2,32,256]{3,2,1,0:T(8,128)S(1)}, f32[32,256]{1,0:T(8,128)S(1)}, f32[32,256]{1,0:T(8,128)S(1)}) custom-call(s32[3]{0:T(128)S(1)} %copy-done.3, f32[5,32,256]{2,1,0:T(8,128)S(1)} %copy-done.2, f32[5,32,256]{2,1,0:T(8,128)S(1)} %collective-permute-done.3.other, ...), custom_call_target="tpu_custom_call" | custom-call | flops 10000000 | bytes 2000000 | tf_op jit(solution)/shard_map/pallas_call | solution.py:23
  25.5 0.8 %collective-permute-start.7 = (f32[2,2,32,256]{3,2,1,0:T(8,128)S(1)}, f32[2,2,32,256]{3,2,1,0:T(8,128)S(1)}, u32[]{:S(2)}, u32[]{:S(2)}) collective-permute-start(f32[2,2,32,256]{3,2,1,0:T(8,128)S(1)} %get-tuple-element.51.block), channel_id=1, source_target_pairs={{0,4},{2,6},{4,0},{6,2},{8,12},{10,14},{12,8},{14,10},{1,5},{3,7},... | collective-permute-start | bytes 393224 | tf_op jit(solution)/shard_map/ppermute | solution.py:763
  26.3 1.8 %collective-permute-start.4 = (f32[3,32,256]{2,1,0:T(8,128)S(1)}, f32[3,32,256]{2,1,0:T(8,128)S(1)}, u32[]{:S(2)}, u32[]{:S(2)}) collective-permute-start(f32[3,32,256]{2,1,0:T(8,128)S(1)} %get-tuple-element.45), channel_id=1, source_target_pairs={{0,2},{2,0},{4,6},{6,4},{8,10},{10,8},{12,14},{14,12},{1,3},{3,1},... | collective-permute-start | bytes 294920 | tf_op jit(solution)/shard_map/ppermute | solution.py:764
  28.1 2.3 %collective-permute-done.4.got = f32[3,32,256]{2,1,0:T(8,128)S(1)} collective-permute-done((f32[3,32,256]{2,1,0:T(8,128)S(1)}, f32[3,32,256]{2,1,0:T(8,128)S(1)}, u32[]{:S(2)}, u32[]{:S(2)}) %collective-permute-start.4) | collective-permute-done | bytes 98336 | tf_op jit(solution)/shard_map/ppermute | solution.py:764
  30.4 0.6 %shard_map.63 = (f32[3,32,128]{2,1,0:T(8,128)S(1)}, f32[3,32,128]{2,1,0:T(8,128)S(1)}) custom-call(s32[3]{0:T(128)S(1)} %copy-done.3, f32[3,32,256]{2,1,0:T(8,128)S(1)} %get-tuple-element.44.keep, f32[3,32,256]{2,1,0:T(8,128)S(1)} %collective-permute-done.4.got, f32[32,256]{1,0:T(8,128)S(1)} %get-tuple-element.47.mine_scale, ...), custom_call_target="tpu_custom_call" | custom-call | flops 10000000 | bytes 2000000 | tf_op jit(solution)/shard_map/pallas_call | solution.py:23
  31.2 1.2 %shard_map.64 = (f32[2,2,32,256]{3,2,1,0:T(8,128)S(1)}, f32[2,2,32,256]{3,2,1,0:T(8,128)S(1)}, f32[2,32,256]{2,1,0:T(8,128)S(1)}, f32[32,128]{1,0:T(8,128)S(1)}, f32[32,128]{1,0:T(8,128)S(1)}) custom-call(s32[3]{0:T(128)S(1)} %copy-done.3, f32[5,32,256]{2,1,0:T(8,128)S(1)} %copy-done.2, f32[5,32,256]{2,1,0:T(8,128)S(1)} %collective-permute-done.3.other, ...), custom_call_target="tpu_custom_call" | custom-call | flops 10000000 | bytes 2000000 | tf_op jit(solution)/shard_map/pallas_call | solution.py:23
  32.4 2.0 %collective-permute-start.9 = (f32[2,32,256]{2,1,0:T(8,128)S(1)}, f32[2,32,256]{2,1,0:T(8,128)S(1)}, u32[]{:S(2)}, u32[]{:S(2)}) collective-permute-start(f32[2,32,256]{2,1,0:T(8,128)S(1)} %get-tuple-element.56), channel_id=1, source_target_pairs={{0,8},{2,10},{4,12},{6,14},{8,0},{10,2},{12,4},{14,6},{1,9},{3,11}... | collective-permute-start | bytes 196616 | tf_op jit(solution)/shard_map/ppermute | solution.py:763
  34.4 0.6 shard_map.65.keep
  35.0 1.3 %collective-permute-start.8 = (f32[3,32,128]{2,1,0:T(8,128)S(1)}, f32[3,32,128]{2,1,0:T(8,128)S(1)}, u32[]{:S(2)}, u32[]{:S(2)}) collective-permute-start(f32[3,32,128]{2,1,0:T(8,128)S(1)} %shard_map.65.keep), channel_id=1, source_target_pairs={{0,8},{2,10},{4,12},{6,14},{8,0},{10,2},{12,4},{14,6},{1,9},{3,11}... | collective-permute-start | bytes 147464 | tf_op jit(solution)/shard_map/ppermute | solution.py:764
  36.3 2.5 %shard_map.69.cols5 = f32[5,2,8,32,256]{4,3,2,1,0:T(8,128)S(1)} custom-call(s32[3]{0:T(128)S(1)} %copy-done.3, f32[5,32,256]{2,1,0:T(8,128)S(1)} %copy-done.2, f32[5,32,256]{2,1,0:T(8,128)S(1)} %collective-permute-done.3.other, f32[2,4,6,32,256]{4,3,2,1,0:T(8,128)S(1)} %get-tuple-element.63.vals, f32[2,4,2,32,256]{4,3,2,1,0:T(8,128)S(1)} %get-tuple-element.64.rim, ...), custom_call_target="tpu_custom_call" | custom-call | flops 10000000 | bytes 2000000 | tf_op jit(solution)/shard_map/pallas_call | solution.py:23
  38.8 1.2 %shard_map.66 = (f32[2,2,32,256]{3,2,1,0:T(8,128)S(1)}, f32[32,128]{1,0:T(8,128)S(1)}, f32[32,128]{1,0:T(8,128)S(1)}) custom-call(s32[3]{0:T(128)S(1)} %copy-done.3, f32[5,32,256]{2,1,0:T(8,128)S(1)} %copy-done.2, f32[5,32,256]{2,1,0:T(8,128)S(1)} %collective-permute-done.3.other, f32[2,2,32,256]{3,2,1,0:T(8,128)S(1)} %get-tuple-element.55.block, ...), custom_call_target="tpu_custom_call" | custom-call | flops 10000000 | bytes 2000000 | tf_op jit(solution)/shard_map/pallas_call | solution.py:23
  40.0 1.6 %shard_map.70 = (f32[4,2,8,32,256]{4,3,2,1,0:T(8,128)S(1)}, f32[4,8,256]{2,1,0:T(8,128)S(1)}, f32[32,128]{1,0:T(8,128)S(1)}, f32[8,128]{1,0:T(8,128)S(1)}) custom-call(s32[3]{0:T(128)S(1)} %copy-done.3, f32[2,2,32,256]{3,2,1,0:T(8,128)S(1)} %get-tuple-element.62.reach_rest, f32[5,2,8,32,256]{4,3,2,1,0:T(8,128)S(1)} %shard_map.69.cols5, ...), custom_call_target="tpu_custom_call" | custom-call | flops 10000000 | bytes 2000000 | tf_op jit(solution)/shard_map/pallas_call | solution.py:23
  41.7 5.6 %collective-permute-start.11 = (f32[4,8,256]{2,1,0:T(8,128)S(1)}, f32[4,8,256]{2,1,0:T(8,128)S(1)}, u32[]{:S(2)}, u32[]{:S(2)}) collective-permute-start(f32[4,8,256]{2,1,0:T(8,128)S(1)} %get-tuple-element.67), channel_id=1, source_target_pairs={{0,1},{1,0},{2,3},{3,2},{4,5},{5,4},{6,7},{7,6},{8,9},{9,8},{10,11... | collective-permute-start | bytes 98312 | tf_op jit(solution)/shard_map/ppermute | solution.py:810
  47.3 0.6 %shard_map.67 = (f32[3,32,64]{2,1,0:T(8,128)S(1)}, f32[3,32,64]{2,1,0:T(8,128)S(1)}) custom-call(s32[3]{0:T(128)S(1)} %copy-done.3, f32[3,32,128]{2,1,0:T(8,128)S(1)} %shard_map.65.keep, f32[3,32,128]{2,1,0:T(8,128)S(1)} %collective-permute-done.8.got, f32[32,128]{1,0:T(8,128)S(1)} %get-tuple-element.58.mine_scale, f32[32,128]{1,0:T(8,128)S(1)} %get-tuple-element.59.their_scale), custom_call_target="tpu_custom_call" | custom-call | flops 10000000 | bytes 2000000 | tf_op jit(solution)/shard_map/pallas_call | solution.py:23
  47.9 1.2 %collective-permute-start.10 = (f32[3,32,64]{2,1,0:T(8,128)S(1)}, f32[3,32,64]{2,1,0:T(8,128)S(1)}, u32[]{:S(2)}, u32[]{:S(2)}) collective-permute-start(f32[3,32,64]{2,1,0:T(8,128)S(1)} %get-tuple-element.61), channel_id=1, source_target_pairs={{0,16},{16,0},{1,17},{17,1},{2,18},{18,2},{3,19},{19,3},{4,20},{20... | collective-permute-start | bytes 73736 | tf_op jit(solution)/shard_map/ppermute | solution.py:840
  49.1 0.4 collective-permute-start.12
  49.5 1.6 %collective-permute-start.13 = (f32[8,128]{1,0:T(8,128)S(1)}, f32[8,128]{1,0:T(8,128)S(1)}, u32[]{:S(2)}, u32[]{:S(2)}) collective-permute-start(f32[8,128]{1,0:T(8,128)S(1)} %get-tuple-element.69), channel_id=1, source_target_pairs={{0,17},{1,16},{16,1},{17,0},{2,19},{3,18},{18,3},{19,2},{4,21},{5,... | collective-permute-start | bytes 12296 | tf_op jit(solution)/shard_map/ppermute | solution.py:809
  51.1 2.0 %scatter.1.grad_in = f32[4,8,32,256]{3,2,1,0:T(8,128)S(1)} custom-call(f32[4,2,8,32,256]{4,3,2,1,0:T(8,128)S(1)} %get-tuple-element.66.columns, f32[5,32,256]{2,1,0:T(8,128)S(1)} %copy-done.2, f32[5,32,256]{2,1,0:T(8,128)S(1)} %collective-permute-done.3.other), custom_call_target="tpu_custom_call" | custom-call | flops 10000000 | bytes 2000000 | tf_op jit(solution)/shard_map/scatter/pallas_call | solution.py:811
  53.1 1.2 %shard_map.68 = f32[1,3,32,64]{3,2,1,0:T(8,128)} custom-call(s32[3]{0:T(128)S(1)} %copy-done.3, f32[3,32,64]{2,1,0:T(8,128)S(1)} %get-tuple-element.60.mine, f32[3,32,64]{2,1,0:T(8,128)S(1)} %collective-permute-done.10.got), custom_call_target="tpu_custom_call" | custom-call | flops 10000000 | bytes 2000000 | tf_op jit(solution)/shard_map/pallas_call | solution.py:23
  54.3 1.6 %finish.1 = f32[4,8,32,256]{3,2,1,0:T(8,128)} custom-call(s32[3]{0:T(128)S(1)} %copy-done.3, f32[4,8,32,256]{3,2,1,0:T(8,128)S(1)} %scatter.1.grad_in, f32[4,8,256]{2,1,0:T(8,128)S(1)} %collective-permute-done.11.line, f32[32,128]{1,0:T(8,128)S(1)} %collective-permute-done.12.edge, f32[8,128]{1,0:T(8,128)S(1)} %collective-permute-done.13.corner), custom_call_target="tpu_custom_call" | custom-call | flops 10000000 | bytes 2000000 | tf_op jit(solution)/shard_map/finish/pallas_call | solution.py:821
  (20 shorter events, 0.3 us)
Async XLA Ops:
  1.2 5.5 %copy-start.3 = (s32[3]{0:T(128)S(1)}, s32[3]{0:T(128)}, u32[]{:S(2)}) copy-start(s32[3]{0:T(128)} %pad_add_fusion.info) | copy-start | bytes 40
  4.0 2.8 %collective-permute-start = (f32[4,8,512]{2,1,0:T(8,128)}, f32[4,8,512]{2,1,0:T(8,128)S(1)}, u32[]{:S(2)}, u32[]{:S(2)}) collective-permute-start(f32[4,8,512]{2,1,0:T(8,128)} %get-tuple-element.36), channel_id=1, source_target_pairs={{0,1},{1,0},{2,3},{3,2},{4,5},{5,4},{6,7},{7,6},{8,9},{9,8},{10,11... | collective-permute-start | bytes 196616 | tf_op jit(solution)/shard_map/ppermute | solution.py:716
  4.1 7.4 %collective-permute-start.3 = (f32[5,32,256]{2,1,0:T(8,128)}, f32[5,32,256]{2,1,0:T(8,128)S(1)}, u32[]{:S(2)}, u32[]{:S(2)}) collective-permute-start(f32[5,32,256]{2,1,0:T(8,128)} %get-tuple-element.40), channel_id=1, source_target_pairs={{0,16},{16,0},{1,17},{17,1},{2,18},{18,2},{3,19},{19,3},{4,20},{20... | collective-permute-start | bytes 491528 | tf_op jit(solution)/shard_map/ppermute | solution.py:717
  6.8 1.6 %copy-start = (f32[4,8,32,512]{3,2,1,0:T(8,128)S(1)}, f32[4,8,32,512]{3,2,1,0:T(8,128)}, u32[]{:S(2)}) copy-start(f32[4,8,32,512]{3,2,1,0:T(8,128)} %vox.1) | copy-start | bytes 6291460
  8.4 3.1 %copy-start.1 = (f32[4,8,32,512]{3,2,1,0:T(8,128)S(1)}, f32[4,8,32,512]{3,2,1,0:T(8,128)}, u32[]{:S(2)}) copy-start(f32[4,8,32,512]{3,2,1,0:T(8,128)} %vox.1) | copy-start | bytes 6291460
  8.4 3.1 %copy-start.2 = (f32[5,32,256]{2,1,0:T(8,128)S(1)}, f32[5,32,256]{2,1,0:T(8,128)}, u32[]{:S(2)}) copy-start(f32[5,32,256]{2,1,0:T(8,128)} %get-tuple-element.39.own) | copy-start | bytes 491524
  9.0 7.2 %collective-permute-start.1 = (f32[296,128]{1,0:T(8,128)S(1)}, f32[296,128]{1,0:T(8,128)S(1)}, u32[]{:S(2)}, u32[]{:S(2)}) collective-permute-start(f32[296,128]{1,0:T(8,128)S(1)} %get-tuple-element.37), channel_id=1, source_target_pairs={{0,2},{2,0},{4,6},{6,4},{8,10},{10,8},{12,14},{14,12},{1,3},{3,1},... | collective-permute-start | bytes 454664 | tf_op jit(solution)/shard_map/ppermute | solution.py:729
  10.3 5.9 %collective-permute-start.2 = (f32[296,128]{1,0:T(8,128)S(1)}, f32[296,128]{1,0:T(8,128)S(1)}, u32[]{:S(2)}, u32[]{:S(2)}) collective-permute-start(f32[296,128]{1,0:T(8,128)S(1)} %get-tuple-element.38), channel_id=1, source_target_pairs={{2,4},{6,8},{10,12},{4,2},{8,6},{12,10},{3,5},{7,9},{11,13},{5,3},... | collective-permute-start | bytes 454664 | tf_op jit(solution)/shard_map/ppermute | solution.py:729
  18.7 6.2 %collective-permute-start.5 = (f32[2,2,32,256]{3,2,1,0:T(8,128)S(1)}, f32[2,2,32,256]{3,2,1,0:T(8,128)S(1)}, u32[]{:S(2)}, u32[]{:S(2)}) collective-permute-start(f32[2,2,32,256]{3,2,1,0:T(8,128)S(1)} %get-tuple-element.46.block), channel_id=1, source_target_pairs={{0,2},{2,0},{4,6},{6,4},{8,10},{10,8},{12,14},{14,12},{1,3},{3,1},... | collective-permute-start | bytes 393224 | tf_op jit(solution)/shard_map/ppermute | solution.py:763
  25.5 5.6 %collective-permute-start.7 = (f32[2,2,32,256]{3,2,1,0:T(8,128)S(1)}, f32[2,2,32,256]{3,2,1,0:T(8,128)S(1)}, u32[]{:S(2)}, u32[]{:S(2)}) collective-permute-start(f32[2,2,32,256]{3,2,1,0:T(8,128)S(1)} %get-tuple-element.51.block), channel_id=1, source_target_pairs={{0,4},{2,6},{4,0},{6,2},{8,12},{10,14},{12,8},{14,10},{1,5},{3,7},... | collective-permute-start | bytes 393224 | tf_op jit(solution)/shard_map/ppermute | solution.py:763
  26.3 4.1 %collective-permute-start.4 = (f32[3,32,256]{2,1,0:T(8,128)S(1)}, f32[3,32,256]{2,1,0:T(8,128)S(1)}, u32[]{:S(2)}, u32[]{:S(2)}) collective-permute-start(f32[3,32,256]{2,1,0:T(8,128)S(1)} %get-tuple-element.45), channel_id=1, source_target_pairs={{0,2},{2,0},{4,6},{6,4},{8,10},{10,8},{12,14},{14,12},{1,3},{3,1},... | collective-permute-start | bytes 294920 | tf_op jit(solution)/shard_map/ppermute | solution.py:764
  31.0 3.4 %collective-permute-start.6 = (f32[3,32,128]{2,1,0:T(8,128)S(1)}, f32[3,32,128]{2,1,0:T(8,128)S(1)}, u32[]{:S(2)}, u32[]{:S(2)}) collective-permute-start(f32[3,32,128]{2,1,0:T(8,128)S(1)} %get-tuple-element.50), channel_id=1, source_target_pairs={{0,4},{2,6},{4,0},{6,2},{8,12},{10,14},{12,8},{14,10},{1,5},{3,7},... | collective-permute-start | bytes 147464 | tf_op jit(solution)/shard_map/ppermute | solution.py:764
  32.4 6.5 %collective-permute-start.9 = (f32[2,32,256]{2,1,0:T(8,128)S(1)}, f32[2,32,256]{2,1,0:T(8,128)S(1)}, u32[]{:S(2)}, u32[]{:S(2)}) collective-permute-start(f32[2,32,256]{2,1,0:T(8,128)S(1)} %get-tuple-element.56), channel_id=1, source_target_pairs={{0,8},{2,10},{4,12},{6,14},{8,0},{10,2},{12,4},{14,6},{1,9},{3,11}... | collective-permute-start | bytes 196616 | tf_op jit(solution)/shard_map/ppermute | solution.py:763
  35.0 12.3 %collective-permute-start.8 = (f32[3,32,128]{2,1,0:T(8,128)S(1)}, f32[3,32,128]{2,1,0:T(8,128)S(1)}, u32[]{:S(2)}, u32[]{:S(2)}) collective-permute-start(f32[3,32,128]{2,1,0:T(8,128)S(1)} %shard_map.65.keep), channel_id=1, source_target_pairs={{0,8},{2,10},{4,12},{6,14},{8,0},{10,2},{12,4},{14,6},{1,9},{3,11}... | collective-permute-start | bytes 147464 | tf_op jit(solution)/shard_map/ppermute | solution.py:764
  41.7 12.6 %collective-permute-start.11 = (f32[4,8,256]{2,1,0:T(8,128)S(1)}, f32[4,8,256]{2,1,0:T(8,128)S(1)}, u32[]{:S(2)}, u32[]{:S(2)}) collective-permute-start(f32[4,8,256]{2,1,0:T(8,128)S(1)} %get-tuple-element.67), channel_id=1, source_target_pairs={{0,1},{1,0},{2,3},{3,2},{4,5},{5,4},{6,7},{7,6},{8,9},{9,8},{10,11... | collective-permute-start | bytes 98312 | tf_op jit(solution)/shard_map/ppermute | solution.py:810
  47.9 5.2 %collective-permute-start.10 = (f32[3,32,64]{2,1,0:T(8,128)S(1)}, f32[3,32,64]{2,1,0:T(8,128)S(1)}, u32[]{:S(2)}, u32[]{:S(2)}) collective-permute-start(f32[3,32,64]{2,1,0:T(8,128)S(1)} %get-tuple-element.61), channel_id=1, source_target_pairs={{0,16},{16,0},{1,17},{17,1},{2,18},{18,2},{3,19},{19,3},{4,20},{20... | collective-permute-start | bytes 73736 | tf_op jit(solution)/shard_map/ppermute | solution.py:840
  49.1 5.2 %collective-permute-start.12 = (f32[32,128]{1,0:T(8,128)S(1)}, f32[32,128]{1,0:T(8,128)S(1)}, u32[]{:S(2)}, u32[]{:S(2)}) collective-permute-start(f32[32,128]{1,0:T(8,128)S(1)} %get-tuple-element.68), channel_id=1, source_target_pairs={{0,16},{16,0},{1,17},{17,1},{2,18},{18,2},{3,19},{19,3},{4,20},{20... | collective-permute-start | bytes 49160 | tf_op jit(solution)/shard_map/ppermute | solution.py:808
  49.5 4.8 %collective-permute-start.13 = (f32[8,128]{1,0:T(8,128)S(1)}, f32[8,128]{1,0:T(8,128)S(1)}, u32[]{:S(2)}, u32[]{:S(2)}) collective-permute-start(f32[8,128]{1,0:T(8,128)S(1)} %get-tuple-element.69), channel_id=1, source_target_pairs={{0,17},{1,16},{16,1},{17,0},{2,19},{3,18},{18,3},{19,2},{4,21},{5,... | collective-permute-start | bytes 12296 | tf_op jit(solution)/shard_map/ppermute | solution.py:809

commit v5 on v4

--- a/solution.py
+++ b/solution.py
@@ -14,23 +14,23 @@
 SUB = 8
 F32 = jnp.float32
 VMEM = pl.BlockSpec(memory_space=pltpu.VMEM)
-SMEM = pl.BlockSpec(memory_space=pltpu.SMEM)
 MIB = 2**20
 
 
-def call(body, outs, args, scratch=(), limit=16, flops=10**7, specs=None, **statics):
-    inputs = [SMEM] + [VMEM] * (len(args) - 1)
+def call(body, outs, args, scratch=(), limit=16, specs=None, out_specs=None, **statics):
+    def kernel(*refs):
+        body(tuple(lax.axis_index(a) for a in ("dir", "tile", "slab")), *refs, **statics)
+
+    grid = {} if specs is None else dict(grid=(1,))
     return pl.pallas_call(
-        functools.partial(body, **statics),
+        kernel,
         out_shape=outs,
-        grid=() if specs is None else (1,),
-        in_specs=specs or inputs,
-        out_specs=jax.tree.map(lambda _: VMEM, outs),
+        in_specs=specs or [VMEM] * len(args),
+        out_specs=out_specs or jax.tree.map(lambda _: VMEM, outs),
         scratch_shapes=list(scratch),
-        cost_estimate=pl.CostEstimate(
-            flops=flops, bytes_accessed=2 * 10**6, transcendentals=0
-        ),
+        cost_estimate=pl.CostEstimate(flops=10**7, bytes_accessed=2 * 10**6, transcendentals=0),
         compiler_params=pltpu.CompilerParams(vmem_limit_bytes=limit * MIB),
+        **grid,
     )(*args)
 
 
@@ -231,13 +231,8 @@
             )
 
 
-def each_tile(rows, width, body, unroll=False):
+def each_tile(rows, width, body):
     count = width // LANES
-    if unroll:
-        for i in range(rows // SUB):
-            for j in range(count):
-                body(pl.ds(i * SUB, SUB), pl.ds(j * LANES, LANES))
-        return
 
     def step(n, carry):
         row = pl.ds(pl.multiple_of((n // count) * SUB, SUB), SUB)
@@ -506,17 +501,17 @@
                         ray_order(info, bit + 1, heading), out_light, out_depth
                     )
             scales.append((jnp.where(earlier, their_fade, 1.0), jnp.where(earlier, 1.0, fade)))
-        packed = [jnp.where(kept, a, pltpu.roll(b, turn, 1)) for a, b in zip(*scales)]
-        for out, x in zip((mine_scale, their_scale), packed):
-            if not halved:
-                out[row, col] = x
-            else:
-
-                @pl.when(col.start == my_tile * LANES)
-                def _(out=out, x=x):
-                    out[row, :] = x
-
-    each_tile(rows, width, ray, unroll=True)
+        return [jnp.where(kept, a, pltpu.roll(b, turn, 1)) for a, b in zip(*scales)]
+
+    for i in range(rows // SUB):
+        row = pl.ds(i * SUB, SUB)
+        packed = [ray(row, pl.ds(j, LANES)) for j in range(0, width, LANES)]
+        for n, out in enumerate((mine_scale, their_scale)):
+            if halved:
+                out[row, :] = jnp.where(my_tile == 0, packed[0][n], packed[1][n])
+                continue
+            for j, x in enumerate(packed):
+                out[row, j * LANES : (j + 1) * LANES] = x[n]
 
 
 def light_body(info, keep, got, mine_scale, their_scale, *outs, tile_bit):
@@ -615,7 +610,7 @@
     corner[...] = jnp.where(t == 0, lower[:SUB], pltpu.roll(upper[rows - SUB :], 1, 0))
 
 
-def scatter_body(columns, own, other, grad, weights):
+def scatter_body(_, columns, own, other, grad, weights):
     channels, _, planes, rows, width = columns.shape
     lane = iota((rows, width), 1)
     row = iota((rows, width), 0)
@@ -680,8 +675,6 @@
     width = total // dirs
     depth = planes * slabs
     scale = 2.0 / depth
-    h, s, t = (lax.axis_index(a) for a in ("dir", "slab", "tile"))
-    info = jnp.stack([h, t, s]).astype(jnp.int32)
     swap = [(0, 1), (1, 0)]
     count = width // LANES
     grid = lambda n: pltpu.VMEM((3, channels, n, rows + 2 * SUB, width), F32)
@@ -698,21 +691,22 @@
 
     hbm = pl.BlockSpec(memory_space=pltpu.HBM)
     ray = shape(channels + 1, rows, width)
-    own, sent, line = pl.pallas_call(
-        functools.partial(first_body, width=width, depth=depth),
-        out_shape=[ray, ray, shape(channels, planes, total)],
-        in_specs=[SMEM] + [hbm] * 4,
-        out_specs=[VMEM] * 3,
-        scratch_shapes=[
+    own, sent, line = call(
+        first_body,
+        [ray, ray, shape(channels, planes, total)],
+        (offsets, heading, cotangent, voxels),
+        specs=[hbm] * 4,
+        scratch=[
             pltpu.VMEM(offsets.shape, jnp.int32),
             pltpu.VMEM(heading.shape, jnp.int32),
             pltpu.VMEM(cotangent.shape, F32),
             pltpu.VMEM((channels, planes, SUB, total), F32),
             pltpu.SemaphoreType.DMA((4,)),
         ],
-        compiler_params=pltpu.CompilerParams(vmem_limit_bytes=62 * MIB),
-        name="first",
-    )(info, offsets, heading, cotangent, voxels)
+        limit=62,
+        width=width,
+        depth=depth,
+    )
     line = lax.ppermute(line, "tile", swap)
     other = lax.ppermute(sent, "dir", swap)
 
@@ -722,8 +716,8 @@
     near = call(
         pack_body,
         [shape(message_rows(channels, rows, count)[2], LANES)] * 2,
-        (info, voxels, voxels, line),
-        specs=[SMEM, block(0), block(planes - 1), VMEM],
+        (voxels, voxels, line),
+        specs=[block(0), block(planes - 1), VMEM],
         width=width,
     )
     near = [lax.ppermute(x, "slab", p) for x, p in zip(near, (pairs_a, pairs_b))]
@@ -733,7 +727,7 @@
     vals, part, ends, inner = call(
         inner_body,
         [shape(2, channels, planes - 2, rows, width), two, two, shape(channels, 2, rows, width)],
-        (info, voxels, line, own, other),
+        (voxels, line, own, other),
         scratch=[grid(planes)],
         limit=20,
         width=width,
@@ -743,7 +737,7 @@
     pay, rim, ends, keep, send = call(
         rim_body,
         [pair, two, two, light, light],
-        (info, *near, own, other, part, ends, inner),
+        (*near, own, other, part, ends, inner),
         scratch=[grid(2)],
         scale=scale,
         chunk=chunk,
@@ -751,7 +745,7 @@
     cols5 = call(
         column_body,
         shape(channels + 1, 2, planes, rows, width),
-        (info, own, other, vals, rim, ends),
+        (own, other, vals, rim, ends),
         scale=scale,
         slabs=slabs,
     )
@@ -769,7 +763,7 @@
         state, *others, mine_scale, their_scale = call(
             scan_body,
             outs,
-            (info, own, other, pay, theirs) + tuple(state),
+            (own, other, pay, theirs) + tuple(state),
             bit=bit,
             rounds=rounds,
             chunk=chunk,
@@ -785,15 +779,11 @@
         pieces = call(
             light_body,
             [kept] * (1 if split is None else 2),
-            (info, keep, got, mine_scale, their_scale),
+            (keep, got, mine_scale, their_scale),
             tile_bit=split,
         )
         keep, send = (pieces[0], pieces[-1])
 
-    plain = dict(
-        compiler_params=pltpu.CompilerParams(vmem_limit_bytes=16 * MIB),
-        cost_estimate=pl.CostEstimate(flops=10**7, bytes_accessed=2 * 10**6, transcendentals=0),
-    )
     columns, line, edge, corner = call(
         merge_body,
         [
@@ -802,43 +792,38 @@
             shape(rows, LANES),
             shape(SUB, LANES),
         ],
-        (info, state, cols5, own, other),
+        (state, cols5, own, other),
         scratch=[pltpu.VMEM((2, planes, width), F32)],
     )
     edge = lax.ppermute(edge, "dir", swap)
     corner = lax.ppermute(corner, ("dir", "tile"), [(i, 3 - i) for i in range(4)])
     line = lax.ppermute(line, "tile", swap)
-    grad = pl.pallas_call(
+    grad_shape = (channels, planes, rows, width)
+    grad = call(
         scatter_body,
-        out_shape=shape(channels, planes, rows, width),
-        in_specs=[VMEM] * 3,
-        out_specs=VMEM,
-        scratch_shapes=[pltpu.VMEM((2, 9, rows, width), F32)],
-        name="scatter",
-        **plain,
-    )(columns, own, other)
-    grad_shape = (channels, planes, rows, width)
-    voxel_grad = pl.pallas_call(
+        shape(*grad_shape),
+        (columns, own, other),
+        scratch=[pltpu.VMEM((2, 9, rows, width), F32)],
+    )
+    voxel_grad = call(
         finish_body,
-        out_shape=shape(*grad_shape),
-        in_specs=[SMEM] + [VMEM] * 4,
+        shape(*grad_shape),
+        (grad, line, edge, corner),
+        scratch=[pltpu.VMEM(grad_shape, F32), pltpu.SemaphoreType.DMA((channels,))],
         out_specs=hbm,
-        scratch_shapes=[pltpu.VMEM(grad_shape, F32), pltpu.SemaphoreType.DMA((channels,))],
-        name="finish",
-        **plain,
-    )(info, grad, line, edge, corner)
+    )
 
     piece = shape(colours, rows, chunk)
     mine, sent = call(
         image_body,
         [piece, piece],
-        (info, keep, got, mine_scale, their_scale),
+        (keep, got, mine_scale, their_scale),
         chunk=chunk,
         half=half,
         halved=tile_bit is not None,
     )
     got = lax.ppermute(sent, "dir", swap)
-    image = call(choose_body, shape(1, colours, rows, chunk), (info, mine, got), half=half)
+    image = call(choose_body, shape(1, colours, rows, chunk), (mine, got), half=half)
     return (image, voxel_grad)
 
 

time: 56.1 us -> 47.9 us (0.85)
  Pallas kernels: 24.3 us -> 15.3 us
  waiting for transfers between devices: 5.74 us -> 6.65 us
  other arithmetic: 0.62 us -> 0 us
    pallas_call x15, Pallas kernels: 24.3 us -> 15.3 us  [call(): pl.pallas_call(kernel, out_shape=outs, in_specs=specs or [VMEM] * len(arg...]
    ppermute x3, starting transfers between devices: 3.31 us -> 4.15 us  [per_device(): got = lax.ppermute(send, 'slab', pairs)]
    another operation x1 -> x0, other arithmetic: 0.62 us -> none  [per_device(): info = jnp.stack([h, t, s]).astype(jnp.int32)]
    unnamed x8 -> x6, local copies, waits for them, and re-layouts: 1.6 us -> 1.6 us
  transfers between devices with their start and end apart: 14 -> 14, of which waited for: 3 -> 4; matrix products, arithmetic and copies ran while one was open for 0% -> 0% of each run, Pallas kernels for 30% -> 22%
where the time goes in v5:
time: 47.9 us; the launch traced here: 47.8 us
  starting transfers between devices  23.4 us (49%)
  Pallas kernels  15.3 us (32%)
  waiting for transfers between devices  6.65 us (14%)
  local copies, waits for them, and re-layouts  1.6 us (3%)
  between operations  0.75 us (2%)
    pallas_call x15, Pallas kernels, call(): pl.pallas_call(kernel, out_shape=outs, in_specs=specs or [VMEM] * len(arg...  15.3 us
    ppermute x3, starting transfers between devices, per_device(): theirs = lax.ppermute(message, 'slab', pairs)  6.16 us
    ppermute x2, starting transfers between devices, per_device(): line = lax.ppermute(line, 'tile', swap)  5.36 us
    ppermute x3, starting transfers between devices, per_device(): got = lax.ppermute(send, 'slab', pairs)  4.15 us
    ppermute x3, waiting for transfers between devices, per_device(): theirs = lax.ppermute(message, 'slab', pairs)  2.96 us
    ppermute x3, waiting for transfers between devices, per_device(): got = lax.ppermute(send, 'slab', pairs)  2.69 us
    ppermute x1, starting transfers between devices, per_device(): other = lax.ppermute(sent, 'dir', swap)  2.69 us
    ppermute x2, starting transfers between devices, per_device(): lax.ppermute(x, 'slab', p)  1.96 us
  transfers between devices with their start and end apart: 14, of which 4 were waited for; matrix products, arithmetic and copies ran while one was open for 0% of the time, Pallas kernels for 22%

profile of v5, /device:TPU:1, one launch (start us, length us, event | category | flops | bytes accessed | tf_op | source)
XLA Modules:
  0.0 47.8 jit_solution(62820048164789256)
XLA Ops:
  0.6 1.9 %shard_map.59 = (f32[5,32,256]{2,1,0:T(8,128)}, f32[5,32,256]{2,1,0:T(8,128)}, f32[4,8,512]{2,1,0:T(8,128)}) custom-call(s32[1,32,512]{2,1,0:T(8,128)} %refs_0_.3, s32[1,32,512]{2,1,0:T(8,128)} %refs_1_.2, f32[1,3,32,512]{3,2,1,0:T(8,128)} %refs_2_.1, f32[4,8,32,512]{3,2,1,0:T(8,128)} %refs_0_.5), custom_call_target="tpu_custom_call" | custom-call | flops 10000000 | bytes 2000000 | tf_op jit(solution)/shard_map/pallas_call | solution.py:25
  2.6 0.1 collective-permute-start
  2.7 2.7 %collective-permute-start.3 = (f32[5,32,256]{2,1,0:T(8,128)}, f32[5,32,256]{2,1,0:T(8,128)S(1)}, u32[]{:S(2)}, u32[]{:S(2)}) collective-permute-start(f32[5,32,256]{2,1,0:T(8,128)} %get-tuple-element.40), channel_id=1, source_target_pairs={{0,16},{16,0},{1,17},{17,1},{2,18},{18,2},{3,19},{19,3},{4,20},{20... | collective-permute-start | bytes 491528 | tf_op jit(solution)/shard_map/ppermute | solution.py:711
  5.3 1.6 %copy-done = f32[4,8,32,512]{3,2,1,0:T(8,128)S(1)} copy-done((f32[4,8,32,512]{3,2,1,0:T(8,128)S(1)}, f32[4,8,32,512]{3,2,1,0:T(8,128)}, u32[]{:S(2)}) %copy-start) | copy-done | bytes 2097176
  6.9 0.1 shard_map.60
  7.1 1.3 %collective-permute-start.1 = (f32[296,128]{1,0:T(8,128)S(1)}, f32[296,128]{1,0:T(8,128)S(1)}, u32[]{:S(2)}, u32[]{:S(2)}) collective-permute-start(f32[296,128]{1,0:T(8,128)S(1)} %get-tuple-element.37), channel_id=1, source_target_pairs={{0,2},{2,0},{4,6},{6,4},{8,10},{10,8},{12,14},{14,12},{1,3},{3,1},... | collective-permute-start | bytes 454664 | tf_op jit(solution)/shard_map/ppermute | solution.py:723
  8.4 0.7 %collective-permute-start.2 = (f32[296,128]{1,0:T(8,128)S(1)}, f32[296,128]{1,0:T(8,128)S(1)}, u32[]{:S(2)}, u32[]{:S(2)}) collective-permute-start(f32[296,128]{1,0:T(8,128)S(1)} %get-tuple-element.38), channel_id=1, source_target_pairs={{2,4},{6,8},{10,12},{4,2},{8,6},{12,10},{3,5},{7,9},{11,13},{5,3},... | collective-permute-start | bytes 454664 | tf_op jit(solution)/shard_map/ppermute | solution.py:723
  9.1 1.0 %collective-permute-done.3.refs_3_.refs_1_.refs_2_ = f32[5,32,256]{2,1,0:T(8,128)S(1)} collective-permute-done((f32[5,32,256]{2,1,0:T(8,128)}, f32[5,32,256]{2,1,0:T(8,128)S(1)}, u32[]{:S(2)}, u32[]{:S(2)}) %collective-permute-start.3) | collective-permute-done | bytes 163872 | tf_op jit(solution)/shard_map/ppermute | solution.py:711
  10.1 4.2 %shard_map.61 = (f32[2,4,6,32,256]{4,3,2,1,0:T(8,128)S(1)}, f32[2,4,2,32,256]{4,3,2,1,0:T(8,128)S(1)}, f32[2,4,2,32,256]{4,3,2,1,0:T(8,128)S(1)}, f32[4,2,32,256]{3,2,1,0:T(8,128)S(1)}) custom-call(f32[4,8,32,512]{3,2,1,0:T(8,128)S(1)} %copy-done.1, f32[4,8,512]{2,1,0:T(8,128)S(1)} %collective-permute-done.refs_2_.refs_1_, f32[5,32,256]{2,1,0:T(8,128)S(1)} %copy-done.2, ...), custom_call_target="tpu_custom_call" | custom-call | flops 10000000 | bytes 2000000 | tf_op jit(solution)/shard_map/pallas_call | solution.py:25
  14.3 1.9 %shard_map.62 = (f32[2,2,32,256]{3,2,1,0:T(8,128)S(1)}, f32[2,4,2,32,256]{4,3,2,1,0:T(8,128)S(1)}, f32[2,4,2,32,256]{4,3,2,1,0:T(8,128)S(1)}, f32[3,32,256]{2,1,0:T(8,128)S(1)}, f32[3,32,256]{2,1,0:T(8,128)S(1)}) custom-call(f32[296,128]{1,0:T(8,128)S(1)} %collective-permute-done.1.refs_0_, f32[296,128]{1,0:T(8,128)S(1)} %collective-permute-done.2.refs_1_, ...), custom_call_target="tpu_custom_call" | custom-call | flops 10000000 | bytes 2000000 | tf_op jit(solution)/shard_map/pallas_call | solution.py:25
  16.2 2.8 %collective-permute-start.5 = (f32[2,2,32,256]{3,2,1,0:T(8,128)S(1)}, f32[2,2,32,256]{3,2,1,0:T(8,128)S(1)}, u32[]{:S(2)}, u32[]{:S(2)}) collective-permute-start(f32[2,2,32,256]{3,2,1,0:T(8,128)S(1)} %get-tuple-element.46.refs_2_), channel_id=1, source_target_pairs={{0,2},{2,0},{4,6},{6,4},{8,10},{10,8},{12,14},{14,12},{1,3},{3,1},... | collective-permute-start | bytes 393224 | tf_op jit(solution)/shard_map/ppermute | solution.py:757
  18.9 3.0 %collective-permute-done.5.refs_3_ = f32[2,2,32,256]{3,2,1,0:T(8,128)S(1)} collective-permute-done((f32[2,2,32,256]{3,2,1,0:T(8,128)S(1)}, f32[2,2,32,256]{3,2,1,0:T(8,128)S(1)}, u32[]{:S(2)}, u32[]{:S(2)}) %collective-permute-start.5) | collective-permute-done | bytes 131104 | tf_op jit(solution)/shard_map/ppermute | solution.py:757
  21.9 0.1 shard_map.63
  22.0 1.2 %collective-permute-start.7 = (f32[2,2,32,256]{3,2,1,0:T(8,128)S(1)}, f32[2,2,32,256]{3,2,1,0:T(8,128)S(1)}, u32[]{:S(2)}, u32[]{:S(2)}) collective-permute-start(f32[2,2,32,256]{3,2,1,0:T(8,128)S(1)} %get-tuple-element.51.refs_2_), channel_id=1, source_target_pairs={{0,4},{2,6},{4,0},{6,2},{8,12},{10,14},{12,8},{14,10},{1,5},{3,7},... | collective-permute-start | bytes 393224 | tf_op jit(solution)/shard_map/ppermute | solution.py:757
  23.2 1.4 %collective-permute-start.4 = (f32[3,32,256]{2,1,0:T(8,128)S(1)}, f32[3,32,256]{2,1,0:T(8,128)S(1)}, u32[]{:S(2)}, u32[]{:S(2)}) collective-permute-start(f32[3,32,256]{2,1,0:T(8,128)S(1)} %get-tuple-element.45), channel_id=1, source_target_pairs={{0,2},{2,0},{4,6},{6,4},{8,10},{10,8},{12,14},{14,12},{1,3},{3,1},... | collective-permute-start | bytes 294920 | tf_op jit(solution)/shard_map/ppermute | solution.py:758
  24.5 2.1 %collective-permute-done.4.refs_1_ = f32[3,32,256]{2,1,0:T(8,128)S(1)} collective-permute-done((f32[3,32,256]{2,1,0:T(8,128)S(1)}, f32[3,32,256]{2,1,0:T(8,128)S(1)}, u32[]{:S(2)}, u32[]{:S(2)}) %collective-permute-start.4) | collective-permute-done | bytes 98336 | tf_op jit(solution)/shard_map/ppermute | solution.py:758
  26.7 0.4 collective-permute-start.6
  27.1 0.1 shard_map.65
  27.2 2.2 %collective-permute-start.9 = (f32[2,32,256]{2,1,0:T(8,128)S(1)}, f32[2,32,256]{2,1,0:T(8,128)S(1)}, u32[]{:S(2)}, u32[]{:S(2)}) collective-permute-start(f32[2,32,256]{2,1,0:T(8,128)S(1)} %get-tuple-element.56), channel_id=1, source_target_pairs={{0,8},{2,10},{4,12},{6,14},{8,0},{10,2},{12,4},{14,6},{1,9},{3,11}... | collective-permute-start | bytes 196616 | tf_op jit(solution)/shard_map/ppermute | solution.py:757
  29.4 0.6 %collective-permute-done.6.refs_1_ = f32[3,32,128]{2,1,0:T(8,128)S(1)} collective-permute-done((f32[3,32,128]{2,1,0:T(8,128)S(1)}, f32[3,32,128]{2,1,0:T(8,128)S(1)}, u32[]{:S(2)}, u32[]{:S(2)}) %collective-permute-start.6) | collective-permute-done | bytes 49184 | tf_op jit(solution)/shard_map/ppermute | solution.py:758
  30.0 2.4 %collective-permute-start.8 = (f32[3,32,128]{2,1,0:T(8,128)S(1)}, f32[3,32,128]{2,1,0:T(8,128)S(1)}, u32[]{:S(2)}, u32[]{:S(2)}) collective-permute-start(f32[3,32,128]{2,1,0:T(8,128)S(1)} %shard_map.66.refs_0_), channel_id=1, source_target_pairs={{0,8},{2,10},{4,12},{6,14},{8,0},{10,2},{12,4},{14,6},{1,9},{3,11}... | collective-permute-start | bytes 147464 | tf_op jit(solution)/shard_map/ppermute | solution.py:758
  32.4 2.0 %shard_map.70.refs_1_ = f32[5,2,8,32,256]{4,3,2,1,0:T(8,128)S(1)} custom-call(f32[5,32,256]{2,1,0:T(8,128)S(1)} %copy-done.2, f32[5,32,256]{2,1,0:T(8,128)S(1)} %collective-permute-done.3.refs_3_.refs_1_.refs_2_, f32[2,4,6,32,256]{4,3,2,1,0:T(8,128)S(1)} %get-tuple-element.63.refs_2_, f32[2,4,2,32,256]{4,3,2,1,0:T(8,128)S(1)} %get-tuple-element.64.refs_3_, ...), custom_call_target="tpu_custom_call" | custom-call | flops 10000000 | bytes 2000000 | tf_op jit(solution)/shard_map/pallas_call | solution.py:25
  34.4 0.1 shard_map.67
  34.5 1.1 %shard_map.71 = (f32[4,2,8,32,256]{4,3,2,1,0:T(8,128)S(1)}, f32[4,8,256]{2,1,0:T(8,128)S(1)}, f32[32,128]{1,0:T(8,128)S(1)}, f32[8,128]{1,0:T(8,128)S(1)}) custom-call(f32[2,2,32,256]{3,2,1,0:T(8,128)S(1)} %get-tuple-element.62.refs_0_, f32[5,2,8,32,256]{4,3,2,1,0:T(8,128)S(1)} %shard_map.70.refs_1_, f32[5,32,256]{2,1,0:T(8,128)S(1)} %copy-done.2, ...), custom_call_target="tpu_custom_call" | custom-call | flops 10000000 | bytes 2000000 | tf_op jit(solution)/shard_map/pallas_call | solution.py:25
  35.6 5.3 %collective-permute-start.11 = (f32[4,8,256]{2,1,0:T(8,128)S(1)}, f32[4,8,256]{2,1,0:T(8,128)S(1)}, u32[]{:S(2)}, u32[]{:S(2)}) collective-permute-start(f32[4,8,256]{2,1,0:T(8,128)S(1)} %get-tuple-element.67), channel_id=1, source_target_pairs={{0,1},{1,0},{2,3},{3,2},{4,5},{5,4},{6,7},{7,6},{8,9},{9,8},{10,11... | collective-permute-start | bytes 98312 | tf_op jit(solution)/shard_map/ppermute | solution.py:800
  40.9 0.1 shard_map.68
  41.0 1.2 %collective-permute-start.10 = (f32[3,32,64]{2,1,0:T(8,128)S(1)}, f32[3,32,64]{2,1,0:T(8,128)S(1)}, u32[]{:S(2)}, u32[]{:S(2)}) collective-permute-start(f32[3,32,64]{2,1,0:T(8,128)S(1)} %get-tuple-element.61), channel_id=1, source_target_pairs={{0,16},{16,0},{1,17},{17,1},{2,18},{18,2},{3,19},{19,3},{4,20},{20... | collective-permute-start | bytes 73736 | tf_op jit(solution)/shard_map/ppermute | solution.py:825
  42.1 0.4 collective-permute-start.12
  42.5 1.6 %collective-permute-start.13 = (f32[8,128]{1,0:T(8,128)S(1)}, f32[8,128]{1,0:T(8,128)S(1)}, u32[]{:S(2)}, u32[]{:S(2)}) collective-permute-start(f32[8,128]{1,0:T(8,128)S(1)} %get-tuple-element.69), channel_id=1, source_target_pairs={{0,17},{1,16},{16,1},{17,0},{2,19},{3,18},{18,3},{19,2},{4,21},{5,... | collective-permute-start | bytes 12296 | tf_op jit(solution)/shard_map/ppermute | solution.py:799
  44.1 1.9 %shard_map.72.refs_0_ = f32[4,8,32,256]{3,2,1,0:T(8,128)S(1)} custom-call(f32[4,2,8,32,256]{4,3,2,1,0:T(8,128)S(1)} %get-tuple-element.66.refs_0_, f32[5,32,256]{2,1,0:T(8,128)S(1)} %copy-done.2, f32[5,32,256]{2,1,0:T(8,128)S(1)} %collective-permute-done.3.refs_3_.refs_1_.refs_2_), custom_call_target="tpu_custom_call" | custom-call | flops 10000000 | bytes 2000000 | tf_op jit(solution)/shard_map/pallas_call | solution.py:25
  46.0 0.6 %shard_map.69 = f32[1,3,32,64]{3,2,1,0:T(8,128)} custom-call(f32[3,32,64]{2,1,0:T(8,128)S(1)} %get-tuple-element.60.refs_0_, f32[3,32,64]{2,1,0:T(8,128)S(1)} %collective-permute-done.10.refs_1_), custom_call_target="tpu_custom_call" | custom-call | flops 10000000 | bytes 2000000 | tf_op jit(solution)/shard_map/pallas_call | solution.py:25
  46.7 1.1 %shard_map.73 = f32[4,8,32,256]{3,2,1,0:T(8,128)} custom-call(f32[4,8,32,256]{3,2,1,0:T(8,128)S(1)} %shard_map.72.refs_0_, f32[4,8,256]{2,1,0:T(8,128)S(1)} %collective-permute-done.11.refs_1_, f32[32,128]{1,0:T(8,128)S(1)} %collective-permute-done.12.refs_2_, f32[8,128]{1,0:T(8,128)S(1)} %collective-permute-done.13.refs_3_), custom_call_target="tpu_custom_call" | custom-call | flops 10000000 | bytes 2000000 | tf_op jit(solution)/shard_map/pallas_call | solution.py:25
  (17 shorter events, 0.1 us)
Async XLA Ops:
  2.6 2.8 %collective-permute-start = (f32[4,8,512]{2,1,0:T(8,128)}, f32[4,8,512]{2,1,0:T(8,128)S(1)}, u32[]{:S(2)}, u32[]{:S(2)}) collective-permute-start(f32[4,8,512]{2,1,0:T(8,128)} %get-tuple-element.36), channel_id=1, source_target_pairs={{0,1},{1,0},{2,3},{3,2},{4,5},{5,4},{6,7},{7,6},{8,9},{9,8},{10,11... | collective-permute-start | bytes 196616 | tf_op jit(solution)/shard_map/ppermute | solution.py:710
  2.7 7.4 %collective-permute-start.3 = (f32[5,32,256]{2,1,0:T(8,128)}, f32[5,32,256]{2,1,0:T(8,128)S(1)}, u32[]{:S(2)}, u32[]{:S(2)}) collective-permute-start(f32[5,32,256]{2,1,0:T(8,128)} %get-tuple-element.40), channel_id=1, source_target_pairs={{0,16},{16,0},{1,17},{17,1},{2,18},{18,2},{3,19},{19,3},{4,20},{20... | collective-permute-start | bytes 491528 | tf_op jit(solution)/shard_map/ppermute | solution.py:711
  5.3 1.6 %copy-start = (f32[4,8,32,512]{3,2,1,0:T(8,128)S(1)}, f32[4,8,32,512]{3,2,1,0:T(8,128)}, u32[]{:S(2)}) copy-start(f32[4,8,32,512]{3,2,1,0:T(8,128)} %refs_0_.5) | copy-start | bytes 6291460
  6.9 3.1 %copy-start.1 = (f32[4,8,32,512]{3,2,1,0:T(8,128)S(1)}, f32[4,8,32,512]{3,2,1,0:T(8,128)}, u32[]{:S(2)}) copy-start(f32[4,8,32,512]{3,2,1,0:T(8,128)} %refs_0_.5) | copy-start | bytes 6291460
  6.9 3.1 %copy-start.2 = (f32[5,32,256]{2,1,0:T(8,128)S(1)}, f32[5,32,256]{2,1,0:T(8,128)}, u32[]{:S(2)}) copy-start(f32[5,32,256]{2,1,0:T(8,128)} %get-tuple-element.39.refs_2_.refs_0_.refs_1_) | copy-start | bytes 491524
  7.1 7.2 %collective-permute-start.1 = (f32[296,128]{1,0:T(8,128)S(1)}, f32[296,128]{1,0:T(8,128)S(1)}, u32[]{:S(2)}, u32[]{:S(2)}) collective-permute-start(f32[296,128]{1,0:T(8,128)S(1)} %get-tuple-element.37), channel_id=1, source_target_pairs={{0,2},{2,0},{4,6},{6,4},{8,10},{10,8},{12,14},{14,12},{1,3},{3,1},... | collective-permute-start | bytes 454664 | tf_op jit(solution)/shard_map/ppermute | solution.py:723
  8.4 5.9 %collective-permute-start.2 = (f32[296,128]{1,0:T(8,128)S(1)}, f32[296,128]{1,0:T(8,128)S(1)}, u32[]{:S(2)}, u32[]{:S(2)}) collective-permute-start(f32[296,128]{1,0:T(8,128)S(1)} %get-tuple-element.38), channel_id=1, source_target_pairs={{2,4},{6,8},{10,12},{4,2},{8,6},{12,10},{3,5},{7,9},{11,13},{5,3},... | collective-permute-start | bytes 454664 | tf_op jit(solution)/shard_map/ppermute | solution.py:723
  16.2 5.7 %collective-permute-start.5 = (f32[2,2,32,256]{3,2,1,0:T(8,128)S(1)}, f32[2,2,32,256]{3,2,1,0:T(8,128)S(1)}, u32[]{:S(2)}, u32[]{:S(2)}) collective-permute-start(f32[2,2,32,256]{3,2,1,0:T(8,128)S(1)} %get-tuple-element.46.refs_2_), channel_id=1, source_target_pairs={{0,2},{2,0},{4,6},{6,4},{8,10},{10,8},{12,14},{14,12},{1,3},{3,1},... | collective-permute-start | bytes 393224 | tf_op jit(solution)/shard_map/ppermute | solution.py:757
  22.0 5.1 %collective-permute-start.7 = (f32[2,2,32,256]{3,2,1,0:T(8,128)S(1)}, f32[2,2,32,256]{3,2,1,0:T(8,128)S(1)}, u32[]{:S(2)}, u32[]{:S(2)}) collective-permute-start(f32[2,2,32,256]{3,2,1,0:T(8,128)S(1)} %get-tuple-element.51.refs_2_), channel_id=1, source_target_pairs={{0,4},{2,6},{4,0},{6,2},{8,12},{10,14},{12,8},{14,10},{1,5},{3,7},... | collective-permute-start | bytes 393224 | tf_op jit(solution)/shard_map/ppermute | solution.py:757
  23.2 3.5 %collective-permute-start.4 = (f32[3,32,256]{2,1,0:T(8,128)S(1)}, f32[3,32,256]{2,1,0:T(8,128)S(1)}, u32[]{:S(2)}, u32[]{:S(2)}) collective-permute-start(f32[3,32,256]{2,1,0:T(8,128)S(1)} %get-tuple-element.45), channel_id=1, source_target_pairs={{0,2},{2,0},{4,6},{6,4},{8,10},{10,8},{12,14},{14,12},{1,3},{3,1},... | collective-permute-start | bytes 294920 | tf_op jit(solution)/shard_map/ppermute | solution.py:758
  26.7 3.3 %collective-permute-start.6 = (f32[3,32,128]{2,1,0:T(8,128)S(1)}, f32[3,32,128]{2,1,0:T(8,128)S(1)}, u32[]{:S(2)}, u32[]{:S(2)}) collective-permute-start(f32[3,32,128]{2,1,0:T(8,128)S(1)} %get-tuple-element.50), channel_id=1, source_target_pairs={{0,4},{2,6},{4,0},{6,2},{8,12},{10,14},{12,8},{14,10},{1,5},{3,7},... | collective-permute-start | bytes 147464 | tf_op jit(solution)/shard_map/ppermute | solution.py:758
  27.2 7.2 %collective-permute-start.9 = (f32[2,32,256]{2,1,0:T(8,128)S(1)}, f32[2,32,256]{2,1,0:T(8,128)S(1)}, u32[]{:S(2)}, u32[]{:S(2)}) collective-permute-start(f32[2,32,256]{2,1,0:T(8,128)S(1)} %get-tuple-element.56), channel_id=1, source_target_pairs={{0,8},{2,10},{4,12},{6,14},{8,0},{10,2},{12,4},{14,6},{1,9},{3,11}... | collective-permute-start | bytes 196616 | tf_op jit(solution)/shard_map/ppermute | solution.py:757
  30.0 10.9 %collective-permute-start.8 = (f32[3,32,128]{2,1,0:T(8,128)S(1)}, f32[3,32,128]{2,1,0:T(8,128)S(1)}, u32[]{:S(2)}, u32[]{:S(2)}) collective-permute-start(f32[3,32,128]{2,1,0:T(8,128)S(1)} %shard_map.66.refs_0_), channel_id=1, source_target_pairs={{0,8},{2,10},{4,12},{6,14},{8,0},{10,2},{12,4},{14,6},{1,9},{3,11}... | collective-permute-start | bytes 147464 | tf_op jit(solution)/shard_map/ppermute | solution.py:758
  35.6 11.1 %collective-permute-start.11 = (f32[4,8,256]{2,1,0:T(8,128)S(1)}, f32[4,8,256]{2,1,0:T(8,128)S(1)}, u32[]{:S(2)}, u32[]{:S(2)}) collective-permute-start(f32[4,8,256]{2,1,0:T(8,128)S(1)} %get-tuple-element.67), channel_id=1, source_target_pairs={{0,1},{1,0},{2,3},{3,2},{4,5},{5,4},{6,7},{7,6},{8,9},{9,8},{10,11... | collective-permute-start | bytes 98312 | tf_op jit(solution)/shard_map/ppermute | solution.py:800
  41.0 5.0 %collective-permute-start.10 = (f32[3,32,64]{2,1,0:T(8,128)S(1)}, f32[3,32,64]{2,1,0:T(8,128)S(1)}, u32[]{:S(2)}, u32[]{:S(2)}) collective-permute-start(f32[3,32,64]{2,1,0:T(8,128)S(1)} %get-tuple-element.61), channel_id=1, source_target_pairs={{0,16},{16,0},{1,17},{17,1},{2,18},{18,2},{3,19},{19,3},{4,20},{20... | collective-permute-start | bytes 73736 | tf_op jit(solution)/shard_map/ppermute | solution.py:825
  42.1 4.5 %collective-permute-start.12 = (f32[32,128]{1,0:T(8,128)S(1)}, f32[32,128]{1,0:T(8,128)S(1)}, u32[]{:S(2)}, u32[]{:S(2)}) collective-permute-start(f32[32,128]{1,0:T(8,128)S(1)} %get-tuple-element.68), channel_id=1, source_target_pairs={{0,16},{16,0},{1,17},{17,1},{2,18},{18,2},{3,19},{19,3},{4,20},{20... | collective-permute-start | bytes 49160 | tf_op jit(solution)/shard_map/ppermute | solution.py:798
  42.5 4.2 %collective-permute-start.13 = (f32[8,128]{1,0:T(8,128)S(1)}, f32[8,128]{1,0:T(8,128)S(1)}, u32[]{:S(2)}, u32[]{:S(2)}) collective-permute-start(f32[8,128]{1,0:T(8,128)S(1)} %get-tuple-element.69), channel_id=1, source_target_pairs={{0,17},{1,16},{16,1},{17,0},{2,19},{3,18},{18,3},{19,2},{4,21},{5,... | collective-permute-start | bytes 12296 | tf_op jit(solution)/shard_map/ppermute | solution.py:799

commit v6 on v5

--- a/solution.py
+++ b/solution.py
@@ -231,8 +231,13 @@
             )
 
 
-def each_tile(rows, width, body):
+def each_tile(rows, width, body, unroll=False):
     count = width // LANES
+    if unroll:
+        for i in range(rows // SUB):
+            for j in range(count):
+                body(pl.ds(i * SUB, SUB), pl.ds(j * LANES, LANES))
+        return
 
     def step(n, carry):
         row = pl.ds(pl.multiple_of((n // count) * SUB, SUB), SUB)
@@ -253,24 +258,20 @@
     return rising, falling[::-1]
 
 
-def inner_body(info, vox, line, own, other, vals, part, ends, inner, grid, *, width, scale):
-    h, t = (info[0], info[1])
+def place_body(info, vox, line, grid, *, width):
+    h, t, _ = info
     channels, planes, rows, _ = vox.shape
     count = width // LANES
     base, side, source = window_parts(h, width)
     turn = beside_shift(source, h)
-    rays = (own, other)
-
-    def place(k, carry):
+
+    for k in range(planes):
         for c in range(channels):
             tiles = [vox[c, k, :, pl.ds(base + j * LANES, LANES)] for j in range(count)]
             beside = pltpu.roll(vox[c, k, :, pl.ds(side, LANES)], turn, 1)
             for e, xs in enumerate(shifts(tiles, beside, h)):
                 for j, x in enumerate(xs):
                     grid[e, c, k, SUB : SUB + rows, j * LANES : (j + 1) * LANES] = x
-        return carry
-
-    lax.fori_loop(0, planes, place, 0)
     beyond = pl.ds(pl.multiple_of(jnp.where(t == 0, SUB + rows, 0), SUB), SUB)
     for c in range(channels):
         tiles = [line[c, :, pl.ds(base + j * LANES, LANES)] for j in range(count)]
@@ -282,6 +283,12 @@
                         x[k : k + 1], (SUB, LANES)
                     )
 
+
+def inner_body(info, grid, own, other, vals, part, ends, inner, *, scale):
+    t = info[1]
+    _, rows, width = own.shape
+    channels, planes = grid.shape[1:3]
+    rays = (own, other)
     for row0, at, cols, yx, wz in ray_tiles(rays, rows, width, t):
 
         def channel(c, carry, row0=row0, at=at, cols=cols, yx=yx, wz=wz):
@@ -378,7 +385,7 @@
             keep[c, row, col] = jnp.where(kept, a, pltpu.roll(b, turn, 1))
             send[c, row, col] = jnp.where(kept, pltpu.roll(b, LANES - turn, 1), a)
 
-    each_tile(rows, width, shade)
+    each_tile(rows, width, shade, unroll=True)
 
 
 def column_body(info, own, other, vals, rim, ends, cols5, *, scale, slabs):
@@ -528,24 +535,26 @@
         outs[1][c] = jnp.where(tile == 0, high, low)
 
 
-def image_body(info, keep, got, mine_scale, their_scale, mine, sent, *, chunk, half, halved):
-    s = info[2]
+def gather_body(info, edge, line, keep, got, mine_scale, their_scale, mine, out, *, chunk, half, halved):
+    _, t, s = info
+    rows = edge.shape[0]
+    body = line.shape[0] - SUB
     start = lax.rem(s, half) * chunk
     base = 0 if halved else (start // LANES) * LANES
     cols = pl.ds(pl.multiple_of(base, LANES), LANES)
     start = lax.rem(start, LANES)
     there = jnp.where(lax.rem(s, 2) == 1, start - chunk, start + chunk)
+    border = iota((rows, LANES), 0) == jnp.where(t == 0, rows - 1, 0)
+    out[:rows, :] = edge[...] + jnp.where(border, line[body : body + 1, :LANES], 0.0)
     for c in range(keep.shape[0]):
         both = mine_scale[:, cols] * keep[c, :, cols] + their_scale[:, cols] * got[c, :, cols]
         mine[c] = pltpu.roll(both, lax.rem(LANES - start, LANES), 1)[:, :chunk]
-        sent[c] = pltpu.roll(both, lax.rem(LANES - there, LANES), 1)[:, :chunk]
-
-
-def choose_body(info, mine, got, image, *, half):
-    image[0] = jnp.where(info[2] // half == info[0], mine[...], got[...])
-
-
-def merge_body(info, reach_rest, cols5, own, other, columns, line, edge, corner, strips):
+        out[(c + 1) * rows : (c + 2) * rows, :] = pltpu.roll(
+            both, lax.rem(LANES - there, LANES), 1
+        )
+
+
+def merge_body(info, reach_rest, cols5, own, other, columns, line, edge, strips):
     h, t = (info[0], info[1])
     channels, _, planes, rows, width = columns.shape
     last = LANES - 1
@@ -581,7 +590,7 @@
         ]
         plus = jnp.where(lane == 0, 0.0, pltpu.roll(plus, 1, 1))
         minus = jnp.where(lane == width - 1, 0.0, pltpu.roll(minus, width - 1, 1))
-        line[c] = same + plus + minus
+        line[c * planes : (c + 1) * planes, :] = same + plus + minus
 
     side = pl.ds(pl.multiple_of(jnp.where(h == 0, width - LANES, 0), LANES), LANES)
     source = jnp.where(h == 0, last, 0)
@@ -607,7 +616,7 @@
     edge[...] = (
         part[1] + jnp.where(row == 0, 0.0, lower) + jnp.where(row == rows - 1, 0.0, upper)
     )
-    corner[...] = jnp.where(t == 0, lower[:SUB], pltpu.roll(upper[rows - SUB :], 1, 0))
+    line[channels * planes :, :LANES] = jnp.where(t == 0, lower[:SUB], pltpu.roll(upper[rows - SUB :], 1, 0))
 
 
 def scatter_body(_, columns, own, other, grad, weights):
@@ -646,20 +655,25 @@
     lax.fori_loop(0, planes, plane, 0)
 
 
-def finish_body(info, grad_in, line, edge, corner, grad, buffer, sems):
-    h, t = (info[0], info[1])
+def finish_body(info, grad_in, line, cross, mine, grad, image, buffer, picture, sems, *, half):
+    h, t, s = info
     channels, planes, rows, width = buffer.shape
     source = jnp.where(h == 0, LANES - 1, 0)
     side = pl.ds(pl.multiple_of(jnp.where(h == 0, width - LANES, 0), LANES), LANES)
     last = jnp.where(t == 0, rows - 1, 0)
     at_row = iota((rows, width), 0) == last
     at_lane = iota((rows, LANES), 1) == source
-    packed = edge[...] + jnp.where(iota((rows, LANES), 0) == last, corner[:1], 0.0)
-    copies = []
+    packed = cross[:rows, :]
+    here = s // half == h
+    for c in range(channels - 1):
+        picture[0, c] = jnp.where(here, mine[c], cross[(c + 1) * rows : (c + 2) * rows, : picture.shape[3]])
+    copies = [pltpu.make_async_copy(picture, image, sems.at[channels])]
+    copies[0].start()
     for c in range(channels):
         for p in range(planes):
-            buffer[c, p] = grad_in[c, p] + jnp.where(at_row, line[c, p : p + 1, :], 0.0)
-            turn = lax.rem(source - (c * planes + p) + LANES, LANES)
+            at = c * planes + p
+            buffer[c, p] = grad_in[c, p] + jnp.where(at_row, line[at : at + 1, :], 0.0)
+            turn = lax.rem(source - at + LANES, LANES)
             buffer[c, p, :, side] += jnp.where(at_lane, pltpu.roll(packed, turn, 1), 0.0)
         copies.append(pltpu.make_async_copy(buffer.at[c], grad.at[c], sems.at[c]))
         copies[-1].start()
@@ -694,7 +708,10 @@
     own, sent, line = call(
         first_body,
         [ray, ray, shape(channels, planes, total)],
-        (offsets, heading, cotangent, voxels),
+        tuple(
+            pltpu.with_memory_space_constraint(x, pltpu.HBM)
+            for x in (offsets, heading, cotangent, voxels)
+        ),
         specs=[hbm] * 4,
         scratch=[
             pltpu.VMEM(offsets.shape, jnp.int32),
@@ -703,7 +720,7 @@
             pltpu.VMEM((channels, planes, SUB, total), F32),
             pltpu.SemaphoreType.DMA((4,)),
         ],
-        limit=62,
+        limit=8,
         width=width,
         depth=depth,
     )
@@ -720,17 +737,19 @@
         specs=[block(0), block(planes - 1), VMEM],
         width=width,
     )
-    near = [lax.ppermute(x, "slab", p) for x, p in zip(near, (pairs_a, pairs_b))]
+    near = list(near)
+    near[0] = lax.ppermute(near[0], "slab", pairs_a)
+    near[1] = lax.ppermute(near[1], "slab", pairs_b)
 
     two = shape(2, channels, 2, rows, width)
     pair = shape(2, 2, rows, width)
+    placed = call(
+        place_body, shape(3, channels, planes, rows + 2 * SUB, width), (voxels, line), width=width
+    )
     vals, part, ends, inner = call(
         inner_body,
         [shape(2, channels, planes - 2, rows, width), two, two, shape(channels, 2, rows, width)],
-        (voxels, line, own, other),
-        scratch=[grid(planes)],
-        limit=20,
-        width=width,
+        (placed, own, other),
         scale=scale,
     )
     light = shape(colours, rows, width)
@@ -784,20 +803,26 @@
         )
         keep, send = (pieces[0], pieces[-1])
 
-    columns, line, edge, corner = call(
+    columns, line, edge = call(
         merge_body,
         [
             shape(channels, 2, planes, rows, width),
-            shape(channels, planes, width),
+            shape(channels * planes + SUB, width),
             shape(rows, LANES),
-            shape(SUB, LANES),
         ],
         (state, cols5, own, other),
         scratch=[pltpu.VMEM((2, planes, width), F32)],
     )
-    edge = lax.ppermute(edge, "dir", swap)
-    corner = lax.ppermute(corner, ("dir", "tile"), [(i, 3 - i) for i in range(4)])
     line = lax.ppermute(line, "tile", swap)
+    mine, message = call(
+        gather_body,
+        [shape(colours, rows, chunk), shape((colours + 1) * rows, LANES)],
+        (edge, line, keep, got, mine_scale, their_scale),
+        chunk=chunk,
+        half=half,
+        halved=tile_bit is not None,
+    )
+    message = lax.ppermute(message, "dir", swap)
     grad_shape = (channels, planes, rows, width)
     grad = call(
         scatter_body,
@@ -805,25 +830,18 @@
         (columns, own, other),
         scratch=[pltpu.VMEM((2, 9, rows, width), F32)],
     )
-    voxel_grad = call(
+    voxel_grad, image = call(
         finish_body,
-        shape(*grad_shape),
-        (grad, line, edge, corner),
-        scratch=[pltpu.VMEM(grad_shape, F32), pltpu.SemaphoreType.DMA((channels,))],
-        out_specs=hbm,
-    )
-
-    piece = shape(colours, rows, chunk)
-    mine, sent = call(
-        image_body,
-        [piece, piece],
-        (keep, got, mine_scale, their_scale),
-        chunk=chunk,
+        [shape(*grad_shape), shape(1, colours, rows, chunk)],
+        (grad, line, message, mine),
+        scratch=[
+            pltpu.VMEM(grad_shape, F32),
+            pltpu.VMEM((1, colours, rows, chunk), F32),
+            pltpu.SemaphoreType.DMA((channels + 1,)),
+        ],
+        out_specs=[hbm, hbm],
         half=half,
-        halved=tile_bit is not None,
-    )
-    got = lax.ppermute(sent, "dir", swap)
-    image = call(choose_body, shape(1, colours, rows, chunk), (mine, got), half=half)
+    )
     return (image, voxel_grad)
 
 

time: 47.9 us -> 45.4 us (0.948)
  the two profiles are of different devices: /device:TPU:1 before, /device:TPU:0 now
where the time goes in v6:
time: 45.4 us; the launch traced here: 45.3 us
  starting transfers between devices  19.7 us (43%)
  Pallas kernels  13.1 us (29%)
  waiting for transfers between devices  11.7 us (26%)
  between operations  0.76 us (2%)
    pallas_call x15, Pallas kernels, call(): pl.pallas_call(kernel, out_shape=outs, in_specs=specs or [VMEM] * len(arg...  13.1 us
    ppermute x3, starting transfers between devices, per_device(): theirs = lax.ppermute(message, 'slab', pairs)  10 us
    ppermute x3, waiting for transfers between devices, per_device(): theirs = lax.ppermute(message, 'slab', pairs)  5.15 us
    ppermute x3, waiting for transfers between devices, per_device(): got = lax.ppermute(send, 'slab', pairs)  3.67 us
    ppermute x3, starting transfers between devices, per_device(): got = lax.ppermute(send, 'slab', pairs)  3.02 us
    ppermute x1, starting transfers between devices, per_device(): other = lax.ppermute(sent, 'dir', swap)  2.55 us
    ppermute x1, starting transfers between devices, per_device(): near[0] = lax.ppermute(near[0], 'slab', pairs_a)  1.58 us
    ppermute x1, waiting for transfers between devices, per_device(): other = lax.ppermute(sent, 'dir', swap)  1.57 us
  transfers between devices with their start and end apart: 12, of which 7 were waited for; matrix products, arithmetic and copies ran while one was open for 0% of the time, Pallas kernels for 20%

profile of v6, /device:TPU:0, one launch (start us, length us, event | category | flops | bytes accessed | tf_op | source)
XLA Modules:
  0.0 45.3 jit_solution(16481071533841796926)
XLA Ops:
  0.6 1.3 %shard_map.59 = (f32[5,32,256]{2,1,0:T(8,128)S(1)}, f32[5,32,256]{2,1,0:T(8,128)S(1)}, f32[4,8,512]{2,1,0:T(8,128)S(1)}) custom-call(s32[1,32,512]{2,1,0:T(8,128)} %refs_0_.3, s32[1,32,512]{2,1,0:T(8,128)} %refs_1_.2, f32[1,3,32,512]{3,2,1,0:T(8,128)} %refs_2_.1, f32[4,8,32,512]{3,2,1,0:T(8,128)} %refs_0_.5), custom_call_target="tpu_custom_call" | custom-call | flops 10000000 | bytes 2000000 | tf_op jit(solution)/shard_map/pallas_call | solution.py:25
  2.0 0.6 %collective-permute-start.1 = (f32[4,8,512]{2,1,0:T(8,128)S(1)}, f32[4,8,512]{2,1,0:T(8,128)S(1)}, u32[]{:S(2)}, u32[]{:S(2)}) collective-permute-start(f32[4,8,512]{2,1,0:T(8,128)S(1)} %get-tuple-element.39), channel_id=1, source_target_pairs={{0,1},{1,0},{2,3},{3,2},{4,5},{5,4},{6,7},{7,6},{8,9},{9,8},{10,11... | collective-permute-start | bytes 196616 | tf_op jit(solution)/shard_map/ppermute | solution.py:727
  2.5 2.6 %collective-permute-start = (f32[5,32,256]{2,1,0:T(8,128)S(1)}, f32[5,32,256]{2,1,0:T(8,128)S(1)}, u32[]{:S(2)}, u32[]{:S(2)}) collective-permute-start(f32[5,32,256]{2,1,0:T(8,128)S(1)} %get-tuple-element.38), channel_id=1, source_target_pairs={{0,16},{16,0},{1,17},{17,1},{2,18},{18,2},{3,19},{19,3},{4,20},{20... | collective-permute-start | bytes 491528 | tf_op jit(solution)/shard_map/ppermute | solution.py:728
  5.1 0.2 shard_map.60
  5.3 1.6 %collective-permute-start.2 = (f32[296,128]{1,0:T(8,128)S(1)}, f32[296,128]{1,0:T(8,128)S(1)}, u32[]{:S(2)}, u32[]{:S(2)}) collective-permute-start(f32[296,128]{1,0:T(8,128)S(1)} %get-tuple-element.40), channel_id=1, source_target_pairs={{0,2},{2,0},{4,6},{6,4},{8,10},{10,8},{12,14},{14,12},{1,3},{3,1},... | collective-permute-start | bytes 454664 | tf_op jit(solution)/shard_map/ppermute | solution.py:741
  6.8 0.7 %collective-permute-start.3 = (f32[296,128]{1,0:T(8,128)S(1)}, f32[296,128]{1,0:T(8,128)S(1)}, u32[]{:S(2)}, u32[]{:S(2)}) collective-permute-start(f32[296,128]{1,0:T(8,128)S(1)} %get-tuple-element.41), channel_id=1, source_target_pairs={{2,4},{6,8},{10,12},{4,2},{8,6},{12,10},{3,5},{7,9},{11,13},{5,3},... | collective-permute-start | bytes 454664 | tf_op jit(solution)/shard_map/ppermute | solution.py:742
  7.5 0.8 %shard_map.61.refs_0_ = f32[3,4,8,48,256]{4,3,2,1,0:T(8,128)S(1)} custom-call(f32[4,8,32,512]{3,2,1,0:T(8,128)S(1)} %copy-done, f32[4,8,512]{2,1,0:T(8,128)S(1)} %collective-permute-done.1.refs_2_.refs_1_), custom_call_target="tpu_custom_call" | custom-call | flops 10000000 | bytes 2000000 | tf_op jit(solution)/shard_map/pallas_call | solution.py:25
  8.3 1.6 %collective-permute-done.refs_2_.refs_3_.refs_1_ = f32[5,32,256]{2,1,0:T(8,128)S(1)} collective-permute-done((f32[5,32,256]{2,1,0:T(8,128)S(1)}, f32[5,32,256]{2,1,0:T(8,128)S(1)}, u32[]{:S(2)}, u32[]{:S(2)}) %collective-permute-start) | collective-permute-done | bytes 163872 | tf_op jit(solution)/shard_map/ppermute | solution.py:728
  9.9 2.9 %shard_map.62 = (f32[2,4,6,32,256]{4,3,2,1,0:T(8,128)S(1)}, f32[2,4,2,32,256]{4,3,2,1,0:T(8,128)S(1)}, f32[2,4,2,32,256]{4,3,2,1,0:T(8,128)S(1)}, f32[4,2,32,256]{3,2,1,0:T(8,128)S(1)}) custom-call(f32[3,4,8,48,256]{4,3,2,1,0:T(8,128)S(1)} %shard_map.61.refs_0_, f32[5,32,256]{2,1,0:T(8,128)S(1)} %get-tuple-element.37.refs_1_.refs_2_.refs_0_, ...), custom_call_target="tpu_custom_call" | custom-call | flops 10000000 | bytes 2000000 | tf_op jit(solution)/shard_map/pallas_call | solution.py:25
  12.8 1.2 %shard_map.63 = (f32[2,2,32,256]{3,2,1,0:T(8,128)S(1)}, f32[2,4,2,32,256]{4,3,2,1,0:T(8,128)S(1)}, f32[2,4,2,32,256]{4,3,2,1,0:T(8,128)S(1)}, f32[3,32,256]{2,1,0:T(8,128)S(1)}, f32[3,32,256]{2,1,0:T(8,128)S(1)}) custom-call(f32[296,128]{1,0:T(8,128)S(1)} %collective-permute-done.2.refs_0_, f32[296,128]{1,0:T(8,128)S(1)} %collective-permute-done.3.refs_1_, ...), custom_call_target="tpu_custom_call" | custom-call | flops 10000000 | bytes 2000000 | tf_op jit(solution)/shard_map/pallas_call | solution.py:25
  14.0 3.4 %collective-permute-start.4 = (f32[2,2,32,256]{3,2,1,0:T(8,128)S(1)}, f32[2,2,32,256]{3,2,1,0:T(8,128)S(1)}, u32[]{:S(2)}, u32[]{:S(2)}) collective-permute-start(f32[2,2,32,256]{3,2,1,0:T(8,128)S(1)} %get-tuple-element.45.refs_2_), channel_id=1, source_target_pairs={{0,2},{2,0},{4,6},{6,4},{8,10},{10,8},{12,14},{14,12},{1,3},{3,1},... | collective-permute-start | bytes 393224 | tf_op jit(solution)/shard_map/ppermute | solution.py:776
  17.4 2.9 %collective-permute-done.4.refs_3_ = f32[2,2,32,256]{3,2,1,0:T(8,128)S(1)} collective-permute-done((f32[2,2,32,256]{3,2,1,0:T(8,128)S(1)}, f32[2,2,32,256]{3,2,1,0:T(8,128)S(1)}, u32[]{:S(2)}, u32[]{:S(2)}) %collective-permute-start.4) | collective-permute-done | bytes 131104 | tf_op jit(solution)/shard_map/ppermute | solution.py:776
  20.3 0.1 shard_map.64
  20.4 2.9 %collective-permute-start.5 = (f32[2,2,32,256]{3,2,1,0:T(8,128)S(1)}, f32[2,2,32,256]{3,2,1,0:T(8,128)S(1)}, u32[]{:S(2)}, u32[]{:S(2)}) collective-permute-start(f32[2,2,32,256]{3,2,1,0:T(8,128)S(1)} %get-tuple-element.46.refs_2_), channel_id=1, source_target_pairs={{0,4},{2,6},{4,0},{6,2},{8,12},{10,14},{12,8},{14,10},{1,5},{3,7},... | collective-permute-start | bytes 393224 | tf_op jit(solution)/shard_map/ppermute | solution.py:776
  23.3 0.8 %collective-permute-start.8 = (f32[3,32,256]{2,1,0:T(8,128)S(1)}, f32[3,32,256]{2,1,0:T(8,128)S(1)}, u32[]{:S(2)}, u32[]{:S(2)}) collective-permute-start(f32[3,32,256]{2,1,0:T(8,128)S(1)} %get-tuple-element.59), channel_id=1, source_target_pairs={{0,2},{2,0},{4,6},{6,4},{8,10},{10,8},{12,14},{14,12},{1,3},{3,1},... | collective-permute-start | bytes 294920 | tf_op jit(solution)/shard_map/ppermute | solution.py:777
  24.1 2.2 %collective-permute-done.5.refs_3_ = f32[2,2,32,256]{3,2,1,0:T(8,128)S(1)} collective-permute-done((f32[2,2,32,256]{3,2,1,0:T(8,128)S(1)}, f32[2,2,32,256]{3,2,1,0:T(8,128)S(1)}, u32[]{:S(2)}, u32[]{:S(2)}) %collective-permute-start.5) | collective-permute-done | bytes 131104 | tf_op jit(solution)/shard_map/ppermute | solution.py:776
  26.3 0.1 shard_map.65
  26.4 3.7 %collective-permute-start.6 = (f32[2,32,256]{2,1,0:T(8,128)S(1)}, f32[2,32,256]{2,1,0:T(8,128)S(1)}, u32[]{:S(2)}, u32[]{:S(2)}) collective-permute-start(f32[2,32,256]{2,1,0:T(8,128)S(1)} %get-tuple-element.49), channel_id=1, source_target_pairs={{0,8},{2,10},{4,12},{6,14},{8,0},{10,2},{12,4},{14,6},{1,9},{3,11}... | collective-permute-start | bytes 196616 | tf_op jit(solution)/shard_map/ppermute | solution.py:776
  30.1 1.4 %collective-permute-start.9 = (f32[3,32,128]{2,1,0:T(8,128)S(1)}, f32[3,32,128]{2,1,0:T(8,128)S(1)}, u32[]{:S(2)}, u32[]{:S(2)}) collective-permute-start(f32[3,32,128]{2,1,0:T(8,128)S(1)} %get-tuple-element.63), channel_id=1, source_target_pairs={{0,4},{2,6},{4,0},{6,2},{8,12},{10,14},{12,8},{14,10},{1,5},{3,7},... | collective-permute-start | bytes 147464 | tf_op jit(solution)/shard_map/ppermute | solution.py:777
  31.5 2.8 %collective-permute-done.9.refs_1_ = f32[3,32,128]{2,1,0:T(8,128)S(1)} collective-permute-done((f32[3,32,128]{2,1,0:T(8,128)S(1)}, f32[3,32,128]{2,1,0:T(8,128)S(1)}, u32[]{:S(2)}, u32[]{:S(2)}) %collective-permute-start.9) | collective-permute-done | bytes 49184 | tf_op jit(solution)/shard_map/ppermute | solution.py:777
  34.3 0.9 %collective-permute-start.10 = (f32[3,32,128]{2,1,0:T(8,128)S(1)}, f32[3,32,128]{2,1,0:T(8,128)S(1)}, u32[]{:S(2)}, u32[]{:S(2)}) collective-permute-start(f32[3,32,128]{2,1,0:T(8,128)S(1)} %shard_map.71.refs_2_), channel_id=1, source_target_pairs={{0,8},{2,10},{4,12},{6,14},{8,0},{10,2},{12,4},{14,6},{1,9},{3,11}... | collective-permute-start | bytes 147464 | tf_op jit(solution)/shard_map/ppermute | solution.py:777
  35.2 2.0 %shard_map.67.refs_1_ = f32[5,2,8,32,256]{4,3,2,1,0:T(8,128)S(1)} custom-call(f32[5,32,256]{2,1,0:T(8,128)S(1)} %get-tuple-element.37.refs_1_.refs_2_.refs_0_, f32[5,32,256]{2,1,0:T(8,128)S(1)} %collective-permute-done.refs_2_.refs_3_.refs_1_, f32[2,4,6,32,256]{4,3,2,1,0:T(8,128)S(1)} %get-tuple-element.52.refs_2_, ...), custom_call_target="tpu_custom_call" | custom-call | flops 10000000 | bytes 2000000 | tf_op jit(solution)/shard_map/pallas_call | solution.py:25
  37.2 0.1 shard_map.66
  37.3 1.1 %shard_map.68 = (f32[4,2,8,32,256]{4,3,2,1,0:T(8,128)S(1)}, f32[40,256]{1,0:T(8,128)S(1)}, f32[32,128]{1,0:T(8,128)S(1)}) custom-call(f32[2,2,32,256]{3,2,1,0:T(8,128)S(1)} %get-tuple-element.51.refs_0_, f32[5,2,8,32,256]{4,3,2,1,0:T(8,128)S(1)} %shard_map.67.refs_1_, f32[5,32,256]{2,1,0:T(8,128)S(1)} %get-tuple-element.37.refs_1_.refs_2_.refs_0_, ...), custom_call_target="tpu_custom_call" | custom-call | flops 10000000 | bytes 2000000 | tf_op jit(solution)/shard_map/pallas_call | solution.py:25
  38.5 0.1 collective-permute-start.7
  38.5 0.9 %collective-permute-done.10.refs_3_ = f32[3,32,128]{2,1,0:T(8,128)S(1)} collective-permute-done((f32[3,32,128]{2,1,0:T(8,128)S(1)}, f32[3,32,128]{2,1,0:T(8,128)S(1)}, u32[]{:S(2)}, u32[]{:S(2)}) %collective-permute-start.10) | collective-permute-done | bytes 49184 | tf_op jit(solution)/shard_map/ppermute | solution.py:777
  39.4 0.3 collective-permute-done.7.refs_1_
  39.7 0.1 shard_map.72
  39.8 1.2 %collective-permute-start.11 = (f32[128,128]{1,0:T(8,128)S(1)}, f32[128,128]{1,0:T(8,128)S(1)}, u32[]{:S(2)}, u32[]{:S(2)}) collective-permute-start(f32[128,128]{1,0:T(8,128)S(1)} %get-tuple-element.68), channel_id=1, source_target_pairs={{0,16},{16,0},{1,17},{17,1},{2,18},{18,2},{3,19},{19,3},{4,20},{20... | collective-permute-start | bytes 196616 | tf_op jit(solution)/shard_map/ppermute | solution.py:825
  41.1 2.1 %shard_map.69.refs_0_ = f32[4,8,32,256]{3,2,1,0:T(8,128)S(1)} custom-call(f32[4,2,8,32,256]{4,3,2,1,0:T(8,128)S(1)} %get-tuple-element.55.refs_0_, f32[5,32,256]{2,1,0:T(8,128)S(1)} %get-tuple-element.37.refs_1_.refs_2_.refs_0_, f32[5,32,256]{2,1,0:T(8,128)S(1)} %collective-permute-done.refs_2_.refs_3_.refs_1_), custom_call_target="tpu_custom_call" | custom-call | flops 10000000 | bytes 2000000 | tf_op jit(solution)/shard_map/pallas_call | solution.py:25
  43.2 1.0 %collective-permute-done.11.refs_2_ = f32[128,128]{1,0:T(8,128)S(1)} collective-permute-done((f32[128,128]{1,0:T(8,128)S(1)}, f32[128,128]{1,0:T(8,128)S(1)}, u32[]{:S(2)}, u32[]{:S(2)}) %collective-permute-start.11) | collective-permute-done | bytes 65568 | tf_op jit(solution)/shard_map/ppermute | solution.py:825
  44.2 1.1 %shard_map.73 = (f32[4,8,32,256]{3,2,1,0:T(8,128)}, f32[1,3,32,64]{3,2,1,0:T(8,128)}) custom-call(f32[4,8,32,256]{3,2,1,0:T(8,128)S(1)} %shard_map.69.refs_0_, f32[40,256]{1,0:T(8,128)S(1)} %collective-permute-done.7.refs_1_, f32[128,128]{1,0:T(8,128)S(1)} %collective-permute-done.11.refs_2_, f32[3,32,64]{2,1,0:T(8,128)S(1)} %get-tuple-element.69.refs_3_), custom_call_target="tpu_custom_call" | custom-call | flops 10000000 | bytes 2000000 | tf_op jit(solution)/shard_map/pallas_call | solution.py:25
  (9 shorter events, 0.1 us)
Async XLA Ops:
  0.6 4.5 %copy-start = (f32[4,8,32,512]{3,2,1,0:T(8,128)S(1)}, f32[4,8,32,512]{3,2,1,0:T(8,128)}, u32[]{:S(2)}) copy-start(f32[4,8,32,512]{3,2,1,0:T(8,128)} %refs_0_.5) | copy-start | bytes 6291460
  2.0 3.1 %collective-permute-start.1 = (f32[4,8,512]{2,1,0:T(8,128)S(1)}, f32[4,8,512]{2,1,0:T(8,128)S(1)}, u32[]{:S(2)}, u32[]{:S(2)}) collective-permute-start(f32[4,8,512]{2,1,0:T(8,128)S(1)} %get-tuple-element.39), channel_id=1, source_target_pairs={{0,1},{1,0},{2,3},{3,2},{4,5},{5,4},{6,7},{7,6},{8,9},{9,8},{10,11... | collective-permute-start | bytes 196616 | tf_op jit(solution)/shard_map/ppermute | solution.py:727
  2.5 7.3 %collective-permute-start = (f32[5,32,256]{2,1,0:T(8,128)S(1)}, f32[5,32,256]{2,1,0:T(8,128)S(1)}, u32[]{:S(2)}, u32[]{:S(2)}) collective-permute-start(f32[5,32,256]{2,1,0:T(8,128)S(1)} %get-tuple-element.38), channel_id=1, source_target_pairs={{0,16},{16,0},{1,17},{17,1},{2,18},{18,2},{3,19},{19,3},{4,20},{20... | collective-permute-start | bytes 491528 | tf_op jit(solution)/shard_map/ppermute | solution.py:728
  5.3 7.5 %collective-permute-start.2 = (f32[296,128]{1,0:T(8,128)S(1)}, f32[296,128]{1,0:T(8,128)S(1)}, u32[]{:S(2)}, u32[]{:S(2)}) collective-permute-start(f32[296,128]{1,0:T(8,128)S(1)} %get-tuple-element.40), channel_id=1, source_target_pairs={{0,2},{2,0},{4,6},{6,4},{8,10},{10,8},{12,14},{14,12},{1,3},{3,1},... | collective-permute-start | bytes 454664 | tf_op jit(solution)/shard_map/ppermute | solution.py:741
  6.8 5.9 %collective-permute-start.3 = (f32[296,128]{1,0:T(8,128)S(1)}, f32[296,128]{1,0:T(8,128)S(1)}, u32[]{:S(2)}, u32[]{:S(2)}) collective-permute-start(f32[296,128]{1,0:T(8,128)S(1)} %get-tuple-element.41), channel_id=1, source_target_pairs={{2,4},{6,8},{10,12},{4,2},{8,6},{12,10},{3,5},{7,9},{11,13},{5,3},... | collective-permute-start | bytes 454664 | tf_op jit(solution)/shard_map/ppermute | solution.py:742
  14.0 6.3 %collective-permute-start.4 = (f32[2,2,32,256]{3,2,1,0:T(8,128)S(1)}, f32[2,2,32,256]{3,2,1,0:T(8,128)S(1)}, u32[]{:S(2)}, u32[]{:S(2)}) collective-permute-start(f32[2,2,32,256]{3,2,1,0:T(8,128)S(1)} %get-tuple-element.45.refs_2_), channel_id=1, source_target_pairs={{0,2},{2,0},{4,6},{6,4},{8,10},{10,8},{12,14},{14,12},{1,3},{3,1},... | collective-permute-start | bytes 393224 | tf_op jit(solution)/shard_map/ppermute | solution.py:776
  20.4 5.9 %collective-permute-start.5 = (f32[2,2,32,256]{3,2,1,0:T(8,128)S(1)}, f32[2,2,32,256]{3,2,1,0:T(8,128)S(1)}, u32[]{:S(2)}, u32[]{:S(2)}) collective-permute-start(f32[2,2,32,256]{3,2,1,0:T(8,128)S(1)} %get-tuple-element.46.refs_2_), channel_id=1, source_target_pairs={{0,4},{2,6},{4,0},{6,2},{8,12},{10,14},{12,8},{14,10},{1,5},{3,7},... | collective-permute-start | bytes 393224 | tf_op jit(solution)/shard_map/ppermute | solution.py:776
  23.3 6.8 %collective-permute-start.8 = (f32[3,32,256]{2,1,0:T(8,128)S(1)}, f32[3,32,256]{2,1,0:T(8,128)S(1)}, u32[]{:S(2)}, u32[]{:S(2)}) collective-permute-start(f32[3,32,256]{2,1,0:T(8,128)S(1)} %get-tuple-element.59), channel_id=1, source_target_pairs={{0,2},{2,0},{4,6},{6,4},{8,10},{10,8},{12,14},{14,12},{1,3},{3,1},... | collective-permute-start | bytes 294920 | tf_op jit(solution)/shard_map/ppermute | solution.py:777
  26.4 10.8 %collective-permute-start.6 = (f32[2,32,256]{2,1,0:T(8,128)S(1)}, f32[2,32,256]{2,1,0:T(8,128)S(1)}, u32[]{:S(2)}, u32[]{:S(2)}) collective-permute-start(f32[2,32,256]{2,1,0:T(8,128)S(1)} %get-tuple-element.49), channel_id=1, source_target_pairs={{0,8},{2,10},{4,12},{6,14},{8,0},{10,2},{12,4},{14,6},{1,9},{3,11}... | collective-permute-start | bytes 196616 | tf_op jit(solution)/shard_map/ppermute | solution.py:776
  30.1 4.2 %collective-permute-start.9 = (f32[3,32,128]{2,1,0:T(8,128)S(1)}, f32[3,32,128]{2,1,0:T(8,128)S(1)}, u32[]{:S(2)}, u32[]{:S(2)}) collective-permute-start(f32[3,32,128]{2,1,0:T(8,128)S(1)} %get-tuple-element.63), channel_id=1, source_target_pairs={{0,4},{2,6},{4,0},{6,2},{8,12},{10,14},{12,8},{14,10},{1,5},{3,7},... | collective-permute-start | bytes 147464 | tf_op jit(solution)/shard_map/ppermute | solution.py:777
  34.3 5.1 %collective-permute-start.10 = (f32[3,32,128]{2,1,0:T(8,128)S(1)}, f32[3,32,128]{2,1,0:T(8,128)S(1)}, u32[]{:S(2)}, u32[]{:S(2)}) collective-permute-start(f32[3,32,128]{2,1,0:T(8,128)S(1)} %shard_map.71.refs_2_), channel_id=1, source_target_pairs={{0,8},{2,10},{4,12},{6,14},{8,0},{10,2},{12,4},{14,6},{1,9},{3,11}... | collective-permute-start | bytes 147464 | tf_op jit(solution)/shard_map/ppermute | solution.py:777
  38.5 1.3 %collective-permute-start.7 = (f32[40,256]{1,0:T(8,128)S(1)}, f32[40,256]{1,0:T(8,128)S(1)}, u32[]{:S(2)}, u32[]{:S(2)}) collective-permute-start(f32[40,256]{1,0:T(8,128)S(1)} %get-tuple-element.56), channel_id=1, source_target_pairs={{0,1},{1,0},{2,3},{3,2},{4,5},{5,4},{6,7},{7,6},{8,9},{9,8},{10,11... | collective-permute-start | bytes 122888 | tf_op jit(solution)/shard_map/ppermute | solution.py:816
  39.8 4.3 %collective-permute-start.11 = (f32[128,128]{1,0:T(8,128)S(1)}, f32[128,128]{1,0:T(8,128)S(1)}, u32[]{:S(2)}, u32[]{:S(2)}) collective-permute-start(f32[128,128]{1,0:T(8,128)S(1)} %get-tuple-element.68), channel_id=1, source_target_pairs={{0,16},{16,0},{1,17},{17,1},{2,18},{18,2},{3,19},{19,3},{4,20},{20... | collective-permute-start | bytes 196616 | tf_op jit(solution)/shard_map/ppermute | solution.py:825

commit v7 on v6

--- a/solution.py
+++ b/solution.py
@@ -124,7 +124,7 @@
 def message_rows(channels, rows, count):
     body = channels * count * rows
     lines = -(-channels * count // SUB) * SUB
-    return body, body + lines, body + lines + rows
+    return body, body + lines, body + lines + SUB
 
 
 def pack_body(info, first, last, line, out_a, out_b, *, width):
@@ -151,7 +151,7 @@
             corner = jnp.broadcast_to(line[c, k : k + 1, cols], (SUB, LANES))
             corner = pltpu.roll(corner, turn, 1)[:1]
             edge = jnp.where(lane == channels + c, corner, edge)
-        out[at_edge:, :] = edge
+        out[at_edge:, :rows] = jnp.transpose(edge)[:SUB]
 
     @pl.when(s % 2 == 0)
     def _():
@@ -164,16 +164,22 @@
         fill(last, planes - 1, out_b)
 
 
-def spread_message(msg, grid, plane, info, channels, rows, count):
+def spread_message(msg, grid, plane, info, channels, rows, count, live):
     h, t = (info[0], info[1])
     at_line, at_edge, _ = message_rows(channels, rows, count)
-    edge = msg[at_edge:, :]
+    edge = jnp.transpose(
+        jnp.concatenate([msg[at_edge:, :] * live, jnp.zeros((LANES - SUB, LANES), F32)], axis=0)
+    )[:rows]
     beyond = pl.ds(pl.multiple_of(jnp.where(t == 0, SUB + rows, 0), SUB), SUB)
     for c in range(channels):
         first = c * count
-        tiles = [msg[(first + j) * rows : (first + j + 1) * rows, :] for j in range(count)]
+        tiles = [
+            msg[(first + j) * rows : (first + j + 1) * rows, :] * live for j in range(count)
+        ]
         lines = [
-            jnp.broadcast_to(msg[at_line + first + j : at_line + first + j + 1, :], (SUB, LANES))
+            jnp.broadcast_to(
+                msg[at_line + first + j : at_line + first + j + 1, :] * live, (SUB, LANES)
+            )
             for j in range(count)
         ]
         side = pltpu.roll(edge, beside_shift(c, h), 1)
@@ -339,14 +345,15 @@
     return bit == mine, jnp.where(mine == 1, LANES - chunk, chunk)
 
 
-def rim_body(info, near_a, near_b, own, other, part, ends, inner, pay, rim, ends_out, keep, send, grid, *, scale, chunk):
+def rim_body(info, near_a, near_b, own, other, part, ends, inner, pay, rim, ends_out, keep, send, grid, *, scale, chunk, slabs):
     t, s = (info[1], info[2])
     _, channels, _, rows, width = part.shape
     count = width // LANES
     even = s % 2 == 0
     rays = (own, other)
-    spread_message(near_a, grid, jnp.where(even, 1, 0), info, channels, rows, count)
-    spread_message(near_b, grid, jnp.where(even, 0, 1), info, channels, rows, count)
+    inside = jnp.where((s == 0) | (s == slabs - 1), 0.0, 1.0)
+    spread_message(near_a, grid, jnp.where(even, 1, 0), info, channels, rows, count, 1.0)
+    spread_message(near_b, grid, jnp.where(even, 0, 1), info, channels, rows, count, inside)
     for row0, at, cols, yx, wz in ray_tiles(rays, rows, width, t):
 
         def channel(c, carry, row0=row0, at=at, cols=cols, yx=yx, wz=wz):
@@ -554,73 +561,89 @@
         )
 
 
-def merge_body(info, reach_rest, cols5, own, other, columns, line, edge, strips):
-    h, t = (info[0], info[1])
-    channels, _, planes, rows, width = columns.shape
+def strips_body(info, cols5, own, other, rows5, packs, down, across):
+    h, t, _ = info
+    fields, _, planes, rows, width = cols5.shape
     last = LANES - 1
-    rays = (own, other)
-
-    def ray(row, col):
-        for q in range(2):
-            near, far = (reach_rest[0, q, row, col], reach_rest[1, q, row, col])
-            for p in range(planes):
-                columns[0, q, p, row, col] = (
-                    near * cols5[0, q, p, row, col] - far * cols5[1, q, p, row, col]
-                )
-                for c in range(1, channels):
-                    columns[c, q, p, row, col] = near * cols5[c + 1, q, p, row, col]
-
-    each_tile(rows, width, ray)
-
-    down = []
-    for r in rays:
+    side = pl.ds(pl.multiple_of(jnp.where(h == 0, width - LANES, 0), LANES), LANES)
+    source = jnp.where(h == 0, last, 0)
+    lane = iota((rows, LANES), 1)
+    for q, r in enumerate((own, other)):
         code = jnp.where(t == 0, r[0, rows - 1 : rows, :], r[0, :1, :])
         _, wy, wx = [three(x) for x in split_code(jnp.broadcast_to(code, (planes, width)))]
         y = jnp.where(t == 0, wy[2], wy[0])
-        down.append([y * x for x in wx])
+        for e in range(3):
+            down[q, e] = y * wx[e]
+        code = pltpu.roll(r[0, :, side], lax.rem(LANES - source, LANES), 1)
+        _, wy, wx = [three(x) for x in split_code(jnp.broadcast_to(code[:, :1], (rows, LANES)))]
+        x = jnp.where(h == 0, wx[2], wx[0])
+        for b in range(3):
+            across[q, b] = wy[b] * x
+        both = [jnp.zeros((rows, LANES), F32) for _ in range(2)]
+        for n in range(fields):
+            for p in range(planes):
+                rows5[q, n, p : p + 1, :] = jnp.where(
+                    t == 0, cols5[n, q, p, rows - 1 : rows, :], cols5[n, q, p, :1, :]
+                )
+                at = p if n < 2 else (n - 1) * planes + p
+                turn = lax.rem(at - source + LANES, LANES)
+                k = 1 if n == 1 else 0
+                both[k] = jnp.where(
+                    lane == at, pltpu.roll(cols5[n, q, p, :, side], turn, 1), both[k]
+                )
+        for k in range(2):
+            packs[q, k] = both[k]
+
+
+def border_body(info, reach_rest, rows5, packs, down, across, line, edge):
+    h, t, _ = info
+    _, fields, planes, width = rows5.shape
+    rows = edge.shape[0]
+    last = LANES - 1
     lane = iota((planes, width), 1)
-    for c in range(channels):
-        for q in range(2):
-            for p in range(planes):
-                strips[q, p : p + 1, :] = jnp.where(
-                    t == 0, columns[c, q, p, rows - 1 : rows, :], columns[c, q, p, :1, :]
-                )
+    row = iota((rows, LANES), 0)
+
+    def at_row(n, q):
+        x = jnp.where(t == 0, reach_rest[n, q, rows - 1 : rows, :], reach_rest[n, q, :1, :])
+        return jnp.broadcast_to(x, (planes, width))
+
+    near = [at_row(0, q) for q in range(2)]
+    far = [at_row(1, q) for q in range(2)]
+    for c in range(fields - 1):
+        strip = [near[q] * rows5[q, c + 1 if c else 0] for q in range(2)]
+        if c == 0:
+            strip = [strip[q] - far[q] * rows5[q, 1] for q in range(2)]
         minus, same, plus = [
-            down[0][e] * strips[0] + down[1][e] * strips[1] for e in range(3)
+            down[0, e] * strip[0] + down[1, e] * strip[1] for e in range(3)
         ]
         plus = jnp.where(lane == 0, 0.0, pltpu.roll(plus, 1, 1))
         minus = jnp.where(lane == width - 1, 0.0, pltpu.roll(minus, width - 1, 1))
         line[c * planes : (c + 1) * planes, :] = same + plus + minus
 
     side = pl.ds(pl.multiple_of(jnp.where(h == 0, width - LANES, 0), LANES), LANES)
-    source = jnp.where(h == 0, last, 0)
-    lane = iota((rows, LANES), 1)
-    row = iota((rows, LANES), 0)
-    packed, across = ([], [])
-    for q, r in enumerate(rays):
-        code = pltpu.roll(r[0, :, side], lax.rem(LANES - source, LANES), 1)
-        code = jnp.broadcast_to(code[:, :1], (rows, LANES))
-        _, wy, wx = [three(x) for x in split_code(code)]
-        x = jnp.where(h == 0, wx[2], wx[0])
-        across.append([y * x for y in wy])
-        both = jnp.zeros((rows, LANES), F32)
-        for c in range(channels):
-            for p in range(planes):
-                at = c * planes + p
-                turn = lax.rem(at - source + LANES, LANES)
-                both = jnp.where(lane == at, pltpu.roll(columns[c, q, p, :, side], turn, 1), both)
-        packed.append(both)
-    part = [across[0][b] * packed[0] + across[1][b] * packed[1] for b in range(3)]
+    turn = lax.rem(LANES - jnp.where(h == 0, last, 0), LANES)
+
+    def at_column(n, q):
+        x = pltpu.roll(reach_rest[n, q, :, side], turn, 1)
+        return jnp.broadcast_to(x[:, :1], (rows, LANES))
+
+    packed = [
+        at_column(0, q) * packs[q, 0] - at_column(1, q) * packs[q, 1] for q in range(2)
+    ]
+    part = [across[0, b] * packed[0] + across[1, b] * packed[1] for b in range(3)]
     lower = pltpu.roll(part[2], 1, 0)
     upper = pltpu.roll(part[0], rows - 1, 0)
     edge[...] = (
         part[1] + jnp.where(row == 0, 0.0, lower) + jnp.where(row == rows - 1, 0.0, upper)
     )
-    line[channels * planes :, :LANES] = jnp.where(t == 0, lower[:SUB], pltpu.roll(upper[rows - SUB :], 1, 0))
-
-
-def scatter_body(_, columns, own, other, grad, weights):
-    channels, _, planes, rows, width = columns.shape
+    line[(fields - 1) * planes :, :LANES] = jnp.where(
+        t == 0, lower[:SUB], pltpu.roll(upper[rows - SUB :], 1, 0)
+    )
+
+
+def scatter_body(_, reach_rest, cols5, own, other, grad, weights):
+    fields, _, planes, rows, width = cols5.shape
+    channels = fields - 1
     lane = iota((rows, width), 1)
     row = iota((rows, width), 0)
     for q, r in enumerate((own, other)):
@@ -631,7 +654,9 @@
 
     def plane(p, carry):
         for c in range(channels):
-            col = [columns[c, q, p] for q in range(2)]
+            col = [reach_rest[0, q] * cols5[c + 1 if c else 0, q, p] for q in range(2)]
+            if c == 0:
+                col = [col[q] - reach_rest[1, q] * cols5[1, q, p] for q in range(2)]
             summed = []
             for e in range(3):
                 part = [
@@ -686,6 +711,8 @@
     dirs, slabs, cores = (lax.axis_size(a) for a in ("dir", "slab", "tile"))
     if dirs != 2 or cores != 2 or slabs & (slabs - 1) or 2 * total > slabs * LANES:
         raise ValueError("mesh")
+    if 2 * channels > SUB:
+        raise ValueError("channels")
     width = total // dirs
     depth = planes * slabs
     scale = 2.0 / depth
@@ -701,7 +728,11 @@
 
     pairs_a = [(i, i ^ 1) for i in range(slabs)]
     pairs_b = [(i, i + 1) for i in range(1, slabs - 1, 2)]
+    pairs_b = [(a * cores + i, b * cores + i) for a, b in pairs_b for i in range(cores)]
     pairs_b = pairs_b + [(b, a) for a, b in pairs_b]
+    pairs_b = pairs_b + [
+        (a * cores + i, a * cores + 1 - i) for a in (0, slabs - 1) for i in range(cores)
+    ]
 
     hbm = pl.BlockSpec(memory_space=pltpu.HBM)
     ray = shape(channels + 1, rows, width)
@@ -739,7 +770,7 @@
     )
     near = list(near)
     near[0] = lax.ppermute(near[0], "slab", pairs_a)
-    near[1] = lax.ppermute(near[1], "slab", pairs_b)
+    near[1] = lax.ppermute(near[1], ("slab", "tile"), pairs_b)
 
     two = shape(2, channels, 2, rows, width)
     pair = shape(2, 2, rows, width)
@@ -760,6 +791,7 @@
         scratch=[grid(2)],
         scale=scale,
         chunk=chunk,
+        slabs=slabs,
     )
     cols5 = call(
         column_body,
@@ -767,6 +799,17 @@
         (own, other, vals, rim, ends),
         scale=scale,
         slabs=slabs,
+    )
+
+    strips = call(
+        strips_body,
+        [
+            shape(2, channels + 1, planes, width),
+            shape(2, 2, rows, LANES),
+            shape(2, 3, planes, width),
+            shape(2, 3, rows, LANES),
+        ],
+        (cols5, own, other),
     )
 
     message, state = (pay, ())
@@ -803,15 +846,8 @@
         )
         keep, send = (pieces[0], pieces[-1])
 
-    columns, line, edge = call(
-        merge_body,
-        [
-            shape(channels, 2, planes, rows, width),
-            shape(channels * planes + SUB, width),
-            shape(rows, LANES),
-        ],
-        (state, cols5, own, other),
-        scratch=[pltpu.VMEM((2, planes, width), F32)],
+    line, edge = call(
+        border_body, [shape(channels * planes + SUB, width), shape(rows, LANES)], (state, *strips)
     )
     line = lax.ppermute(line, "tile", swap)
     mine, message = call(
@@ -827,7 +863,7 @@
     grad = call(
         scatter_body,
         shape(*grad_shape),
-        (columns, own, other),
+        (state, cols5, own, other),
         scratch=[pltpu.VMEM((2, 9, rows, width), F32)],
     )
     voxel_grad, image = call(

time: 45.4 us -> 44 us (0.969)
  starting transfers between devices: 19.7 us -> 18.8 us
    ppermute x3, starting transfers between devices: 10 us -> 8.37 us  [per_device(): theirs = lax.ppermute(message, 'slab', pairs)]
    ppermute x3, starting transfers between devices: 3.02 us -> 4.4 us  [per_device(): got = lax.ppermute(send, 'slab', pairs)]
    ppermute x3, waiting for transfers between devices: 5.15 us -> 4.39 us  [per_device(): theirs = lax.ppermute(message, 'slab', pairs)]
    ppermute x1, waiting for transfers between devices: 1.57 us -> 2.24 us  [per_device(): other = lax.ppermute(sent, 'dir', swap)]
    ppermute x1, starting transfers between devices: 0.66 us -> 0.01 us  [per_device(): near[1] = lax.ppermute(near[1], ('slab', 'tile'), pairs_b)]
    pallas_call x15 -> x16, Pallas kernels: 13.1 us -> 12.9 us  [call(): pl.pallas_call(kernel, out_shape=outs, in_specs=specs or [VMEM] * len(arg...]
  transfers between devices with their start and end apart: 12 -> 12, of which waited for: 7 -> 8; matrix products, arithmetic and copies ran while one was open for 0% -> 0% of each run, Pallas kernels for 20% -> 20%
where the time goes in v7:
time: 44 us; the launch traced here: 43.8 us
  starting transfers between devices  18.8 us (43%)
  Pallas kernels  12.9 us (29%)
  waiting for transfers between devices  11.4 us (26%)
  between operations  0.74 us (2%)
    pallas_call x16, Pallas kernels, call(): pl.pallas_call(kernel, out_shape=outs, in_specs=specs or [VMEM] * len(arg...  12.9 us
    ppermute x3, starting transfers between devices, per_device(): theirs = lax.ppermute(message, 'slab', pairs)  8.37 us
    ppermute x3, starting transfers between devices, per_device(): got = lax.ppermute(send, 'slab', pairs)  4.4 us
    ppermute x3, waiting for transfers between devices, per_device(): theirs = lax.ppermute(message, 'slab', pairs)  4.39 us
    ppermute x3, waiting for transfers between devices, per_device(): got = lax.ppermute(send, 'slab', pairs)  3.38 us
    ppermute x1, starting transfers between devices, per_device(): other = lax.ppermute(sent, 'dir', swap)  2.55 us
    ppermute x1, waiting for transfers between devices, per_device(): other = lax.ppermute(sent, 'dir', swap)  2.24 us
    ppermute x1, starting transfers between devices, per_device(): near[0] = lax.ppermute(near[0], 'slab', pairs_a)  1.54 us
  transfers between devices with their start and end apart: 12, of which 8 were waited for; matrix products, arithmetic and copies ran while one was open for 0% of the time, Pallas kernels for 20%

profile of v7, /device:TPU:0, one launch (start us, length us, event | category | flops | bytes accessed | tf_op | source)
XLA Modules:
  0.0 43.8 jit_solution(4757636585842831074)
XLA Ops:
  0.6 1.3 %shard_map.59 = (f32[5,32,256]{2,1,0:T(8,128)S(1)}, f32[5,32,256]{2,1,0:T(8,128)S(1)}, f32[4,8,512]{2,1,0:T(8,128)S(1)}) custom-call(s32[1,32,512]{2,1,0:T(8,128)} %refs_0_.3, s32[1,32,512]{2,1,0:T(8,128)} %refs_1_.2, f32[1,3,32,512]{3,2,1,0:T(8,128)} %refs_2_.1, f32[4,8,32,512]{3,2,1,0:T(8,128)} %refs_0_.5), custom_call_target="tpu_custom_call" | custom-call | flops 10000000 | bytes 2000000 | tf_op jit(solution)/shard_map/pallas_call | solution.py:25
  2.0 0.6 %collective-permute-start.1 = (f32[4,8,512]{2,1,0:T(8,128)S(1)}, f32[4,8,512]{2,1,0:T(8,128)S(1)}, u32[]{:S(2)}, u32[]{:S(2)}) collective-permute-start(f32[4,8,512]{2,1,0:T(8,128)S(1)} %get-tuple-element.42), channel_id=1, source_target_pairs={{0,1},{1,0},{2,3},{3,2},{4,5},{5,4},{6,7},{7,6},{8,9},{9,8},{10,11... | collective-permute-start | bytes 196616 | tf_op jit(solution)/shard_map/ppermute | solution.py:758
  2.5 2.6 %collective-permute-start = (f32[5,32,256]{2,1,0:T(8,128)S(1)}, f32[5,32,256]{2,1,0:T(8,128)S(1)}, u32[]{:S(2)}, u32[]{:S(2)}) collective-permute-start(f32[5,32,256]{2,1,0:T(8,128)S(1)} %get-tuple-element.41), channel_id=1, source_target_pairs={{0,16},{16,0},{1,17},{17,1},{2,18},{18,2},{3,19},{19,3},{4,20},{20... | collective-permute-start | bytes 491528 | tf_op jit(solution)/shard_map/ppermute | solution.py:759
  5.1 0.2 shard_map.60
  5.3 1.5 %collective-permute-start.2 = (f32[272,128]{1,0:T(8,128)S(1)}, f32[272,128]{1,0:T(8,128)S(1)}, u32[]{:S(2)}, u32[]{:S(2)}) collective-permute-start(f32[272,128]{1,0:T(8,128)S(1)} %get-tuple-element.43), channel_id=1, source_target_pairs={{0,2},{2,0},{4,6},{6,4},{8,10},{10,8},{12,14},{14,12},{1,3},{3,1},... | collective-permute-start | bytes 417800 | tf_op jit(solution)/shard_map/ppermute | solution.py:772
  6.9 0.8 %shard_map.61.refs_0_ = f32[3,4,8,48,256]{4,3,2,1,0:T(8,128)S(1)} custom-call(f32[4,8,32,512]{3,2,1,0:T(8,128)S(1)} %copy-done, f32[4,8,512]{2,1,0:T(8,128)S(1)} %collective-permute-done.1.refs_2_.refs_1_), custom_call_target="tpu_custom_call" | custom-call | flops 10000000 | bytes 2000000 | tf_op jit(solution)/shard_map/pallas_call | solution.py:25
  7.7 2.2 %collective-permute-done.refs_2_.refs_3_.refs_1_ = f32[5,32,256]{2,1,0:T(8,128)S(1)} collective-permute-done((f32[5,32,256]{2,1,0:T(8,128)S(1)}, f32[5,32,256]{2,1,0:T(8,128)S(1)}, u32[]{:S(2)}, u32[]{:S(2)}) %collective-permute-start) | collective-permute-done | bytes 163872 | tf_op jit(solution)/shard_map/ppermute | solution.py:759
  9.9 2.9 %shard_map.62 = (f32[2,4,6,32,256]{4,3,2,1,0:T(8,128)S(1)}, f32[2,4,2,32,256]{4,3,2,1,0:T(8,128)S(1)}, f32[2,4,2,32,256]{4,3,2,1,0:T(8,128)S(1)}, f32[4,2,32,256]{3,2,1,0:T(8,128)S(1)}) custom-call(f32[3,4,8,48,256]{4,3,2,1,0:T(8,128)S(1)} %shard_map.61.refs_0_, f32[5,32,256]{2,1,0:T(8,128)S(1)} %get-tuple-element.40.refs_1_.refs_2_.refs_0_, ...), custom_call_target="tpu_custom_call" | custom-call | flops 10000000 | bytes 2000000 | tf_op jit(solution)/shard_map/pallas_call | solution.py:25
  12.8 0.3 collective-permute-done.2.refs_0_
  13.1 1.3 %shard_map.63 = (f32[2,2,32,256]{3,2,1,0:T(8,128)S(1)}, f32[2,4,2,32,256]{4,3,2,1,0:T(8,128)S(1)}, f32[2,4,2,32,256]{4,3,2,1,0:T(8,128)S(1)}, f32[3,32,256]{2,1,0:T(8,128)S(1)}, f32[3,32,256]{2,1,0:T(8,128)S(1)}) custom-call(f32[272,128]{1,0:T(8,128)S(1)} %collective-permute-done.2.refs_0_, f32[272,128]{1,0:T(8,128)S(1)} %collective-permute-done.3.refs_1_, ...), custom_call_target="tpu_custom_call" | custom-call | flops 10000000 | bytes 2000000 | tf_op jit(solution)/shard_map/pallas_call | solution.py:25
  14.4 2.5 %collective-permute-start.4 = (f32[2,2,32,256]{3,2,1,0:T(8,128)S(1)}, f32[2,2,32,256]{3,2,1,0:T(8,128)S(1)}, u32[]{:S(2)}, u32[]{:S(2)}) collective-permute-start(f32[2,2,32,256]{3,2,1,0:T(8,128)S(1)} %get-tuple-element.48.refs_2_), channel_id=1, source_target_pairs={{0,2},{2,0},{4,6},{6,4},{8,10},{10,8},{12,14},{14,12},{1,3},{3,1},... | collective-permute-start | bytes 393224 | tf_op jit(solution)/shard_map/ppermute | solution.py:819
  17.0 3.0 %collective-permute-done.4.refs_3_ = f32[2,2,32,256]{3,2,1,0:T(8,128)S(1)} collective-permute-done((f32[2,2,32,256]{3,2,1,0:T(8,128)S(1)}, f32[2,2,32,256]{3,2,1,0:T(8,128)S(1)}, u32[]{:S(2)}, u32[]{:S(2)}) %collective-permute-start.4) | collective-permute-done | bytes 131104 | tf_op jit(solution)/shard_map/ppermute | solution.py:819
  19.9 0.1 shard_map.64
  20.0 2.1 %collective-permute-start.5 = (f32[2,2,32,256]{3,2,1,0:T(8,128)S(1)}, f32[2,2,32,256]{3,2,1,0:T(8,128)S(1)}, u32[]{:S(2)}, u32[]{:S(2)}) collective-permute-start(f32[2,2,32,256]{3,2,1,0:T(8,128)S(1)} %get-tuple-element.49.refs_2_), channel_id=1, source_target_pairs={{0,4},{2,6},{4,0},{6,2},{8,12},{10,14},{12,8},{14,10},{1,5},{3,7},... | collective-permute-start | bytes 393224 | tf_op jit(solution)/shard_map/ppermute | solution.py:819
  22.1 1.5 %collective-permute-start.8 = (f32[3,32,256]{2,1,0:T(8,128)S(1)}, f32[3,32,256]{2,1,0:T(8,128)S(1)}, u32[]{:S(2)}, u32[]{:S(2)}) collective-permute-start(f32[3,32,256]{2,1,0:T(8,128)S(1)} %get-tuple-element.65), channel_id=1, source_target_pairs={{0,2},{2,0},{4,6},{6,4},{8,10},{10,8},{12,14},{14,12},{1,3},{3,1},... | collective-permute-start | bytes 294920 | tf_op jit(solution)/shard_map/ppermute | solution.py:820
  23.7 1.4 %collective-permute-done.5.refs_3_ = f32[2,2,32,256]{3,2,1,0:T(8,128)S(1)} collective-permute-done((f32[2,2,32,256]{3,2,1,0:T(8,128)S(1)}, f32[2,2,32,256]{3,2,1,0:T(8,128)S(1)}, u32[]{:S(2)}, u32[]{:S(2)}) %collective-permute-start.5) | collective-permute-done | bytes 131104 | tf_op jit(solution)/shard_map/ppermute | solution.py:819
  25.1 0.1 shard_map.65
  25.2 3.7 %collective-permute-start.6 = (f32[2,32,256]{2,1,0:T(8,128)S(1)}, f32[2,32,256]{2,1,0:T(8,128)S(1)}, u32[]{:S(2)}, u32[]{:S(2)}) collective-permute-start(f32[2,32,256]{2,1,0:T(8,128)S(1)} %get-tuple-element.52), channel_id=1, source_target_pairs={{0,8},{2,10},{4,12},{6,14},{8,0},{10,2},{12,4},{14,6},{1,9},{3,11}... | collective-permute-start | bytes 196616 | tf_op jit(solution)/shard_map/ppermute | solution.py:819
  28.9 1.9 %collective-permute-start.9 = (f32[3,32,128]{2,1,0:T(8,128)S(1)}, f32[3,32,128]{2,1,0:T(8,128)S(1)}, u32[]{:S(2)}, u32[]{:S(2)}) collective-permute-start(f32[3,32,128]{2,1,0:T(8,128)S(1)} %get-tuple-element.69), channel_id=1, source_target_pairs={{0,4},{2,6},{4,0},{6,2},{8,12},{10,14},{12,8},{14,10},{1,5},{3,7},... | collective-permute-start | bytes 147464 | tf_op jit(solution)/shard_map/ppermute | solution.py:820
  30.8 2.3 %collective-permute-done.9.refs_1_ = f32[3,32,128]{2,1,0:T(8,128)S(1)} collective-permute-done((f32[3,32,128]{2,1,0:T(8,128)S(1)}, f32[3,32,128]{2,1,0:T(8,128)S(1)}, u32[]{:S(2)}, u32[]{:S(2)}) %collective-permute-start.9) | collective-permute-done | bytes 49184 | tf_op jit(solution)/shard_map/ppermute | solution.py:820
  33.1 1.0 %collective-permute-start.10 = (f32[3,32,128]{2,1,0:T(8,128)S(1)}, f32[3,32,128]{2,1,0:T(8,128)S(1)}, u32[]{:S(2)}, u32[]{:S(2)}) collective-permute-start(f32[3,32,128]{2,1,0:T(8,128)S(1)} %shard_map.72.refs_2_), channel_id=1, source_target_pairs={{0,8},{2,10},{4,12},{6,14},{8,0},{10,2},{12,4},{14,6},{1,9},{3,11}... | collective-permute-start | bytes 147464 | tf_op jit(solution)/shard_map/ppermute | solution.py:820
  34.1 2.0 %shard_map.67.refs_1_.refs_0_ = f32[5,2,8,32,256]{4,3,2,1,0:T(8,128)S(1)} custom-call(f32[5,32,256]{2,1,0:T(8,128)S(1)} %get-tuple-element.40.refs_1_.refs_2_.refs_0_, f32[5,32,256]{2,1,0:T(8,128)S(1)} %collective-permute-done.refs_2_.refs_3_.refs_1_, f32[2,4,6,32,256]{4,3,2,1,0:T(8,128)S(1)} %get-tuple-element.55.refs_2_, ...), custom_call_target="tpu_custom_call" | custom-call | flops 10000000 | bytes 2000000 | tf_op jit(solution)/shard_map/pallas_call | solution.py:25
  36.1 0.6 %shard_map.69 = (f32[2,5,8,256]{3,2,1,0:T(8,128)S(1)}, f32[2,2,32,128]{3,2,1,0:T(8,128)S(1)}, f32[2,3,8,256]{3,2,1,0:T(8,128)S(1)}, f32[2,3,32,128]{3,2,1,0:T(8,128)S(1)}) custom-call(f32[5,2,8,32,256]{4,3,2,1,0:T(8,128)S(1)} %shard_map.67.refs_1_.refs_0_, f32[5,32,256]{2,1,0:T(8,128)S(1)} %get-tuple-element.40.refs_1_.refs_2_.refs_0_, ...), custom_call_target="tpu_custom_call" | custom-call | flops 10000000 | bytes 2000000 | tf_op jit(solution)/shard_map/pallas_call | solution.py:25
  36.7 0.1 shard_map.66
  36.8 0.2 shard_map.70
  37.1 1.1 %collective-permute-done.10.refs_3_ = f32[3,32,128]{2,1,0:T(8,128)S(1)} collective-permute-done((f32[3,32,128]{2,1,0:T(8,128)S(1)}, f32[3,32,128]{2,1,0:T(8,128)S(1)}, u32[]{:S(2)}, u32[]{:S(2)}) %collective-permute-start.10) | collective-permute-done | bytes 49184 | tf_op jit(solution)/shard_map/ppermute | solution.py:820
  38.1 0.1 collective-permute-done.7.refs_1_
  38.3 0.1 shard_map.73
  38.4 1.3 %collective-permute-start.11 = (f32[128,128]{1,0:T(8,128)S(1)}, f32[128,128]{1,0:T(8,128)S(1)}, u32[]{:S(2)}, u32[]{:S(2)}) collective-permute-start(f32[128,128]{1,0:T(8,128)S(1)} %get-tuple-element.74), channel_id=1, source_target_pairs={{0,16},{16,0},{1,17},{17,1},{2,18},{18,2},{3,19},{19,3},{4,20},{20... | collective-permute-start | bytes 196616 | tf_op jit(solution)/shard_map/ppermute | solution.py:861
  39.6 2.1 %shard_map.68.refs_0_ = f32[4,8,32,256]{3,2,1,0:T(8,128)S(1)} custom-call(f32[2,2,32,256]{3,2,1,0:T(8,128)S(1)} %get-tuple-element.54.refs_0_, f32[5,2,8,32,256]{4,3,2,1,0:T(8,128)S(1)} %shard_map.67.refs_1_.refs_0_, f32[5,32,256]{2,1,0:T(8,128)S(1)} %get-tuple-element.40.refs_1_.refs_2_.refs_0_, f32[5,32,256]{2,1,0:T(8,128)S(1)} %collective-permute-done.refs_2_.refs_3_.refs_1_), custom_call_target="tpu_custom_call" | custom-call | flops 10000000 | bytes 2000000 | tf_op jit(solution)/shard_map/pallas_call | solution.py:25
  41.7 1.0 %collective-permute-done.11.refs_2_ = f32[128,128]{1,0:T(8,128)S(1)} collective-permute-done((f32[128,128]{1,0:T(8,128)S(1)}, f32[128,128]{1,0:T(8,128)S(1)}, u32[]{:S(2)}, u32[]{:S(2)}) %collective-permute-start.11) | collective-permute-done | bytes 65568 | tf_op jit(solution)/shard_map/ppermute | solution.py:861
  42.7 1.1 %shard_map.74 = (f32[4,8,32,256]{3,2,1,0:T(8,128)}, f32[1,3,32,64]{3,2,1,0:T(8,128)}) custom-call(f32[4,8,32,256]{3,2,1,0:T(8,128)S(1)} %shard_map.68.refs_0_, f32[40,256]{1,0:T(8,128)S(1)} %collective-permute-done.7.refs_1_, f32[128,128]{1,0:T(8,128)S(1)} %collective-permute-done.11.refs_2_, f32[3,32,64]{2,1,0:T(8,128)S(1)} %get-tuple-element.75.refs_3_), custom_call_target="tpu_custom_call" | custom-call | flops 10000000 | bytes 2000000 | tf_op jit(solution)/shard_map/pallas_call | solution.py:25
  (10 shorter events, 0.1 us)
Async XLA Ops:
  0.6 4.5 %copy-start = (f32[4,8,32,512]{3,2,1,0:T(8,128)S(1)}, f32[4,8,32,512]{3,2,1,0:T(8,128)}, u32[]{:S(2)}) copy-start(f32[4,8,32,512]{3,2,1,0:T(8,128)} %refs_0_.5) | copy-start | bytes 6291460
  2.0 3.1 %collective-permute-start.1 = (f32[4,8,512]{2,1,0:T(8,128)S(1)}, f32[4,8,512]{2,1,0:T(8,128)S(1)}, u32[]{:S(2)}, u32[]{:S(2)}) collective-permute-start(f32[4,8,512]{2,1,0:T(8,128)S(1)} %get-tuple-element.42), channel_id=1, source_target_pairs={{0,1},{1,0},{2,3},{3,2},{4,5},{5,4},{6,7},{7,6},{8,9},{9,8},{10,11... | collective-permute-start | bytes 196616 | tf_op jit(solution)/shard_map/ppermute | solution.py:758
  2.5 7.3 %collective-permute-start = (f32[5,32,256]{2,1,0:T(8,128)S(1)}, f32[5,32,256]{2,1,0:T(8,128)S(1)}, u32[]{:S(2)}, u32[]{:S(2)}) collective-permute-start(f32[5,32,256]{2,1,0:T(8,128)S(1)} %get-tuple-element.41), channel_id=1, source_target_pairs={{0,16},{16,0},{1,17},{17,1},{2,18},{18,2},{3,19},{19,3},{4,20},{20... | collective-permute-start | bytes 491528 | tf_op jit(solution)/shard_map/ppermute | solution.py:759
  5.3 7.8 %collective-permute-start.2 = (f32[272,128]{1,0:T(8,128)S(1)}, f32[272,128]{1,0:T(8,128)S(1)}, u32[]{:S(2)}, u32[]{:S(2)}) collective-permute-start(f32[272,128]{1,0:T(8,128)S(1)} %get-tuple-element.43), channel_id=1, source_target_pairs={{0,2},{2,0},{4,6},{6,4},{8,10},{10,8},{12,14},{14,12},{1,3},{3,1},... | collective-permute-start | bytes 417800 | tf_op jit(solution)/shard_map/ppermute | solution.py:772
  6.9 6.2 %collective-permute-start.3 = (f32[272,128]{1,0:T(8,128)S(1)}, f32[272,128]{1,0:T(8,128)S(1)}, u32[]{:S(2)}, u32[]{:S(2)}) collective-permute-start(f32[272,128]{1,0:T(8,128)S(1)} %get-tuple-element.44), channel_id=1, source_target_pairs={{2,4},{3,5},{6,8},{7,9},{10,12},{11,13},{4,2},{5,3},{8,6},{9,7},{1... | collective-permute-start | bytes 417800 | tf_op jit(solution)/shard_map/ppermute | solution.py:773
  14.4 5.5 %collective-permute-start.4 = (f32[2,2,32,256]{3,2,1,0:T(8,128)S(1)}, f32[2,2,32,256]{3,2,1,0:T(8,128)S(1)}, u32[]{:S(2)}, u32[]{:S(2)}) collective-permute-start(f32[2,2,32,256]{3,2,1,0:T(8,128)S(1)} %get-tuple-element.48.refs_2_), channel_id=1, source_target_pairs={{0,2},{2,0},{4,6},{6,4},{8,10},{10,8},{12,14},{14,12},{1,3},{3,1},... | collective-permute-start | bytes 393224 | tf_op jit(solution)/shard_map/ppermute | solution.py:819
  20.0 5.1 %collective-permute-start.5 = (f32[2,2,32,256]{3,2,1,0:T(8,128)S(1)}, f32[2,2,32,256]{3,2,1,0:T(8,128)S(1)}, u32[]{:S(2)}, u32[]{:S(2)}) collective-permute-start(f32[2,2,32,256]{3,2,1,0:T(8,128)S(1)} %get-tuple-element.49.refs_2_), channel_id=1, source_target_pairs={{0,4},{2,6},{4,0},{6,2},{8,12},{10,14},{12,8},{14,10},{1,5},{3,7},... | collective-permute-start | bytes 393224 | tf_op jit(solution)/shard_map/ppermute | solution.py:819
  22.1 6.7 %collective-permute-start.8 = (f32[3,32,256]{2,1,0:T(8,128)S(1)}, f32[3,32,256]{2,1,0:T(8,128)S(1)}, u32[]{:S(2)}, u32[]{:S(2)}) collective-permute-start(f32[3,32,256]{2,1,0:T(8,128)S(1)} %get-tuple-element.65), channel_id=1, source_target_pairs={{0,2},{2,0},{4,6},{6,4},{8,10},{10,8},{12,14},{14,12},{1,3},{3,1},... | collective-permute-start | bytes 294920 | tf_op jit(solution)/shard_map/ppermute | solution.py:820
  25.2 11.5 %collective-permute-start.6 = (f32[2,32,256]{2,1,0:T(8,128)S(1)}, f32[2,32,256]{2,1,0:T(8,128)S(1)}, u32[]{:S(2)}, u32[]{:S(2)}) collective-permute-start(f32[2,32,256]{2,1,0:T(8,128)S(1)} %get-tuple-element.52), channel_id=1, source_target_pairs={{0,8},{2,10},{4,12},{6,14},{8,0},{10,2},{12,4},{14,6},{1,9},{3,11}... | collective-permute-start | bytes 196616 | tf_op jit(solution)/shard_map/ppermute | solution.py:819
  28.9 4.2 %collective-permute-start.9 = (f32[3,32,128]{2,1,0:T(8,128)S(1)}, f32[3,32,128]{2,1,0:T(8,128)S(1)}, u32[]{:S(2)}, u32[]{:S(2)}) collective-permute-start(f32[3,32,128]{2,1,0:T(8,128)S(1)} %get-tuple-element.69), channel_id=1, source_target_pairs={{0,4},{2,6},{4,0},{6,2},{8,12},{10,14},{12,8},{14,10},{1,5},{3,7},... | collective-permute-start | bytes 147464 | tf_op jit(solution)/shard_map/ppermute | solution.py:820
  33.1 5.1 %collective-permute-start.10 = (f32[3,32,128]{2,1,0:T(8,128)S(1)}, f32[3,32,128]{2,1,0:T(8,128)S(1)}, u32[]{:S(2)}, u32[]{:S(2)}) collective-permute-start(f32[3,32,128]{2,1,0:T(8,128)S(1)} %shard_map.72.refs_2_), channel_id=1, source_target_pairs={{0,8},{2,10},{4,12},{6,14},{8,0},{10,2},{12,4},{14,6},{1,9},{3,11}... | collective-permute-start | bytes 147464 | tf_op jit(solution)/shard_map/ppermute | solution.py:820
  37.0 1.3 %collective-permute-start.7 = (f32[40,256]{1,0:T(8,128)S(1)}, f32[40,256]{1,0:T(8,128)S(1)}, u32[]{:S(2)}, u32[]{:S(2)}) collective-permute-start(f32[40,256]{1,0:T(8,128)S(1)} %get-tuple-element.62), channel_id=1, source_target_pairs={{0,1},{1,0},{2,3},{3,2},{4,5},{5,4},{6,7},{7,6},{8,9},{9,8},{10,11... | collective-permute-start | bytes 122888 | tf_op jit(solution)/shard_map/ppermute | solution.py:852
  38.4 4.3 %collective-permute-start.11 = (f32[128,128]{1,0:T(8,128)S(1)}, f32[128,128]{1,0:T(8,128)S(1)}, u32[]{:S(2)}, u32[]{:S(2)}) collective-permute-start(f32[128,128]{1,0:T(8,128)S(1)} %get-tuple-element.74), channel_id=1, source_target_pairs={{0,16},{16,0},{1,17},{17,1},{2,18},{18,2},{3,19},{19,3},{4,20},{20... | collective-permute-start | bytes 196616 | tf_op jit(solution)/shard_map/ppermute | solution.py:861

commit v8 on v7

--- a/solution.py
+++ b/solution.py
@@ -542,23 +542,28 @@
         outs[1][c] = jnp.where(tile == 0, high, low)
 
 
-def gather_body(info, edge, line, keep, got, mine_scale, their_scale, mine, out, *, chunk, half, halved):
-    _, t, s = info
+def corner_body(info, edge, line, out):
     rows = edge.shape[0]
     body = line.shape[0] - SUB
+    border = iota((rows, LANES), 0) == jnp.where(info[1] == 0, rows - 1, 0)
+    out[...] = edge[...] + jnp.where(border, line[body : body + 1, :LANES], 0.0)
+
+
+def gather_body(info, keep, got, mine_scale, their_scale, mine, sent, *, chunk, half, halved):
+    s = info[2]
     start = lax.rem(s, half) * chunk
     base = 0 if halved else (start // LANES) * LANES
     cols = pl.ds(pl.multiple_of(base, LANES), LANES)
     start = lax.rem(start, LANES)
     there = jnp.where(lax.rem(s, 2) == 1, start - chunk, start + chunk)
-    border = iota((rows, LANES), 0) == jnp.where(t == 0, rows - 1, 0)
-    out[:rows, :] = edge[...] + jnp.where(border, line[body : body + 1, :LANES], 0.0)
     for c in range(keep.shape[0]):
         both = mine_scale[:, cols] * keep[c, :, cols] + their_scale[:, cols] * got[c, :, cols]
         mine[c] = pltpu.roll(both, lax.rem(LANES - start, LANES), 1)[:, :chunk]
-        out[(c + 1) * rows : (c + 2) * rows, :] = pltpu.roll(
-            both, lax.rem(LANES - there, LANES), 1
-        )
+        sent[c] = pltpu.roll(both, lax.rem(LANES - there, LANES), 1)[:, :chunk]
+
+
+def choose_body(info, mine, theirs, image, *, half):
+    image[0] = jnp.where(info[2] // half == info[0], mine[...], theirs[...])
 
 
 def strips_body(info, cols5, own, other, rows5, packs, down, across):
@@ -680,20 +685,16 @@
     lax.fori_loop(0, planes, plane, 0)
 
 
-def finish_body(info, grad_in, line, cross, mine, grad, image, buffer, picture, sems, *, half):
-    h, t, s = info
+def finish_body(info, grad_in, line, edge, grad, buffer, sems):
+    h, t, _ = info
     channels, planes, rows, width = buffer.shape
     source = jnp.where(h == 0, LANES - 1, 0)
     side = pl.ds(pl.multiple_of(jnp.where(h == 0, width - LANES, 0), LANES), LANES)
     last = jnp.where(t == 0, rows - 1, 0)
     at_row = iota((rows, width), 0) == last
     at_lane = iota((rows, LANES), 1) == source
-    packed = cross[:rows, :]
-    here = s // half == h
-    for c in range(channels - 1):
-        picture[0, c] = jnp.where(here, mine[c], cross[(c + 1) * rows : (c + 2) * rows, : picture.shape[3]])
-    copies = [pltpu.make_async_copy(picture, image, sems.at[channels])]
-    copies[0].start()
+    packed = edge[...]
+    copies = []
     for c in range(channels):
         for p in range(planes):
             at = c * planes + p
@@ -850,15 +851,18 @@
         border_body, [shape(channels * planes + SUB, width), shape(rows, LANES)], (state, *strips)
     )
     line = lax.ppermute(line, "tile", swap)
-    mine, message = call(
+    edge = call(corner_body, shape(rows, LANES), (edge, line))
+    edge = lax.ppermute(edge, "dir", swap)
+    piece = shape(colours, rows, chunk)
+    mine, sent = call(
         gather_body,
-        [shape(colours, rows, chunk), shape((colours + 1) * rows, LANES)],
-        (edge, line, keep, got, mine_scale, their_scale),
+        [piece, piece],
+        (keep, got, mine_scale, their_scale),
         chunk=chunk,
         half=half,
         halved=tile_bit is not None,
     )
-    message = lax.ppermute(message, "dir", swap)
+    theirs = lax.ppermute(sent, "dir", swap)
     grad_shape = (channels, planes, rows, width)
     grad = call(
         scatter_body,
@@ -866,18 +870,14 @@
         (state, cols5, own, other),
         scratch=[pltpu.VMEM((2, 9, rows, width), F32)],
     )
-    voxel_grad, image = call(
+    voxel_grad = call(
         finish_body,
-        [shape(*grad_shape), shape(1, colours, rows, chunk)],
-        (grad, line, message, mine),
-        scratch=[
-            pltpu.VMEM(grad_shape, F32),
-            pltpu.VMEM((1, colours, rows, chunk), F32),
-            pltpu.SemaphoreType.DMA((channels + 1,)),
-        ],
-        out_specs=[hbm, hbm],
-        half=half,
-    )
+        shape(*grad_shape),
+        (grad, line, edge),
+        scratch=[pltpu.VMEM(grad_shape, F32), pltpu.SemaphoreType.DMA((channels,))],
+        out_specs=hbm,
+    )
+    image = call(choose_body, shape(1, colours, rows, chunk), (mine, theirs), half=half)
     return (image, voxel_grad)
 
 

time: 44 us -> 45.8 us (1.041)
  waiting for transfers between devices: 11.4 us -> 15 us
  starting transfers between devices: 18.8 us -> 16.4 us
  Pallas kernels: 12.9 us -> 13.6 us
    ppermute x3, waiting for transfers between devices: 3.38 us -> 9.3 us  [per_device(): got = lax.ppermute(send, 'slab', pairs)]
    ppermute x3, starting transfers between devices: 4.4 us -> 2.14 us  [per_device(): got = lax.ppermute(send, 'slab', pairs)]
    ppermute x3, waiting for transfers between devices: 4.39 us -> 2.96 us  [per_device(): theirs = lax.ppermute(message, 'slab', pairs)]
    ppermute x3, starting transfers between devices: 8.37 us -> 7.34 us  [per_device(): theirs = lax.ppermute(message, 'slab', pairs)]
    ppermute x1 -> x2, starting transfers between devices: 1.26 us -> 2.16 us  [the longest x1 1.24 us: per_device(): theirs = lax.ppermute(sent, 'dir', swap)]
    ppermute x1 -> x2, waiting for transfers between devices: 0.98 us -> 0.15 us  [the longest x1 0.15 us: per_device(): edge = lax.ppermute(edge, 'dir', swap)]
    pallas_call x16 -> x18, Pallas kernels: 12.9 us -> 13.6 us  [call(): pl.pallas_call(kernel, out_shape=outs, in_specs=specs or [VMEM] * len(arg...]
  transfers between devices with their start and end apart: 12 -> 13, of which waited for: 8 -> 7; matrix products, arithmetic and copies ran while one was open for 0% -> 0% of each run, Pallas kernels for 20% -> 21%
where the time goes in v8:
time: 45.8 us; the launch traced here: 45.7 us
  starting transfers between devices  16.4 us (36%)
  waiting for transfers between devices  15 us (33%)
  Pallas kernels  13.6 us (30%)
  between operations  0.77 us (2%)
    pallas_call x18, Pallas kernels, call(): pl.pallas_call(kernel, out_shape=outs, in_specs=specs or [VMEM] * len(arg...  13.6 us
    ppermute x3, waiting for transfers between devices, per_device(): got = lax.ppermute(send, 'slab', pairs)  9.3 us
    ppermute x3, starting transfers between devices, per_device(): theirs = lax.ppermute(message, 'slab', pairs)  7.34 us
    ppermute x3, waiting for transfers between devices, per_device(): theirs = lax.ppermute(message, 'slab', pairs)  2.96 us
    ppermute x1, starting transfers between devices, per_device(): other = lax.ppermute(sent, 'dir', swap)  2.55 us
    ppermute x1, waiting for transfers between devices, per_device(): other = lax.ppermute(sent, 'dir', swap)  2.24 us
    ppermute x3, starting transfers between devices, per_device(): got = lax.ppermute(send, 'slab', pairs)  2.14 us
    ppermute x1, starting transfers between devices, per_device(): near[0] = lax.ppermute(near[0], 'slab', pairs_a)  1.54 us
  transfers between devices with their start and end apart: 13, of which 7 were waited for; matrix products, arithmetic and copies ran while one was open for 0% of the time, Pallas kernels for 21%

profile of v8, /device:TPU:0, one launch (start us, length us, event | category | flops | bytes accessed | tf_op | source)
XLA Modules:
  0.0 45.7 jit_solution(2156106381520412609)
XLA Ops:
  0.6 1.3 %shard_map.59 = (f32[5,32,256]{2,1,0:T(8,128)S(1)}, f32[5,32,256]{2,1,0:T(8,128)S(1)}, f32[4,8,512]{2,1,0:T(8,128)S(1)}) custom-call(s32[1,32,512]{2,1,0:T(8,128)} %refs_0_.3, s32[1,32,512]{2,1,0:T(8,128)} %refs_1_.2, f32[1,3,32,512]{3,2,1,0:T(8,128)} %refs_2_.1, f32[4,8,32,512]{3,2,1,0:T(8,128)} %refs_0_.5), custom_call_target="tpu_custom_call" | custom-call | flops 10000000 | bytes 2000000 | tf_op jit(solution)/shard_map/pallas_call | solution.py:25
  2.0 0.6 %collective-permute-start = (f32[4,8,512]{2,1,0:T(8,128)S(1)}, f32[4,8,512]{2,1,0:T(8,128)S(1)}, u32[]{:S(2)}, u32[]{:S(2)}) collective-permute-start(f32[4,8,512]{2,1,0:T(8,128)S(1)} %get-tuple-element.38), channel_id=1, source_target_pairs={{0,1},{1,0},{2,3},{3,2},{4,5},{5,4},{6,7},{7,6},{8,9},{9,8},{10,11... | collective-permute-start | bytes 196616 | tf_op jit(solution)/shard_map/ppermute | solution.py:759
  2.5 2.6 %collective-permute-start.3 = (f32[5,32,256]{2,1,0:T(8,128)S(1)}, f32[5,32,256]{2,1,0:T(8,128)S(1)}, u32[]{:S(2)}, u32[]{:S(2)}) collective-permute-start(f32[5,32,256]{2,1,0:T(8,128)S(1)} %get-tuple-element.42), channel_id=1, source_target_pairs={{0,16},{16,0},{1,17},{17,1},{2,18},{18,2},{3,19},{19,3},{4,20},{20... | collective-permute-start | bytes 491528 | tf_op jit(solution)/shard_map/ppermute | solution.py:760
  5.1 0.2 shard_map.60
  5.3 1.5 %collective-permute-start.1 = (f32[272,128]{1,0:T(8,128)S(1)}, f32[272,128]{1,0:T(8,128)S(1)}, u32[]{:S(2)}, u32[]{:S(2)}) collective-permute-start(f32[272,128]{1,0:T(8,128)S(1)} %get-tuple-element.39), channel_id=1, source_target_pairs={{0,2},{2,0},{4,6},{6,4},{8,10},{10,8},{12,14},{14,12},{1,3},{3,1},... | collective-permute-start | bytes 417800 | tf_op jit(solution)/shard_map/ppermute | solution.py:773
  6.9 0.8 %shard_map.61.refs_0_ = f32[3,4,8,48,256]{4,3,2,1,0:T(8,128)S(1)} custom-call(f32[4,8,32,512]{3,2,1,0:T(8,128)S(1)} %copy-done, f32[4,8,512]{2,1,0:T(8,128)S(1)} %collective-permute-done.refs_2_.refs_1_), custom_call_target="tpu_custom_call" | custom-call | flops 10000000 | bytes 2000000 | tf_op jit(solution)/shard_map/pallas_call | solution.py:25
  7.7 2.2 %collective-permute-done.3.refs_2_.refs_3_.refs_1_ = f32[5,32,256]{2,1,0:T(8,128)S(1)} collective-permute-done((f32[5,32,256]{2,1,0:T(8,128)S(1)}, f32[5,32,256]{2,1,0:T(8,128)S(1)}, u32[]{:S(2)}, u32[]{:S(2)}) %collective-permute-start.3) | collective-permute-done | bytes 163872 | tf_op jit(solution)/shard_map/ppermute | solution.py:760
  9.9 2.9 %shard_map.62 = (f32[2,4,6,32,256]{4,3,2,1,0:T(8,128)S(1)}, f32[2,4,2,32,256]{4,3,2,1,0:T(8,128)S(1)}, f32[2,4,2,32,256]{4,3,2,1,0:T(8,128)S(1)}, f32[4,2,32,256]{3,2,1,0:T(8,128)S(1)}) custom-call(f32[3,4,8,48,256]{4,3,2,1,0:T(8,128)S(1)} %shard_map.61.refs_0_, f32[5,32,256]{2,1,0:T(8,128)S(1)} %get-tuple-element.41.refs_1_.refs_2_.refs_0_, ...), custom_call_target="tpu_custom_call" | custom-call | flops 10000000 | bytes 2000000 | tf_op jit(solution)/shard_map/pallas_call | solution.py:25
  12.8 0.3 collective-permute-done.1.refs_0_
  13.1 1.3 %shard_map.63 = (f32[2,2,32,256]{3,2,1,0:T(8,128)S(1)}, f32[2,4,2,32,256]{4,3,2,1,0:T(8,128)S(1)}, f32[2,4,2,32,256]{4,3,2,1,0:T(8,128)S(1)}, f32[3,32,256]{2,1,0:T(8,128)S(1)}, f32[3,32,256]{2,1,0:T(8,128)S(1)}) custom-call(f32[272,128]{1,0:T(8,128)S(1)} %collective-permute-done.1.refs_0_, f32[272,128]{1,0:T(8,128)S(1)} %collective-permute-done.2.refs_1_, ...), custom_call_target="tpu_custom_call" | custom-call | flops 10000000 | bytes 2000000 | tf_op jit(solution)/shard_map/pallas_call | solution.py:25
  14.4 2.5 %collective-permute-start.5 = (f32[2,2,32,256]{3,2,1,0:T(8,128)S(1)}, f32[2,2,32,256]{3,2,1,0:T(8,128)S(1)}, u32[]{:S(2)}, u32[]{:S(2)}) collective-permute-start(f32[2,2,32,256]{3,2,1,0:T(8,128)S(1)} %get-tuple-element.48.refs_2_), channel_id=1, source_target_pairs={{0,2},{2,0},{4,6},{6,4},{8,10},{10,8},{12,14},{14,12},{1,3},{3,1},... | collective-permute-start | bytes 393224 | tf_op jit(solution)/shard_map/ppermute | solution.py:820
  17.0 3.0 %collective-permute-done.5.refs_3_ = f32[2,2,32,256]{3,2,1,0:T(8,128)S(1)} collective-permute-done((f32[2,2,32,256]{3,2,1,0:T(8,128)S(1)}, f32[2,2,32,256]{3,2,1,0:T(8,128)S(1)}, u32[]{:S(2)}, u32[]{:S(2)}) %collective-permute-start.5) | collective-permute-done | bytes 131104 | tf_op jit(solution)/shard_map/ppermute | solution.py:820
  19.9 0.1 shard_map.64
  20.0 2.1 %collective-permute-start.7 = (f32[2,2,32,256]{3,2,1,0:T(8,128)S(1)}, f32[2,2,32,256]{3,2,1,0:T(8,128)S(1)}, u32[]{:S(2)}, u32[]{:S(2)}) collective-permute-start(f32[2,2,32,256]{3,2,1,0:T(8,128)S(1)} %get-tuple-element.53.refs_2_), channel_id=1, source_target_pairs={{0,4},{2,6},{4,0},{6,2},{8,12},{10,14},{12,8},{14,10},{1,5},{3,7},... | collective-permute-start | bytes 393224 | tf_op jit(solution)/shard_map/ppermute | solution.py:820
  22.1 1.5 %collective-permute-start.4 = (f32[3,32,256]{2,1,0:T(8,128)S(1)}, f32[3,32,256]{2,1,0:T(8,128)S(1)}, u32[]{:S(2)}, u32[]{:S(2)}) collective-permute-start(f32[3,32,256]{2,1,0:T(8,128)S(1)} %get-tuple-element.47), channel_id=1, source_target_pairs={{0,2},{2,0},{4,6},{6,4},{8,10},{10,8},{12,14},{14,12},{1,3},{3,1},... | collective-permute-start | bytes 294920 | tf_op jit(solution)/shard_map/ppermute | solution.py:821
  23.7 3.1 %collective-permute-done.4.refs_1_ = f32[3,32,256]{2,1,0:T(8,128)S(1)} collective-permute-done((f32[3,32,256]{2,1,0:T(8,128)S(1)}, f32[3,32,256]{2,1,0:T(8,128)S(1)}, u32[]{:S(2)}, u32[]{:S(2)}) %collective-permute-start.4) | collective-permute-done | bytes 98336 | tf_op jit(solution)/shard_map/ppermute | solution.py:821
  26.8 0.1 shard_map.66
  26.9 2.7 %collective-permute-start.9 = (f32[2,32,256]{2,1,0:T(8,128)S(1)}, f32[2,32,256]{2,1,0:T(8,128)S(1)}, u32[]{:S(2)}, u32[]{:S(2)}) collective-permute-start(f32[2,32,256]{2,1,0:T(8,128)S(1)} %get-tuple-element.58), channel_id=1, source_target_pairs={{0,8},{2,10},{4,12},{6,14},{8,0},{10,2},{12,4},{14,6},{1,9},{3,11}... | collective-permute-start | bytes 196616 | tf_op jit(solution)/shard_map/ppermute | solution.py:820
  29.6 0.6 %collective-permute-start.6 = (f32[3,32,128]{2,1,0:T(8,128)S(1)}, f32[3,32,128]{2,1,0:T(8,128)S(1)}, u32[]{:S(2)}, u32[]{:S(2)}) collective-permute-start(f32[3,32,128]{2,1,0:T(8,128)S(1)} %get-tuple-element.52), channel_id=1, source_target_pairs={{0,4},{2,6},{4,0},{6,2},{8,12},{10,14},{12,8},{14,10},{1,5},{3,7},... | collective-permute-start | bytes 147464 | tf_op jit(solution)/shard_map/ppermute | solution.py:821
  30.1 4.0 %collective-permute-done.6.refs_1_ = f32[3,32,128]{2,1,0:T(8,128)S(1)} collective-permute-done((f32[3,32,128]{2,1,0:T(8,128)S(1)}, f32[3,32,128]{2,1,0:T(8,128)S(1)}, u32[]{:S(2)}, u32[]{:S(2)}) %collective-permute-start.6) | collective-permute-done | bytes 49184 | tf_op jit(solution)/shard_map/ppermute | solution.py:821
  34.3 2.0 %shard_map.71.refs_1_.refs_0_ = f32[5,2,8,32,256]{4,3,2,1,0:T(8,128)S(1)} custom-call(f32[5,32,256]{2,1,0:T(8,128)S(1)} %get-tuple-element.41.refs_1_.refs_2_.refs_0_, f32[5,32,256]{2,1,0:T(8,128)S(1)} %collective-permute-done.3.refs_2_.refs_3_.refs_1_, f32[2,4,6,32,256]{4,3,2,1,0:T(8,128)S(1)} %get-tuple-element.65.refs_2_, ...), custom_call_target="tpu_custom_call" | custom-call | flops 10000000 | bytes 2000000 | tf_op jit(solution)/shard_map/pallas_call | solution.py:25
  36.3 0.6 %shard_map.73 = (f32[2,5,8,256]{3,2,1,0:T(8,128)S(1)}, f32[2,2,32,128]{3,2,1,0:T(8,128)S(1)}, f32[2,3,8,256]{3,2,1,0:T(8,128)S(1)}, f32[2,3,32,128]{3,2,1,0:T(8,128)S(1)}) custom-call(f32[5,2,8,32,256]{4,3,2,1,0:T(8,128)S(1)} %shard_map.71.refs_1_.refs_0_, f32[5,32,256]{2,1,0:T(8,128)S(1)} %get-tuple-element.41.refs_1_.refs_2_.refs_0_, ...), custom_call_target="tpu_custom_call" | custom-call | flops 10000000 | bytes 2000000 | tf_op jit(solution)/shard_map/pallas_call | solution.py:25
  36.9 0.1 shard_map.68
  37.0 0.2 shard_map.74
  37.2 2.2 %collective-permute-done.8.refs_1_ = f32[3,32,128]{2,1,0:T(8,128)S(1)} collective-permute-done((f32[3,32,128]{2,1,0:T(8,128)S(1)}, f32[3,32,128]{2,1,0:T(8,128)S(1)}, u32[]{:S(2)}, u32[]{:S(2)}) %collective-permute-start.8) | collective-permute-done | bytes 49184 | tf_op jit(solution)/shard_map/ppermute | solution.py:821
  39.4 0.1 shard_map.69
  39.5 1.2 %collective-permute-start.10 = (f32[3,32,64]{2,1,0:T(8,128)S(1)}, f32[3,32,64]{2,1,0:T(8,128)S(1)}, u32[]{:S(2)}, u32[]{:S(2)}) collective-permute-start(f32[3,32,64]{2,1,0:T(8,128)S(1)} %get-tuple-element.63), channel_id=1, source_target_pairs={{0,16},{16,0},{1,17},{17,1},{2,18},{18,2},{3,19},{19,3},{4,20},{20... | collective-permute-start | bytes 73736 | tf_op jit(solution)/shard_map/ppermute | solution.py:865
  40.7 0.9 %collective-permute-start.12 = (f32[32,128]{1,0:T(8,128)S(1)}, f32[32,128]{1,0:T(8,128)S(1)}, u32[]{:S(2)}, u32[]{:S(2)}) collective-permute-start(f32[32,128]{1,0:T(8,128)S(1)} %shard_map.75), channel_id=1, source_target_pairs={{0,16},{16,0},{1,17},{17,1},{2,18},{18,2},{3,19},{19,3},{4,20},{20... | collective-permute-start | bytes 49160 | tf_op jit(solution)/shard_map/ppermute | solution.py:855
  41.7 2.1 %shard_map.72.refs_0_ = f32[4,8,32,256]{3,2,1,0:T(8,128)S(1)} custom-call(f32[2,2,32,256]{3,2,1,0:T(8,128)S(1)} %get-tuple-element.64.refs_0_, f32[5,2,8,32,256]{4,3,2,1,0:T(8,128)S(1)} %shard_map.71.refs_1_.refs_0_, f32[5,32,256]{2,1,0:T(8,128)S(1)} %get-tuple-element.41.refs_1_.refs_2_.refs_0_, f32[5,32,256]{2,1,0:T(8,128)S(1)} %collective-permute-done.3.refs_2_.refs_3_.refs_1_), custom_call_target="tpu_custom_call" | custom-call | flops 10000000 | bytes 2000000 | tf_op jit(solution)/shard_map/pallas_call | solution.py:25
  43.8 0.6 %shard_map.70 = f32[1,3,32,64]{3,2,1,0:T(8,128)} custom-call(f32[3,32,64]{2,1,0:T(8,128)S(1)} %get-tuple-element.62.refs_0_, f32[3,32,64]{2,1,0:T(8,128)S(1)} %collective-permute-done.10.refs_1_), custom_call_target="tpu_custom_call" | custom-call | flops 10000000 | bytes 2000000 | tf_op jit(solution)/shard_map/pallas_call | solution.py:25
  44.4 0.1 collective-permute-done.12.refs_2_
  44.5 1.1 %shard_map.76 = f32[4,8,32,256]{3,2,1,0:T(8,128)} custom-call(f32[4,8,32,256]{3,2,1,0:T(8,128)S(1)} %shard_map.72.refs_0_, f32[40,256]{1,0:T(8,128)S(1)} %collective-permute-done.11.refs_1_, f32[32,128]{1,0:T(8,128)S(1)} %collective-permute-done.12.refs_2_), custom_call_target="tpu_custom_call" | custom-call | flops 10000000 | bytes 2000000 | tf_op jit(solution)/shard_map/pallas_call | solution.py:25
  (14 shorter events, 0.2 us)
Async XLA Ops:
  0.6 4.5 %copy-start = (f32[4,8,32,512]{3,2,1,0:T(8,128)S(1)}, f32[4,8,32,512]{3,2,1,0:T(8,128)}, u32[]{:S(2)}) copy-start(f32[4,8,32,512]{3,2,1,0:T(8,128)} %refs_0_.5) | copy-start | bytes 6291460
  2.0 3.1 %collective-permute-start = (f32[4,8,512]{2,1,0:T(8,128)S(1)}, f32[4,8,512]{2,1,0:T(8,128)S(1)}, u32[]{:S(2)}, u32[]{:S(2)}) collective-permute-start(f32[4,8,512]{2,1,0:T(8,128)S(1)} %get-tuple-element.38), channel_id=1, source_target_pairs={{0,1},{1,0},{2,3},{3,2},{4,5},{5,4},{6,7},{7,6},{8,9},{9,8},{10,11... | collective-permute-start | bytes 196616 | tf_op jit(solution)/shard_map/ppermute | solution.py:759
  2.5 7.3 %collective-permute-start.3 = (f32[5,32,256]{2,1,0:T(8,128)S(1)}, f32[5,32,256]{2,1,0:T(8,128)S(1)}, u32[]{:S(2)}, u32[]{:S(2)}) collective-permute-start(f32[5,32,256]{2,1,0:T(8,128)S(1)} %get-tuple-element.42), channel_id=1, source_target_pairs={{0,16},{16,0},{1,17},{17,1},{2,18},{18,2},{3,19},{19,3},{4,20},{20... | collective-permute-start | bytes 491528 | tf_op jit(solution)/shard_map/ppermute | solution.py:760
  5.3 7.8 %collective-permute-start.1 = (f32[272,128]{1,0:T(8,128)S(1)}, f32[272,128]{1,0:T(8,128)S(1)}, u32[]{:S(2)}, u32[]{:S(2)}) collective-permute-start(f32[272,128]{1,0:T(8,128)S(1)} %get-tuple-element.39), channel_id=1, source_target_pairs={{0,2},{2,0},{4,6},{6,4},{8,10},{10,8},{12,14},{14,12},{1,3},{3,1},... | collective-permute-start | bytes 417800 | tf_op jit(solution)/shard_map/ppermute | solution.py:773
  6.9 6.2 %collective-permute-start.2 = (f32[272,128]{1,0:T(8,128)S(1)}, f32[272,128]{1,0:T(8,128)S(1)}, u32[]{:S(2)}, u32[]{:S(2)}) collective-permute-start(f32[272,128]{1,0:T(8,128)S(1)} %get-tuple-element.40), channel_id=1, source_target_pairs={{2,4},{3,5},{6,8},{7,9},{10,12},{11,13},{4,2},{5,3},{8,6},{9,7},{1... | collective-permute-start | bytes 417800 | tf_op jit(solution)/shard_map/ppermute | solution.py:774
  14.4 5.5 %collective-permute-start.5 = (f32[2,2,32,256]{3,2,1,0:T(8,128)S(1)}, f32[2,2,32,256]{3,2,1,0:T(8,128)S(1)}, u32[]{:S(2)}, u32[]{:S(2)}) collective-permute-start(f32[2,2,32,256]{3,2,1,0:T(8,128)S(1)} %get-tuple-element.48.refs_2_), channel_id=1, source_target_pairs={{0,2},{2,0},{4,6},{6,4},{8,10},{10,8},{12,14},{14,12},{1,3},{3,1},... | collective-permute-start | bytes 393224 | tf_op jit(solution)/shard_map/ppermute | solution.py:820
  20.0 6.8 %collective-permute-start.7 = (f32[2,2,32,256]{3,2,1,0:T(8,128)S(1)}, f32[2,2,32,256]{3,2,1,0:T(8,128)S(1)}, u32[]{:S(2)}, u32[]{:S(2)}) collective-permute-start(f32[2,2,32,256]{3,2,1,0:T(8,128)S(1)} %get-tuple-element.53.refs_2_), channel_id=1, source_target_pairs={{0,4},{2,6},{4,0},{6,2},{8,12},{10,14},{12,8},{14,10},{1,5},{3,7},... | collective-permute-start | bytes 393224 | tf_op jit(solution)/shard_map/ppermute | solution.py:820
  22.1 4.6 %collective-permute-start.4 = (f32[3,32,256]{2,1,0:T(8,128)S(1)}, f32[3,32,256]{2,1,0:T(8,128)S(1)}, u32[]{:S(2)}, u32[]{:S(2)}) collective-permute-start(f32[3,32,256]{2,1,0:T(8,128)S(1)} %get-tuple-element.47), channel_id=1, source_target_pairs={{0,2},{2,0},{4,6},{6,4},{8,10},{10,8},{12,14},{14,12},{1,3},{3,1},... | collective-permute-start | bytes 294920 | tf_op jit(solution)/shard_map/ppermute | solution.py:821
  26.9 10.0 %collective-permute-start.9 = (f32[2,32,256]{2,1,0:T(8,128)S(1)}, f32[2,32,256]{2,1,0:T(8,128)S(1)}, u32[]{:S(2)}, u32[]{:S(2)}) collective-permute-start(f32[2,32,256]{2,1,0:T(8,128)S(1)} %get-tuple-element.58), channel_id=1, source_target_pairs={{0,8},{2,10},{4,12},{6,14},{8,0},{10,2},{12,4},{14,6},{1,9},{3,11}... | collective-permute-start | bytes 196616 | tf_op jit(solution)/shard_map/ppermute | solution.py:820
  29.6 4.6 %collective-permute-start.6 = (f32[3,32,128]{2,1,0:T(8,128)S(1)}, f32[3,32,128]{2,1,0:T(8,128)S(1)}, u32[]{:S(2)}, u32[]{:S(2)}) collective-permute-start(f32[3,32,128]{2,1,0:T(8,128)S(1)} %get-tuple-element.52), channel_id=1, source_target_pairs={{0,4},{2,6},{4,0},{6,2},{8,12},{10,14},{12,8},{14,10},{1,5},{3,7},... | collective-permute-start | bytes 147464 | tf_op jit(solution)/shard_map/ppermute | solution.py:821
  34.2 5.2 %collective-permute-start.8 = (f32[3,32,128]{2,1,0:T(8,128)S(1)}, f32[3,32,128]{2,1,0:T(8,128)S(1)}, u32[]{:S(2)}, u32[]{:S(2)}) collective-permute-start(f32[3,32,128]{2,1,0:T(8,128)S(1)} %shard_map.67.refs_0_), channel_id=1, source_target_pairs={{0,8},{2,10},{4,12},{6,14},{8,0},{10,2},{12,4},{14,6},{1,9},{3,11}... | collective-permute-start | bytes 147464 | tf_op jit(solution)/shard_map/ppermute | solution.py:821
  37.2 3.6 %collective-permute-start.11 = (f32[40,256]{1,0:T(8,128)S(1)}, f32[40,256]{1,0:T(8,128)S(1)}, u32[]{:S(2)}, u32[]{:S(2)}) collective-permute-start(f32[40,256]{1,0:T(8,128)S(1)} %get-tuple-element.72), channel_id=1, source_target_pairs={{0,1},{1,0},{2,3},{3,2},{4,5},{5,4},{6,7},{7,6},{8,9},{9,8},{10,11... | collective-permute-start | bytes 122888 | tf_op jit(solution)/shard_map/ppermute | solution.py:853
  39.5 4.3 %collective-permute-start.10 = (f32[3,32,64]{2,1,0:T(8,128)S(1)}, f32[3,32,64]{2,1,0:T(8,128)S(1)}, u32[]{:S(2)}, u32[]{:S(2)}) collective-permute-start(f32[3,32,64]{2,1,0:T(8,128)S(1)} %get-tuple-element.63), channel_id=1, source_target_pairs={{0,16},{16,0},{1,17},{17,1},{2,18},{18,2},{3,19},{19,3},{4,20},{20... | collective-permute-start | bytes 73736 | tf_op jit(solution)/shard_map/ppermute | solution.py:865
  40.7 3.8 %collective-permute-start.12 = (f32[32,128]{1,0:T(8,128)S(1)}, f32[32,128]{1,0:T(8,128)S(1)}, u32[]{:S(2)}, u32[]{:S(2)}) collective-permute-start(f32[32,128]{1,0:T(8,128)S(1)} %shard_map.75), channel_id=1, source_target_pairs={{0,16},{16,0},{1,17},{17,1},{2,18},{18,2},{3,19},{19,3},{4,20},{20... | collective-permute-start | bytes 49160 | tf_op jit(solution)/shard_map/ppermute | solution.py:855
